TPU v7x, 512 devices: a whole 4x8x8 slice. The times are simulated.
512 devices in a mesh: row: 32 (over z, y_hi, core), col: 16 (over y_lo, x).
Axes of the slice: x: 4, y: 8 (y_hi: 2, y_lo: 4; y = y_hi * 4 + y_lo), z: 8, core: 2. Of those that a mesh axis runs over, the one named last changes fastest.
Arguments:
- patches: bfloat16 [1024, 1024, 256], P('row', 'col'), may hold values from -6 to 6
- norm_gain: float32 [256], replicated, may hold values from 0.1 to 1.9
- w_first: bfloat16 [2, 4, 64, 64], replicated, may hold values from -0.5 to 0.5
- w_second: bfloat16 [2, 4, 64, 64], replicated, may hold values from -0.5 to 0.5
- depth_kernel: float32 [3, 3, 256], replicated, may hold values from -2 to 2
Outputs:
- mixed: bfloat16 [1024, 1024, 256], P('row', 'col')
All inputs are finite; a program needn't handle non-finite values.
Results may differ from a plain program's by a relative error of at most 0.008.
Values may be sent and summed in bfloat16 or wider, within the bound.
No kernel may reach another device: no remote copies, remote signals or barrier semaphores. Data moves between devices by JAX's collectives and lax.ppermute only.
A program may use at most 64 MiB of HBM per device.

v0:
```python
import math

import jax
import jax.numpy as jnp
from jax import lax
from jax.sharding import PartitionSpec as P


def with_halo(shard, sides, width):
    for axis, dim in sides:
        devices, length = (lax.axis_size(axis), shard.shape[dim])
        up = [(i, (i + 1) % devices) for i in range(devices)]
        down = [(j, i) for i, j in up]
        last = lax.slice_in_dim(shard, length - width, length, axis=dim)
        leading = lax.slice_in_dim(shard, 0, width, axis=dim)
        before = lax.ppermute(last, axis, up)
        after = lax.ppermute(leading, axis, down)
        shard = jnp.concatenate([before, shard, after], axis=dim)
    return shard


def phase_table(first_idx, second_idx, length):
    product = first_idx[:, None] * second_idx[None, :] % length
    phase = product.astype(jnp.float32) * (2.0 * math.pi / length)
    return (jnp.cos(phase).astype(jnp.bfloat16), jnp.sin(phase).astype(jnp.bfloat16))


def shrink(values):
    level = 0.25
    return jnp.where(
        values > level, values - level, jnp.where(values < -level, values + level, 0.0 * values)
    )


def block_product(left, weight):
    return jnp.einsum("qmbc,bcd->qmbd", left, weight, preferred_element_type=jnp.float32)


def local(patches, norm_gain, w_first, w_second, depth_kernel):
    n_row = lax.axis_size("row")
    n_col = lax.axis_size("col")
    rows_dev, cols_dev, chans = patches.shape
    patch_grid_height = rows_dev * n_row
    grid_w = cols_dev * n_col
    half = grid_w // 2
    blocks = w_first.shape[1]
    width = w_first.shape[2]
    width_factors = 1.0 / math.sqrt(grid_w)
    height_factors = 1.0 / math.sqrt(patch_grid_height)
    xf = patches.astype(jnp.float32)
    mean = jnp.mean(xf, axis=-1, keepdims=True)
    var = jnp.mean((xf - mean) ** 2, axis=-1, keepdims=True)
    normed = ((xf - mean) * lax.rsqrt(var + 1e-05) * norm_gain).astype(jnp.bfloat16)
    padded = with_halo(normed, (("row", 0), ("col", 1)), 1)
    conv = jnp.zeros((rows_dev, cols_dev, chans), jnp.float32)
    for i in range(3):
        for j in range(3):
            conv = conv + padded[i : i + rows_dev, j : j + cols_dev] * depth_kernel[i, j]
    strips = lax.all_to_all(normed, "col", split_axis=0, concat_axis=1, tiled=True)
    cos_w, sin_w = phase_table(
        jnp.arange(grid_w, dtype=jnp.int32), jnp.arange(half, dtype=jnp.int32), grid_w
    )
    forward_w = jnp.concatenate([cos_w, -sin_w], axis=1)
    spectrum_values = jnp.einsum(
        "hwc,wk->hkc", strips, forward_w, preferred_element_type=jnp.float32
    )
    spectrum_values = (spectrum_values * width_factors).astype(jnp.bfloat16)
    wre = spectrum_values[:, :half]
    wim = spectrum_values[:, half:]
    positions = jnp.arange(patch_grid_height, dtype=jnp.int32)
    across_re, across_im = (
        lax.all_to_all(wre, "col", split_axis=1, concat_axis=0, tiled=True),
        lax.all_to_all(wim, "col", split_axis=1, concat_axis=0, tiled=True),
    )
    full_re, full_im = (
        lax.all_to_all(across_re, "row", split_axis=1, concat_axis=0, tiled=True),
        lax.all_to_all(across_im, "row", split_axis=1, concat_axis=0, tiled=True),
    )
    cos_h, sin_h = phase_table(positions, positions, patch_grid_height)
    big_table = jnp.concatenate(
        [jnp.concatenate([cos_h, sin_h], axis=1), jnp.concatenate([-sin_h, cos_h], axis=1)], axis=0
    )
    stacked = jnp.concatenate([full_re, full_im], axis=0)
    spectrum = jnp.einsum("qp,pmc->qmc", big_table, stacked, preferred_element_type=jnp.float32)
    spectrum = (spectrum * height_factors).astype(jnp.bfloat16)
    modes = spectrum.shape[1]
    zre = spectrum[:patch_grid_height].reshape(patch_grid_height, modes, blocks, width)
    zim = spectrum[patch_grid_height:].reshape(patch_grid_height, modes, blocks, width)
    hre = jnp.tanh(block_product(zre, w_first[0]) - block_product(zim, w_first[1])).astype(
        jnp.bfloat16
    )
    him = jnp.tanh(block_product(zre, w_first[1]) + block_product(zim, w_first[0])).astype(
        jnp.bfloat16
    )
    spectrum_real = shrink(
        block_product(hre, w_second[0]) - block_product(him, w_second[1])
    ).astype(jnp.bfloat16)
    spectrum_imaginary = shrink(
        block_product(hre, w_second[1]) + block_product(him, w_second[0])
    ).astype(jnp.bfloat16)
    filtered = jnp.concatenate(
        [
            spectrum_real.reshape(patch_grid_height, modes, chans),
            spectrum_imaginary.reshape(patch_grid_height, modes, chans),
        ],
        axis=0,
    )
    inverse_transform = jnp.einsum(
        "qp,qmc->pmc", big_table, filtered, preferred_element_type=jnp.float32
    )
    inverse_transform = (inverse_transform * height_factors).astype(jnp.bfloat16)
    value_real = inverse_transform[:patch_grid_height]
    value_imaginary = inverse_transform[patch_grid_height:]
    part_re, part_im = (
        lax.all_to_all(value_real, "row", split_axis=0, concat_axis=1, tiled=True),
        lax.all_to_all(value_imaginary, "row", split_axis=0, concat_axis=1, tiled=True),
    )
    line_re, line_im = (
        lax.all_to_all(part_re, "col", split_axis=0, concat_axis=1, tiled=True),
        lax.all_to_all(part_im, "col", split_axis=0, concat_axis=1, tiled=True),
    )
    filter_coefficient = jnp.where(jnp.arange(half) == 0, 1.0, 2.0).astype(jnp.float32)
    inverse_w = jnp.concatenate(
        [
            (cos_w.astype(jnp.float32) * filter_coefficient).T,
            -(sin_w.astype(jnp.float32) * filter_coefficient).T,
        ],
        axis=0,
    ).astype(jnp.bfloat16)
    lines = jnp.concatenate([line_re, line_im], axis=1)
    spectral = jnp.einsum("hkc,kw->hwc", lines, inverse_w, preferred_element_type=jnp.float32)
    spectral = (spectral * width_factors).astype(jnp.bfloat16)
    home = lax.all_to_all(spectral, "col", split_axis=1, concat_axis=0, tiled=True)
    return (xf + home.astype(jnp.float32) + conv).astype(jnp.bfloat16)


def solution(mesh):
    return jax.shard_map(
        local,
        mesh=mesh,
        in_specs=(P("row", "col", None), P(), P(), P(), P()),
        out_specs=P("row", "col", None),
        check_vma=False,
    )
```

profile of v0, /device:TPU:63, one launch (start us, length us, event | category | flops | bytes accessed | tf_op | source)
XLA Modules:
  0.0 328.7 jit_solution(4939369207946088311)
XLA Ops:
  5.1 6.9 %all-to-all-start = ((bf16[32,64,256]{2,1,0:T(8,128)(2,1)}), bf16[32,64,256]{2,1,0:T(8,128)(2,1)S(1)}, u32[]{:S(2)}, u32[]{:S(2)}) async-start(bf16[32,64,256]{2,1,0:T(8,128)(2,1)} %fusion.12), calls=%async_computation | async-start | bytes 2097152 | tf_op jit(solution)/shard_map/all_to_all | solution.py:59
  12.1 7.8 %cosine_convert_fusion.1 = bf16[1024,512]{0,1:T(8,128)(2,1)S(1)} fusion(), kind=kLoop, calls=%fused_computation.50 | loop fusion | flops 7864320 | bytes 1048576 | tf_op jit(solution)/shard_map/convert_element_type | solution.py:25
  19.8 8.6 %fusion.41 = bf16[1024,512]{0,1:T(8,128)(2,1)} fusion(), kind=kLoop, calls=%fused_computation.75 | loop fusion | flops 9437184 | bytes 1048576 | tf_op jit(solution)/shard_map/neg | solution.py:63
  28.4 6.1 %all-to-all-done = bf16[32,64,256]{2,1,0:T(8,128)(2,1)S(1)} async-done(((bf16[32,64,256]{2,1,0:T(8,128)(2,1)}), bf16[32,64,256]{2,1,0:T(8,128)(2,1)S(1)}, u32[]{:S(2)}, u32[]{:S(2)}) %all-to-all-start) | async-done | bytes 1048608 | tf_op jit(solution)/shard_map/all_to_all | solution.py:59
  38.4 7.4 %all-to-all-start.1 = ((bf16[2,512,256]{2,0,1:T(2,128)(2,1)}), bf16[2,512,256]{2,0,1:T(2,128)(2,1)S(1)}, u32[]{:S(2)}, u32[]{:S(2)}) async-start(bf16[2,512,256]{2,0,1:T(2,128)(2,1)} %copy.51), calls=%async_computation.1 | async-start | bytes 1048576 | tf_op jit(solution)/shard_map/all_to_all | solution.py:72
  47.1 10.5 %all-to-all-done.1 = bf16[2,512,256]{2,0,1:T(2,128)(2,1)S(1)} async-done(((bf16[2,512,256]{2,0,1:T(2,128)(2,1)}), bf16[2,512,256]{2,0,1:T(2,128)(2,1)S(1)}, u32[]{:S(2)}, u32[]{:S(2)}) %all-to-all-start.1) | async-done | bytes 524320 | tf_op jit(solution)/shard_map/all_to_all | solution.py:72
  57.7 6.7 %all-to-all-start.3 = ((bf16[2,512,256]{2,0,1:T(2,128)(2,1)}), bf16[2,512,256]{2,0,1:T(2,128)(2,1)S(1)}, u32[]{:S(2)}, u32[]{:S(2)}) async-start(bf16[2,512,256]{2,0,1:T(2,128)(2,1)} %copy.55), calls=%async_computation.3 | async-start | bytes 1048576 | tf_op jit(solution)/shard_map/all_to_all | solution.py:73
  65.5 10.0 %all-to-all-done.3 = bf16[2,512,256]{2,0,1:T(2,128)(2,1)S(1)} async-done(((bf16[2,512,256]{2,0,1:T(2,128)(2,1)}), bf16[2,512,256]{2,0,1:T(2,128)(2,1)S(1)}, u32[]{:S(2)}, u32[]{:S(2)}) %all-to-all-start.3) | async-done | bytes 524320 | tf_op jit(solution)/shard_map/all_to_all | solution.py:73
  75.5 17.7 %all-to-all-start.2 = ((bf16[32,32,256]{2,0,1:T(8,128)(2,1)}), bf16[32,32,256]{2,0,1:T(8,128)(2,1)S(1)}, u32[]{:S(2)}, u32[]{:S(2)}) async-start(bf16[32,32,256]{2,0,1:T(8,128)(2,1)} %copy.54), calls=%async_computation.2 | async-start | bytes 1048576 | tf_op jit(solution)/shard_map/all_to_all | solution.py:76
  94.4 16.0 %all-to-all-done.2 = bf16[32,32,256]{2,0,1:T(8,128)(2,1)S(1)} async-done(((bf16[32,32,256]{2,0,1:T(8,128)(2,1)}), bf16[32,32,256]{2,0,1:T(8,128)(2,1)S(1)}, u32[]{:S(2)}, u32[]{:S(2)}) %all-to-all-start.2) | async-done | bytes 524320 | tf_op jit(solution)/shard_map/all_to_all | solution.py:76
  111.2 8.0 %all-to-all-start.4 = ((bf16[32,32,256]{2,0,1:T(8,128)(2,1)}), bf16[32,32,256]{2,0,1:T(8,128)(2,1)}, u32[]{:S(2)}, u32[]{:S(2)}) async-start(bf16[32,32,256]{2,0,1:T(8,128)(2,1)} %copy.58), calls=%async_computation.4 | async-start | bytes 1048576 | tf_op jit(solution)/shard_map/all_to_all | solution.py:77
  119.2 15.8 %fusion.49 = bf16[1024,1024]{1,0:T(8,128)(2,1)S(1)} fusion(), kind=kLoop, calls=%fused_computation.89 | loop fusion | flops 18874368 | bytes 2097152 | tf_op jit(solution)/shard_map/neg | solution.py:81
  135.1 17.7 %sine_convert_fusion = (bf16[1024,1024]{1,0:T(8,128)(2,1)}, bf16[1024,1024]{1,0:T(8,128)(2,1)}) fusion(), kind=kLoop, calls=%fused_computation.7 | loop fusion | flops 16777216 | bytes 4194304 | tf_op jit(solution)/shard_map/convert_element_type | solution.py:25
  152.8 14.9 %fusion.6 = bf16[2048,256]{0,1:T(8,128)(2,1)S(1)} fusion(bf16[1024,1024]{1,0:T(8,128)(2,1)} %get-tuple-element.29, bf16[1024,1024]{1,0:T(8,128)(2,1)S(1)} %fusion.49, bf16[1024,1024]{1,0:T(8,128)(2,1)} %get-tuple-element.28, bf16[1024,1,256]{2,0,1:T(8,128)(2,1)} %bitcast.17, bf16[1024,1,256]{2,0,1:T(8,128)(2,1)} %bitcast.166), kind=kOutput, calls=%fused_computation.23 | convolution fusion | flops 2184183808 | bytes 8388608 | tf_op jit(solution)/shard_map/qp,pmc->qmc/dot_general | solution.py:84
  173.1 2.4 fusion.7
  178.2 12.2 %all-to-all-start.5 = ((bf16[32,2,4096]{2,1,0:T(2,128)(2,1)}), bf16[32,2,4096]{2,1,0:T(2,128)(2,1)S(1)}, u32[]{:S(2)}, u32[]{:S(2)}) async-start(bf16[32,2,4096]{2,1,0:T(2,128)(2,1)} %reshape.124), calls=%async_computation.5 | async-start | bytes 1048576 | tf_op jit(solution)/shard_map/all_to_all | solution.py:115
  192.6 14.9 %all-to-all-done.5 = bf16[32,2,4096]{2,1,0:T(2,128)(2,1)S(1)} async-done(((bf16[32,2,4096]{2,1,0:T(2,128)(2,1)}), bf16[32,2,4096]{2,1,0:T(2,128)(2,1)S(1)}, u32[]{:S(2)}, u32[]{:S(2)}) %all-to-all-start.5) | async-done | bytes 524320 | tf_op jit(solution)/shard_map/all_to_all | solution.py:115
  207.5 8.0 %all-to-all-start.7 = ((bf16[32,2,4096]{2,1,0:T(2,128)(2,1)}), bf16[32,2,4096]{2,1,0:T(2,128)(2,1)S(1)}, u32[]{:S(2)}, u32[]{:S(2)}) async-start(bf16[32,2,4096]{2,1,0:T(2,128)(2,1)} %reshape.122), calls=%async_computation.7 | async-start | bytes 1048576 | tf_op jit(solution)/shard_map/all_to_all | solution.py:116
  217.3 15.3 %all-to-all-done.7 = bf16[32,2,4096]{2,1,0:T(2,128)(2,1)S(1)} async-done(((bf16[32,2,4096]{2,1,0:T(2,128)(2,1)}), bf16[32,2,4096]{2,1,0:T(2,128)(2,1)S(1)}, u32[]{:S(2)}, u32[]{:S(2)}) %all-to-all-start.7) | async-done | bytes 524320 | tf_op jit(solution)/shard_map/all_to_all | solution.py:116
  232.6 7.9 %all-to-all-start.6 = ((bf16[32,32,256]{2,1,0:T(8,128)(2,1)}), bf16[32,32,256]{2,1,0:T(8,128)(2,1)S(1)}, u32[]{:S(2)}, u32[]{:S(2)}) async-start(bf16[32,32,256]{2,1,0:T(8,128)(2,1)} %copy.65), calls=%async_computation.6 | async-start | bytes 1048576 | tf_op jit(solution)/shard_map/all_to_all | solution.py:119
  242.2 10.2 %all-to-all-done.6 = bf16[32,32,256]{2,1,0:T(8,128)(2,1)S(1)} async-done(((bf16[32,32,256]{2,1,0:T(8,128)(2,1)}), bf16[32,32,256]{2,1,0:T(8,128)(2,1)S(1)}, u32[]{:S(2)}, u32[]{:S(2)}) %all-to-all-start.6) | async-done | bytes 524320 | tf_op jit(solution)/shard_map/all_to_all | solution.py:119
  252.4 6.9 %all-to-all-start.8 = ((bf16[32,32,256]{2,1,0:T(8,128)(2,1)}), bf16[32,32,256]{2,1,0:T(8,128)(2,1)S(1)}, u32[]{:S(2)}, u32[]{:S(2)}) async-start(bf16[32,32,256]{2,1,0:T(8,128)(2,1)} %copy.68), calls=%async_computation.8 | async-start | bytes 1048576 | tf_op jit(solution)/shard_map/all_to_all | solution.py:120
  259.3 9.4 %multiply_convert_fusion.2 = (bf16[512,1024]{0,1:T(8,128)(2,1)S(1)}, bf16[512,1024]{0,1:T(8,128)(2,1)}) fusion(f32[512]{0:T(512)S(1)} %fusion.70), kind=kLoop, calls=%fused_computation.55 | loop fusion | flops 12058624 | bytes 2099200 | tf_op jit(solution)/shard_map/convert.7
  271.1 2.6 fusion.34
  275.7 6.8 %all-to-all-start.9 = ((bf16[2,1024,256]{2,0,1:T(2,128)(2,1)}), bf16[2,1024,256]{2,0,1:T(2,128)(2,1)}, u32[]{:S(2)}, u32[]{:S(2)}) async-start(bf16[2,1024,256]{2,0,1:T(2,128)(2,1)} %copy.70), calls=%async_computation.9 | async-start | bytes 2097152 | tf_op jit(solution)/shard_map/all_to_all | solution.py:133
  283.3 8.8 %collective-permute-start = (bf16[1,64,256]{2,1,0:T(8,128)(2,1)S(1)}, bf16[1,64,256]{2,1,0:T(8,128)(2,1)S(1)}, u32[]{:S(2)}, u32[]{:S(2)}) collective-permute-start(bf16[1,64,256]{2,1,0:T(8,128)(2,1)S(1)} %get-tuple-element.9), channel_id=1, source_target_pairs={{0,16},{16,32},{32,48},{48,64},{64,80},{80,96},{96,112},{112,128},... | collective-permute-start | bytes 98312 | tf_op jit(solution)/shard_map/ppermute | solution.py:16
  294.1 4.3 %collective-permute-done = bf16[1,64,256]{2,1,0:T(8,128)(2,1)S(1)} collective-permute-done((bf16[1,64,256]{2,1,0:T(8,128)(2,1)S(1)}, bf16[1,64,256]{2,1,0:T(8,128)(2,1)S(1)}, u32[]{:S(2)}, u32[]{:S(2)}) %collective-permute-start) | collective-permute-done | bytes 32800 | tf_op jit(solution)/shard_map/ppermute | solution.py:16
  298.4 8.2 %collective-permute-done.1 = bf16[1,64,256]{2,1,0:T(8,128)(2,1)S(1)} collective-permute-done((bf16[1,64,256]{2,1,0:T(8,128)(2,1)S(1)}, bf16[1,64,256]{2,1,0:T(8,128)(2,1)S(1)}, u32[]{:S(2)}, u32[]{:S(2)}) %collective-permute-start.1) | collective-permute-done | bytes 32800 | tf_op jit(solution)/shard_map/ppermute | solution.py:17
  309.6 3.6 %collective-permute-start.3 = (bf16[34,1,256]{2,1,0:T(2,128)(2,1)S(1)}, bf16[34,1,256]{2,1,0:T(2,128)(2,1)S(1)}, u32[]{:S(2)}, u32[]{:S(2)}) collective-permute-start(bf16[34,1,256]{2,1,0:T(2,128)(2,1)S(1)} %get-tuple-element.8), channel_id=1, source_target_pairs={{1,0},{2,1},{3,2},{4,3},{5,4},{6,5},{7,6},{8,7},{9,8},{10,9},{11,1... | collective-permute-start | bytes 52232 | tf_op jit(solution)/shard_map/ppermute | solution.py:17
  313.8 4.3 %collective-permute-done.3 = bf16[34,1,256]{2,1,0:T(2,128)(2,1)S(1)} collective-permute-done((bf16[34,1,256]{2,1,0:T(2,128)(2,1)S(1)}, bf16[34,1,256]{2,1,0:T(2,128)(2,1)S(1)}, u32[]{:S(2)}, u32[]{:S(2)}) %collective-permute-start.3) | collective-permute-done | bytes 17440 | tf_op jit(solution)/shard_map/ppermute | solution.py:17
  318.2 2.3 maximum_maximum_fusion.3
  323.4 5.2 %fusion.14 = bf16[32,64,256]{2,1,0:T(8,128)(2,1)} fusion(bf16[32,64,256]{2,1,0:T(8,128)(2,1)S(1)} %copy-done, f32[16,2,64,256]{3,2,1,0:T(8,128)S(1)} %copy.71, bf16[32,64,256]{2,1,0:T(8,128)(2,1)} %fusion.12, bf16[34,65,256]{2,1,0:T(8,128)(2,1)S(1)} %get-tuple-element.6, bf16[1,64,256]{2,1,0:T(8,128)(2,1)S(1)} %copy-done.9, ...), kind=kLoop, calls=%fused_computation.31 | loop fusion | flops 16777216 | bytes 11609088 | tf_op jit(solution)/shard_map/convert_element_type | solution.py:134
  (98 shorter events, 40.6 us)
Async XLA Ops:
  0.0 3.6 %copy-start = (bf16[32,64,256]{2,1,0:T(8,128)(2,1)S(1)}, bf16[32,64,256]{2,1,0:T(8,128)(2,1)}, u32[]{:S(2)}) copy-start(bf16[32,64,256]{2,1,0:T(8,128)(2,1)} %param.5) | copy-start | bytes 3145732
  0.0 3.6 %copy-start.21 = (f32[256]{0:T(256)S(1)}, f32[256]{0:T(256)}, u32[]{:S(2)}) copy-start(f32[256]{0:T(256)} %param.6) | copy-start | bytes 3076
  5.1 29.4 %all-to-all-start = ((bf16[32,64,256]{2,1,0:T(8,128)(2,1)}), bf16[32,64,256]{2,1,0:T(8,128)(2,1)S(1)}, u32[]{:S(2)}, u32[]{:S(2)}) async-start(bf16[32,64,256]{2,1,0:T(8,128)(2,1)} %fusion.12), calls=%async_computation | async-start | bytes 2097152 | tf_op jit(solution)/shard_map/all_to_all | solution.py:59
  34.5 1.2 copy-start.3
  38.4 19.3 %all-to-all-start.1 = ((bf16[2,512,256]{2,0,1:T(2,128)(2,1)}), bf16[2,512,256]{2,0,1:T(2,128)(2,1)S(1)}, u32[]{:S(2)}, u32[]{:S(2)}) async-start(bf16[2,512,256]{2,0,1:T(2,128)(2,1)} %copy.51), calls=%async_computation.1 | async-start | bytes 1048576 | tf_op jit(solution)/shard_map/all_to_all | solution.py:72
  57.7 17.8 %all-to-all-start.3 = ((bf16[2,512,256]{2,0,1:T(2,128)(2,1)}), bf16[2,512,256]{2,0,1:T(2,128)(2,1)S(1)}, u32[]{:S(2)}, u32[]{:S(2)}) async-start(bf16[2,512,256]{2,0,1:T(2,128)(2,1)} %copy.55), calls=%async_computation.3 | async-start | bytes 1048576 | tf_op jit(solution)/shard_map/all_to_all | solution.py:73
  75.5 34.8 %all-to-all-start.2 = ((bf16[32,32,256]{2,0,1:T(8,128)(2,1)}), bf16[32,32,256]{2,0,1:T(8,128)(2,1)S(1)}, u32[]{:S(2)}, u32[]{:S(2)}) async-start(bf16[32,32,256]{2,0,1:T(8,128)(2,1)} %copy.54), calls=%async_computation.2 | async-start | bytes 1048576 | tf_op jit(solution)/shard_map/all_to_all | solution.py:76
  110.3 0.8 copy-start.5
  111.2 41.6 %all-to-all-start.4 = ((bf16[32,32,256]{2,0,1:T(8,128)(2,1)}), bf16[32,32,256]{2,0,1:T(8,128)(2,1)}, u32[]{:S(2)}, u32[]{:S(2)}) async-start(bf16[32,32,256]{2,0,1:T(8,128)(2,1)} %copy.58), calls=%async_computation.4 | async-start | bytes 1048576 | tf_op jit(solution)/shard_map/all_to_all | solution.py:77
  167.6 0.9 copy-start.4
  168.9 0.9 copy-start.10
  170.8 1.6 copy-start.1
  170.9 2.2 copy-start.2
  178.2 29.3 %all-to-all-start.5 = ((bf16[32,2,4096]{2,1,0:T(2,128)(2,1)}), bf16[32,2,4096]{2,1,0:T(2,128)(2,1)S(1)}, u32[]{:S(2)}, u32[]{:S(2)}) async-start(bf16[32,2,4096]{2,1,0:T(2,128)(2,1)} %reshape.124), calls=%async_computation.5 | async-start | bytes 1048576 | tf_op jit(solution)/shard_map/all_to_all | solution.py:115
  207.5 25.1 %all-to-all-start.7 = ((bf16[32,2,4096]{2,1,0:T(2,128)(2,1)}), bf16[32,2,4096]{2,1,0:T(2,128)(2,1)S(1)}, u32[]{:S(2)}, u32[]{:S(2)}) async-start(bf16[32,2,4096]{2,1,0:T(2,128)(2,1)} %reshape.122), calls=%async_computation.7 | async-start | bytes 1048576 | tf_op jit(solution)/shard_map/all_to_all | solution.py:116
  232.6 19.8 %all-to-all-start.6 = ((bf16[32,32,256]{2,1,0:T(8,128)(2,1)}), bf16[32,32,256]{2,1,0:T(8,128)(2,1)S(1)}, u32[]{:S(2)}, u32[]{:S(2)}) async-start(bf16[32,32,256]{2,1,0:T(8,128)(2,1)} %copy.65), calls=%async_computation.6 | async-start | bytes 1048576 | tf_op jit(solution)/shard_map/all_to_all | solution.py:119
  252.4 18.6 %all-to-all-start.8 = ((bf16[32,32,256]{2,1,0:T(8,128)(2,1)}), bf16[32,32,256]{2,1,0:T(8,128)(2,1)S(1)}, u32[]{:S(2)}, u32[]{:S(2)}) async-start(bf16[32,32,256]{2,1,0:T(8,128)(2,1)} %copy.68), calls=%async_computation.8 | async-start | bytes 1048576 | tf_op jit(solution)/shard_map/all_to_all | solution.py:120
  275.7 37.5 %copy-start.11 = (f32[3,3,256]{2,1,0:T(4,128)S(1)}, f32[3,3,256]{2,1,0:T(4,128)}, u32[]{:S(2)}) copy-start(f32[3,3,256]{2,1,0:T(4,128)} %param.9) | copy-start | bytes 27652
  275.7 44.7 %all-to-all-start.9 = ((bf16[2,1024,256]{2,0,1:T(2,128)(2,1)}), bf16[2,1024,256]{2,0,1:T(2,128)(2,1)}, u32[]{:S(2)}, u32[]{:S(2)}) async-start(bf16[2,1024,256]{2,0,1:T(2,128)(2,1)} %copy.70), calls=%async_computation.9 | async-start | bytes 2097152 | tf_op jit(solution)/shard_map/all_to_all | solution.py:133
  283.3 15.0 %collective-permute-start = (bf16[1,64,256]{2,1,0:T(8,128)(2,1)S(1)}, bf16[1,64,256]{2,1,0:T(8,128)(2,1)S(1)}, u32[]{:S(2)}, u32[]{:S(2)}) collective-permute-start(bf16[1,64,256]{2,1,0:T(8,128)(2,1)S(1)} %get-tuple-element.9), channel_id=1, source_target_pairs={{0,16},{16,32},{32,48},{48,64},{64,80},{80,96},{96,112},{112,128},... | collective-permute-start | bytes 98312 | tf_op jit(solution)/shard_map/ppermute | solution.py:16
  292.2 14.4 %collective-permute-start.1 = (bf16[1,64,256]{2,1,0:T(8,128)(2,1)S(1)}, bf16[1,64,256]{2,1,0:T(8,128)(2,1)S(1)}, u32[]{:S(2)}, u32[]{:S(2)}) collective-permute-start(bf16[1,64,256]{2,1,0:T(8,128)(2,1)S(1)} %get-tuple-element.10), channel_id=1, source_target_pairs={{16,0},{32,16},{48,32},{64,48},{80,64},{96,80},{112,96},{128,112},... | collective-permute-start | bytes 98312 | tf_op jit(solution)/shard_map/ppermute | solution.py:17
  298.4 19.8 %copy-start.6 = (bf16[1,64,256]{2,1,0:T(8,128)(2,1)}, bf16[1,64,256]{2,1,0:T(8,128)(2,1)S(1)}, u32[]{:S(2)}) copy-start(bf16[1,64,256]{2,1,0:T(8,128)(2,1)S(1)} %collective-permute-done) | copy-start | bytes 98308
  306.6 11.6 %copy-start.8 = (bf16[1,64,256]{2,1,0:T(8,128)(2,1)}, bf16[1,64,256]{2,1,0:T(8,128)(2,1)S(1)}, u32[]{:S(2)}) copy-start(bf16[1,64,256]{2,1,0:T(8,128)(2,1)S(1)} %collective-permute-done.1) | copy-start | bytes 98308
  307.6 6.2 %collective-permute-start.2 = (bf16[34,1,256]{2,1,0:T(2,128)(2,1)S(1)}, bf16[34,1,256]{2,1,0:T(2,128)(2,1)S(1)}, u32[]{:S(2)}, u32[]{:S(2)}) collective-permute-start(bf16[34,1,256]{2,1,0:T(2,128)(2,1)S(1)} %get-tuple-element.7), channel_id=1, source_target_pairs={{0,1},{1,2},{2,3},{3,4},{4,5},{5,6},{6,7},{7,8},{8,9},{9,10},{10,1... | collective-permute-start | bytes 52232 | tf_op jit(solution)/shard_map/ppermute | solution.py:16
  309.6 8.6 %collective-permute-start.3 = (bf16[34,1,256]{2,1,0:T(2,128)(2,1)S(1)}, bf16[34,1,256]{2,1,0:T(2,128)(2,1)S(1)}, u32[]{:S(2)}, u32[]{:S(2)}) collective-permute-start(bf16[34,1,256]{2,1,0:T(2,128)(2,1)S(1)} %get-tuple-element.8), channel_id=1, source_target_pairs={{1,0},{2,1},{3,2},{4,3},{5,4},{6,5},{7,6},{8,7},{9,8},{10,9},{11,1... | collective-permute-start | bytes 52232 | tf_op jit(solution)/shard_map/ppermute | solution.py:17
  322.6 0.8 copy-start.7
  322.6 0.8 copy-start.9
  322.6 0.8 copy-start.12
  322.6 0.8 copy-start.13
  322.6 0.7 copy-start.14
  322.7 0.7 copy-start.15
  322.7 0.7 copy-start.16
  (4 other events, 2.9 us)
where the time goes:
time: 330 us; the launch traced here: 329 us
  starting transfers between devices  105 us (32%)
  waiting for transfers between devices  101 us (31%)
  other arithmetic  77.1 us (23%)
  matrix products  24.2 us (7%)
  local copies, waits for them, and re-layouts  20.7 us (6%)
    convert_element_type x1, other arithmetic, phase_table(): jnp.sin(phase).astype(jnp.bfloat16)  17.7 us
    all_to_all x1, starting transfers between devices, local(): lax.all_to_all(across_re, 'row', split_axis=1, concat_axis=0, tiled=True)  17.7 us
    all_to_all x1, waiting for transfers between devices, local(): lax.all_to_all(across_re, 'row', split_axis=1, concat_axis=0, tiled=True)  16 us
    neg x1, other arithmetic, local(): -sin_h  15.8 us
    all_to_all x1, waiting for transfers between devices, local(): lax.all_to_all(value_imaginary, 'row', split_axis=0, concat_axis=1, tiled...  15.3 us
    all_to_all x1, waiting for transfers between devices, local(): lax.all_to_all(value_real, 'row', split_axis=0, concat_axis=1, tiled=True)  14.9 us
    dot_general x1, matrix products, local(): jnp.einsum('qp,pmc->qmc', big_table, stacked, preferred_element_type=jnp....  14.9 us
    ppermute x2, waiting for transfers between devices, with_halo(): after = lax.ppermute(leading, axis, down)  12.5 us
  transfers between devices with their start and end apart: 14, of which 11 were waited for; matrix products, arithmetic and copies ran while one was open for 23% of the time, Pallas kernels for 0%

commit v1 on v0

v1 whole, which is shorter than its diff:
```python
import math

import jax
import jax.numpy as jnp
import numpy as np
from jax import lax
from jax.experimental import pallas as pl
from jax.experimental.pallas import tpu as pltpu
from jax.sharding import Mesh
from jax.sharding import PartitionSpec as P

TURN = 1024
CHUNKS = 2
F32 = jnp.float32
BF16 = jnp.bfloat16


def cos_of(idx):
    return jnp.cos((idx % TURN).astype(F32) * (2.0 * math.pi / TURN))


def sin_of(idx):
    return jnp.sin((idx % TURN).astype(F32) * (2.0 * math.pi / TURN))


def outer_table(e1, e2, f1, f2):
    e1, e2, f1, f2 = lax.optimization_barrier((e1, e2, f1, f2))
    out = e1[:, None, :] * f1[None] + e2[:, None, :] * f2[None]
    return out.astype(BF16).reshape(e1.shape[0] * f1.shape[0], e1.shape[1])


def phase_table(ia, ib, scale):
    return outer_table(cos_of(ia), sin_of(ia), cos_of(ib) * scale, -sin_of(ib) * scale)


def column(values):
    return jnp.asarray(values, jnp.int32)[:, None]


def split(idx, *sizes):
    out = []
    for s in reversed(sizes):
        out.append(idx % s)
        idx = idx // s
    return out[::-1]


def make_tables():
    lane = jnp.arange(1024, dtype=jnp.int32)[None, :]
    scale = 1.0 / 32.0
    a16 = jnp.arange(16, dtype=jnp.int32)[:, None]
    b64 = jnp.arange(64, dtype=jnp.int32)[:, None]
    pl_, ri, i = split(b64, 8, 2, 4)
    fwd_w = phase_table(32 * a16 * lane, (4 * pl_ + i) * lane + 256 * ri, scale)
    p, lri, li = split(lane, 128, 2, 4)
    k = 4 * p + li
    weight = jnp.where(k == 0, 1.0, 2.0).astype(F32) * scale
    inv_w = phase_table(64 * a16 * k, b64 * k + 256 * lri, weight)
    qhh, ro, qhl = split(a16, CHUNKS, 2, 8 // CHUNKS)
    qh = qhh * (8 // CHUNKS) + qhl
    bi, ql = split(b64, 4, 16)
    mask = jnp.where(bi == li, scale, 0.0).astype(F32)
    fwd_h = phase_table(128 * qh * p + 256 * (ro - lri), 8 * ql * p, mask)
    lqhh, lro, lqhl, lli, lql = split(lane, CHUNKS, 2, 8 // CHUNKS, 4, 16)
    lq0 = 16 * (lqhh * (8 // CHUNKS) + lqhl) + lql
    mask_t = jnp.where(i == lli, scale, 0.0).astype(F32)
    inv_h = phase_table(64 * a16 * lq0, 8 * pl_ * lq0 + 256 * (lro - ri), mask_t)
    t, gri, e = split(a16, 4, 2, 2)
    gro, gh8, gc = split(lane, 2, 8, 64)
    e1 = cos_of(128 * (2 * t + e) * gh8 - 256 * (gro - gri))
    eye = jnp.where(b64 == gc, 1.0, 0.0).astype(F32)
    e1, eye = lax.optimization_barrier((e1, eye))
    eight = (e1[:, None, :] * eye[None]).astype(BF16).reshape(1024, 1024)
    q0 = jnp.arange(128, dtype=jnp.int32)[:, None]
    h8 = jnp.arange(512, dtype=jnp.int32)[None, :] // 64
    return fwd_w, inv_w, fwd_h, inv_h, eight, cos_of(q0 * h8), sin_of(q0 * h8)


def first_layer(w0, w1):
    lane = jnp.arange(1024, dtype=jnp.int32)[None, :]
    ri, h8 = split(jnp.arange(16, dtype=jnp.int32)[:, None], 2, 8)
    t, ro, e, _ = split(lane, 4, 2, 2, 64)
    angle = 128 * (2 * t + e) * h8 + 256 * (ro - ri)
    return outer_table(
        cos_of(angle), sin_of(angle), jnp.tile(w0.astype(F32), (1, 16)), jnp.tile(w1.astype(F32), (1, 16))
    )


def second_layer(w0, w1):
    z = jnp.zeros_like(w0)
    b0 = jnp.block([[w0, z], [z, w0]])
    b1 = jnp.block([[w1, z], [z, w1]])
    return jnp.block([[b0, b1], [-b1, b0]])


def norm_kernel(x_ref, gain_ref, normed_ref, packed_ref):
    low = lax.broadcasted_iota(jnp.int32, (64, 128), 1) < 64

    def normed_row(h):
        xf = x_ref[h].astype(F32)
        mean = jnp.mean(xf, axis=-1, keepdims=True)
        d = xf - mean
        var = jnp.mean(d * d, axis=-1, keepdims=True)
        return d * lax.rsqrt(var + 1e-05) * gain_ref[...]

    for t in range(4):
        a, b = normed_row(2 * t), normed_row(2 * t + 1)
        normed_ref[2 * t] = a.astype(BF16)
        normed_ref[2 * t + 1] = b.astype(BF16)
        lanes = slice(128 * t, 128 * t + 128)
        for m in range(2):
            am, bm = a[:, 128 * m : 128 * m + 128], b[:, 128 * m : 128 * m + 128]
            ar, br = pltpu.roll(am, 64, 1), pltpu.roll(bm, 64, 1)
            packed_ref[2 * m, :, lanes] = jnp.where(low, am, br).astype(BF16)
            packed_ref[2 * m + 1, :, lanes] = jnp.where(low, ar, bm).astype(BF16)


def norm_and_pack(patches, gain):
    return pl.pallas_call(
        norm_kernel,
        grid=(4,),
        in_specs=[
            pl.BlockSpec((8, 64, 256), lambda g: (g, 0, 0)),
            pl.BlockSpec((1, 256), lambda g: (0, 0)),
        ],
        out_specs=[
            pl.BlockSpec((8, 64, 256), lambda g: (g, 0, 0)),
            pl.BlockSpec((4, 64, 512), lambda g: (g, 0, 0)),
        ],
        out_shape=[
            jax.ShapeDtypeStruct((32, 64, 256), BF16),
            jax.ShapeDtypeStruct((16, 64, 512), BF16),
        ],
        name="norm_pack",
    )(patches, gain.reshape(1, 256))


def final_kernel(base_ref, home_ref, out_ref):
    low = lax.broadcasted_iota(jnp.int32, (64, 128), 1) < 64
    for t in range(4):
        lanes = slice(128 * t, 128 * t + 128)
        for m in range(2):
            u = home_ref[2 * m, :, lanes].astype(F32)
            v = home_ref[2 * m + 1, :, lanes].astype(F32)
            even = jnp.where(low, u, pltpu.roll(v, 64, 1))
            odd = jnp.where(low, pltpu.roll(u, 64, 1), v)
            chans = slice(128 * m, 128 * m + 128)
            out_ref[2 * t, :, chans] = (base_ref[2 * t, :, chans] + even).astype(BF16)
            out_ref[2 * t + 1, :, chans] = (base_ref[2 * t + 1, :, chans] + odd).astype(BF16)


def unpack_and_add(base, home):
    return pl.pallas_call(
        final_kernel,
        grid=(4,),
        in_specs=[
            pl.BlockSpec((8, 64, 256), lambda g: (g, 0, 0)),
            pl.BlockSpec((4, 64, 512), lambda g: (g, 0, 0)),
        ],
        out_specs=pl.BlockSpec((8, 64, 256), lambda g: (g, 0, 0)),
        out_shape=jax.ShapeDtypeStruct((32, 64, 256), BF16),
        name="unpack_add",
    )(base, home)


def dot(a, b):
    return jnp.dot(a, b, preferred_element_type=F32)


def middle_kernel(
    z_any, fwd_any, first_any, eight_any, inv_any, second_ref, cos_ref, sin_ref, out_ref,
    z, fwd, first, eight, inv, held, sems,
):
    copies = []
    for n, (src, dst) in enumerate(
        ((z_any, z), (fwd_any, fwd), (first_any, first), (eight_any, eight), (inv_any, inv))
    ):
        copy = pltpu.make_async_copy(src, dst, sems.at[n])
        copy.start()
        copies.append(copy)
    copies[0].wait()
    copies[1].wait()
    rows = 512 // CHUNKS
    groups = 8 // CHUNKS
    for m in range(CHUNKS):
        u = dot(fwd[2 * rows * m : 2 * rows * (m + 1), :], z[...])
        shape = (groups, 4, 16, 512)
        ur, ui = u[:rows].reshape(shape), u[rows:].reshape(shape)
        c = cos_ref[16 * groups * m : 16 * groups * (m + 1), :].reshape(groups, 1, 16, 512)
        s = sin_ref[16 * groups * m : 16 * groups * (m + 1), :].reshape(groups, 1, 16, 512)
        vr = (ur * c + ui * s).astype(BF16).reshape(rows, 512)
        vi = (ui * c - ur * s).astype(BF16).reshape(rows, 512)
        if m == 0:
            copies[2].wait()
        hidden = jnp.tanh(dot(vr, first[:512, :]) + dot(vi, first[512:, :])).astype(BF16)
        parts = []
        for t in range(4):
            v = dot(hidden[:, 256 * t : 256 * t + 256], second_ref[...])
            v = jnp.where(v > 0.25, v - 0.25, jnp.where(v < -0.25, v + 0.25, 0.0 * v))
            parts.append(v.astype(BF16))
        if m == 0:
            copies[3].wait()
        y = dot(jnp.concatenate(parts, axis=1), eight[...])
        yr, yi = y[:, :512].reshape(shape), y[:, 512:].reshape(shape)
        held[2 * rows * m : 2 * rows * m + rows, :] = (yr * c - yi * s).astype(BF16).reshape(rows, 512)
        held[2 * rows * m + rows : 2 * rows * (m + 1), :] = (
            (yi * c + yr * s).astype(BF16).reshape(rows, 512)
        )
    copies[4].wait()
    for m in range(4):
        out_ref[256 * m : 256 * m + 256, :] = dot(inv[256 * m : 256 * m + 256, :], held[...]).astype(BF16)


def middle(z, fwd, first, eight, inv, second, cos, sin):
    anywhere = pl.BlockSpec(memory_space=pl.ANY)
    vmem = pl.BlockSpec(memory_space=pltpu.VMEM)
    return pl.pallas_call(
        middle_kernel,
        in_specs=[anywhere] * 5 + [vmem] * 3,
        out_specs=vmem,
        out_shape=jax.ShapeDtypeStruct((1024, 512), BF16),
        scratch_shapes=[
            pltpu.VMEM((1024, 512), BF16),
            pltpu.VMEM((1024, 1024), BF16),
            pltpu.VMEM((1024, 1024), BF16),
            pltpu.VMEM((1024, 1024), BF16),
            pltpu.VMEM((1024, 1024), BF16),
            pltpu.VMEM((1024, 512), BF16),
            pltpu.SemaphoreType.DMA((5,)),
        ],
        compiler_params=pltpu.CompilerParams(vmem_limit_bytes=40 * 1024 * 1024),
        name="filter_rows",
    )(z, fwd, first, eight, inv, second, cos, sin)


def with_halo(shard, sides, width):
    for axis, dim in sides:
        devices, length = (lax.axis_size(axis), shard.shape[dim])
        up = [(i, (i + 1) % devices) for i in range(devices)]
        down = [(j, i) for i, j in up]
        last = lax.slice_in_dim(shard, length - width, length, axis=dim)
        leading = lax.slice_in_dim(shard, 0, width, axis=dim)
        before = lax.ppermute(last, axis, up)
        after = lax.ppermute(leading, axis, down)
        shard = jnp.concatenate([before, shard, after], axis=dim)
    return shard


def local(patches, norm_gain, w_first, w_second, depth_kernel):
    rows_dev, cols_dev, chans = patches.shape
    normed, packed = norm_and_pack(patches, norm_gain)
    lines = lax.all_to_all(packed, ("yl", "x"), 0, 0, tiled=True).reshape(1024, 512)

    fwd_w, inv_w, fwd_h, inv_h, eight, cos, sin = make_tables()
    block = lax.axis_index("x")
    wf = lax.dynamic_index_in_dim(w_first, block, 1, keepdims=False)
    ws = lax.dynamic_index_in_dim(w_second, block, 1, keepdims=False)
    first = first_layer(wf[0], wf[1])
    second = second_layer(ws[0], ws[1])

    padded = with_halo(normed, (("row", 0), (("yl", "x"), 1)), 1)
    base = patches.astype(F32)
    for i in range(3):
        for j in range(3):
            base = base + padded[i : i + rows_dev, j : j + cols_dev] * depth_kernel[i, j]

    freqs = dot(fwd_w, lines).astype(BF16).reshape(128, 8, 512)
    whole = lax.all_to_all(freqs, ("row", "yl"), 0, 0, tiled=True).reshape(1024, 512)
    filtered = middle(whole, fwd_h, first, eight, inv_h, second, cos, sin)
    back = lax.all_to_all(filtered.reshape(128, 8, 512), ("row", "yl"), 0, 0, tiled=True)
    spectral = dot(inv_w, back.reshape(1024, 512)).astype(BF16).reshape(16, 64, 512)
    home = lax.all_to_all(spectral, ("yl", "x"), 0, 0, tiled=True)
    return unpack_and_add(base, home)


def solution(mesh):
    fine = Mesh(np.asarray(mesh.devices).reshape(32, 4, 4), ("row", "yl", "x"))
    return jax.shard_map(
        local,
        mesh=fine,
        in_specs=(P("row", ("yl", "x"), None), P(), P(), P(), P()),
        out_specs=P("row", ("yl", "x"), None),
        check_vma=False,
    )
```

time: 330 us -> 189 us (0.57)
  the two profiles are of different devices: /device:TPU:63 before, /device:TPU:1 now
where the time goes in v1:
time: 189 us; the launch traced here: 188 us
  waiting for transfers between devices  70.8 us (37%)
  starting transfers between devices  58 us (31%)
  other arithmetic  29.4 us (16%)
  Pallas kernels  15.1 us (8%)
  local copies, waits for them, and re-layouts  9.97 us (5%)
  matrix products  4.44 us (2%)
    all_to_all x1, waiting for transfers between devices, local(): lax.all_to_all(filtered.reshape(128, 8, 512), ('row', 'yl'), 0, 0, tiled=...  28.4 us
    all_to_all x1, starting transfers between devices, local(): lax.all_to_all(freqs, ('row', 'yl'), 0, 0, tiled=True).reshape(1024, 512)  19.3 us
    all_to_all x1, waiting for transfers between devices, local(): lax.all_to_all(freqs, ('row', 'yl'), 0, 0, tiled=True).reshape(1024, 512)  18 us
    ppermute x2, starting transfers between devices, with_halo(): before = lax.ppermute(last, axis, up)  10.5 us
    all_to_all x1, waiting for transfers between devices, local(): lax.all_to_all(packed, ('yl', 'x'), 0, 0, tiled=True).reshape(1024, 512)  10.1 us
    all_to_all x1, starting transfers between devices, local(): lax.all_to_all(packed, ('yl', 'x'), 0, 0, tiled=True).reshape(1024, 512)  7.99 us
    unnamed x50, local copies, waits for them, and re-layouts  7.91 us
    ppermute x2, starting transfers between devices, with_halo(): after = lax.ppermute(leading, axis, down)  7.91 us
  transfers between devices with their start and end apart: 8, of which 6 were waited for; matrix products, arithmetic and copies ran while one was open for 17% of the time, Pallas kernels for 0%

profile of v1, /device:TPU:1, one launch (start us, length us, event | category | flops | bytes accessed | tf_op | source)
XLA Modules:
  0.0 188.0 jit_solution(7696635295891451127)
XLA Ops:
  0.0 4.5 %norm_pack.1 = (bf16[32,64,256]{2,1,0:T(8,128)(2,1)}, bf16[16,64,512]{2,1,0:T(8,128)(2,1)}) custom-call(bf16[32,64,256]{2,1,0:T(8,128)(2,1)} %x_ref.1, f32[1,256]{1,0:T(1,128)} %bitcast.61), custom_call_target="tpu_custom_call" | custom-call | tf_op jit(solution)/shard_map/norm_pack/pallas_call | solution.py:119
  4.5 8.0 %all-to-all-start = ((bf16[16,64,512]{2,1,0:T(8,128)(2,1)}), bf16[16,64,512]{2,1,0:T(8,128)(2,1)S(1)}, u32[]{:S(2)}, u32[]{:S(2)}) async-start(bf16[16,64,512]{2,1,0:T(8,128)(2,1)} %get-tuple-element.38), calls=%async_computation | async-start | bytes 2097152 | tf_op jit(solution)/shard_map/all_to_all | solution.py:252
  13.1 1.9 %negate_multiply_fusion = (f32[64,1024]{1,0:T(8,128)S(1)}, f32[64,1024]{1,0:T(8,128)}) fusion(s32[64]{0:T(128)S(1)} %get-tuple-element.107, s32[64]{0:T(128)S(1)} %get-tuple-element.106), kind=kLoop, calls=%fused_computation.66 | loop fusion | flops 1179648 | bytes 524800 | tf_op jit(solution)/shard_map/mul | solution.py:33
  18.7 1.3 fusion.55
  20.0 2.0 %select_multiply_fusion.2 = (f32[64,1024]{1,0:T(8,128)}, f32[64,1024]{1,0:T(8,128)}) fusion(s32[1024]{0:T(1024)S(1)} %fusion.61, s32[1024]{0:T(1024)S(1)} %get-tuple-element.113, s32[64]{0:T(128)S(1)} %get-tuple-element.103, s32[64]{0:T(128)S(1)} %get-tuple-element.100), kind=kLoop, calls=%fused_computation.46 | loop fusion | flops 1245184 | bytes 532992 | tf_op jit(solution)/shard_map/mul | solution.py:33
  22.0 2.0 %select_multiply_fusion = (f32[64,1024]{1,0:T(8,128)}, f32[64,1024]{1,0:T(8,128)}) fusion(s32[1024]{0:T(1024)S(1)} %get-tuple-element.118, s32[64]{0:T(128)S(1)} %get-tuple-element.101, s32[1024]{0:T(1024)S(1)} %get-tuple-element.119, s32[1024]{0:T(1024)S(1)} %get-tuple-element.110, s32[64]{0:T(128)S(1)} %broadcast_multiply_fusion.2, ...), kind=kLoop, calls=%fused_computation.44 | loop fusion | flops 1441792 | bytes 537344 | tf_op jit(solution)/shard_map/mul | solution.py:33
  24.5 10.1 %all-to-all-done = bf16[16,64,512]{2,1,0:T(8,128)(2,1)S(1)} async-done(((bf16[16,64,512]{2,1,0:T(8,128)(2,1)}), bf16[16,64,512]{2,1,0:T(8,128)(2,1)S(1)}, u32[]{:S(2)}, u32[]{:S(2)}) %all-to-all-start) | async-done | bytes 1048608 | tf_op jit(solution)/shard_map/all_to_all | solution.py:252
  34.6 2.2 %fusion = bf16[128,8,512]{2,1,0:T(8,128)(2,1)} fusion(bf16[1024,1024]{1,0:T(8,128)(2,1)S(1)} %bitcast.48, bf16[1024,512]{1,0:T(8,128)(2,1)S(1)} %bitcast.50), kind=kOutput, calls=%fused_computation.13 | convolution fusion | flops 1074266112 | bytes 4194304 | tf_op jit(solution)/shard_map/dot_general | solution.py:167
  36.8 19.3 %all-to-all-start.1 = ((bf16[128,8,512]{2,1,0:T(8,128)(2,1)}), bf16[128,8,512]{2,1,0:T(8,128)(2,1)S(1)}, u32[]{:S(2)}, u32[]{:S(2)}) async-start(bf16[128,8,512]{2,1,0:T(8,128)(2,1)} %fusion), calls=%async_computation.1 | async-start | bytes 2097152 | tf_op jit(solution)/shard_map/all_to_all | solution.py:268
  59.0 1.8 fusion.25
  60.8 1.5 multiply_convert_fusion
  62.4 1.9 %add_convert_fusion.1 = bf16[16,64,1024]{2,1,0:T(8,128)(2,1)} fusion(f32[64,1024]{1,0:T(8,128)S(1)} %copy-done.8, f32[16,1024]{1,0:T(8,128)S(1)} %copy-done.15, f32[64,1024]{1,0:T(8,128)S(1)} %copy-done.9, f32[16,1024]{1,0:T(8,128)S(1)} %copy-done.16), kind=kLoop, calls=%fused_computation.2 | loop fusion | flops 4194304 | bytes 2752512 | tf_op jit(solution)/shard_map/convert_element_type | solution.py:29
  64.3 2.0 %add_convert_fusion = bf16[16,64,1024]{2,1,0:T(8,128)(2,1)} fusion(f32[64,1024]{1,0:T(8,128)S(1)} %copy-done.10, f32[16,1024]{1,0:T(8,128)S(1)} %copy-done.21, f32[64,1024]{1,0:T(8,128)S(1)} %copy-done.11, f32[16,1024]{1,0:T(8,128)S(1)} %copy-done.22), kind=kLoop, calls=%fused_computation | loop fusion | flops 4194304 | bytes 2752512 | tf_op jit(solution)/shard_map/convert_element_type | solution.py:29
  66.3 2.0 %add_convert_fusion.2 = bf16[16,64,1024]{2,1,0:T(8,128)(2,1)} fusion(f32[64,1024]{1,0:T(8,128)S(1)} %copy-done.12, f32[16,1024]{1,0:T(8,128)S(1)} %copy-done.17, f32[64,1024]{1,0:T(8,128)S(1)} %copy-done.13, f32[16,1024]{1,0:T(8,128)S(1)} %copy-done.18), kind=kLoop, calls=%fused_computation.3 | loop fusion | flops 4194304 | bytes 2752512 | tf_op jit(solution)/shard_map/convert_element_type | solution.py:29
  68.3 18.0 %all-to-all-done.1 = bf16[128,8,512]{2,1,0:T(8,128)(2,1)S(1)} async-done(((bf16[128,8,512]{2,1,0:T(8,128)(2,1)}), bf16[128,8,512]{2,1,0:T(8,128)(2,1)S(1)}, u32[]{:S(2)}, u32[]{:S(2)}) %all-to-all-start.1) | async-done | bytes 1048608 | tf_op jit(solution)/shard_map/all_to_all | solution.py:268
  86.3 1.6 copy-done
  87.9 1.6 copy-done.1
  89.5 1.6 copy-done.2
  92.0 6.5 %filter_rows.1 = bf16[1024,512]{1,0:T(8,128)(2,1)S(1)} custom-call(bf16[1024,512]{1,0:T(8,128)(2,1)S(1)} %bitcast.46, bf16[1024,1024]{1,0:T(8,128)(2,1)S(1)} %bitcast.45, bf16[1024,1024]{1,0:T(8,128)(2,1)S(1)} %bitcast.43, bf16[1024,1024]{1,0:T(8,128)(2,1)S(1)} %bitcast.42, bf16[1024,1024]{1,0:T(8,128)(2,1)S(1)} %bitcast.44, ...), custom_call_target="tpu_custom_call" | custom-call | tf_op jit(solution)/shard_map/filter_rows/pallas_call | solution.py:217
  99.6 7.4 %all-to-all-start.2 = ((bf16[128,8,512]{2,1,0:T(8,128)(2,1)}), bf16[128,8,512]{2,1,0:T(8,128)(2,1)S(1)}, u32[]{:S(2)}, u32[]{:S(2)}) async-start(bf16[128,8,512]{2,1,0:T(8,128)(2,1)} %bitcast.47), calls=%async_computation.2 | async-start | bytes 2097152 | tf_op jit(solution)/shard_map/all_to_all | solution.py:270
  107.0 1.1 negate_multiply_fusion.1
  108.7 28.4 %all-to-all-done.2 = bf16[128,8,512]{2,1,0:T(8,128)(2,1)S(1)} async-done(((bf16[128,8,512]{2,1,0:T(8,128)(2,1)}), bf16[128,8,512]{2,1,0:T(8,128)(2,1)S(1)}, u32[]{:S(2)}, u32[]{:S(2)}) %all-to-all-start.2) | async-done | bytes 1048608 | tf_op jit(solution)/shard_map/all_to_all | solution.py:270
  137.1 2.2 %convolution_convert_fusion = bf16[1024,512]{1,0:T(8,128)(2,1)} fusion(bf16[1024,1024]{1,0:T(8,128)(2,1)S(1)} %bitcast.49, bf16[128,8,512]{2,1,0:T(8,128)(2,1)S(1)} %all-to-all-done.2), kind=kOutput, calls=%fused_computation.11 | convolution fusion | flops 1074266112 | bytes 4194304 | tf_op jit(solution)/shard_map/dot_general | solution.py:167
  139.3 5.0 %all-to-all-start.3 = ((bf16[16,64,512]{2,1,0:T(8,128)(2,1)}), bf16[16,64,512]{2,1,0:T(8,128)(2,1)S(1)}, u32[]{:S(2)}, u32[]{:S(2)}) async-start(bf16[16,64,512]{2,1,0:T(8,128)(2,1)} %bitcast.51), calls=%async_computation.3 | async-start | bytes 2097152 | tf_op jit(solution)/shard_map/all_to_all | solution.py:272
  144.3 7.1 %collective-permute-start = (bf16[1,64,256]{2,1,0:T(8,128)(2,1)S(1)}, bf16[1,64,256]{2,1,0:T(8,128)(2,1)S(1)}, u32[]{:S(2)}, u32[]{:S(2)}) collective-permute-start(bf16[1,64,256]{2,1,0:T(8,128)(2,1)S(1)} %get-tuple-element.56), channel_id=1, source_target_pairs={{0,16},{16,32},{32,48},{48,64},{64,80},{80,96},{96,112},{112,128},... | collective-permute-start | bytes 98312 | tf_op jit(solution)/shard_map/ppermute | solution.py:243
  151.4 1.9 %collective-permute-start.1 = (bf16[1,64,256]{2,1,0:T(8,128)(2,1)S(1)}, bf16[1,64,256]{2,1,0:T(8,128)(2,1)S(1)}, u32[]{:S(2)}, u32[]{:S(2)}) collective-permute-start(bf16[1,64,256]{2,1,0:T(8,128)(2,1)S(1)} %get-tuple-element.55), channel_id=1, source_target_pairs={{16,0},{32,16},{48,32},{64,48},{80,64},{96,80},{112,96},{128,112},... | collective-permute-start | bytes 98312 | tf_op jit(solution)/shard_map/ppermute | solution.py:244
  153.4 7.4 %collective-permute-done = bf16[1,64,256]{2,1,0:T(8,128)(2,1)S(1)} collective-permute-done((bf16[1,64,256]{2,1,0:T(8,128)(2,1)S(1)}, bf16[1,64,256]{2,1,0:T(8,128)(2,1)S(1)}, u32[]{:S(2)}, u32[]{:S(2)}) %collective-permute-start) | collective-permute-done | bytes 32800 | tf_op jit(solution)/shard_map/ppermute | solution.py:243
  160.9 5.9 %collective-permute-done.1 = bf16[1,64,256]{2,1,0:T(8,128)(2,1)S(1)} collective-permute-done((bf16[1,64,256]{2,1,0:T(8,128)(2,1)S(1)}, bf16[1,64,256]{2,1,0:T(8,128)(2,1)S(1)}, u32[]{:S(2)}, u32[]{:S(2)}) %collective-permute-start.1) | collective-permute-done | bytes 32800 | tf_op jit(solution)/shard_map/ppermute | solution.py:244
  166.8 3.4 %collective-permute-start.2 = (bf16[34,1,256]{2,1,0:T(2,128)(2,1)S(1)}, bf16[34,1,256]{2,1,0:T(2,128)(2,1)S(1)}, u32[]{:S(2)}, u32[]{:S(2)}) collective-permute-start(bf16[34,1,256]{2,1,0:T(2,128)(2,1)S(1)} %get-tuple-element.53), channel_id=1, source_target_pairs={{0,1},{1,2},{2,3},{3,4},{4,5},{5,6},{6,7},{7,8},{8,9},{9,10},{10,1... | collective-permute-start | bytes 52232 | tf_op jit(solution)/shard_map/ppermute | solution.py:243
  170.2 6.0 %collective-permute-start.3 = (bf16[34,1,256]{2,1,0:T(2,128)(2,1)S(1)}, bf16[34,1,256]{2,1,0:T(2,128)(2,1)S(1)}, u32[]{:S(2)}, u32[]{:S(2)}) collective-permute-start(bf16[34,1,256]{2,1,0:T(2,128)(2,1)S(1)} %get-tuple-element.54), channel_id=1, source_target_pairs={{1,0},{2,1},{3,2},{4,3},{5,4},{6,5},{7,6},{8,7},{9,8},{10,9},{11,1... | collective-permute-start | bytes 52232 | tf_op jit(solution)/shard_map/ppermute | solution.py:244
  177.2 5.8 %multiply_add_fusion.base_ref = f32[32,64,256]{2,1,0:T(8,128)} fusion(bf16[32,64,256]{2,1,0:T(8,128)(2,1)S(1)} %copy-done.5, bf16[32,64,256]{2,1,0:T(8,128)(2,1)S(1)} %copy-done.6, bf16[34,64,256]{2,1,0:T(8,128)(2,1)S(1)} %constant_dynamic-update-slice_fusion, bf16[34,1,256]{2,1,0:T(2,128)(2,1)S(1)} %collective-permute-done.3, ...), kind=kLoop, calls=%fused_computation.6 | loop fusion | flops 27262976 | bytes 5417984 | tf_op jit(solution)/shard_map/add | solution.py:265
  184.1 4.0 %unpack_add.1 = bf16[32,64,256]{2,1,0:T(8,128)(2,1)} custom-call(f32[32,64,256]{2,1,0:T(8,128)} %multiply_add_fusion.base_ref, bf16[16,64,512]{2,1,0:T(8,128)(2,1)} %copy-done.7), custom_call_target="tpu_custom_call" | custom-call | tf_op jit(solution)/shard_map/unpack_add/pallas_call | solution.py:153
  (89 shorter events, 12.4 us)
Async XLA Ops:
  4.5 30.1 %all-to-all-start = ((bf16[16,64,512]{2,1,0:T(8,128)(2,1)}), bf16[16,64,512]{2,1,0:T(8,128)(2,1)S(1)}, u32[]{:S(2)}, u32[]{:S(2)}) async-start(bf16[16,64,512]{2,1,0:T(8,128)(2,1)} %get-tuple-element.38), calls=%async_computation | async-start | bytes 2097152 | tf_op jit(solution)/shard_map/all_to_all | solution.py:252
  15.1 8.9 %copy-start.14 = (f32[64,1024]{1,0:T(8,128)S(1)}, f32[64,1024]{1,0:T(8,128)}, u32[]{:S(2)}) copy-start(f32[64,1024]{1,0:T(8,128)} %get-tuple-element.35) | copy-start | bytes 786436
  36.8 49.5 %all-to-all-start.1 = ((bf16[128,8,512]{2,1,0:T(8,128)(2,1)}), bf16[128,8,512]{2,1,0:T(8,128)(2,1)S(1)}, u32[]{:S(2)}, u32[]{:S(2)}) async-start(bf16[128,8,512]{2,1,0:T(8,128)(2,1)} %fusion), calls=%async_computation.1 | async-start | bytes 2097152 | tf_op jit(solution)/shard_map/all_to_all | solution.py:268
  58.8 3.5 %copy-start.8 = (f32[64,1024]{1,0:T(8,128)S(1)}, f32[64,1024]{1,0:T(8,128)}, u32[]{:S(2)}) copy-start(f32[64,1024]{1,0:T(8,128)} %tile.21) | copy-start | bytes 786436
  58.8 3.5 %copy-start.9 = (f32[64,1024]{1,0:T(8,128)S(1)}, f32[64,1024]{1,0:T(8,128)}, u32[]{:S(2)}) copy-start(f32[64,1024]{1,0:T(8,128)} %tile.9) | copy-start | bytes 786436
  58.8 3.5 %copy-start.15 = (f32[16,1024]{1,0:T(8,128)S(1)}, f32[16,1024]{1,0:T(8,128)}, u32[]{:S(2)}) copy-start(f32[16,1024]{1,0:T(8,128)} %get-tuple-element.45) | copy-start | bytes 196612
  58.8 3.5 %copy-start.16 = (f32[16,1024]{1,0:T(8,128)S(1)}, f32[16,1024]{1,0:T(8,128)}, u32[]{:S(2)}) copy-start(f32[16,1024]{1,0:T(8,128)} %get-tuple-element.43) | copy-start | bytes 196612
  60.8 3.5 %copy-start.10 = (f32[64,1024]{1,0:T(8,128)S(1)}, f32[64,1024]{1,0:T(8,128)}, u32[]{:S(2)}) copy-start(f32[64,1024]{1,0:T(8,128)} %get-tuple-element.52) | copy-start | bytes 786436
  60.8 3.5 %copy-start.11 = (f32[64,1024]{1,0:T(8,128)S(1)}, f32[64,1024]{1,0:T(8,128)}, u32[]{:S(2)}) copy-start(f32[64,1024]{1,0:T(8,128)} %get-tuple-element.50) | copy-start | bytes 786436
  60.8 3.5 %copy-start.21 = (f32[16,1024]{1,0:T(8,128)S(1)}, f32[16,1024]{1,0:T(8,128)}, u32[]{:S(2)}) copy-start(f32[16,1024]{1,0:T(8,128)} %get-tuple-element.51) | copy-start | bytes 196612
  60.8 3.5 %copy-start.22 = (f32[16,1024]{1,0:T(8,128)S(1)}, f32[16,1024]{1,0:T(8,128)}, u32[]{:S(2)}) copy-start(f32[16,1024]{1,0:T(8,128)} %get-tuple-element.49) | copy-start | bytes 196612
  62.3 4.0 %copy-start.12 = (f32[64,1024]{1,0:T(8,128)S(1)}, f32[64,1024]{1,0:T(8,128)}, u32[]{:S(2)}) copy-start(f32[64,1024]{1,0:T(8,128)} %get-tuple-element.42) | copy-start | bytes 786436
  62.3 4.0 %copy-start.13 = (f32[64,1024]{1,0:T(8,128)S(1)}, f32[64,1024]{1,0:T(8,128)}, u32[]{:S(2)}) copy-start(f32[64,1024]{1,0:T(8,128)} %get-tuple-element.40) | copy-start | bytes 786436
  62.4 4.0 %copy-start.17 = (f32[16,1024]{1,0:T(8,128)S(1)}, f32[16,1024]{1,0:T(8,128)}, u32[]{:S(2)}) copy-start(f32[16,1024]{1,0:T(8,128)} %get-tuple-element.41) | copy-start | bytes 196612
  62.4 3.9 %copy-start.18 = (f32[16,1024]{1,0:T(8,128)S(1)}, f32[16,1024]{1,0:T(8,128)}, u32[]{:S(2)}) copy-start(f32[16,1024]{1,0:T(8,128)} %get-tuple-element.39) | copy-start | bytes 196612
  86.3 1.6 copy-start
  87.9 1.6 copy-start.1
  89.5 1.6 copy-start.2
  91.1 0.9 copy-start.4
  98.6 1.0 copy-start.3
  99.6 8.5 %copy-start.19 = (f32[16,1024]{1,0:T(8,128)S(1)}, f32[16,1024]{1,0:T(8,128)}, u32[]{:S(2)}) copy-start(f32[16,1024]{1,0:T(8,128)} %get-tuple-element.30) | copy-start | bytes 196612
  99.6 8.5 %copy-start.20 = (f32[16,1024]{1,0:T(8,128)S(1)}, f32[16,1024]{1,0:T(8,128)}, u32[]{:S(2)}) copy-start(f32[16,1024]{1,0:T(8,128)} %get-tuple-element.32) | copy-start | bytes 196612
  99.6 37.5 %all-to-all-start.2 = ((bf16[128,8,512]{2,1,0:T(8,128)(2,1)}), bf16[128,8,512]{2,1,0:T(8,128)(2,1)S(1)}, u32[]{:S(2)}, u32[]{:S(2)}) async-start(bf16[128,8,512]{2,1,0:T(8,128)(2,1)} %bitcast.47), calls=%async_computation.2 | async-start | bytes 2097152 | tf_op jit(solution)/shard_map/all_to_all | solution.py:270
  139.3 5.0 %copy-start.5 = (bf16[32,64,256]{2,1,0:T(8,128)(2,1)S(1)}, bf16[32,64,256]{2,1,0:T(8,128)(2,1)}, u32[]{:S(2)}) copy-start(bf16[32,64,256]{2,1,0:T(8,128)(2,1)} %get-tuple-element.29) | copy-start | bytes 3145732
  139.3 36.9 %copy-start.23 = (f32[3,3,256]{2,1,0:T(4,128)S(1)}, f32[3,3,256]{2,1,0:T(4,128)}, u32[]{:S(2)}) copy-start(f32[3,3,256]{2,1,0:T(4,128)} %param.9) | copy-start | bytes 27652
  139.3 37.9 %copy-start.6 = (bf16[32,64,256]{2,1,0:T(8,128)(2,1)S(1)}, bf16[32,64,256]{2,1,0:T(8,128)(2,1)}, u32[]{:S(2)}) copy-start(bf16[32,64,256]{2,1,0:T(8,128)(2,1)} %x_ref.1) | copy-start | bytes 3145732
  139.3 43.8 %all-to-all-start.3 = ((bf16[16,64,512]{2,1,0:T(8,128)(2,1)}), bf16[16,64,512]{2,1,0:T(8,128)(2,1)S(1)}, u32[]{:S(2)}, u32[]{:S(2)}) async-start(bf16[16,64,512]{2,1,0:T(8,128)(2,1)} %bitcast.51), calls=%async_computation.3 | async-start | bytes 2097152 | tf_op jit(solution)/shard_map/all_to_all | solution.py:272
  144.3 16.5 %collective-permute-start = (bf16[1,64,256]{2,1,0:T(8,128)(2,1)S(1)}, bf16[1,64,256]{2,1,0:T(8,128)(2,1)S(1)}, u32[]{:S(2)}, u32[]{:S(2)}) collective-permute-start(bf16[1,64,256]{2,1,0:T(8,128)(2,1)S(1)} %get-tuple-element.56), channel_id=1, source_target_pairs={{0,16},{16,32},{32,48},{48,64},{64,80},{80,96},{96,112},{112,128},... | collective-permute-start | bytes 98312 | tf_op jit(solution)/shard_map/ppermute | solution.py:243
  151.4 15.4 %collective-permute-start.1 = (bf16[1,64,256]{2,1,0:T(8,128)(2,1)S(1)}, bf16[1,64,256]{2,1,0:T(8,128)(2,1)S(1)}, u32[]{:S(2)}, u32[]{:S(2)}) collective-permute-start(bf16[1,64,256]{2,1,0:T(8,128)(2,1)S(1)} %get-tuple-element.55), channel_id=1, source_target_pairs={{16,0},{32,16},{48,32},{64,48},{80,64},{96,80},{112,96},{128,112},... | collective-permute-start | bytes 98312 | tf_op jit(solution)/shard_map/ppermute | solution.py:244
  166.8 9.4 %collective-permute-start.2 = (bf16[34,1,256]{2,1,0:T(2,128)(2,1)S(1)}, bf16[34,1,256]{2,1,0:T(2,128)(2,1)S(1)}, u32[]{:S(2)}, u32[]{:S(2)}) collective-permute-start(bf16[34,1,256]{2,1,0:T(2,128)(2,1)S(1)} %get-tuple-element.53), channel_id=1, source_target_pairs={{0,1},{1,2},{2,3},{3,4},{4,5},{5,6},{6,7},{7,8},{8,9},{9,10},{10,1... | collective-permute-start | bytes 52232 | tf_op jit(solution)/shard_map/ppermute | solution.py:243
  170.2 7.0 %collective-permute-start.3 = (bf16[34,1,256]{2,1,0:T(2,128)(2,1)S(1)}, bf16[34,1,256]{2,1,0:T(2,128)(2,1)S(1)}, u32[]{:S(2)}, u32[]{:S(2)}) collective-permute-start(bf16[34,1,256]{2,1,0:T(2,128)(2,1)S(1)} %get-tuple-element.54), channel_id=1, source_target_pairs={{1,0},{2,1},{3,2},{4,3},{5,4},{6,5},{7,6},{8,7},{9,8},{10,9},{11,1... | collective-permute-start | bytes 52232 | tf_op jit(solution)/shard_map/ppermute | solution.py:244
  183.1 1.0 copy-start.7

commit v2 on v1

v2 whole, which is shorter than its diff:
```python
import functools
import math

import jax
import jax.numpy as jnp
import numpy as np
from jax import lax
from jax.experimental import pallas as pl
from jax.experimental.pallas import tpu as pltpu
from jax.sharding import Mesh
from jax.sharding import PartitionSpec as P

TURN = 1024
CHUNKS = 2
MIB = 1024 * 1024
F32 = jnp.float32
BF16 = jnp.bfloat16


def cos_of(idx):
    return jnp.cos((idx % TURN).astype(F32) * (2.0 * math.pi / TURN))


def sin_of(idx):
    return jnp.sin((idx % TURN).astype(F32) * (2.0 * math.pi / TURN))


def expand_kernel(steps, *refs):
    out_ref, half = refs[-1], (len(refs) - 1) // 2
    first = 0 if steps == 16 else steps * pl.program_id(0)

    def step(a, carry):
        v = None
        for e_ref, f_ref in zip(refs[:half], refs[half:-1]):
            term = e_ref[pl.ds(first + a, 1), :] * f_ref[...]
            v = term if v is None else v + term
        out_ref[pl.ds(pl.multiple_of(64 * a, 64), 64), :] = v.astype(BF16)
        return carry

    lax.fori_loop(0, steps, step, 0)


def outer_table(space, es, fs):
    whole = pl.BlockSpec(memory_space=pltpu.VMEM)
    stay = space == pltpu.VMEM
    return pl.pallas_call(
        functools.partial(expand_kernel, 16 if stay else 4),
        grid=(1,) if stay else (4,),
        in_specs=[whole] * (len(es) + len(fs)),
        out_specs=whole if stay else pl.BlockSpec((256, 1024), lambda g: (g, 0)),
        out_shape=space((1024, 1024), BF16),
        cost_estimate=pl.CostEstimate(flops=3 * 2**20, bytes_accessed=2**21, transcendentals=0),
        compiler_params=pltpu.CompilerParams(vmem_limit_bytes=4 * MIB),
        name="expand_table",
    )(*es, *fs)


def phase_table(space, ia, ib, scale):
    return outer_table(space, (cos_of(ia), sin_of(ia)), (cos_of(ib) * scale, -sin_of(ib) * scale))


def column(values):
    return jnp.asarray(values, jnp.int32)[:, None]


def split(idx, *sizes):
    out = []
    for s in reversed(sizes):
        out.append(idx % s)
        idx = idx // s
    return out[::-1]


def make_tables():
    lane = jnp.arange(1024, dtype=jnp.int32)[None, :]
    scale = 1.0 / 32.0
    a16 = jnp.arange(16, dtype=jnp.int32)[:, None]
    b64 = jnp.arange(64, dtype=jnp.int32)[:, None]
    pl_, ri, i = split(b64, 8, 2, 4)
    fwd_w = phase_table(pltpu.VMEM, 32 * a16 * lane, (4 * pl_ + i) * lane + 256 * ri, scale)
    p, lri, li = split(lane, 128, 2, 4)
    k = 4 * p + li
    weight = jnp.where(k == 0, 1.0, 2.0).astype(F32) * scale
    inv_w = phase_table(pltpu.VMEM, 64 * a16 * k, b64 * k + 256 * lri, weight)
    qhh, ro, qhl = split(a16, CHUNKS, 2, 8 // CHUNKS)
    qh = qhh * (8 // CHUNKS) + qhl
    bi, ql = split(b64, 4, 16)
    mask = jnp.where(bi == li, scale, 0.0).astype(F32)
    fwd_h = phase_table(pltpu.VMEM, 128 * qh * p + 256 * (ro - lri), 8 * ql * p, mask)
    lqhh, lro, lqhl, lli, lql = split(lane, CHUNKS, 2, 8 // CHUNKS, 4, 16)
    lq0 = 16 * (lqhh * (8 // CHUNKS) + lqhl) + lql
    mask_t = jnp.where(i == lli, scale, 0.0).astype(F32)
    inv_h = phase_table(pltpu.HBM, 64 * a16 * lq0, 8 * pl_ * lq0 + 256 * (lro - ri), mask_t)
    t, gri, e = split(a16, 4, 2, 2)
    gro, gh8, gc = split(lane, 2, 8, 64)
    e1 = cos_of(128 * (2 * t + e) * gh8 - 256 * (gro - gri))
    eye = jnp.where(b64 == gc, 1.0, 0.0).astype(F32)
    eight = outer_table(pltpu.HBM, (e1,), (eye,))
    q0 = jnp.arange(128, dtype=jnp.int32)[:, None]
    h8 = jnp.arange(512, dtype=jnp.int32)[None, :] // 64
    return fwd_w, inv_w, fwd_h, inv_h, eight, cos_of(q0 * h8), sin_of(q0 * h8)


def first_layer(w0, w1):
    lane = jnp.arange(1024, dtype=jnp.int32)[None, :]
    ri, h8 = split(jnp.arange(16, dtype=jnp.int32)[:, None], 2, 8)
    t, ro, e, _ = split(lane, 4, 2, 2, 64)
    angle = 128 * (2 * t + e) * h8 + 256 * (ro - ri)
    weights = (jnp.tile(w0.astype(F32), (1, 16)), jnp.tile(w1.astype(F32), (1, 16)))
    return outer_table(pltpu.HBM, (cos_of(angle), sin_of(angle)), weights)


def second_layer(w0, w1):
    z = jnp.zeros_like(w0)
    b0 = jnp.block([[w0, z], [z, w0]])
    b1 = jnp.block([[w1, z], [z, w1]])
    return jnp.block([[b0, b1], [-b1, b0]])


def low_half(rows):
    return lax.broadcasted_iota(jnp.int32, (rows, 128), 1) < 64


def swap(v):
    return pltpu.roll(v, 64, 1)


def norm_kernel(x_ref, gain_ref, packed_ref):
    low = low_half(64)
    ones = jnp.ones((256, 128), BF16)
    x = x_ref[...].reshape(512, 256)
    mean = dot(x, ones) * (1.0 / 256.0)
    d0, d1 = x[:, :128].astype(F32) - mean, x[:, 128:].astype(F32) - mean
    square = d0 * d0 + d1 * d1
    coarse = square.astype(BF16)
    fine = (square - coarse.astype(F32)).astype(BF16)
    var = dot(jnp.concatenate([coarse, fine], axis=1), ones) * (1.0 / 256.0)
    scale = lax.rsqrt(var + 1e-05)
    halves = (d0 * scale * gain_ref[:, :128], d1 * scale * gain_ref[:, 128:])
    for t in range(4):
        lanes = slice(128 * t, 128 * t + 128)
        for m in range(2):
            a = halves[m][128 * t : 128 * t + 64]
            b = halves[m][128 * t + 64 : 128 * t + 128]
            packed_ref[2 * m, :, lanes] = jnp.where(low, a, swap(b)).astype(BF16)
            packed_ref[2 * m + 1, :, lanes] = jnp.where(low, swap(a), b).astype(BF16)


def norm_and_pack(patches, gain):
    return pl.pallas_call(
        norm_kernel,
        grid=(4,),
        in_specs=[
            pl.BlockSpec((8, 64, 256), lambda g: (g, 0, 0)),
            pl.BlockSpec((1, 256), lambda g: (0, 0)),
        ],
        out_specs=pl.BlockSpec((4, 64, 512), lambda g: (g, 0, 0)),
        out_shape=pltpu.HBM((16, 64, 512), BF16),
        compiler_params=pltpu.CompilerParams(vmem_limit_bytes=12 * MIB),
        name="norm_pack",
    )(patches, gain.reshape(1, 256))


def final_kernel(x_ref, home_ref, out_ref):
    low = low_half(64)
    first = 4 * pl.program_id(0)
    for t in range(4):
        lanes = slice(128 * t, 128 * t + 128)
        for m in range(2):
            u = home_ref[first + 2 * m, :, lanes].astype(F32)
            v = home_ref[first + 2 * m + 1, :, lanes].astype(F32)
            chans = slice(128 * m, 128 * m + 128)
            even, odd = jnp.where(low, u, swap(v)), jnp.where(low, swap(u), v)
            out_ref[2 * t, :, chans] = (x_ref[2 * t, :, chans].astype(F32) + even).astype(BF16)
            out_ref[2 * t + 1, :, chans] = (x_ref[2 * t + 1, :, chans].astype(F32) + odd).astype(BF16)


def unpack_and_add(patches, home):
    return pl.pallas_call(
        final_kernel,
        grid=(4,),
        in_specs=[
            pl.BlockSpec((8, 64, 256), lambda g: (g, 0, 0)),
            pl.BlockSpec(memory_space=pltpu.VMEM),
        ],
        out_specs=pl.BlockSpec((8, 64, 256), lambda g: (g, 0, 0)),
        out_shape=jax.ShapeDtypeStruct((32, 64, 256), BF16),
        compiler_params=pltpu.CompilerParams(vmem_limit_bytes=8 * MIB),
        name="unpack_add",
    )(patches, resident(home))


def dot(a, b):
    return jnp.dot(a, b, preferred_element_type=F32)


def resident(v):
    return pltpu.with_memory_space_constraint(v, pltpu.VMEM)


def remaining(v):
    return pltpu.with_memory_space_constraint(v, pltpu.HBM)


def stream_dot(table, operand, extra, held, out, sems):
    copies = []
    for m in range(4):
        rows = slice(256 * m, 256 * m + 256)
        v = dot(table[rows, :], operand[...])
        if extra is not None:
            extra[m].wait()
            v = v + extra[4][rows, :]
        held[rows, :] = v.astype(BF16)
        copies.append(pltpu.make_async_copy(held.at[rows, :], out.at[rows, :], sems.at[m]))
        copies[-1].start()
    for copy in copies:
        copy.wait()


def columns_kernel(table_ref, x_ref, out_any, held, sems):
    stream_dot(table_ref, x_ref, None, held, out_any, sems)


def columns_add_kernel(table_ref, x_ref, extra_any, out_any, held, sems, extra, extra_sems):
    fetches = []
    for m in range(4):
        rows = slice(256 * m, 256 * m + 256)
        fetches.append(
            pltpu.make_async_copy(extra_any.at[rows, :], extra.at[rows, :], extra_sems.at[m])
        )
        fetches[-1].start()
    stream_dot(table_ref, x_ref, (*fetches, extra), held, out_any, sems)


def columns(table, x, *extra):
    scratch = [pltpu.VMEM((1024, 512), BF16), pltpu.SemaphoreType.DMA((4,))]
    if extra:
        scratch += [pltpu.VMEM((1024, 512), F32), pltpu.SemaphoreType.DMA((4,))]
    return pl.pallas_call(
        columns_add_kernel if extra else columns_kernel,
        in_specs=[pl.BlockSpec(memory_space=pltpu.VMEM)] * 2
        + [pl.BlockSpec(memory_space=pltpu.HBM)] * len(extra),
        out_specs=pl.BlockSpec(memory_space=pltpu.HBM),
        out_shape=pltpu.HBM((1024, 512), BF16),
        scratch_shapes=scratch,
        cost_estimate=pl.CostEstimate(flops=2**30, bytes_accessed=2**21, transcendentals=0),
        compiler_params=pltpu.CompilerParams(vmem_limit_bytes=12 * MIB),
        name="along_columns",
    )(resident(table), resident(x), *[remaining(e) for e in extra])


def stencil_kernel(x_ref, above_ref, below_ref, taps_ref, out_ref):
    low = low_half(512)

    def tile(t):
        return x_ref[:, 128 * t : 128 * t + 128].astype(F32)

    def between(t):
        if t < 0:
            other = above_ref[...].astype(F32)
            return jnp.concatenate(
                [
                    jnp.where(low, other, swap(tile(0)[:512])),
                    jnp.where(low, swap(other), swap(tile(0)[512:])),
                ],
                axis=0,
            )
        if t == 3:
            other = below_ref[...].astype(F32)
            return jnp.concatenate(
                [
                    jnp.where(low, swap(tile(3)[:512]), swap(other)),
                    jnp.where(low, swap(tile(3)[512:]), other),
                ],
                axis=0,
            )
        return jnp.where(low_half(1024), swap(tile(t)), swap(tile(t + 1)))

    for t in range(4):
        rows = (between(t - 1), tile(t), between(t))
        total = None
        for j in range(3):
            part = rows[0] * taps_ref[j : j + 1, :]
            part = part + rows[1] * taps_ref[3 + j : 4 + j, :]
            part = part + rows[2] * taps_ref[6 + j : 7 + j, :]
            if j != 1:
                part = pltpu.roll(part, 1 if j == 0 else 1023, 0)
            total = part if total is None else total + part
        out_ref[:, 128 * t : 128 * t + 128] = total


def stencil(x, above, below, taps):
    return pl.pallas_call(
        stencil_kernel,
        in_specs=[pl.BlockSpec(memory_space=pltpu.VMEM)] * 4,
        grid=(1,),
        out_specs=pl.BlockSpec((1024, 512), lambda g: (0, 0)),
        out_shape=pltpu.HBM((1024, 512), F32),
        cost_estimate=pl.CostEstimate(flops=2**24, bytes_accessed=2**22, transcendentals=0),
        compiler_params=pltpu.CompilerParams(vmem_limit_bytes=16 * MIB),
        name="stencil",
    )(resident(x), above, below, taps)


def middle_kernel(
    z, fwd, second_ref, cos_any, sin_any, first_any, eight_any, inv_any, out_any,
    cos_ref, sin_ref, first, eight, inv, held, done, sems, fetch_sems,
):
    fetches = []
    for n, (src, dst) in enumerate(
        (
            (cos_any, cos_ref),
            (sin_any, sin_ref),
            (first_any, first),
            (eight_any, eight),
            (inv_any, inv),
        )
    ):
        fetches.append(pltpu.make_async_copy(src, dst, fetch_sems.at[n]))
        fetches[-1].start()
    rows = 512 // CHUNKS
    groups = 8 // CHUNKS
    for m in range(CHUNKS):
        u = dot(fwd[2 * rows * m : 2 * rows * (m + 1), :], z[...])
        shape = (groups, 4, 16, 512)
        ur, ui = u[:rows].reshape(shape), u[rows:].reshape(shape)
        if m == 0:
            fetches[0].wait()
            fetches[1].wait()
        c = cos_ref[16 * groups * m : 16 * groups * (m + 1), :].reshape(groups, 1, 16, 512)
        s = sin_ref[16 * groups * m : 16 * groups * (m + 1), :].reshape(groups, 1, 16, 512)
        vr = (ur * c + ui * s).astype(BF16).reshape(rows, 512)
        vi = (ui * c - ur * s).astype(BF16).reshape(rows, 512)
        if m == 0:
            fetches[2].wait()
        hidden = jnp.tanh(dot(vr, first[:512, :]) + dot(vi, first[512:, :])).astype(BF16)
        parts = []
        for t in range(4):
            v = dot(hidden[:, 256 * t : 256 * t + 256], second_ref[...])
            v = jnp.where(v > 0.25, v - 0.25, jnp.where(v < -0.25, v + 0.25, 0.0 * v))
            parts.append(v.astype(BF16))
        if m == 0:
            fetches[3].wait()
        y = dot(jnp.concatenate(parts, axis=1), eight[...])
        yr, yi = y[:, :512].reshape(shape), y[:, 512:].reshape(shape)
        held[2 * rows * m : 2 * rows * m + rows, :] = (yr * c - yi * s).astype(BF16).reshape(rows, 512)
        held[2 * rows * m + rows : 2 * rows * (m + 1), :] = (
            (yi * c + yr * s).astype(BF16).reshape(rows, 512)
        )
    fetches[4].wait()
    stream_dot(inv, held, None, done, out_any, sems)


def middle(z, fwd, first, eight, inv, second, cos, sin):
    vmem, hbm = pl.BlockSpec(memory_space=pltpu.VMEM), pl.BlockSpec(memory_space=pltpu.HBM)
    return pl.pallas_call(
        middle_kernel,
        in_specs=[vmem] * 3 + [hbm] * 5,
        out_specs=hbm,
        out_shape=pltpu.HBM((1024, 512), BF16),
        scratch_shapes=[
            pltpu.VMEM((128, 512), F32),
            pltpu.VMEM((128, 512), F32),
            pltpu.VMEM((1024, 1024), BF16),
            pltpu.VMEM((1024, 1024), BF16),
            pltpu.VMEM((1024, 1024), BF16),
            pltpu.VMEM((1024, 512), BF16),
            pltpu.VMEM((1024, 512), BF16),
            pltpu.SemaphoreType.DMA((4,)),
            pltpu.SemaphoreType.DMA((5,)),
        ],
        cost_estimate=pl.CostEstimate(flops=5 * 2**30, bytes_accessed=2**21, transcendentals=2**19),
        compiler_params=pltpu.CompilerParams(vmem_limit_bytes=28 * MIB),
        name="filter_rows",
    )(
        resident(z), resident(fwd), second, remaining(cos), remaining(sin), remaining(first),
        remaining(eight), remaining(inv),
    )


def packed_row(lines, lane):
    return jnp.concatenate([lines[:512, lane : lane + 64], lines[512:, lane : lane + 64]], axis=1)


def local(patches, norm_gain, w_first, w_second, depth_kernel):
    packed = norm_and_pack(patches, norm_gain)
    lines = lax.all_to_all(packed, ("yl", "x"), 0, 0, tiled=True).reshape(1024, 512)

    fwd_w, inv_w, fwd_h, inv_h, eight, cos, sin = make_tables()
    block = lax.axis_index("x")
    wf = lax.dynamic_index_in_dim(w_first, block, 1, keepdims=False)
    ws = lax.dynamic_index_in_dim(w_second, block, 1, keepdims=False)
    taps = lax.dynamic_slice_in_dim(depth_kernel.reshape(9, 256), 64 * block, 64, 1)
    taps = jnp.concatenate([taps, taps], axis=1)
    first = first_layer(wf[0], wf[1])
    second = second_layer(ws[0], ws[1])

    freqs = columns(fwd_w, lines).reshape(128, 8, 512)
    whole = lax.all_to_all(freqs, ("row", "yl"), 0, 0, tiled=True).reshape(1024, 512)
    groups = 128
    down = [(i, (i + 1) % groups) for i in range(groups)]
    up = [(j, i) for i, j in down]
    above = lax.ppermute(packed_row(lines, 448), ("row", "yl"), down)
    below = lax.ppermute(packed_row(lines, 0), ("row", "yl"), up)
    conv = stencil(lines, above, below, taps)

    filtered = middle(whole, fwd_h, first, eight, inv_h, second, cos, sin)
    back = lax.all_to_all(filtered.reshape(128, 8, 512), ("row", "yl"), 0, 0, tiled=True)
    summed = columns(inv_w, back.reshape(1024, 512), conv).reshape(16, 64, 512)
    home = lax.all_to_all(summed, ("yl", "x"), 0, 0, tiled=True)
    return unpack_and_add(patches, home)


def solution(mesh):
    fine = Mesh(np.asarray(mesh.devices).reshape(32, 4, 4), ("row", "yl", "x"))
    return jax.shard_map(
        local,
        mesh=fine,
        in_specs=(P("row", ("yl", "x"), None), P(), P(), P(), P()),
        out_specs=P("row", ("yl", "x"), None),
        check_vma=False,
    )
```

time: 189 us -> 173 us (0.915)
  the two profiles are of different devices: /device:TPU:1 before, /device:TPU:8 now
where the time goes in v2:
time: 173 us; the launch traced here: 172 us
  waiting for transfers between devices  51.2 us (30%)
  starting transfers between devices  38 us (22%)
  Pallas kernels  32.3 us (19%)
  blocking collectives  31.7 us (18%)
  other arithmetic  15 us (9%)
  local copies, waits for them, and re-layouts  3.72 us (2%)
    all_to_all x1, blocking collectives, local(): home = lax.all_to_all(summed, ('yl', 'x'), 0, 0, tiled=True)  31.7 us
    ppermute x1, waiting for transfers between devices, local(): above = lax.ppermute(packed_row(lines, 448), ('row', 'yl'), down)  18.5 us
    all_to_all x1, waiting for transfers between devices, local(): lax.all_to_all(freqs, ('row', 'yl'), 0, 0, tiled=True).reshape(1024, 512)  17.1 us
    all_to_all x1, starting transfers between devices, local(): lax.all_to_all(freqs, ('row', 'yl'), 0, 0, tiled=True).reshape(1024, 512)  15.4 us
    all_to_all x1, waiting for transfers between devices, local(): lax.all_to_all(packed, ('yl', 'x'), 0, 0, tiled=True).reshape(1024, 512)  14.2 us
    all_to_all x1, starting transfers between devices, local(): lax.all_to_all(packed, ('yl', 'x'), 0, 0, tiled=True).reshape(1024, 512)  9.29 us
    pallas_call x1, Pallas kernels, middle(): pl.pallas_call(middle_kernel, in_specs=[vmem] * 3 + [hbm] * 5, out_specs=...  8.86 us
    pallas_call x6, Pallas kernels, outer_table(): pl.pallas_call(functools.partial(expand_kernel, 16 if stay else 4), grid=...  8.14 us
  transfers between devices with their start and end apart: 5, of which 4 were waited for; matrix products, arithmetic and copies ran while one was open for 9% of the time, Pallas kernels for 7%

profile of v2, /device:TPU:8, one launch (start us, length us, event | category | flops | bytes accessed | tf_op | source)
XLA Modules:
  0.0 172.3 jit_solution(8211307451124829340)
XLA Ops:
  0.0 1.2 copy-done
  1.2 0.7 copy-done.4
  1.9 2.9 %norm_pack.1 = bf16[16,64,512]{2,1,0:T(8,128)(2,1)} custom-call(bf16[32,64,256]{2,1,0:T(8,128)(2,1)S(1)} %copy-done, f32[1,256]{1,0:T(1,128)S(1)} %bitcast.24), custom_call_target="tpu_custom_call" | custom-call | tf_op jit(solution)/shard_map/norm_pack/pallas_call | solution.py:150
  4.8 9.3 %all-to-all-start = ((bf16[16,64,512]{2,1,0:T(8,128)(2,1)}), bf16[16,64,512]{2,1,0:T(8,128)(2,1)S(1)}, u32[]{:S(2)}, u32[]{:S(2)}) async-start(bf16[16,64,512]{2,1,0:T(8,128)(2,1)} %norm_pack.1), calls=%async_computation | async-start | bytes 2097152 | tf_op jit(solution)/shard_map/all_to_all | solution.py:387
  14.1 1.9 %negate_multiply_fusion = (f32[64,1024]{1,0:T(8,128)S(1)}, f32[64,1024]{1,0:T(8,128)}) fusion(s32[64]{0:T(128)S(1)} %get-tuple-element.50, s32[64]{0:T(128)S(1)} %get-tuple-element.49), kind=kLoop, calls=%fused_computation.39 | loop fusion | flops 1179648 | bytes 524800 | tf_op jit(solution)/shard_map/mul | solution.py:59
  16.4 0.9 copy-done.2
  20.7 0.6 fusion.85
  21.4 1.4 fusion.53
  23.1 1.0 fusion.45
  24.1 14.2 %all-to-all-done = bf16[16,64,512]{2,1,0:T(8,128)(2,1)S(1)} async-done(((bf16[16,64,512]{2,1,0:T(8,128)(2,1)}), bf16[16,64,512]{2,1,0:T(8,128)(2,1)S(1)}, u32[]{:S(2)}, u32[]{:S(2)}) %all-to-all-start) | async-done | bytes 1048608 | tf_op jit(solution)/shard_map/all_to_all | solution.py:387
  38.3 2.0 %along_columns.2 = bf16[1024,512]{1,0:T(8,128)(2,1)} custom-call(bf16[1024,1024]{1,0:T(8,128)(2,1)S(1)} %expand_table.7.table_ref, bf16[1024,512]{1,0:T(8,128)(2,1)S(1)} %bitcast.21), custom_call_target="tpu_custom_call" | custom-call | flops 1073741824 | bytes 2097152 | tf_op jit(solution)/shard_map/along_columns/pallas_call | solution.py:239
  40.3 15.4 %all-to-all-start.1 = ((bf16[128,8,512]{2,1,0:T(8,128)(2,1)}), bf16[128,8,512]{2,1,0:T(8,128)(2,1)}, u32[]{:S(2)}, u32[]{:S(2)}) async-start(bf16[128,8,512]{2,1,0:T(8,128)(2,1)} %bitcast.25), calls=%async_computation.1 | async-start | bytes 2097152 | tf_op jit(solution)/shard_map/all_to_all | solution.py:399
  56.3 2.0 %expand_table.10.eight_any = bf16[1024,1024]{1,0:T(8,128)(2,1)} custom-call(f32[16,1024]{1,0:T(8,128)S(1)} %fusion.35.refs_0_, f32[64,1024]{1,0:T(8,128)S(1)} %fusion.18.refs_1_), custom_call_target="tpu_custom_call" | custom-call | flops 3145728 | bytes 2097152 | tf_op jit(solution)/shard_map/expand_table/pallas_call | solution.py:46
  58.3 2.1 %expand_table.9.first_any = bf16[1024,1024]{1,0:T(8,128)(2,1)} custom-call(f32[16,1024]{1,0:T(8,128)S(1)} %copy-done.3, f32[16,1024]{1,0:T(8,128)S(1)} %get-tuple-element.21.refs_1_, f32[64,1024]{1,0:T(8,128)S(1)} %tile.9.refs_2_, f32[64,1024]{1,0:T(8,128)S(1)} %tile.21.refs_3_), custom_call_target="tpu_custom_call" | custom-call | flops 3145728 | bytes 2097152 | tf_op jit(solution)/shard_map/expand_table/pallas_call | solution.py:46
  61.1 1.2 select_multiply_fusion
  62.3 2.1 %expand_table.11.inv_any = bf16[1024,1024]{1,0:T(8,128)(2,1)} custom-call(f32[16,1024]{1,0:T(8,128)S(1)} %get-tuple-element.28.refs_0_, f32[16,1024]{1,0:T(8,128)S(1)} %get-tuple-element.27.refs_1_, f32[64,1024]{1,0:T(8,128)S(1)} %get-tuple-element.18.refs_2_, f32[64,1024]{1,0:T(8,128)S(1)} %get-tuple-element.17.refs_3_), custom_call_target="tpu_custom_call" | custom-call | flops 3145728 | bytes 2097152 | tf_op jit(solution)/shard_map/expand_table/pallas_call | solution.py:46
  64.8 1.1 select_multiply_fusion.2
  66.0 0.6 expand_table.8.fwd
  66.8 1.8 %fusion.19 = (f32[128,512]{1,0:T(8,128)}, f32[128,512]{1,0:T(8,128)}) fusion(s32[512]{0:T(512)S(1)} %add_select_fusion.34), kind=kLoop, calls=%fused_computation.48 | loop fusion | flops 917504 | bytes 526336 | tf_op jit(solution)/shard_map/sin | solution.py:25
  68.7 17.1 %all-to-all-done.1 = bf16[128,8,512]{2,1,0:T(8,128)(2,1)} async-done(((bf16[128,8,512]{2,1,0:T(8,128)(2,1)}), bf16[128,8,512]{2,1,0:T(8,128)(2,1)}, u32[]{:S(2)}, u32[]{:S(2)}) %all-to-all-start.1) | async-done | bytes 1048608 | tf_op jit(solution)/shard_map/all_to_all | solution.py:399
  85.8 8.9 %filter_rows.1 = bf16[1024,512]{1,0:T(8,128)(2,1)} custom-call(bf16[1024,512]{1,0:T(8,128)(2,1)} %bitcast.3.z, bf16[1024,1024]{1,0:T(8,128)(2,1)S(1)} %expand_table.8.fwd, bf16[256,256]{1,0:T(8,128)(2,1)S(1)} %maximum_maximum_fusion.second_ref, f32[128,512]{1,0:T(8,128)} %get-tuple-element.32.cos_any, f32[128,512]{1,0:T(8,128)} %get-tuple-element.31.sin_any, ...), custom_call_target="tpu_custom_call" | custom-call | flops 5368709120 | bytes 2097152 | tf_op jit(solution)/shard_map/filter_rows/pallas_call | solution.py:356
  94.7 7.5 %all-to-all-start.2 = ((bf16[128,8,512]{2,1,0:T(8,128)(2,1)}), bf16[128,8,512]{2,1,0:T(8,128)(2,1)}, u32[]{:S(2)}, u32[]{:S(2)}) async-start(bf16[128,8,512]{2,1,0:T(8,128)(2,1)} %bitcast.27), calls=%async_computation.2 | async-start | bytes 2097152 | tf_op jit(solution)/shard_map/all_to_all | solution.py:408
  102.2 1.1 negate_multiply_fusion.1
  103.6 3.4 %collective-permute-start = (bf16[512,128]{1,0:T(8,128)(2,1)S(1)}, bf16[512,128]{1,0:T(8,128)(2,1)S(1)}, u32[]{:S(2)}, u32[]{:S(2)}) collective-permute-start(bf16[512,128]{1,0:T(8,128)(2,1)S(1)} %pad_maximum_fusion), channel_id=1, source_target_pairs={{0,4},{4,8},{8,12},{12,16},{16,20},{20,24},{24,28},{28,32},{32,36}... | collective-permute-start | bytes 393224 | tf_op jit(solution)/shard_map/ppermute | solution.py:403
  107.0 2.5 %collective-permute-start.1 = (bf16[512,128]{1,0:T(8,128)(2,1)S(1)}, bf16[512,128]{1,0:T(8,128)(2,1)S(1)}, u32[]{:S(2)}, u32[]{:S(2)}) collective-permute-start(bf16[512,128]{1,0:T(8,128)(2,1)S(1)} %pad_maximum_fusion.1), channel_id=1, source_target_pairs={{4,0},{8,4},{12,8},{16,12},{20,16},{24,20},{28,24},{32,28},{36,32}... | collective-permute-start | bytes 393224 | tf_op jit(solution)/shard_map/ppermute | solution.py:404
  109.6 0.6 expand_table.6.table_ref
  110.3 18.5 %collective-permute-done.above_ref = bf16[512,128]{1,0:T(8,128)(2,1)S(1)} collective-permute-done((bf16[512,128]{1,0:T(8,128)(2,1)S(1)}, bf16[512,128]{1,0:T(8,128)(2,1)S(1)}, u32[]{:S(2)}, u32[]{:S(2)}) %collective-permute-start) | collective-permute-done | bytes 131104 | tf_op jit(solution)/shard_map/ppermute | solution.py:403
  128.9 1.3 collective-permute-done.1.below_ref
  130.2 3.7 %stencil.1.extra_any = f32[1024,512]{1,0:T(8,128)} custom-call(bf16[1024,512]{1,0:T(8,128)(2,1)S(1)} %bitcast.23, bf16[512,128]{1,0:T(8,128)(2,1)S(1)} %collective-permute-done.above_ref, bf16[512,128]{1,0:T(8,128)(2,1)S(1)} %collective-permute-done.1.below_ref, f32[9,128]{1,0:T(8,128)S(1)} %pad_maximum_fusion.2.taps_ref), custom_call_target="tpu_custom_call" | custom-call | flops 16777216 | bytes 4194304 | tf_op jit(solution)/shard_map/stencil/pallas_call | solution.py:293
  133.8 4.8 %along_columns.3 = bf16[1024,512]{1,0:T(8,128)(2,1)} custom-call(bf16[1024,1024]{1,0:T(8,128)(2,1)S(1)} %expand_table.6.table_ref, bf16[1024,512]{1,0:T(8,128)(2,1)} %bitcast.9.x_ref, f32[1024,512]{1,0:T(8,128)} %stencil.1.extra_any), custom_call_target="tpu_custom_call" | custom-call | flops 1073741824 | bytes 2097152 | tf_op jit(solution)/shard_map/along_columns/pallas_call | solution.py:239
  138.7 31.7 %all_to_all.20.home_ref = bf16[16,64,512]{2,1,0:T(8,128)(2,1)S(1)} all-to-all(bf16[16,64,512]{2,1,0:T(8,128)(2,1)} %bitcast.26), channel_id=1, replica_groups=mesh['row'=32,'yl'=4,'x'=4] {'yl','x'}, dimensions={0} | all-to-all | bytes 2097152 | tf_op jit(solution)/shard_map/all_to_all | solution.py:410
  170.4 1.9 %unpack_add.1 = bf16[32,64,256]{2,1,0:T(8,128)(2,1)} custom-call(bf16[32,64,256]{2,1,0:T(8,128)(2,1)S(1)} %copy-done.1, bf16[16,64,512]{2,1,0:T(8,128)(2,1)S(1)} %all_to_all.20.home_ref), custom_call_target="tpu_custom_call" | custom-call | tf_op jit(solution)/shard_map/unpack_add/pallas_call | solution.py:179
  (74 shorter events, 6.3 us)
Async XLA Ops:
  0.0 1.2 copy-start
  1.2 0.7 copy-start.4
  4.8 33.5 %all-to-all-start = ((bf16[16,64,512]{2,1,0:T(8,128)(2,1)}), bf16[16,64,512]{2,1,0:T(8,128)(2,1)S(1)}, u32[]{:S(2)}, u32[]{:S(2)}) async-start(bf16[16,64,512]{2,1,0:T(8,128)(2,1)} %norm_pack.1), calls=%async_computation | async-start | bytes 2097152 | tf_op jit(solution)/shard_map/all_to_all | solution.py:387
  16.4 1.0 copy-start.2
  40.3 15.5 %copy-start.6 = (f32[64,64]{1,0:T(8,128)S(1)}, f32[64,64]{1,0:T(8,128)}, u32[]{:S(2)}) copy-start(f32[64,64]{1,0:T(8,128)} %get-tuple-element.9) | copy-start | bytes 49156
  40.3 15.7 %copy-start.5 = (f32[64,64]{1,0:T(8,128)S(1)}, f32[64,64]{1,0:T(8,128)}, u32[]{:S(2)}) copy-start(f32[64,64]{1,0:T(8,128)} %get-tuple-element.10) | copy-start | bytes 49156
  40.3 45.5 %all-to-all-start.1 = ((bf16[128,8,512]{2,1,0:T(8,128)(2,1)}), bf16[128,8,512]{2,1,0:T(8,128)(2,1)}, u32[]{:S(2)}, u32[]{:S(2)}) async-start(bf16[128,8,512]{2,1,0:T(8,128)(2,1)} %bitcast.25), calls=%async_computation.1 | async-start | bytes 2097152 | tf_op jit(solution)/shard_map/all_to_all | solution.py:399
  55.8 2.4 %copy-start.3 = (f32[16,1024]{1,0:T(8,128)S(1)}, f32[16,1024]{1,0:T(8,128)}, u32[]{:S(2)}) copy-start(f32[16,1024]{1,0:T(8,128)} %get-tuple-element.22.refs_0_) | copy-start | bytes 196612
  56.3 4.2 %copy-start.8 = (s32[1024]{0:T(1024)S(1)}, s32[1024]{0:T(1024)}, u32[]{:S(2)}) copy-start(s32[1024]{0:T(1024)} %get-tuple-element.54) | copy-start | bytes 12292
  56.3 4.2 %copy-start.10 = (s32[1024]{0:T(1024)S(1)}, s32[1024]{0:T(1024)}, u32[]{:S(2)}) copy-start(s32[1024]{0:T(1024)} %get-tuple-element.53) | copy-start | bytes 12292
  58.3 2.8 %copy-start.14 = (s32[64]{0:T(128)S(1)}, s32[64]{0:T(128)}, u32[]{:S(2)}) copy-start(s32[64]{0:T(128)} %broadcast_multiply_fusion.2) | copy-start | bytes 772
  58.3 2.8 %copy-start.15 = (s32[64]{0:T(128)S(1)}, s32[64]{0:T(128)}, u32[]{:S(2)}) copy-start(s32[64]{0:T(128)} %get-tuple-element.44) | copy-start | bytes 772
  58.3 2.8 %copy-start.16 = (s32[64]{0:T(128)S(1)}, s32[64]{0:T(128)}, u32[]{:S(2)}) copy-start(s32[64]{0:T(128)} %get-tuple-element.45) | copy-start | bytes 772
  60.4 4.0 %copy-start.12 = (s32[16]{0:T(128)S(1)}, s32[16]{0:T(128)}, u32[]{:S(2)}) copy-start(s32[16]{0:T(128)} %get-tuple-element.42) | copy-start | bytes 196
  60.4 4.0 %copy-start.13 = (s32[16]{0:T(128)S(1)}, s32[16]{0:T(128)}, u32[]{:S(2)}) copy-start(s32[16]{0:T(128)} %get-tuple-element.48) | copy-start | bytes 196
  60.4 4.4 %copy-start.17 = (s32[64]{0:T(128)S(1)}, s32[64]{0:T(128)}, u32[]{:S(2)}) copy-start(s32[64]{0:T(128)} %get-tuple-element.43) | copy-start | bytes 772
  60.4 4.4 %copy-start.18 = (s32[64]{0:T(128)S(1)}, s32[64]{0:T(128)}, u32[]{:S(2)}) copy-start(s32[64]{0:T(128)} %get-tuple-element.46) | copy-start | bytes 772
  64.4 2.2 %copy-start.7 = (bf16[64,64]{1,0:T(8,128)(2,1)S(1)}, bf16[64,64]{1,0:T(8,128)(2,1)}, u32[]{:S(2)}) copy-start(bf16[64,64]{1,0:T(8,128)(2,1)} %get-tuple-element.52) | copy-start | bytes 24580
  94.7 7.5 %copy-start.11 = (f32[3,3,256]{2,1,0:T(4,128)S(1)}, f32[3,3,256]{2,1,0:T(4,128)}, u32[]{:S(2)}) copy-start(f32[3,3,256]{2,1,0:T(4,128)} %param.9) | copy-start | bytes 27652
  94.7 7.5 %copy-start.9 = (s32[1024]{0:T(1024)S(1)}, s32[1024]{0:T(1024)}, u32[]{:S(2)}) copy-start(s32[1024]{0:T(1024)} %get-tuple-element.54) | copy-start | bytes 12292
  94.7 39.1 %all-to-all-start.2 = ((bf16[128,8,512]{2,1,0:T(8,128)(2,1)}), bf16[128,8,512]{2,1,0:T(8,128)(2,1)}, u32[]{:S(2)}, u32[]{:S(2)}) async-start(bf16[128,8,512]{2,1,0:T(8,128)(2,1)} %bitcast.27), calls=%async_computation.2 | async-start | bytes 2097152 | tf_op jit(solution)/shard_map/all_to_all | solution.py:408
  103.6 25.3 %collective-permute-start = (bf16[512,128]{1,0:T(8,128)(2,1)S(1)}, bf16[512,128]{1,0:T(8,128)(2,1)S(1)}, u32[]{:S(2)}, u32[]{:S(2)}) collective-permute-start(bf16[512,128]{1,0:T(8,128)(2,1)S(1)} %pad_maximum_fusion), channel_id=1, source_target_pairs={{0,4},{4,8},{8,12},{12,16},{16,20},{20,24},{24,28},{28,32},{32,36}... | collective-permute-start | bytes 393224 | tf_op jit(solution)/shard_map/ppermute | solution.py:403
  107.0 23.1 %collective-permute-start.1 = (bf16[512,128]{1,0:T(8,128)(2,1)S(1)}, bf16[512,128]{1,0:T(8,128)(2,1)S(1)}, u32[]{:S(2)}, u32[]{:S(2)}) collective-permute-start(bf16[512,128]{1,0:T(8,128)(2,1)S(1)} %pad_maximum_fusion.1), channel_id=1, source_target_pairs={{4,0},{8,4},{12,8},{16,12},{20,16},{24,20},{28,24},{32,28},{36,32}... | collective-permute-start | bytes 393224 | tf_op jit(solution)/shard_map/ppermute | solution.py:404
  138.7 31.7 %copy-start.1 = (bf16[32,64,256]{2,1,0:T(8,128)(2,1)S(1)}, bf16[32,64,256]{2,1,0:T(8,128)(2,1)}, u32[]{:S(2)}) copy-start(bf16[32,64,256]{2,1,0:T(8,128)(2,1)} %x_ref.3) | copy-start | bytes 3145732

commit v3 on v2

--- a/solution.py
+++ b/solution.py
@@ -158,7 +158,7 @@
         out_shape=pltpu.HBM((16, 64, 512), BF16),
         compiler_params=pltpu.CompilerParams(vmem_limit_bytes=12 * MIB),
         name="norm_pack",
-    )(patches, gain.reshape(1, 256))
+    )(remaining(patches), gain.reshape(1, 256))
 
 
 def final_kernel(x_ref, home_ref, out_ref):
@@ -217,8 +217,41 @@
         copy.wait()
 
 
-def columns_kernel(table_ref, x_ref, out_any, held, sems):
+def columns_kernel(
+    table_ref, x_ref, out_any, lines_any, last_ref, leading_ref, held, sems, line_sem
+):
+    keep = pltpu.make_async_copy(x_ref, lines_any, line_sem)
+    keep.start()
     stream_dot(table_ref, x_ref, None, held, out_any, sems)
+    low = low_half(512)
+    top, bottom = x_ref[:512, 384:].astype(F32), x_ref[512:, 384:].astype(F32)
+    last_ref[...] = jnp.where(low, swap(top), bottom).astype(BF16)
+    top, bottom = x_ref[:512, :128].astype(F32), x_ref[512:, :128].astype(F32)
+    leading_ref[...] = jnp.where(low, top, swap(bottom)).astype(BF16)
+    keep.wait()
+
+
+def forward_columns(table, x):
+    vmem, hbm = pl.BlockSpec(memory_space=pltpu.VMEM), pl.BlockSpec(memory_space=pltpu.HBM)
+    return pl.pallas_call(
+        columns_kernel,
+        in_specs=[vmem] * 2,
+        out_specs=[hbm, hbm, vmem, vmem],
+        out_shape=[
+            pltpu.HBM((1024, 512), BF16),
+            pltpu.HBM((1024, 512), BF16),
+            jax.ShapeDtypeStruct((512, 128), BF16),
+            jax.ShapeDtypeStruct((512, 128), BF16),
+        ],
+        scratch_shapes=[
+            pltpu.VMEM((1024, 512), BF16),
+            pltpu.SemaphoreType.DMA((4,)),
+            pltpu.SemaphoreType.DMA,
+        ],
+        cost_estimate=pl.CostEstimate(flops=2**30, bytes_accessed=2**21, transcendentals=0),
+        compiler_params=pltpu.CompilerParams(vmem_limit_bytes=12 * MIB),
+        name="forward_columns",
+    )(resident(table), resident(x))
 
 
 def columns_add_kernel(table_ref, x_ref, extra_any, out_any, held, sems, extra, extra_sems):
@@ -232,21 +265,23 @@
     stream_dot(table_ref, x_ref, (*fetches, extra), held, out_any, sems)
 
 
-def columns(table, x, *extra):
-    scratch = [pltpu.VMEM((1024, 512), BF16), pltpu.SemaphoreType.DMA((4,))]
-    if extra:
-        scratch += [pltpu.VMEM((1024, 512), F32), pltpu.SemaphoreType.DMA((4,))]
-    return pl.pallas_call(
-        columns_add_kernel if extra else columns_kernel,
-        in_specs=[pl.BlockSpec(memory_space=pltpu.VMEM)] * 2
-        + [pl.BlockSpec(memory_space=pltpu.HBM)] * len(extra),
-        out_specs=pl.BlockSpec(memory_space=pltpu.HBM),
+def backward_columns(table, x, extra):
+    vmem, hbm = pl.BlockSpec(memory_space=pltpu.VMEM), pl.BlockSpec(memory_space=pltpu.HBM)
+    return pl.pallas_call(
+        columns_add_kernel,
+        in_specs=[vmem, vmem, hbm],
+        out_specs=hbm,
         out_shape=pltpu.HBM((1024, 512), BF16),
-        scratch_shapes=scratch,
+        scratch_shapes=[
+            pltpu.VMEM((1024, 512), BF16),
+            pltpu.SemaphoreType.DMA((4,)),
+            pltpu.VMEM((1024, 512), F32),
+            pltpu.SemaphoreType.DMA((4,)),
+        ],
         cost_estimate=pl.CostEstimate(flops=2**30, bytes_accessed=2**21, transcendentals=0),
         compiler_params=pltpu.CompilerParams(vmem_limit_bytes=12 * MIB),
-        name="along_columns",
-    )(resident(table), resident(x), *[remaining(e) for e in extra])
+        name="backward_columns",
+    )(resident(table), resident(x), remaining(extra))
 
 
 def stencil_kernel(x_ref, above_ref, below_ref, taps_ref, out_ref):
@@ -299,7 +334,7 @@
         cost_estimate=pl.CostEstimate(flops=2**24, bytes_accessed=2**22, transcendentals=0),
         compiler_params=pltpu.CompilerParams(vmem_limit_bytes=16 * MIB),
         name="stencil",
-    )(resident(x), above, below, taps)
+    )(x, above, below, taps)
 
 
 def middle_kernel(
@@ -378,10 +413,6 @@
     )
 
 
-def packed_row(lines, lane):
-    return jnp.concatenate([lines[:512, lane : lane + 64], lines[512:, lane : lane + 64]], axis=1)
-
-
 def local(patches, norm_gain, w_first, w_second, depth_kernel):
     packed = norm_and_pack(patches, norm_gain)
     lines = lax.all_to_all(packed, ("yl", "x"), 0, 0, tiled=True).reshape(1024, 512)
@@ -395,18 +426,20 @@
     first = first_layer(wf[0], wf[1])
     second = second_layer(ws[0], ws[1])
 
-    freqs = columns(fwd_w, lines).reshape(128, 8, 512)
-    whole = lax.all_to_all(freqs, ("row", "yl"), 0, 0, tiled=True).reshape(1024, 512)
+    freqs, kept, last, leading = forward_columns(fwd_w, lines)
+    whole = lax.all_to_all(freqs.reshape(128, 8, 512), ("row", "yl"), 0, 0, tiled=True)
     groups = 128
     down = [(i, (i + 1) % groups) for i in range(groups)]
     up = [(j, i) for i, j in down]
-    above = lax.ppermute(packed_row(lines, 448), ("row", "yl"), down)
-    below = lax.ppermute(packed_row(lines, 0), ("row", "yl"), up)
-    conv = stencil(lines, above, below, taps)
-
-    filtered = middle(whole, fwd_h, first, eight, inv_h, second, cos, sin)
+    above = lax.ppermute(last, ("row", "yl"), down)
+    below = lax.ppermute(leading, ("row", "yl"), up)
+    whole, above, below = lax.optimization_barrier((whole, above, below))
+
+    filtered = middle(whole.reshape(1024, 512), fwd_h, first, eight, inv_h, second, cos, sin)
+    filtered, above, below = lax.optimization_barrier((filtered, above, below))
     back = lax.all_to_all(filtered.reshape(128, 8, 512), ("row", "yl"), 0, 0, tiled=True)
-    summed = columns(inv_w, back.reshape(1024, 512), conv).reshape(16, 64, 512)
+    conv = stencil(kept, above, below, taps)
+    summed = backward_columns(inv_w, back.reshape(1024, 512), conv).reshape(16, 64, 512)
     home = lax.all_to_all(summed, ("yl", "x"), 0, 0, tiled=True)
     return unpack_and_add(patches, home)
 

time: 173 us -> 174 us (level)
  waiting for transfers between devices: 51.2 us -> 41 us
  local copies, waits for them, and re-layouts: 3.72 us -> 8.44 us
  starting transfers between devices: 38 us -> 41.5 us
  other arithmetic: 15 us -> 17.2 us
    all_to_all x1, waiting for transfers between devices: 0.01 us -> 22.6 us  [local(): lax.all_to_all(filtered.reshape(128, 8, 512), ('row', 'yl'), 0, 0, tiled=...]
    ppermute x2, waiting for transfers between devices: 19.9 us -> 2.22 us  [the longest x1 1.57 us: local(): below = lax.ppermute(leading, ('row', 'yl'), up)]
    all_to_all x1, waiting for transfers between devices: 17.1 us -> 1.8 us  [local(): lax.all_to_all(freqs.reshape(128, 8, 512), ('row', 'yl'), 0, 0, tiled=True)]
    all_to_all x1, starting transfers between devices: 7.45 us -> 11.2 us  [local(): lax.all_to_all(filtered.reshape(128, 8, 512), ('row', 'yl'), 0, 0, tiled=...]
    mul x4, other arithmetic: 5.31 us -> 7.41 us  [phase_table(): -sin_of(ib) * scale]
    another operation x2, local copies, waits for them, and re-layouts: 0.21 us -> 2.02 us  [first_layer(): jnp.tile(w0.astype(F32), (1, 16))]
    another operation x2, local copies, waits for them, and re-layouts: 0.21 us -> 2.02 us  [first_layer(): jnp.tile(w1.astype(F32), (1, 16))]
  transfers between devices with their start and end apart: 5 -> 5, of which waited for: 4 -> 5; matrix products, arithmetic and copies ran while one was open for 9% -> 13% of each run, Pallas kernels for 7% -> 7%
where the time goes in v3:
time: 174 us; the launch traced here: 173 us
  starting transfers between devices  41.5 us (24%)
  waiting for transfers between devices  41 us (24%)
  Pallas kernels  33.1 us (19%)
  blocking collectives  31.6 us (18%)
  other arithmetic  17.2 us (10%)
  local copies, waits for them, and re-layouts  8.44 us (5%)
    all_to_all x1, blocking collectives, local(): home = lax.all_to_all(summed, ('yl', 'x'), 0, 0, tiled=True)  31.6 us
    all_to_all x1, waiting for transfers between devices, local(): lax.all_to_all(filtered.reshape(128, 8, 512), ('row', 'yl'), 0, 0, tiled=...  22.6 us
    all_to_all x1, starting transfers between devices, local(): lax.all_to_all(freqs.reshape(128, 8, 512), ('row', 'yl'), 0, 0, tiled=True)  15 us
    all_to_all x1, waiting for transfers between devices, local(): lax.all_to_all(packed, ('yl', 'x'), 0, 0, tiled=True).reshape(1024, 512)  14.4 us
    all_to_all x1, starting transfers between devices, local(): lax.all_to_all(filtered.reshape(128, 8, 512), ('row', 'yl'), 0, 0, tiled=...  11.2 us
    all_to_all x1, starting transfers between devices, local(): lax.all_to_all(packed, ('yl', 'x'), 0, 0, tiled=True).reshape(1024, 512)  9.29 us
    pallas_call x6, Pallas kernels, outer_table(): pl.pallas_call(functools.partial(expand_kernel, 16 if stay else 4), grid=...  8.14 us
    pallas_call x1, Pallas kernels, middle(): pl.pallas_call(middle_kernel, in_specs=[vmem] * 3 + [hbm] * 5, out_specs=...  7.65 us
  transfers between devices with their start and end apart: 5, of which 5 were waited for; matrix products, arithmetic and copies ran while one was open for 13% of the time, Pallas kernels for 7%

profile of v3, /device:TPU:8, one launch (start us, length us, event | category | flops | bytes accessed | tf_op | source)
XLA Modules:
  0.0 173.4 jit_solution(18371762691099804225)
XLA Ops:
  0.7 4.3 %norm_pack.1 = bf16[16,64,512]{2,1,0:T(8,128)(2,1)} custom-call(bf16[32,64,256]{2,1,0:T(8,128)(2,1)} %x_ref.3, f32[1,256]{1,0:T(1,128)S(1)} %bitcast.24), custom_call_target="tpu_custom_call" | custom-call | tf_op jit(solution)/shard_map/norm_pack/pallas_call | solution.py:150
  5.0 9.3 %all-to-all-start = ((bf16[16,64,512]{2,1,0:T(8,128)(2,1)}), bf16[16,64,512]{2,1,0:T(8,128)(2,1)S(1)}, u32[]{:S(2)}, u32[]{:S(2)}) async-start(bf16[16,64,512]{2,1,0:T(8,128)(2,1)} %norm_pack.1), calls=%async_computation | async-start | bytes 2097152 | tf_op jit(solution)/shard_map/all_to_all | solution.py:418
  14.6 1.9 %negate_multiply_fusion = (f32[64,1024]{1,0:T(8,128)S(1)}, f32[64,1024]{1,0:T(8,128)}) fusion(s32[64]{0:T(128)S(1)} %get-tuple-element.66, s32[64]{0:T(128)S(1)} %get-tuple-element.65), kind=kLoop, calls=%fused_computation.39 | loop fusion | flops 1179648 | bytes 524800 | tf_op jit(solution)/shard_map/mul | solution.py:59
  17.2 0.9 copy-done.3
  21.3 1.4 fusion.53
  24.1 14.4 %all-to-all-done = bf16[16,64,512]{2,1,0:T(8,128)(2,1)S(1)} async-done(((bf16[16,64,512]{2,1,0:T(8,128)(2,1)}), bf16[16,64,512]{2,1,0:T(8,128)(2,1)S(1)}, u32[]{:S(2)}, u32[]{:S(2)}) %all-to-all-start) | async-done | bytes 1048608 | tf_op jit(solution)/shard_map/all_to_all | solution.py:418
  38.5 2.9 %forward_columns.1 = (bf16[1024,512]{1,0:T(8,128)(2,1)}, bf16[1024,512]{1,0:T(8,128)(2,1)}, bf16[512,128]{1,0:T(8,128)(2,1)}, bf16[512,128]{1,0:T(8,128)(2,1)}) custom-call(bf16[1024,1024]{1,0:T(8,128)(2,1)S(1)} %expand_table.7.table_ref, bf16[1024,512]{1,0:T(8,128)(2,1)S(1)} %bitcast.23), custom_call_target="tpu_custom_call" | custom-call | flops 1073741824 | bytes 2097152 | tf_op jit(solution)/shard_map/forward_columns/pallas_call | solution.py:236
  41.5 15.0 %all-to-all-start.1 = ((bf16[128,8,512]{2,1,0:T(8,128)(2,1)}), bf16[128,8,512]{2,1,0:T(8,128)(2,1)S(1)}, u32[]{:S(2)}, u32[]{:S(2)}) async-start(bf16[128,8,512]{2,1,0:T(8,128)(2,1)} %bitcast.26), calls=%async_computation.1 | async-start | bytes 2097152 | tf_op jit(solution)/shard_map/all_to_all | solution.py:430
  57.6 1.2 fusion.49
  58.8 1.8 %fusion.19 = (f32[128,512]{1,0:T(8,128)}, f32[128,512]{1,0:T(8,128)}) fusion(s32[512]{0:T(512)S(1)} %add_select_fusion.34), kind=kLoop, calls=%fused_computation.46 | loop fusion | flops 917504 | bytes 526336 | tf_op jit(solution)/shard_map/sin | solution.py:25
  60.6 2.6 %select_multiply_fusion.2 = (f32[64,1024]{1,0:T(8,128)S(1)}, f32[64,1024]{1,0:T(8,128)}) fusion(s32[1024]{0:T(1024)S(1)} %copy-done.20, s32[1024]{0:T(1024)} %copy-done.17, s32[64]{0:T(128)S(1)} %copy-done.26, s32[64]{0:T(128)S(1)} %copy-done.25), kind=kLoop, calls=%fused_computation.19 | loop fusion | flops 1245184 | bytes 532992 | tf_op jit(solution)/shard_map/mul | solution.py:59
  63.3 1.9 %select_multiply_fusion = (f32[64,1024]{1,0:T(8,128)S(1)}, f32[64,1024]{1,0:T(8,128)S(1)}) fusion(s32[1024]{0:T(1024)S(1)} %copy-done.18, s32[64]{0:T(128)S(1)} %copy-done.23, s32[1024]{0:T(1024)S(1)} %copy-done.19, s32[1024]{0:T(1024)} %copy-done.16, s32[64]{0:T(128)S(1)} %copy-done.22, s32[64]{0:T(128)S(1)} %copy-done.24), kind=kLoop, calls=%fused_computation.17 | loop fusion | flops 1441792 | bytes 537344 | tf_op jit(solution)/shard_map/mul | solution.py:59
  65.1 3.4 %collective-permute-start = (bf16[512,128]{1,0:T(8,128)(2,1)}, bf16[512,128]{1,0:T(8,128)(2,1)}, u32[]{:S(2)}, u32[]{:S(2)}) collective-permute-start(bf16[512,128]{1,0:T(8,128)(2,1)} %get-tuple-element.16), channel_id=1, source_target_pairs={{0,4},{4,8},{8,12},{12,16},{16,20},{20,24},{24,28},{28,32},{32,36}... | collective-permute-start | bytes 393224 | tf_op jit(solution)/shard_map/ppermute | solution.py:434
  68.5 2.7 %collective-permute-start.1 = (bf16[512,128]{1,0:T(8,128)(2,1)}, bf16[512,128]{1,0:T(8,128)(2,1)}, u32[]{:S(2)}, u32[]{:S(2)}) collective-permute-start(bf16[512,128]{1,0:T(8,128)(2,1)} %get-tuple-element.17), channel_id=1, source_target_pairs={{4,0},{8,4},{12,8},{16,12},{20,16},{24,20},{28,24},{32,28},{36,32}... | collective-permute-start | bytes 393224 | tf_op jit(solution)/shard_map/ppermute | solution.py:435
  71.8 0.8 tile.20
  72.6 1.2 tile.21.refs_3_
  73.8 0.8 tile.8
  74.7 1.2 tile.9.refs_2_
  75.8 2.0 %expand_table.10.eight_any = bf16[1024,1024]{1,0:T(8,128)(2,1)} custom-call(f32[16,1024]{1,0:T(8,128)S(1)} %fusion.35.refs_0_, f32[64,1024]{1,0:T(8,128)S(1)} %fusion.18.refs_1_), custom_call_target="tpu_custom_call" | custom-call | flops 3145728 | bytes 2097152 | tf_op jit(solution)/shard_map/expand_table/pallas_call | solution.py:46
  77.8 2.1 %expand_table.9.first_any = bf16[1024,1024]{1,0:T(8,128)(2,1)} custom-call(f32[16,1024]{1,0:T(8,128)S(1)} %get-tuple-element.38.refs_0_, f32[16,1024]{1,0:T(8,128)S(1)} %get-tuple-element.37.refs_1_, f32[64,1024]{1,0:T(8,128)S(1)} %tile.9.refs_2_, f32[64,1024]{1,0:T(8,128)S(1)} %tile.21.refs_3_), custom_call_target="tpu_custom_call" | custom-call | flops 3145728 | bytes 2097152 | tf_op jit(solution)/shard_map/expand_table/pallas_call | solution.py:46
  80.0 2.1 %expand_table.11.inv_any = bf16[1024,1024]{1,0:T(8,128)(2,1)} custom-call(f32[16,1024]{1,0:T(8,128)S(1)} %get-tuple-element.44.refs_0_, f32[16,1024]{1,0:T(8,128)S(1)} %get-tuple-element.43.refs_1_, f32[64,1024]{1,0:T(8,128)S(1)} %get-tuple-element.34.refs_2_, f32[64,1024]{1,0:T(8,128)S(1)} %get-tuple-element.33.refs_3_), custom_call_target="tpu_custom_call" | custom-call | flops 3145728 | bytes 2097152 | tf_op jit(solution)/shard_map/expand_table/pallas_call | solution.py:46
  83.5 1.6 collective-permute-done.1.below_ref
  85.0 1.8 %all-to-all-done.1 = bf16[128,8,512]{2,1,0:T(8,128)(2,1)S(1)} async-done(((bf16[128,8,512]{2,1,0:T(8,128)(2,1)}), bf16[128,8,512]{2,1,0:T(8,128)(2,1)S(1)}, u32[]{:S(2)}, u32[]{:S(2)}) %all-to-all-start.1) | async-done | bytes 1048608 | tf_op jit(solution)/shard_map/all_to_all | solution.py:430
  86.8 7.7 %filter_rows.1 = bf16[1024,512]{1,0:T(8,128)(2,1)} custom-call(bf16[1024,512]{1,0:T(8,128)(2,1)S(1)} %bitcast.22, bf16[1024,1024]{1,0:T(8,128)(2,1)S(1)} %expand_table.8.fwd, bf16[256,256]{1,0:T(8,128)(2,1)S(1)} %maximum_maximum_fusion.second_ref, f32[128,512]{1,0:T(8,128)} %get-tuple-element.48.cos_any, f32[128,512]{1,0:T(8,128)} %get-tuple-element.47.sin_any, ...), custom_call_target="tpu_custom_call" | custom-call | flops 5368709120 | bytes 2097152 | tf_op jit(solution)/shard_map/filter_rows/pallas_call | solution.py:391
  94.5 11.2 %all-to-all-start.2 = ((bf16[128,8,512]{2,1,0:T(8,128)(2,1)}), bf16[128,8,512]{2,1,0:T(8,128)(2,1)S(1)}, u32[]{:S(2)}, u32[]{:S(2)}) async-start(bf16[128,8,512]{2,1,0:T(8,128)(2,1)} %bitcast.27), calls=%async_computation.2 | async-start | bytes 2097152 | tf_op jit(solution)/shard_map/all_to_all | solution.py:440
  105.8 1.1 negate_multiply_fusion.1
  107.7 1.2 copy-done.1
  108.9 4.6 %stencil.1.extra_any = f32[1024,512]{1,0:T(8,128)} custom-call(bf16[1024,512]{1,0:T(8,128)(2,1)S(1)} %copy-done.1, bf16[512,128]{1,0:T(8,128)(2,1)} %collective-permute-done.above_ref, bf16[512,128]{1,0:T(8,128)(2,1)} %collective-permute-done.1.below_ref, f32[9,128]{1,0:T(8,128)S(1)} %pad_maximum_fusion.taps_ref), custom_call_target="tpu_custom_call" | custom-call | flops 16777216 | bytes 4194304 | tf_op jit(solution)/shard_map/stencil/pallas_call | solution.py:328
  113.6 22.6 %all-to-all-done.2 = bf16[128,8,512]{2,1,0:T(8,128)(2,1)S(1)} async-done(((bf16[128,8,512]{2,1,0:T(8,128)(2,1)}), bf16[128,8,512]{2,1,0:T(8,128)(2,1)S(1)}, u32[]{:S(2)}, u32[]{:S(2)}) %all-to-all-start.2) | async-done | bytes 1048608 | tf_op jit(solution)/shard_map/all_to_all | solution.py:440
  136.2 3.6 %backward_columns.1 = bf16[1024,512]{1,0:T(8,128)(2,1)} custom-call(bf16[1024,1024]{1,0:T(8,128)(2,1)S(1)} %expand_table.6.table_ref, bf16[1024,512]{1,0:T(8,128)(2,1)S(1)} %bitcast.21, f32[1024,512]{1,0:T(8,128)} %stencil.1.extra_any), custom_call_target="tpu_custom_call" | custom-call | flops 1073741824 | bytes 2097152 | tf_op jit(solution)/shard_map/backward_columns/pallas_call | solution.py:270
  139.8 31.6 %all_to_all.20.home_ref = bf16[16,64,512]{2,1,0:T(8,128)(2,1)S(1)} all-to-all(bf16[16,64,512]{2,1,0:T(8,128)(2,1)} %bitcast.25), channel_id=1, replica_groups=mesh['row'=32,'yl'=4,'x'=4] {'yl','x'}, dimensions={0} | all-to-all | bytes 2097152 | tf_op jit(solution)/shard_map/all_to_all | solution.py:443
  171.5 1.9 %unpack_add.1 = bf16[32,64,256]{2,1,0:T(8,128)(2,1)} custom-call(bf16[32,64,256]{2,1,0:T(8,128)(2,1)S(1)} %copy-done, bf16[16,64,512]{2,1,0:T(8,128)(2,1)S(1)} %all_to_all.20.home_ref), custom_call_target="tpu_custom_call" | custom-call | tf_op jit(solution)/shard_map/unpack_add/pallas_call | solution.py:179
  (87 shorter events, 10.0 us)
Async XLA Ops:
  0.0 0.7 copy-start.6
  5.0 33.5 %all-to-all-start = ((bf16[16,64,512]{2,1,0:T(8,128)(2,1)}), bf16[16,64,512]{2,1,0:T(8,128)(2,1)S(1)}, u32[]{:S(2)}, u32[]{:S(2)}) async-start(bf16[16,64,512]{2,1,0:T(8,128)(2,1)} %norm_pack.1), calls=%async_computation | async-start | bytes 2097152 | tf_op jit(solution)/shard_map/all_to_all | solution.py:418
  17.2 0.9 copy-start.3
  20.6 36.9 %copy-start.14 = (s32[1024]{0:T(1024)}, s32[1024]{0:T(1024)S(1)}, u32[]{:S(2)}) copy-start(s32[1024]{0:T(1024)S(1)} %get-tuple-element.70) | copy-start | bytes 12292
  20.6 36.9 %copy-start.16 = (s32[1024]{0:T(1024)}, s32[1024]{0:T(1024)S(1)}, u32[]{:S(2)}) copy-start(s32[1024]{0:T(1024)S(1)} %get-tuple-element.69) | copy-start | bytes 12292
  21.3 35.9 %copy-start.17 = (s32[1024]{0:T(1024)}, s32[1024]{0:T(1024)S(1)}, u32[]{:S(2)}) copy-start(s32[1024]{0:T(1024)S(1)} %get-tuple-element.72) | copy-start | bytes 12292
  41.4 19.3 %copy-start.20 = (s32[1024]{0:T(1024)S(1)}, s32[1024]{0:T(1024)}, u32[]{:S(2)}) copy-start(s32[1024]{0:T(1024)} %fusion.55) | copy-start | bytes 12292
  41.4 19.2 %copy-start.25 = (s32[64]{0:T(128)S(1)}, s32[64]{0:T(128)}, u32[]{:S(2)}) copy-start(s32[64]{0:T(128)} %get-tuple-element.59) | copy-start | bytes 772
  41.4 19.2 %copy-start.26 = (s32[64]{0:T(128)S(1)}, s32[64]{0:T(128)}, u32[]{:S(2)}) copy-start(s32[64]{0:T(128)} %get-tuple-element.62) | copy-start | bytes 772
  41.4 21.8 %copy-start.18 = (s32[1024]{0:T(1024)S(1)}, s32[1024]{0:T(1024)}, u32[]{:S(2)}) copy-start(s32[1024]{0:T(1024)} %get-tuple-element.77) | copy-start | bytes 12292
  41.4 21.8 %copy-start.19 = (s32[1024]{0:T(1024)S(1)}, s32[1024]{0:T(1024)}, u32[]{:S(2)}) copy-start(s32[1024]{0:T(1024)} %get-tuple-element.78) | copy-start | bytes 12292
  41.4 21.8 %copy-start.22 = (s32[64]{0:T(128)S(1)}, s32[64]{0:T(128)}, u32[]{:S(2)}) copy-start(s32[64]{0:T(128)} %broadcast_multiply_fusion.2) | copy-start | bytes 772
  41.4 21.8 %copy-start.23 = (s32[64]{0:T(128)S(1)}, s32[64]{0:T(128)}, u32[]{:S(2)}) copy-start(s32[64]{0:T(128)} %get-tuple-element.60) | copy-start | bytes 772
  41.4 21.8 %copy-start.24 = (s32[64]{0:T(128)S(1)}, s32[64]{0:T(128)}, u32[]{:S(2)}) copy-start(s32[64]{0:T(128)} %get-tuple-element.61) | copy-start | bytes 772
  41.5 29.7 %copy-start.7 = (bf16[64,128]{1,0:T(8,128)(2,1)S(1)}, bf16[64,128]{1,0:T(8,128)(2,1)}, u32[]{:S(2)}) copy-start(bf16[64,128]{1,0:T(8,128)(2,1)} %get-tuple-element.30) | copy-start | bytes 49156
  41.5 30.3 %copy-start.10 = (f32[64,64]{1,0:T(8,128)S(1)}, f32[64,64]{1,0:T(8,128)}, u32[]{:S(2)}) copy-start(f32[64,64]{1,0:T(8,128)} %get-tuple-element.25) | copy-start | bytes 49156
  41.5 45.4 %all-to-all-start.1 = ((bf16[128,8,512]{2,1,0:T(8,128)(2,1)}), bf16[128,8,512]{2,1,0:T(8,128)(2,1)S(1)}, u32[]{:S(2)}, u32[]{:S(2)}) async-start(bf16[128,8,512]{2,1,0:T(8,128)(2,1)} %bitcast.26), calls=%async_computation.1 | async-start | bytes 2097152 | tf_op jit(solution)/shard_map/all_to_all | solution.py:430
  56.5 17.4 %copy-start.9 = (f32[64,64]{1,0:T(8,128)S(1)}, f32[64,64]{1,0:T(8,128)}, u32[]{:S(2)}) copy-start(f32[64,64]{1,0:T(8,128)} %get-tuple-element.26) | copy-start | bytes 49156
  65.1 18.4 %collective-permute-start = (bf16[512,128]{1,0:T(8,128)(2,1)}, bf16[512,128]{1,0:T(8,128)(2,1)}, u32[]{:S(2)}, u32[]{:S(2)}) collective-permute-start(bf16[512,128]{1,0:T(8,128)(2,1)} %get-tuple-element.16), channel_id=1, source_target_pairs={{0,4},{4,8},{8,12},{12,16},{16,20},{20,24},{24,28},{28,32},{32,36}... | collective-permute-start | bytes 393224 | tf_op jit(solution)/shard_map/ppermute | solution.py:434
  68.5 16.5 %collective-permute-start.1 = (bf16[512,128]{1,0:T(8,128)(2,1)}, bf16[512,128]{1,0:T(8,128)(2,1)}, u32[]{:S(2)}, u32[]{:S(2)}) collective-permute-start(bf16[512,128]{1,0:T(8,128)(2,1)} %get-tuple-element.17), channel_id=1, source_target_pairs={{4,0},{8,4},{12,8},{16,12},{20,16},{24,20},{28,24},{32,28},{36,32}... | collective-permute-start | bytes 393224 | tf_op jit(solution)/shard_map/ppermute | solution.py:435
  77.8 4.3 %copy-start.2 = (f32[64,1024]{1,0:T(8,128)S(1)}, f32[64,1024]{1,0:T(8,128)}, u32[]{:S(2)}) copy-start(f32[64,1024]{1,0:T(8,128)} %get-tuple-element.40.refs_2_) | copy-start | bytes 786436
  80.0 2.8 %copy-start.8 = (bf16[64,128]{1,0:T(8,128)(2,1)S(1)}, bf16[64,128]{1,0:T(8,128)(2,1)}, u32[]{:S(2)}) copy-start(bf16[64,128]{1,0:T(8,128)(2,1)} %get-tuple-element.30) | copy-start | bytes 49156
  80.0 2.8 %copy-start.11 = (bf16[128,128]{1,0:T(8,128)(2,1)S(1)}, bf16[128,128]{1,0:T(8,128)(2,1)}, u32[]{:S(2)}) copy-start(bf16[128,128]{1,0:T(8,128)(2,1)} %maximum_negate_fusion) | copy-start | bytes 98308
  80.0 2.8 %copy-start.12 = (bf16[64,128]{1,0:T(8,128)(2,1)S(1)}, bf16[64,128]{1,0:T(8,128)(2,1)}, u32[]{:S(2)}) copy-start(bf16[64,128]{1,0:T(8,128)(2,1)} %get-tuple-element.31) | copy-start | bytes 49156
  80.0 2.8 %copy-start.13 = (bf16[64,128]{1,0:T(8,128)(2,1)S(1)}, bf16[64,128]{1,0:T(8,128)(2,1)}, u32[]{:S(2)}) copy-start(bf16[64,128]{1,0:T(8,128)(2,1)} %get-tuple-element.32) | copy-start | bytes 49156
  94.5 11.3 %copy-start.21 = (f32[3,3,256]{2,1,0:T(4,128)S(1)}, f32[3,3,256]{2,1,0:T(4,128)}, u32[]{:S(2)}) copy-start(f32[3,3,256]{2,1,0:T(4,128)} %param.9) | copy-start | bytes 27652
  94.5 11.3 %copy-start.15 = (s32[1024]{0:T(1024)S(1)}, s32[1024]{0:T(1024)}, u32[]{:S(2)}) copy-start(s32[1024]{0:T(1024)} %copy-done.14) | copy-start | bytes 12292
  94.5 12.4 %copy-start.4 = (f32[16,1024]{1,0:T(8,128)S(1)}, f32[16,1024]{1,0:T(8,128)}, u32[]{:S(2)}) copy-start(f32[16,1024]{1,0:T(8,128)} %get-tuple-element.51.refs_0_) | copy-start | bytes 196612
  94.5 12.4 %copy-start.5 = (f32[16,1024]{1,0:T(8,128)S(1)}, f32[16,1024]{1,0:T(8,128)}, u32[]{:S(2)}) copy-start(f32[16,1024]{1,0:T(8,128)} %get-tuple-element.52.refs_1_) | copy-start | bytes 196612
  94.5 41.6 %all-to-all-start.2 = ((bf16[128,8,512]{2,1,0:T(8,128)(2,1)}), bf16[128,8,512]{2,1,0:T(8,128)(2,1)S(1)}, u32[]{:S(2)}, u32[]{:S(2)}) async-start(bf16[128,8,512]{2,1,0:T(8,128)(2,1)} %bitcast.27), calls=%async_computation.2 | async-start | bytes 2097152 | tf_op jit(solution)/shard_map/all_to_all | solution.py:440
  107.7 1.2 copy-start.1
  139.8 31.7 %copy-start = (bf16[32,64,256]{2,1,0:T(8,128)(2,1)S(1)}, bf16[32,64,256]{2,1,0:T(8,128)(2,1)}, u32[]{:S(2)}) copy-start(bf16[32,64,256]{2,1,0:T(8,128)(2,1)} %x_ref.3) | copy-start | bytes 3145732

commit v4 on v3

v4 whole, which is shorter than its diff:
```python
import functools
import math

import jax
import jax.numpy as jnp
import numpy as np
from jax import lax
from jax.experimental import pallas as pl
from jax.experimental.pallas import tpu as pltpu
from jax.sharding import Mesh
from jax.sharding import PartitionSpec as P

TURN = 1024
CHUNKS = 2
MIB = 1024 * 1024
F32 = jnp.float32
BF16 = jnp.bfloat16


def iota(shape, dim):
    return lax.broadcasted_iota(jnp.int32, shape, dim)


def digit(idx, shift, bits):
    return (idx >> shift) & ((1 << bits) - 1)


def cos_sin(idx):
    idx = idx & (TURN - 1)
    quarter = (idx + TURN // 8) >> 8
    x = (idx - (quarter << 8)).astype(F32) * (2.0 * math.pi / TURN)
    y = x * x
    s = x * (1.0 + y * (-1.0 / 6 + y * (1.0 / 120 + y * (-1.0 / 5040 + y * (1.0 / 362880)))))
    c = 1.0 + y * (-1.0 / 2 + y * (1.0 / 24 + y * (-1.0 / 720 + y * (1.0 / 40320))))
    odd = (quarter & 1) == 1
    cos, sin = jnp.where(odd, s, c), jnp.where(odd, c, s)
    turned = (quarter + 1) & 3
    cos = jnp.where(turned >= 2, -cos, cos)
    sin = jnp.where((quarter & 3) >= 2, -sin, sin)
    return cos, sin


SCALE = 1.0 / 32.0


def forward_columns_phases():
    a, b = iota((16, 1024), 0), iota((64, 1024), 0)
    w = iota((64, 1024), 1)
    k = 4 * digit(b, 3, 3) + digit(b, 0, 2)
    return 32 * a * w[:16], k * w + 256 * digit(b, 2, 1), SCALE


def backward_columns_phases():
    a, b, lane = iota((16, 1024), 0), iota((64, 1024), 0), iota((64, 1024), 1)
    k = 4 * (lane >> 3) + digit(lane, 0, 2)
    weight = jnp.where(k == 0, SCALE, 2.0 * SCALE)
    return 64 * a * k[:16], b * k + 256 * digit(lane, 2, 1), weight


def forward_rows_phases():
    a, b, lane = iota((16, 1024), 0), iota((64, 1024), 0), iota((64, 1024), 1)
    qh = 4 * digit(a, 3, 1) + digit(a, 0, 2)
    p, ri = lane >> 3, digit(lane, 2, 1)
    ia = 128 * qh * p[:16] + 256 * (digit(a, 2, 1) - ri[:16])
    weight = jnp.where(digit(b, 4, 2) == digit(lane, 0, 2), SCALE, 0.0)
    return ia, 8 * digit(b, 0, 4) * p, weight


def backward_rows_phases():
    a, b, lane = iota((16, 1024), 0), iota((64, 1024), 0), iota((64, 1024), 1)
    q0 = 16 * (4 * digit(lane, 9, 1) + digit(lane, 6, 2)) + digit(lane, 0, 4)
    ro = digit(lane, 8, 1)
    weight = jnp.where(digit(b, 0, 2) == digit(lane, 4, 2), SCALE, 0.0)
    return 64 * a * q0[:16], 8 * digit(b, 3, 3) * q0 + 256 * (ro - digit(b, 2, 1)), weight


def table_kernel(phases, with_twiddles, stay, waited, *refs):
    refs = refs[waited:]
    out_ref, (ec, es, fc, fs) = refs[0], refs[-4:]
    steps = 16 if stay else 4

    @pl.when(pl.program_id(0) == 0)
    def _():
        ia, ib, weight = phases()
        ec[...], es[...] = cos_sin(ia)
        c, s = cos_sin(ib)
        fc[...], fs[...] = c * weight, s * weight
        if with_twiddles:
            angle = iota((128, 512), 0) * (iota((128, 512), 1) >> 6)
            refs[1][...], refs[2][...] = cos_sin(angle)

    first = 0 if stay else steps * pl.program_id(0)

    def step(a, carry):
        row = pl.ds(first + a, 1)
        out_ref[pl.ds(pl.multiple_of(64 * a, 64), 64), :] = (
            ec[row, :] * fc[...] - es[row, :] * fs[...]
        ).astype(BF16)
        return carry

    lax.fori_loop(0, steps, step, 0)


def table(space, phases, with_twiddles=False, after=()):
    stay = space == pltpu.VMEM
    whole = pl.BlockSpec(memory_space=pltpu.VMEM)
    twiddle_spec = pl.BlockSpec((128, 512), lambda g: (0, 0))
    out = pl.pallas_call(
        functools.partial(table_kernel, phases, with_twiddles, stay, len(after)),
        grid=(1,) if stay else (4,),
        in_specs=[pl.BlockSpec(memory_space=pltpu.HBM)] * len(after),
        out_specs=[whole if stay else pl.BlockSpec((256, 1024), lambda g: (g, 0))]
        + [twiddle_spec] * (2 * with_twiddles),
        out_shape=[space((1024, 1024), BF16)] + [pltpu.HBM((128, 512), F32)] * (2 * with_twiddles),
        scratch_shapes=[pltpu.VMEM((n, 1024), F32) for n in (16, 16, 64, 64)],
        cost_estimate=pl.CostEstimate(flops=2**23, bytes_accessed=2**21, transcendentals=0),
        compiler_params=pltpu.CompilerParams(vmem_limit_bytes=6 * MIB),
        name=phases.__name__,
    )(*[remaining(v) for v in after])
    return out if with_twiddles else out[0]


def blocks_kernel(first_w, second_w, first_ref, eight_ref, second_ref, acc, ass, bcc):
    block = lax.axis_index("x")
    low = low_half(64)

    def twice(ref, n):
        w = ref[n, block].astype(F32)
        return jnp.concatenate([w, w], axis=1)

    @pl.when(pl.program_id(0) == 0)
    def _():
        a, lane = iota((16, 1024), 0), iota((16, 1024), 1)
        q1 = 2 * digit(lane, 8, 2) + digit(lane, 6, 1)
        acc[...], ass[...] = cos_sin(
            128 * q1 * digit(a, 0, 3) + 256 * (digit(lane, 7, 1) - digit(a, 3, 1))
        )
        q1 = 2 * digit(a, 2, 2) + digit(a, 0, 1)
        bcc[...], _unused = cos_sin(
            128 * q1 * digit(lane, 6, 3) - 256 * (digit(lane, 9, 1) - digit(a, 1, 1))
        )
        w0, w1 = twice(second_w, 0), twice(second_w, 1)
        zero = jnp.zeros_like(w0)
        for half in range(2):
            def own(v):
                return (jnp.where(low, v, zero) if half == 0 else jnp.where(low, zero, v)).astype(BF16)

            re, im = slice(64 * half, 64 * half + 64), slice(128 + 64 * half, 192 + 64 * half)
            second_ref[re, :128], second_ref[re, 128:] = own(w0), own(w1)
            second_ref[im, :128], second_ref[im, 128:] = own(-w1), own(w0)

    w0, w1 = twice(first_w, 0), twice(first_w, 1)
    eye = jnp.where(iota((64, 128), 0) == (iota((64, 128), 1) & 63), 1.0, 0.0)
    first = 4 * pl.program_id(0)

    def step(a, carry):
        rows = pl.ds(pl.multiple_of(64 * a, 64), 64)
        row = pl.ds(first + a, 1)
        c, s, back = acc[row, :], ass[row, :], bcc[row, :]
        for t in range(8):
            lanes = slice(128 * t, 128 * t + 128)
            first_ref[rows, lanes] = (c[:, lanes] * w0 + s[:, lanes] * w1).astype(BF16)
            eight_ref[rows, lanes] = (back[:, lanes] * eye).astype(BF16)
        return carry

    lax.fori_loop(0, 4, step, 0)


def block_tables(w_first, w_second):
    vmem = pl.BlockSpec(memory_space=pltpu.VMEM)
    quarter = pl.BlockSpec((256, 1024), lambda g: (g, 0))
    return pl.pallas_call(
        blocks_kernel,
        grid=(4,),
        in_specs=[vmem, vmem],
        out_specs=[quarter, quarter, pl.BlockSpec((256, 256), lambda g: (0, 0))],
        out_shape=[
            pltpu.HBM((1024, 1024), BF16),
            pltpu.HBM((1024, 1024), BF16),
            pltpu.HBM((256, 256), BF16),
        ],
        scratch_shapes=[pltpu.VMEM((16, 1024), F32)] * 3,
        cost_estimate=pl.CostEstimate(flops=2**23, bytes_accessed=2**22, transcendentals=0),
        compiler_params=pltpu.CompilerParams(vmem_limit_bytes=8 * MIB),
        name="block_tables",
    )(w_first, w_second)


def low_half(rows):
    return lax.broadcasted_iota(jnp.int32, (rows, 128), 1) < 64


def swap(v):
    return pltpu.roll(v, 64, 1)


def norm_kernel(x_any, gain_ref, out_any, x_all, packed, in_sems, out_sems):
    low = low_half(64)
    ones = jnp.ones((256, 128), BF16)
    fetches, sends = [], []
    for g in range(4):
        rows = slice(8 * g, 8 * g + 8)
        fetches.append(pltpu.make_async_copy(x_any.at[rows], x_all.at[rows], in_sems.at[g]))
        fetches[-1].start()
    for g in range(4):
        fetches[g].wait()
        x = x_all[8 * g : 8 * g + 8].reshape(512, 256)
        mean = dot(x, ones) * (1.0 / 256.0)
        d0, d1 = x[:, :128].astype(F32) - mean, x[:, 128:].astype(F32) - mean
        square = d0 * d0 + d1 * d1
        coarse = square.astype(BF16)
        fine = (square - coarse.astype(F32)).astype(BF16)
        var = dot(jnp.concatenate([coarse, fine], axis=1), ones) * (1.0 / 256.0)
        scale = lax.rsqrt(var + 1e-05)
        halves = (d0 * scale * gain_ref[:, :128], d1 * scale * gain_ref[:, 128:])
        for t in range(4):
            lanes = slice(128 * t, 128 * t + 128)
            for m in range(2):
                a = halves[m][128 * t : 128 * t + 64]
                b = halves[m][128 * t + 64 : 128 * t + 128]
                packed[4 * g + 2 * m, :, lanes] = jnp.where(low, a, swap(b)).astype(BF16)
                packed[4 * g + 2 * m + 1, :, lanes] = jnp.where(low, swap(a), b).astype(BF16)
        parts = slice(4 * g, 4 * g + 4)
        sends.append(pltpu.make_async_copy(packed.at[parts], out_any.at[parts], out_sems.at[g]))
        sends[-1].start()
    for send in sends:
        send.wait()


def norm_and_pack(patches, gain):
    return pl.pallas_call(
        norm_kernel,
        in_specs=[pl.BlockSpec(memory_space=pltpu.HBM), pl.BlockSpec(memory_space=pltpu.VMEM)],
        out_specs=pl.BlockSpec(memory_space=pltpu.HBM),
        out_shape=pltpu.HBM((16, 64, 512), BF16),
        scratch_shapes=[
            pltpu.VMEM((32, 64, 256), BF16),
            pltpu.VMEM((16, 64, 512), BF16),
            pltpu.SemaphoreType.DMA((4,)),
            pltpu.SemaphoreType.DMA((4,)),
        ],
        compiler_params=pltpu.CompilerParams(vmem_limit_bytes=16 * MIB),
        name="norm_pack",
    )(remaining(patches), remaining(gain.reshape(1, 256)))


def final_kernel(x_ref, home_ref, out_ref):
    low = low_half(64)
    first = 4 * pl.program_id(0)
    for t in range(4):
        lanes = slice(128 * t, 128 * t + 128)
        for m in range(2):
            u = home_ref[first + 2 * m, :, lanes].astype(F32)
            v = home_ref[first + 2 * m + 1, :, lanes].astype(F32)
            chans = slice(128 * m, 128 * m + 128)
            even, odd = jnp.where(low, u, swap(v)), jnp.where(low, swap(u), v)
            out_ref[2 * t, :, chans] = (x_ref[2 * t, :, chans].astype(F32) + even).astype(BF16)
            out_ref[2 * t + 1, :, chans] = (x_ref[2 * t + 1, :, chans].astype(F32) + odd).astype(BF16)


def unpack_and_add(patches, home):
    return pl.pallas_call(
        final_kernel,
        grid=(4,),
        in_specs=[
            pl.BlockSpec((8, 64, 256), lambda g: (g, 0, 0)),
            pl.BlockSpec(memory_space=pltpu.VMEM),
        ],
        out_specs=pl.BlockSpec((8, 64, 256), lambda g: (g, 0, 0)),
        out_shape=jax.ShapeDtypeStruct((32, 64, 256), BF16),
        compiler_params=pltpu.CompilerParams(vmem_limit_bytes=8 * MIB),
        name="unpack_add",
    )(patches, resident(home))


def dot(a, b):
    return jnp.dot(a, b, preferred_element_type=F32)


def resident(v):
    return pltpu.with_memory_space_constraint(v, pltpu.VMEM)


def remaining(v):
    return pltpu.with_memory_space_constraint(v, pltpu.HBM)


def stream_dot(table, operand, extra, held, out, sems):
    copies = []
    for m in range(4):
        rows = slice(256 * m, 256 * m + 256)
        v = dot(table[rows, :], operand[...])
        if extra is not None:
            extra[m].wait()
            v = v + extra[4][rows, :].astype(F32)
        held[rows, :] = v.astype(BF16)
        copies.append(pltpu.make_async_copy(held.at[rows, :], out.at[rows, :], sems.at[m]))
        copies[-1].start()
    for copy in copies:
        copy.wait()


def columns_kernel(table_ref, x_ref, out_any, lines_any, held, sems, line_sem):
    keep = pltpu.make_async_copy(x_ref, lines_any, line_sem)
    keep.start()
    stream_dot(table_ref, x_ref, None, held, out_any, sems)
    keep.wait()


def forward_columns(table, x):
    vmem, hbm = pl.BlockSpec(memory_space=pltpu.VMEM), pl.BlockSpec(memory_space=pltpu.HBM)
    return pl.pallas_call(
        columns_kernel,
        in_specs=[vmem] * 2,
        out_specs=[hbm, hbm],
        out_shape=[pltpu.HBM((1024, 512), BF16), pltpu.HBM((1024, 512), BF16)],
        scratch_shapes=[
            pltpu.VMEM((1024, 512), BF16),
            pltpu.SemaphoreType.DMA((4,)),
            pltpu.SemaphoreType.DMA,
        ],
        cost_estimate=pl.CostEstimate(flops=2**30, bytes_accessed=2**21, transcendentals=0),
        compiler_params=pltpu.CompilerParams(vmem_limit_bytes=12 * MIB),
        name="forward_columns",
    )(resident(table), resident(x))


def rims_kernel(last_tile, leading_tile, last_ref, leading_ref):
    low = low_half(512)
    top, bottom = last_tile[:512].astype(F32), last_tile[512:].astype(F32)
    last_ref[...] = jnp.where(low, swap(top), bottom).astype(BF16)
    top, bottom = leading_tile[:512].astype(F32), leading_tile[512:].astype(F32)
    leading_ref[...] = jnp.where(low, top, swap(bottom)).astype(BF16)


def rims(lines):
    row = pl.BlockSpec((512, 128), lambda g: (0, 0))
    return pl.pallas_call(
        rims_kernel,
        grid=(1,),
        in_specs=[
            pl.BlockSpec((1024, 128), lambda g: (0, 3)),
            pl.BlockSpec((1024, 128), lambda g: (0, 0)),
        ],
        out_specs=[row, row],
        out_shape=[pltpu.HBM((512, 128), BF16)] * 2,
        cost_estimate=pl.CostEstimate(flops=2**17, bytes_accessed=2**20, transcendentals=0),
        compiler_params=pltpu.CompilerParams(vmem_limit_bytes=6 * MIB),
        name="rims",
    )(remaining(lines), remaining(lines))


def columns_add_kernel(table_ref, x_ref, extra_any, out_any, held, sems, extra, extra_sems):
    fetches = []
    for m in range(4):
        rows = slice(256 * m, 256 * m + 256)
        fetches.append(
            pltpu.make_async_copy(extra_any.at[rows, :], extra.at[rows, :], extra_sems.at[m])
        )
        fetches[-1].start()
    stream_dot(table_ref, x_ref, (*fetches, extra), held, out_any, sems)


def backward_columns(table, x, extra):
    vmem, hbm = pl.BlockSpec(memory_space=pltpu.VMEM), pl.BlockSpec(memory_space=pltpu.HBM)
    return pl.pallas_call(
        columns_add_kernel,
        in_specs=[vmem, vmem, hbm],
        out_specs=hbm,
        out_shape=pltpu.HBM((1024, 512), BF16),
        scratch_shapes=[
            pltpu.VMEM((1024, 512), BF16),
            pltpu.SemaphoreType.DMA((4,)),
            pltpu.VMEM((1024, 512), BF16),
            pltpu.SemaphoreType.DMA((4,)),
        ],
        cost_estimate=pl.CostEstimate(flops=2**30, bytes_accessed=2**21, transcendentals=0),
        compiler_params=pltpu.CompilerParams(vmem_limit_bytes=12 * MIB),
        name="backward_columns",
    )(resident(table), resident(x), remaining(extra))


def stencil_kernel(x_ref, above_ref, below_ref, taps_ref, out_ref):
    low = low_half(512)

    def tile(t):
        return x_ref[:, 128 * t : 128 * t + 128].astype(F32)

    def between(t):
        if t < 0:
            other = above_ref[...].astype(F32)
            return jnp.concatenate(
                [
                    jnp.where(low, other, swap(tile(0)[:512])),
                    jnp.where(low, swap(other), swap(tile(0)[512:])),
                ],
                axis=0,
            )
        if t == 3:
            other = below_ref[...].astype(F32)
            return jnp.concatenate(
                [
                    jnp.where(low, swap(tile(3)[:512]), swap(other)),
                    jnp.where(low, swap(tile(3)[512:]), other),
                ],
                axis=0,
            )
        return jnp.where(low_half(1024), swap(tile(t)), swap(tile(t + 1)))

    for t in range(4):
        rows = (between(t - 1), tile(t), between(t))
        total = None
        for j in range(3):
            part = rows[0] * taps_ref[j : j + 1, :]
            part = part + rows[1] * taps_ref[3 + j : 4 + j, :]
            part = part + rows[2] * taps_ref[6 + j : 7 + j, :]
            if j != 1:
                part = pltpu.roll(part, 1 if j == 0 else 1023, 0)
            total = part if total is None else total + part
        out_ref[:, 128 * t : 128 * t + 128] = total.astype(BF16)


def stencil(x, above, below, taps):
    return pl.pallas_call(
        stencil_kernel,
        in_specs=[pl.BlockSpec((1024, 512), lambda g: (0, 0))]
        + [pl.BlockSpec((512, 128), lambda g: (0, 0))] * 2
        + [pl.BlockSpec(memory_space=pltpu.VMEM)],
        grid=(1,),
        out_specs=pl.BlockSpec((1024, 512), lambda g: (0, 0)),
        out_shape=pltpu.HBM((1024, 512), BF16),
        cost_estimate=pl.CostEstimate(flops=2**24, bytes_accessed=2**22, transcendentals=0),
        compiler_params=pltpu.CompilerParams(vmem_limit_bytes=16 * MIB),
        name="stencil",
    )(remaining(x), remaining(above), remaining(below), taps)


def middle_kernel(
    z, fwd, cos_any, sin_any, first_any, eight_any, inv_any, second_any, out_any,
    cos_ref, sin_ref, first, eight, inv, second_ref, held, done, sems, fetch_sems,
):
    fetches = []
    for n, (src, dst) in enumerate(
        (
            (cos_any, cos_ref),
            (sin_any, sin_ref),
            (first_any, first),
            (eight_any, eight),
            (inv_any, inv),
            (second_any, second_ref),
        )
    ):
        fetches.append(pltpu.make_async_copy(src, dst, fetch_sems.at[n]))
    for n in (0, 1, 2, 5):
        fetches[n].start()
    rows = 512 // CHUNKS
    groups = 8 // CHUNKS
    for m in range(CHUNKS):
        u = dot(fwd[2 * rows * m : 2 * rows * (m + 1), :], z[...])
        shape = (groups, 4, 16, 512)
        ur, ui = u[:rows].reshape(shape), u[rows:].reshape(shape)
        if m == 0:
            fetches[0].wait()
            fetches[1].wait()
            fetches[3].start()
        c = cos_ref[16 * groups * m : 16 * groups * (m + 1), :].reshape(groups, 1, 16, 512)
        s = sin_ref[16 * groups * m : 16 * groups * (m + 1), :].reshape(groups, 1, 16, 512)
        vr = (ur * c + ui * s).astype(BF16).reshape(rows, 512)
        vi = (ui * c - ur * s).astype(BF16).reshape(rows, 512)
        if m == 0:
            fetches[2].wait()
            fetches[5].wait()
            fetches[4].start()
        hidden = jnp.tanh(dot(vr, first[:512, :]) + dot(vi, first[512:, :])).astype(BF16)
        parts = []
        for t in range(4):
            v = dot(hidden[:, 256 * t : 256 * t + 256], second_ref[...])
            v = jnp.where(v > 0.25, v - 0.25, jnp.where(v < -0.25, v + 0.25, 0.0 * v))
            parts.append(v.astype(BF16))
        if m == 0:
            fetches[3].wait()
        y = dot(jnp.concatenate(parts, axis=1), eight[...])
        yr, yi = y[:, :512].reshape(shape), y[:, 512:].reshape(shape)
        held[2 * rows * m : 2 * rows * m + rows, :] = (yr * c - yi * s).astype(BF16).reshape(rows, 512)
        held[2 * rows * m + rows : 2 * rows * (m + 1), :] = (
            (yi * c + yr * s).astype(BF16).reshape(rows, 512)
        )
    fetches[4].wait()
    stream_dot(inv, held, None, done, out_any, sems)


def middle(z, fwd, first, eight, inv, second, cos, sin):
    vmem, hbm = pl.BlockSpec(memory_space=pltpu.VMEM), pl.BlockSpec(memory_space=pltpu.HBM)
    return pl.pallas_call(
        middle_kernel,
        in_specs=[vmem] * 2 + [hbm] * 6,
        out_specs=hbm,
        out_shape=pltpu.HBM((1024, 512), BF16),
        scratch_shapes=[
            pltpu.VMEM((128, 512), F32),
            pltpu.VMEM((128, 512), F32),
            pltpu.VMEM((1024, 1024), BF16),
            pltpu.VMEM((1024, 1024), BF16),
            pltpu.VMEM((1024, 1024), BF16),
            pltpu.VMEM((256, 256), BF16),
            pltpu.VMEM((1024, 512), BF16),
            pltpu.VMEM((1024, 512), BF16),
            pltpu.SemaphoreType.DMA((4,)),
            pltpu.SemaphoreType.DMA((6,)),
        ],
        cost_estimate=pl.CostEstimate(flops=5 * 2**30, bytes_accessed=2**21, transcendentals=2**19),
        compiler_params=pltpu.CompilerParams(vmem_limit_bytes=28 * MIB),
        name="filter_rows",
    )(
        resident(z), resident(fwd), remaining(cos), remaining(sin), remaining(first),
        remaining(eight), remaining(inv), remaining(second),
    )


def local(patches, norm_gain, w_first, w_second, depth_kernel):
    packed = norm_and_pack(patches, norm_gain)
    lines = lax.all_to_all(packed, ("yl", "x"), 0, 0, tiled=True).reshape(1024, 512)

    fwd_w = table(pltpu.VMEM, forward_columns_phases)
    inv_w = table(pltpu.VMEM, backward_columns_phases)
    inv_h = table(pltpu.HBM, backward_rows_phases)
    first, eight, second = block_tables(w_first, w_second)
    fwd_h, cos, sin = table(pltpu.VMEM, forward_rows_phases, True, (second, inv_h))
    block = lax.axis_index("x")
    taps = lax.dynamic_slice_in_dim(depth_kernel.reshape(9, 256), 64 * block, 64, 1)
    taps = jnp.concatenate([taps, taps], axis=1)

    freqs, kept = forward_columns(fwd_w, lines)
    last, leading = rims(kept)
    whole = lax.all_to_all(freqs.reshape(128, 8, 512), ("row", "yl"), 0, 0, tiled=True)
    groups = 128
    down = [(i, (i + 1) % groups) for i in range(groups)]
    up = [(j, i) for i, j in down]
    above = lax.ppermute(last, ("row", "yl"), down)
    below = lax.ppermute(leading, ("row", "yl"), up)
    whole, above, below = lax.optimization_barrier((whole, above, below))

    filtered = middle(whole.reshape(1024, 512), fwd_h, first, eight, inv_h, second, cos, sin)
    filtered, above, below = lax.optimization_barrier((filtered, above, below))
    back = lax.all_to_all(filtered.reshape(128, 8, 512), ("row", "yl"), 0, 0, tiled=True)
    conv = stencil(kept, above, below, taps)
    summed = backward_columns(inv_w, back.reshape(1024, 512), conv).reshape(16, 64, 512)
    home = lax.all_to_all(summed, ("yl", "x"), 0, 0, tiled=True)
    return unpack_and_add(patches, home)


def solution(mesh):
    fine = Mesh(np.asarray(mesh.devices).reshape(32, 4, 4), ("row", "yl", "x"))
    return jax.shard_map(
        local,
        mesh=fine,
        in_specs=(P("row", ("yl", "x"), None), P(), P(), P(), P()),
        out_specs=P("row", ("yl", "x"), None),
        check_vma=False,
    )
```

time: 174 us -> 172 us (0.989)
  waiting for transfers between devices: 41 us -> 61.5 us
  other arithmetic: 17.2 us -> 0.08 us
  local copies, waits for them, and re-layouts: 8.44 us -> 0.12 us
  Pallas kernels: 33.1 us -> 36.8 us
    ppermute x1, waiting for transfers between devices: 0.66 us -> 10.5 us  [local(): above = lax.ppermute(last, ('row', 'yl'), down)]
    all_to_all x1, waiting for transfers between devices: 14.4 us -> 23.1 us  [local(): lax.all_to_all(packed, ('yl', 'x'), 0, 0, tiled=True).reshape(1024, 512)]
    mul x10 -> x0, other arithmetic: 8.06 us -> none  [the longest x4 7.41 us: phase_table(): -sin_of(ib) * scale]
    sin x5 -> x0, other arithmetic: 4.11 us -> none  [sin_of(): return jnp.sin((idx % TURN).astype(F32) * (2.0 * math.pi / TURN))]
    another operation x4 -> x0, local copies, waits for them, and re-layouts: 4.04 us -> none  [the longest x2 2.02 us: first_layer(): jnp.tile(w0.astype(F32), (1, 16))]
    pallas_call x10, Pallas kernels: 27.6 us -> 31.3 us  [the longest x1 7.71 us: middle(): pl.pallas_call(middle_kernel, in_specs=[vmem] * 2 + [hbm] * 6, out_specs=...]
    unnamed x54 -> x12, local copies, waits for them, and re-layouts: 2.96 us -> 0.03 us
    select_n x12 -> x0, other arithmetic: 2.47 us -> none  [the longest x10 2.45 us: split(): out.append(idx % s)]
  transfers between devices with their start and end apart: 5 -> 5, of which waited for: 5 -> 5; matrix products, arithmetic and copies ran while one was open for 13% -> 0% of each run, Pallas kernels for 7% -> 10%
where the time goes in v4:
time: 172 us; the launch traced here: 171 us
  waiting for transfers between devices  61.5 us (36%)
  starting transfers between devices  41.1 us (24%)
  Pallas kernels  36.8 us (21%)
  blocking collectives  31.7 us (18%)
    all_to_all x1, blocking collectives, local(): home = lax.all_to_all(summed, ('yl', 'x'), 0, 0, tiled=True)  31.7 us
    all_to_all x1, waiting for transfers between devices, local(): lax.all_to_all(filtered.reshape(128, 8, 512), ('row', 'yl'), 0, 0, tiled=...  24.4 us
    all_to_all x1, waiting for transfers between devices, local(): lax.all_to_all(packed, ('yl', 'x'), 0, 0, tiled=True).reshape(1024, 512)  23.1 us
    all_to_all x1, starting transfers between devices, local(): lax.all_to_all(freqs.reshape(128, 8, 512), ('row', 'yl'), 0, 0, tiled=True)  14.8 us
    all_to_all x1, starting transfers between devices, local(): lax.all_to_all(filtered.reshape(128, 8, 512), ('row', 'yl'), 0, 0, tiled=...  11 us
    ppermute x1, waiting for transfers between devices, local(): above = lax.ppermute(last, ('row', 'yl'), down)  10.5 us
    all_to_all x1, starting transfers between devices, local(): lax.all_to_all(packed, ('yl', 'x'), 0, 0, tiled=True).reshape(1024, 512)  9.3 us
    pallas_call x1, Pallas kernels, middle(): pl.pallas_call(middle_kernel, in_specs=[vmem] * 2 + [hbm] * 6, out_specs=...  7.71 us
  transfers between devices with their start and end apart: 5, of which 5 were waited for; matrix products, arithmetic and copies ran while one was open for 0% of the time, Pallas kernels for 10%

profile of v4, /device:TPU:8, one launch (start us, length us, event | category | flops | bytes accessed | tf_op | source)
XLA Modules:
  0.0 171.5 jit_solution(4830866828774799592)
XLA Ops:
  0.0 4.4 %norm_pack.1 = bf16[16,64,512]{2,1,0:T(8,128)(2,1)} custom-call(bf16[32,64,256]{2,1,0:T(8,128)(2,1)} %x_ref.1, f32[1,256]{1,0:T(1,128)} %bitcast.13), custom_call_target="tpu_custom_call" | custom-call | tf_op jit(solution)/shard_map/norm_pack/pallas_call | solution.py:231
  4.4 9.3 %all-to-all-start = ((bf16[16,64,512]{2,1,0:T(8,128)(2,1)}), bf16[16,64,512]{2,1,0:T(8,128)(2,1)S(1)}, u32[]{:S(2)}, u32[]{:S(2)}) async-start(bf16[16,64,512]{2,1,0:T(8,128)(2,1)} %norm_pack.1), calls=%async_computation | async-start | bytes 2097152 | tf_op jit(solution)/shard_map/all_to_all | solution.py:522
  13.7 1.1 forward_columns_phases.1.table_ref
  14.8 23.1 %all-to-all-done = bf16[16,64,512]{2,1,0:T(8,128)(2,1)S(1)} async-done(((bf16[16,64,512]{2,1,0:T(8,128)(2,1)}), bf16[16,64,512]{2,1,0:T(8,128)(2,1)S(1)}, u32[]{:S(2)}, u32[]{:S(2)}) %all-to-all-start) | async-done | bytes 1048608 | tf_op jit(solution)/shard_map/all_to_all | solution.py:522
  37.9 2.0 %forward_columns.1 = (bf16[1024,512]{1,0:T(8,128)(2,1)}, bf16[1024,512]{1,0:T(8,128)(2,1)}) custom-call(bf16[1024,1024]{1,0:T(8,128)(2,1)S(1)} %forward_columns_phases.1.table_ref, bf16[1024,512]{1,0:T(8,128)(2,1)S(1)} %bitcast.9), custom_call_target="tpu_custom_call" | custom-call | flops 1073741824 | bytes 2097152 | tf_op jit(solution)/shard_map/forward_columns/pallas_call | solution.py:312
  39.9 14.8 %all-to-all-start.1 = ((bf16[128,8,512]{2,1,0:T(8,128)(2,1)}), bf16[128,8,512]{2,1,0:T(8,128)(2,1)S(1)}, u32[]{:S(2)}, u32[]{:S(2)}) async-start(bf16[128,8,512]{2,1,0:T(8,128)(2,1)} %bitcast.12), calls=%async_computation.1 | async-start | bytes 2097152 | tf_op jit(solution)/shard_map/all_to_all | solution.py:535
  54.8 0.0 copy-start.1
  54.8 0.0 copy-start.2
  54.8 1.9 %rims.1 = (bf16[512,128]{1,0:T(8,128)(2,1)}, bf16[512,128]{1,0:T(8,128)(2,1)}) custom-call(bf16[1024,512]{1,0:T(8,128)(2,1)} %get-tuple-element.22.last_tile.leading_tile.x_ref, bf16[1024,512]{1,0:T(8,128)(2,1)} %get-tuple-element.22.last_tile.leading_tile.x_ref), custom_call_target="tpu_custom_call" | custom-call | flops 131072 | bytes 1048576 | tf_op jit(solution)/shard_map/rims/pallas_call | solution.py:338
  56.7 3.4 %collective-permute-start = (bf16[512,128]{1,0:T(8,128)(2,1)}, bf16[512,128]{1,0:T(8,128)(2,1)S(1)}, u32[]{:S(2)}, u32[]{:S(2)}) collective-permute-start(bf16[512,128]{1,0:T(8,128)(2,1)} %get-tuple-element.23), channel_id=1, source_target_pairs={{0,4},{4,8},{8,12},{12,16},{16,20},{20,24},{24,28},{28,32},{32,36}... | collective-permute-start | bytes 393224 | tf_op jit(solution)/shard_map/ppermute | solution.py:539
  60.1 2.7 %collective-permute-start.1 = (bf16[512,128]{1,0:T(8,128)(2,1)}, bf16[512,128]{1,0:T(8,128)(2,1)S(1)}, u32[]{:S(2)}, u32[]{:S(2)}) collective-permute-start(bf16[512,128]{1,0:T(8,128)(2,1)} %get-tuple-element.24), channel_id=1, source_target_pairs={{4,0},{8,4},{12,8},{16,12},{20,16},{24,20},{28,24},{32,28},{36,32}... | collective-permute-start | bytes 393224 | tf_op jit(solution)/shard_map/ppermute | solution.py:540
  62.7 2.7 %backward_rows_phases.1.refs_1_.inv_any = bf16[1024,1024]{1,0:T(8,128)(2,1)} custom-call(), custom_call_target="tpu_custom_call" | custom-call | flops 8388608 | bytes 2097152 | tf_op jit(solution)/shard_map/backward_rows_phases/pallas_call | solution.py:108
  65.4 0.0 copy-done.2
  65.4 3.5 %block_tables.1 = (bf16[1024,1024]{1,0:T(8,128)(2,1)}, bf16[1024,1024]{1,0:T(8,128)(2,1)}, bf16[256,256]{1,0:T(8,128)(2,1)}) custom-call(bf16[2,4,64,64]{3,2,1,0:T(8,128)(2,1)S(1)} %copy-done.1, bf16[2,4,64,64]{3,2,1,0:T(8,128)(2,1)S(1)} %copy-done.2), custom_call_target="tpu_custom_call" | custom-call | flops 8388608 | bytes 4194304 | tf_op jit(solution)/shard_map/block_tables/pallas_call | solution.py:172
  68.9 2.3 %forward_rows_phases.1 = (bf16[1024,1024]{1,0:T(8,128)(2,1)S(1)}, f32[128,512]{1,0:T(8,128)}, f32[128,512]{1,0:T(8,128)}) custom-call(bf16[256,256]{1,0:T(8,128)(2,1)} %get-tuple-element.26.refs_0_.second_any, bf16[1024,1024]{1,0:T(8,128)(2,1)} %backward_rows_phases.1.refs_1_.inv_any), custom_call_target="tpu_custom_call" | custom-call | flops 8388608 | bytes 2097152 | tf_op jit(solution)/shard_map/forward_rows_phases/pallas_call | solution.py:108
  71.2 10.5 %collective-permute-done.above_ref = bf16[512,128]{1,0:T(8,128)(2,1)S(1)} collective-permute-done((bf16[512,128]{1,0:T(8,128)(2,1)}, bf16[512,128]{1,0:T(8,128)(2,1)S(1)}, u32[]{:S(2)}, u32[]{:S(2)}) %collective-permute-start) | collective-permute-done | bytes 131104 | tf_op jit(solution)/shard_map/ppermute | solution.py:539
  81.7 1.6 collective-permute-done.1.below_ref
  83.3 1.9 %all-to-all-done.1 = bf16[128,8,512]{2,1,0:T(8,128)(2,1)S(1)} async-done(((bf16[128,8,512]{2,1,0:T(8,128)(2,1)}), bf16[128,8,512]{2,1,0:T(8,128)(2,1)S(1)}, u32[]{:S(2)}, u32[]{:S(2)}) %all-to-all-start.1) | async-done | bytes 1048608 | tf_op jit(solution)/shard_map/all_to_all | solution.py:535
  85.2 7.7 %filter_rows.1 = bf16[1024,512]{1,0:T(8,128)(2,1)} custom-call(bf16[1024,512]{1,0:T(8,128)(2,1)S(1)} %bitcast.8, bf16[1024,1024]{1,0:T(8,128)(2,1)S(1)} %get-tuple-element.27.fwd, f32[128,512]{1,0:T(8,128)} %get-tuple-element.28.cos_any, f32[128,512]{1,0:T(8,128)} %get-tuple-element.29.sin_any, bf16[1024,1024]{1,0:T(8,128)(2,1)} %get-tuple-element.30.first_any, ...), custom_call_target="tpu_custom_call" | custom-call | flops 5368709120 | bytes 2097152 | tf_op jit(solution)/shard_map/filter_rows/pallas_call | solution.py:494
  92.9 0.0 copy-done.3
  92.9 0.0 copy-done.4
  92.9 0.0 copy-start.5
  92.9 11.0 %all-to-all-start.2 = ((bf16[128,8,512]{2,1,0:T(8,128)(2,1)}), bf16[128,8,512]{2,1,0:T(8,128)(2,1)S(1)}, u32[]{:S(2)}, u32[]{:S(2)}) async-start(bf16[128,8,512]{2,1,0:T(8,128)(2,1)} %bitcast.11), calls=%async_computation.2 | async-start | bytes 2097152 | tf_op jit(solution)/shard_map/all_to_all | solution.py:545
  103.9 1.1 backward_columns_phases.1.table_ref
  105.1 0.1 constant_dynamic-slice_fusion
  105.2 0.1 pad_maximum_fusion.taps_ref
  105.2 4.6 %stencil.1.extra_any = bf16[1024,512]{1,0:T(8,128)(2,1)} custom-call(bf16[1024,512]{1,0:T(8,128)(2,1)} %get-tuple-element.22.last_tile.leading_tile.x_ref, bf16[512,128]{1,0:T(8,128)(2,1)} %copy-done.3, bf16[512,128]{1,0:T(8,128)(2,1)} %copy-done.4, f32[9,128]{1,0:T(8,128)S(1)} %pad_maximum_fusion.taps_ref), custom_call_target="tpu_custom_call" | custom-call | flops 16777216 | bytes 4194304 | tf_op jit(solution)/shard_map/stencil/pallas_call | solution.py:424
  109.9 24.4 %all-to-all-done.2 = bf16[128,8,512]{2,1,0:T(8,128)(2,1)S(1)} async-done(((bf16[128,8,512]{2,1,0:T(8,128)(2,1)}), bf16[128,8,512]{2,1,0:T(8,128)(2,1)S(1)}, u32[]{:S(2)}, u32[]{:S(2)}) %all-to-all-start.2) | async-done | bytes 1048608 | tf_op jit(solution)/shard_map/all_to_all | solution.py:545
  134.3 3.5 %backward_columns.1 = bf16[1024,512]{1,0:T(8,128)(2,1)} custom-call(bf16[1024,1024]{1,0:T(8,128)(2,1)S(1)} %backward_columns_phases.1.table_ref, bf16[1024,512]{1,0:T(8,128)(2,1)S(1)} %bitcast.7, bf16[1024,512]{1,0:T(8,128)(2,1)} %stencil.1.extra_any), custom_call_target="tpu_custom_call" | custom-call | flops 1073741824 | bytes 2097152 | tf_op jit(solution)/shard_map/backward_columns/pallas_call | solution.py:366
  137.9 0.0 copy-start
  137.9 31.7 %all_to_all.20.home_ref = bf16[16,64,512]{2,1,0:T(8,128)(2,1)S(1)} all-to-all(bf16[16,64,512]{2,1,0:T(8,128)(2,1)} %bitcast.10), channel_id=1, replica_groups=mesh['row'=32,'yl'=4,'x'=4] {'yl','x'}, dimensions={0} | all-to-all | bytes 2097152 | tf_op jit(solution)/shard_map/all_to_all | solution.py:548
  169.5 1.9 %unpack_add.1 = bf16[32,64,256]{2,1,0:T(8,128)(2,1)} custom-call(bf16[32,64,256]{2,1,0:T(8,128)(2,1)S(1)} %copy-done, bf16[16,64,512]{2,1,0:T(8,128)(2,1)S(1)} %all_to_all.20.home_ref), custom_call_target="tpu_custom_call" | custom-call | tf_op jit(solution)/shard_map/unpack_add/pallas_call | solution.py:262
  (6 shorter events, 0.0 us)
Async XLA Ops:
  4.4 33.5 %all-to-all-start = ((bf16[16,64,512]{2,1,0:T(8,128)(2,1)}), bf16[16,64,512]{2,1,0:T(8,128)(2,1)S(1)}, u32[]{:S(2)}, u32[]{:S(2)}) async-start(bf16[16,64,512]{2,1,0:T(8,128)(2,1)} %norm_pack.1), calls=%async_computation | async-start | bytes 2097152 | tf_op jit(solution)/shard_map/all_to_all | solution.py:522
  39.9 45.2 %all-to-all-start.1 = ((bf16[128,8,512]{2,1,0:T(8,128)(2,1)}), bf16[128,8,512]{2,1,0:T(8,128)(2,1)S(1)}, u32[]{:S(2)}, u32[]{:S(2)}) async-start(bf16[128,8,512]{2,1,0:T(8,128)(2,1)} %bitcast.12), calls=%async_computation.1 | async-start | bytes 2097152 | tf_op jit(solution)/shard_map/all_to_all | solution.py:535
  54.8 10.6 %copy-start.1 = (bf16[2,4,64,64]{3,2,1,0:T(8,128)(2,1)S(1)}, bf16[2,4,64,64]{3,2,1,0:T(8,128)(2,1)}, u32[]{:S(2)}) copy-start(bf16[2,4,64,64]{3,2,1,0:T(8,128)(2,1)} %first_w.1) | copy-start | bytes 196612
  54.8 10.6 %copy-start.2 = (bf16[2,4,64,64]{3,2,1,0:T(8,128)(2,1)S(1)}, bf16[2,4,64,64]{3,2,1,0:T(8,128)(2,1)}, u32[]{:S(2)}) copy-start(bf16[2,4,64,64]{3,2,1,0:T(8,128)(2,1)} %second_w.1) | copy-start | bytes 196612
  56.7 25.0 %collective-permute-start = (bf16[512,128]{1,0:T(8,128)(2,1)}, bf16[512,128]{1,0:T(8,128)(2,1)S(1)}, u32[]{:S(2)}, u32[]{:S(2)}) collective-permute-start(bf16[512,128]{1,0:T(8,128)(2,1)} %get-tuple-element.23), channel_id=1, source_target_pairs={{0,4},{4,8},{8,12},{12,16},{16,20},{20,24},{24,28},{28,32},{32,36}... | collective-permute-start | bytes 393224 | tf_op jit(solution)/shard_map/ppermute | solution.py:539
  60.1 23.2 %collective-permute-start.1 = (bf16[512,128]{1,0:T(8,128)(2,1)}, bf16[512,128]{1,0:T(8,128)(2,1)S(1)}, u32[]{:S(2)}, u32[]{:S(2)}) collective-permute-start(bf16[512,128]{1,0:T(8,128)(2,1)} %get-tuple-element.24), channel_id=1, source_target_pairs={{4,0},{8,4},{12,8},{16,12},{20,16},{24,20},{28,24},{32,28},{36,32}... | collective-permute-start | bytes 393224 | tf_op jit(solution)/shard_map/ppermute | solution.py:540
  81.7 11.2 %copy-start.3 = (bf16[512,128]{1,0:T(8,128)(2,1)}, bf16[512,128]{1,0:T(8,128)(2,1)S(1)}, u32[]{:S(2)}) copy-start(bf16[512,128]{1,0:T(8,128)(2,1)S(1)} %collective-permute-done.above_ref) | copy-start | bytes 393220
  83.3 9.6 %copy-start.4 = (bf16[512,128]{1,0:T(8,128)(2,1)}, bf16[512,128]{1,0:T(8,128)(2,1)S(1)}, u32[]{:S(2)}) copy-start(bf16[512,128]{1,0:T(8,128)(2,1)S(1)} %collective-permute-done.1.below_ref) | copy-start | bytes 393220
  92.9 11.0 %copy-start.5 = (f32[3,3,256]{2,1,0:T(4,128)S(1)}, f32[3,3,256]{2,1,0:T(4,128)}, u32[]{:S(2)}) copy-start(f32[3,3,256]{2,1,0:T(4,128)} %param.9) | copy-start | bytes 27652
  92.9 41.4 %all-to-all-start.2 = ((bf16[128,8,512]{2,1,0:T(8,128)(2,1)}), bf16[128,8,512]{2,1,0:T(8,128)(2,1)S(1)}, u32[]{:S(2)}, u32[]{:S(2)}) async-start(bf16[128,8,512]{2,1,0:T(8,128)(2,1)} %bitcast.11), calls=%async_computation.2 | async-start | bytes 2097152 | tf_op jit(solution)/shard_map/all_to_all | solution.py:545
  137.9 31.7 %copy-start = (bf16[32,64,256]{2,1,0:T(8,128)(2,1)S(1)}, bf16[32,64,256]{2,1,0:T(8,128)(2,1)}, u32[]{:S(2)}) copy-start(bf16[32,64,256]{2,1,0:T(8,128)(2,1)} %x_ref.1) | copy-start | bytes 3145732

commit v5 on v4

--- a/solution.py
+++ b/solution.py
@@ -194,9 +194,21 @@
     return pltpu.roll(v, 64, 1)
 
 
+def normed_halves(x_ref, gain_ref):
+    ones = jnp.ones((256, 128), BF16)
+    x = x_ref[...].reshape(512, 256)
+    mean = dot(x, ones) * (1.0 / 256.0)
+    d0, d1 = x[:, :128].astype(F32) - mean, x[:, 128:].astype(F32) - mean
+    square = d0 * d0 + d1 * d1
+    coarse = square.astype(BF16)
+    fine = (square - coarse.astype(F32)).astype(BF16)
+    var = dot(jnp.concatenate([coarse, fine], axis=1), ones) * (1.0 / 256.0)
+    scale = lax.rsqrt(var + 1e-05)
+    return d0 * scale * gain_ref[:, :128], d1 * scale * gain_ref[:, 128:]
+
+
 def norm_kernel(x_any, gain_ref, out_any, x_all, packed, in_sems, out_sems):
     low = low_half(64)
-    ones = jnp.ones((256, 128), BF16)
     fetches, sends = [], []
     for g in range(4):
         rows = slice(8 * g, 8 * g + 8)
@@ -204,15 +216,7 @@
         fetches[-1].start()
     for g in range(4):
         fetches[g].wait()
-        x = x_all[8 * g : 8 * g + 8].reshape(512, 256)
-        mean = dot(x, ones) * (1.0 / 256.0)
-        d0, d1 = x[:, :128].astype(F32) - mean, x[:, 128:].astype(F32) - mean
-        square = d0 * d0 + d1 * d1
-        coarse = square.astype(BF16)
-        fine = (square - coarse.astype(F32)).astype(BF16)
-        var = dot(jnp.concatenate([coarse, fine], axis=1), ones) * (1.0 / 256.0)
-        scale = lax.rsqrt(var + 1e-05)
-        halves = (d0 * scale * gain_ref[:, :128], d1 * scale * gain_ref[:, 128:])
+        halves = normed_halves(x_all.at[8 * g : 8 * g + 8], gain_ref)
         for t in range(4):
             lanes = slice(128 * t, 128 * t + 128)
             for m in range(2):
@@ -225,6 +229,25 @@
         sends[-1].start()
     for send in sends:
         send.wait()
+
+
+def home_norm_kernel(x_ref, gain_ref, out_ref):
+    for m, half in enumerate(normed_halves(x_ref, gain_ref)):
+        out_ref[:, :, 128 * m : 128 * m + 128] = half.astype(BF16).reshape(8, 64, 128)
+
+
+def home_norm(patches, gain):
+    block = pl.BlockSpec((8, 64, 256), lambda g: (g, 0, 0))
+    return pl.pallas_call(
+        home_norm_kernel,
+        grid=(4,),
+        in_specs=[block, pl.BlockSpec((1, 256), lambda g: (0, 0))],
+        out_specs=block,
+        out_shape=pltpu.HBM((32, 64, 256), BF16),
+        cost_estimate=pl.CostEstimate(flops=2**24, bytes_accessed=2**21, transcendentals=0),
+        compiler_params=pltpu.CompilerParams(vmem_limit_bytes=12 * MIB),
+        name="home_norm",
+    )(remaining(patches), remaining(gain.reshape(1, 256)))
 
 
 def norm_and_pack(patches, gain):
@@ -244,7 +267,7 @@
     )(remaining(patches), remaining(gain.reshape(1, 256)))
 
 
-def final_kernel(x_ref, home_ref, out_ref):
+def final_kernel(base_ref, home_ref, out_ref):
     low = low_half(64)
     first = 4 * pl.program_id(0)
     for t in range(4):
@@ -254,11 +277,11 @@
             v = home_ref[first + 2 * m + 1, :, lanes].astype(F32)
             chans = slice(128 * m, 128 * m + 128)
             even, odd = jnp.where(low, u, swap(v)), jnp.where(low, swap(u), v)
-            out_ref[2 * t, :, chans] = (x_ref[2 * t, :, chans].astype(F32) + even).astype(BF16)
-            out_ref[2 * t + 1, :, chans] = (x_ref[2 * t + 1, :, chans].astype(F32) + odd).astype(BF16)
-
-
-def unpack_and_add(patches, home):
+            out_ref[2 * t, :, chans] = (base_ref[2 * t, :, chans] + even).astype(BF16)
+            out_ref[2 * t + 1, :, chans] = (base_ref[2 * t + 1, :, chans] + odd).astype(BF16)
+
+
+def unpack_and_add(base, home):
     return pl.pallas_call(
         final_kernel,
         grid=(4,),
@@ -270,7 +293,7 @@
         out_shape=jax.ShapeDtypeStruct((32, 64, 256), BF16),
         compiler_params=pltpu.CompilerParams(vmem_limit_bytes=8 * MIB),
         name="unpack_add",
-    )(patches, resident(home))
+    )(base, resident(home))
 
 
 def dot(a, b):
@@ -285,154 +308,91 @@
     return pltpu.with_memory_space_constraint(v, pltpu.HBM)
 
 
-def stream_dot(table, operand, extra, held, out, sems):
+def stream_dot(table, operand, held, out, sems):
     copies = []
     for m in range(4):
         rows = slice(256 * m, 256 * m + 256)
-        v = dot(table[rows, :], operand[...])
-        if extra is not None:
-            extra[m].wait()
-            v = v + extra[4][rows, :].astype(F32)
-        held[rows, :] = v.astype(BF16)
+        held[rows, :] = dot(table[rows, :], operand[...]).astype(BF16)
         copies.append(pltpu.make_async_copy(held.at[rows, :], out.at[rows, :], sems.at[m]))
         copies[-1].start()
     for copy in copies:
         copy.wait()
 
 
-def columns_kernel(table_ref, x_ref, out_any, lines_any, held, sems, line_sem):
-    keep = pltpu.make_async_copy(x_ref, lines_any, line_sem)
-    keep.start()
-    stream_dot(table_ref, x_ref, None, held, out_any, sems)
-    keep.wait()
-
-
-def forward_columns(table, x):
-    vmem, hbm = pl.BlockSpec(memory_space=pltpu.VMEM), pl.BlockSpec(memory_space=pltpu.HBM)
+def columns_kernel(table_ref, x_ref, out_any, held, sems):
+    stream_dot(table_ref, x_ref, held, out_any, sems)
+
+
+def columns(table, x):
     return pl.pallas_call(
         columns_kernel,
-        in_specs=[vmem] * 2,
-        out_specs=[hbm, hbm],
-        out_shape=[pltpu.HBM((1024, 512), BF16), pltpu.HBM((1024, 512), BF16)],
-        scratch_shapes=[
-            pltpu.VMEM((1024, 512), BF16),
-            pltpu.SemaphoreType.DMA((4,)),
-            pltpu.SemaphoreType.DMA,
-        ],
+        in_specs=[pl.BlockSpec(memory_space=pltpu.VMEM)] * 2,
+        out_specs=pl.BlockSpec(memory_space=pltpu.HBM),
+        out_shape=pltpu.HBM((1024, 512), BF16),
+        scratch_shapes=[pltpu.VMEM((1024, 512), BF16), pltpu.SemaphoreType.DMA((4,))],
         cost_estimate=pl.CostEstimate(flops=2**30, bytes_accessed=2**21, transcendentals=0),
         compiler_params=pltpu.CompilerParams(vmem_limit_bytes=12 * MIB),
-        name="forward_columns",
+        name="along_columns",
     )(resident(table), resident(x))
 
 
-def rims_kernel(last_tile, leading_tile, last_ref, leading_ref):
-    low = low_half(512)
-    top, bottom = last_tile[:512].astype(F32), last_tile[512:].astype(F32)
-    last_ref[...] = jnp.where(low, swap(top), bottom).astype(BF16)
-    top, bottom = leading_tile[:512].astype(F32), leading_tile[512:].astype(F32)
-    leading_ref[...] = jnp.where(low, top, swap(bottom)).astype(BF16)
-
-
-def rims(lines):
-    row = pl.BlockSpec((512, 128), lambda g: (0, 0))
-    return pl.pallas_call(
-        rims_kernel,
-        grid=(1,),
+def stencil_kernel(
+    x_ref, normed_ref, top_ref, bottom_ref, left_ref, right_ref, taps_ref, out_ref,
+    rows, side, left_sum, right_sum,
+):
+    def tap(i, j):
+        return taps_ref[3 * i + j : 3 * i + j + 1, :]
+
+    @pl.when(pl.program_id(0) == 0)
+    def _():
+        rows[0], rows[33] = top_ref[...], bottom_ref[...]
+        rows[1:33] = normed_ref[...]
+        for rim_ref, sum_ref, j in ((left_ref, left_sum, 0), (right_ref, right_sum, 2)):
+            side[...] = rim_ref[...].astype(F32)
+            sum_ref[...] = side[0:32] * tap(0, j) + side[1:33] * tap(1, j) + side[2:34] * tap(2, j)
+
+    column = iota((64, 256), 0)
+
+    def step(r, carry):
+        h = 8 * pl.program_id(0) + r
+        around = [rows[h + i].astype(F32) for i in range(3)]
+
+        def part(j):
+            return around[0] * tap(0, j) + around[1] * tap(1, j) + around[2] * tap(2, j)
+
+        left = jnp.where(column == 0, left_sum[pl.ds(h, 1), :], pltpu.roll(part(0), 1, 0))
+        right = jnp.where(column == 63, right_sum[pl.ds(h, 1), :], pltpu.roll(part(2), 63, 0))
+        out_ref[r] = x_ref[r].astype(F32) + (left + part(1) + right)
+        return carry
+
+    lax.fori_loop(0, 8, step, 0)
+
+
+def stencil(x, normed, top, bottom, left, right, taps):
+    block = pl.BlockSpec((8, 64, 256), lambda g: (g, 0, 0))
+    row = pl.BlockSpec((64, 256), lambda g: (0, 0))
+    side = pl.BlockSpec((34, 256), lambda g: (0, 0))
+    return pl.pallas_call(
+        stencil_kernel,
+        grid=(4,),
         in_specs=[
-            pl.BlockSpec((1024, 128), lambda g: (0, 3)),
-            pl.BlockSpec((1024, 128), lambda g: (0, 0)),
+            block,
+            pl.BlockSpec((32, 64, 256), lambda g: (0, 0, 0)),
+            row, row, side, side,
+            pl.BlockSpec((9, 256), lambda g: (0, 0)),
         ],
-        out_specs=[row, row],
-        out_shape=[pltpu.HBM((512, 128), BF16)] * 2,
-        cost_estimate=pl.CostEstimate(flops=2**17, bytes_accessed=2**20, transcendentals=0),
-        compiler_params=pltpu.CompilerParams(vmem_limit_bytes=6 * MIB),
-        name="rims",
-    )(remaining(lines), remaining(lines))
-
-
-def columns_add_kernel(table_ref, x_ref, extra_any, out_any, held, sems, extra, extra_sems):
-    fetches = []
-    for m in range(4):
-        rows = slice(256 * m, 256 * m + 256)
-        fetches.append(
-            pltpu.make_async_copy(extra_any.at[rows, :], extra.at[rows, :], extra_sems.at[m])
-        )
-        fetches[-1].start()
-    stream_dot(table_ref, x_ref, (*fetches, extra), held, out_any, sems)
-
-
-def backward_columns(table, x, extra):
-    vmem, hbm = pl.BlockSpec(memory_space=pltpu.VMEM), pl.BlockSpec(memory_space=pltpu.HBM)
-    return pl.pallas_call(
-        columns_add_kernel,
-        in_specs=[vmem, vmem, hbm],
-        out_specs=hbm,
-        out_shape=pltpu.HBM((1024, 512), BF16),
+        out_specs=block,
+        out_shape=pltpu.HBM((32, 64, 256), F32),
         scratch_shapes=[
-            pltpu.VMEM((1024, 512), BF16),
-            pltpu.SemaphoreType.DMA((4,)),
-            pltpu.VMEM((1024, 512), BF16),
-            pltpu.SemaphoreType.DMA((4,)),
+            pltpu.VMEM((34, 64, 256), BF16),
+            pltpu.VMEM((34, 256), F32),
+            pltpu.VMEM((32, 256), F32),
+            pltpu.VMEM((32, 256), F32),
         ],
-        cost_estimate=pl.CostEstimate(flops=2**30, bytes_accessed=2**21, transcendentals=0),
+        cost_estimate=pl.CostEstimate(flops=2**24, bytes_accessed=2**22, transcendentals=0),
         compiler_params=pltpu.CompilerParams(vmem_limit_bytes=12 * MIB),
-        name="backward_columns",
-    )(resident(table), resident(x), remaining(extra))
-
-
-def stencil_kernel(x_ref, above_ref, below_ref, taps_ref, out_ref):
-    low = low_half(512)
-
-    def tile(t):
-        return x_ref[:, 128 * t : 128 * t + 128].astype(F32)
-
-    def between(t):
-        if t < 0:
-            other = above_ref[...].astype(F32)
-            return jnp.concatenate(
-                [
-                    jnp.where(low, other, swap(tile(0)[:512])),
-                    jnp.where(low, swap(other), swap(tile(0)[512:])),
-                ],
-                axis=0,
-            )
-        if t == 3:
-            other = below_ref[...].astype(F32)
-            return jnp.concatenate(
-                [
-                    jnp.where(low, swap(tile(3)[:512]), swap(other)),
-                    jnp.where(low, swap(tile(3)[512:]), other),
-                ],
-                axis=0,
-            )
-        return jnp.where(low_half(1024), swap(tile(t)), swap(tile(t + 1)))
-
-    for t in range(4):
-        rows = (between(t - 1), tile(t), between(t))
-        total = None
-        for j in range(3):
-            part = rows[0] * taps_ref[j : j + 1, :]
-            part = part + rows[1] * taps_ref[3 + j : 4 + j, :]
-            part = part + rows[2] * taps_ref[6 + j : 7 + j, :]
-            if j != 1:
-                part = pltpu.roll(part, 1 if j == 0 else 1023, 0)
-            total = part if total is None else total + part
-        out_ref[:, 128 * t : 128 * t + 128] = total.astype(BF16)
-
-
-def stencil(x, above, below, taps):
-    return pl.pallas_call(
-        stencil_kernel,
-        in_specs=[pl.BlockSpec((1024, 512), lambda g: (0, 0))]
-        + [pl.BlockSpec((512, 128), lambda g: (0, 0))] * 2
-        + [pl.BlockSpec(memory_space=pltpu.VMEM)],
-        grid=(1,),
-        out_specs=pl.BlockSpec((1024, 512), lambda g: (0, 0)),
-        out_shape=pltpu.HBM((1024, 512), BF16),
-        cost_estimate=pl.CostEstimate(flops=2**24, bytes_accessed=2**22, transcendentals=0),
-        compiler_params=pltpu.CompilerParams(vmem_limit_bytes=16 * MIB),
         name="stencil",
-    )(remaining(x), remaining(above), remaining(below), taps)
+    )(*[remaining(v) for v in (x, normed, top, bottom, left, right, taps)])
 
 
 def middle_kernel(
@@ -486,7 +446,7 @@
             (yi * c + yr * s).astype(BF16).reshape(rows, 512)
         )
     fetches[4].wait()
-    stream_dot(inv, held, None, done, out_any, sems)
+    stream_dot(inv, held, done, out_any, sems)
 
 
 def middle(z, fwd, first, eight, inv, second, cos, sin):
@@ -526,27 +486,33 @@
     inv_h = table(pltpu.HBM, backward_rows_phases)
     first, eight, second = block_tables(w_first, w_second)
     fwd_h, cos, sin = table(pltpu.VMEM, forward_rows_phases, True, (second, inv_h))
-    block = lax.axis_index("x")
-    taps = lax.dynamic_slice_in_dim(depth_kernel.reshape(9, 256), 64 * block, 64, 1)
-    taps = jnp.concatenate([taps, taps], axis=1)
-
-    freqs, kept = forward_columns(fwd_w, lines)
-    last, leading = rims(kept)
+
+    def neighbours(first, last, axis):
+        n = lax.axis_size(axis)
+        before = lax.ppermute(last, axis, [(i, (i + 1) % n) for i in range(n)])
+        after = lax.ppermute(first, axis, [((i + 1) % n, i) for i in range(n)])
+        return before, after
+
+    normed = home_norm(patches, norm_gain)
+    top, bottom = neighbours(normed[0], normed[31], "row")
+    lines, top, bottom = lax.optimization_barrier((lines, top, bottom))
+
+    freqs = columns(fwd_w, lines)
     whole = lax.all_to_all(freqs.reshape(128, 8, 512), ("row", "yl"), 0, 0, tiled=True)
-    groups = 128
-    down = [(i, (i + 1) % groups) for i in range(groups)]
-    up = [(j, i) for i, j in down]
-    above = lax.ppermute(last, ("row", "yl"), down)
-    below = lax.ppermute(leading, ("row", "yl"), up)
-    whole, above, below = lax.optimization_barrier((whole, above, below))
+    sides = [
+        jnp.concatenate([top[w : w + 1], normed[:, w], bottom[w : w + 1]], axis=0) for w in (0, 63)
+    ]
+    left, right = neighbours(sides[0], sides[1], ("yl", "x"))
+    whole, left, right = lax.optimization_barrier((whole, left, right))
 
     filtered = middle(whole.reshape(1024, 512), fwd_h, first, eight, inv_h, second, cos, sin)
-    filtered, above, below = lax.optimization_barrier((filtered, above, below))
+    filtered, left, right = lax.optimization_barrier((filtered, left, right))
     back = lax.all_to_all(filtered.reshape(128, 8, 512), ("row", "yl"), 0, 0, tiled=True)
-    conv = stencil(kept, above, below, taps)
-    summed = backward_columns(inv_w, back.reshape(1024, 512), conv).reshape(16, 64, 512)
-    home = lax.all_to_all(summed, ("yl", "x"), 0, 0, tiled=True)
-    return unpack_and_add(patches, home)
+    base = stencil(patches, normed, top, bottom, left, right, depth_kernel.reshape(9, 256))
+    spectral = columns(inv_w, back.reshape(1024, 512))
+    spectral, base = lax.optimization_barrier((spectral, base))
+    home = lax.all_to_all(spectral.reshape(16, 64, 512), ("yl", "x"), 0, 0, tiled=True)
+    return unpack_and_add(base, home)
 
 
 def solution(mesh):

time: 172 us -> 169 us (0.983)
  waiting for transfers between devices: 61.5 us -> 45 us
  starting transfers between devices: 41.1 us -> 51.2 us
  local copies, waits for them, and re-layouts: 0.12 us -> 2.47 us
    all_to_all x1, waiting for transfers between devices: 23.1 us -> 2.43 us  [local(): lax.all_to_all(packed, ('yl', 'x'), 0, 0, tiled=True).reshape(1024, 512)]
    ppermute x2 -> x4, starting transfers between devices: 6.01 us -> 18.8 us  [the longest x2 14.7 us: neighbours(): after = lax.ppermute(first, axis, [((i + 1) % n, i) for i in range(n)])]
    all_to_all x1, waiting for transfers between devices: 1.91 us -> 6.96 us  [local(): lax.all_to_all(freqs.reshape(128, 8, 512), ('row', 'yl'), 0, 0, tiled=True)]
    all_to_all x1, starting transfers between devices: 11 us -> 8.09 us  [local(): lax.all_to_all(filtered.reshape(128, 8, 512), ('row', 'yl'), 0, 0, tiled=...]
    ppermute x2 -> x4, waiting for transfers between devices: 12.1 us -> 12.1 us  [the longest x2 7.23 us: neighbours(): after = lax.ppermute(first, axis, [((i + 1) % n, i) for i in range(n)])]
  transfers between devices with their start and end apart: 5 -> 7, of which waited for: 5 -> 6; matrix products, arithmetic and copies ran while one was open for 0% -> 1% of each run, Pallas kernels for 10% -> 12%
where the time goes in v5:
time: 169 us; the launch traced here: 168 us
  starting transfers between devices  51.2 us (30%)
  waiting for transfers between devices  45 us (27%)
  Pallas kernels  37.9 us (22%)
  blocking collectives  31.3 us (19%)
  local copies, waits for them, and re-layouts  2.47 us (1%)
    all_to_all x1, blocking collectives, local(): lax.all_to_all(spectral.reshape(16, 64, 512), ('yl', 'x'), 0, 0, tiled=True)  31.3 us
    all_to_all x1, waiting for transfers between devices, local(): lax.all_to_all(filtered.reshape(128, 8, 512), ('row', 'yl'), 0, 0, tiled=...  23.5 us
    all_to_all x1, starting transfers between devices, local(): lax.all_to_all(freqs.reshape(128, 8, 512), ('row', 'yl'), 0, 0, tiled=True)  15 us
    ppermute x2, starting transfers between devices, neighbours(): after = lax.ppermute(first, axis, [((i + 1) % n, i) for i in range(n)])  14.7 us
    all_to_all x1, starting transfers between devices, local(): lax.all_to_all(packed, ('yl', 'x'), 0, 0, tiled=True).reshape(1024, 512)  9.3 us
    all_to_all x1, starting transfers between devices, local(): lax.all_to_all(filtered.reshape(128, 8, 512), ('row', 'yl'), 0, 0, tiled=...  8.09 us
    pallas_call x1, Pallas kernels, middle(): pl.pallas_call(middle_kernel, in_specs=[vmem] * 2 + [hbm] * 6, out_specs=...  7.72 us
    ppermute x2, waiting for transfers between devices, neighbours(): after = lax.ppermute(first, axis, [((i + 1) % n, i) for i in range(n)])  7.23 us
  transfers between devices with their start and end apart: 7, of which 6 were waited for; matrix products, arithmetic and copies ran while one was open for 1% of the time, Pallas kernels for 12%

profile of v5, /device:TPU:8, one launch (start us, length us, event | category | flops | bytes accessed | tf_op | source)
XLA Modules:
  0.0 168.1 jit_solution(3535123481372385587)
XLA Ops:
  0.0 4.4 %norm_pack.1 = bf16[16,64,512]{2,1,0:T(8,128)(2,1)} custom-call(bf16[32,64,256]{2,1,0:T(8,128)(2,1)} %x_ref.3, f32[1,256]{1,0:T(1,128)} %bitcast.25), custom_call_target="tpu_custom_call" | custom-call | tf_op jit(solution)/shard_map/norm_pack/pallas_call | solution.py:254
  4.4 9.3 %all-to-all-start = ((bf16[16,64,512]{2,1,0:T(8,128)(2,1)}), bf16[16,64,512]{2,1,0:T(8,128)(2,1)S(1)}, u32[]{:S(2)}, u32[]{:S(2)}) async-start(bf16[16,64,512]{2,1,0:T(8,128)(2,1)} %norm_pack.1), calls=%async_computation | async-start | bytes 2097152 | tf_op jit(solution)/shard_map/all_to_all | solution.py:482
  13.7 4.2 %home_norm.1.normed_ref = bf16[32,64,256]{2,1,0:T(8,128)(2,1)} custom-call(bf16[32,64,256]{2,1,0:T(8,128)(2,1)} %x_ref.3, f32[1,256]{1,0:T(1,128)} %bitcast.26), custom_call_target="tpu_custom_call" | custom-call | flops 16777216 | bytes 2097152 | tf_op jit(solution)/shard_map/home_norm/pallas_call | solution.py:241
  17.9 0.8 slice_bitcast_fusion
  18.6 1.9 %collective-permute-start = (bf16[64,256]{1,0:T(8,128)(2,1)S(1)}, bf16[64,256]{1,0:T(8,128)(2,1)S(1)}, u32[]{:S(2)}, u32[]{:S(2)}) collective-permute-start(bf16[64,256]{1,0:T(8,128)(2,1)S(1)} %get-tuple-element.42), channel_id=1, source_target_pairs={{0,16},{16,32},{32,48},{48,64},{64,80},{80,96},{96,112},{112,128},... | collective-permute-start | bytes 98312 | tf_op jit(solution)/shard_map/ppermute | solution.py:492
  20.6 10.9 %collective-permute-start.1 = (bf16[64,256]{1,0:T(8,128)(2,1)S(1)}, bf16[64,256]{1,0:T(8,128)(2,1)S(1)}, u32[]{:S(2)}, u32[]{:S(2)}) collective-permute-start(bf16[64,256]{1,0:T(8,128)(2,1)S(1)} %get-tuple-element.41), channel_id=1, source_target_pairs={{16,0},{32,16},{48,32},{64,48},{80,64},{96,80},{112,96},{128,112},... | collective-permute-start | bytes 98312 | tf_op jit(solution)/shard_map/ppermute | solution.py:493
  31.5 1.1 forward_columns_phases.1.table_ref
  32.6 4.3 %collective-permute-done.top_ref = bf16[64,256]{1,0:T(8,128)(2,1)S(1)} collective-permute-done((bf16[64,256]{1,0:T(8,128)(2,1)S(1)}, bf16[64,256]{1,0:T(8,128)(2,1)S(1)}, u32[]{:S(2)}, u32[]{:S(2)}) %collective-permute-start) | collective-permute-done | bytes 32800 | tf_op jit(solution)/shard_map/ppermute | solution.py:492
  36.9 2.4 %all-to-all-done = bf16[16,64,512]{2,1,0:T(8,128)(2,1)S(1)} async-done(((bf16[16,64,512]{2,1,0:T(8,128)(2,1)}), bf16[16,64,512]{2,1,0:T(8,128)(2,1)S(1)}, u32[]{:S(2)}, u32[]{:S(2)}) %all-to-all-start) | async-done | bytes 1048608 | tf_op jit(solution)/shard_map/all_to_all | solution.py:482
  39.3 2.0 %along_columns.2 = bf16[1024,512]{1,0:T(8,128)(2,1)} custom-call(bf16[1024,1024]{1,0:T(8,128)(2,1)S(1)} %forward_columns_phases.1.table_ref, bf16[1024,512]{1,0:T(8,128)(2,1)S(1)} %bitcast.17), custom_call_target="tpu_custom_call" | custom-call | flops 1073741824 | bytes 2097152 | tf_op jit(solution)/shard_map/along_columns/pallas_call | solution.py:327
  41.3 0.0 copy-start.1
  41.3 0.0 copy-start.2
  41.3 15.0 %all-to-all-start.1 = ((bf16[128,8,512]{2,1,0:T(8,128)(2,1)}), bf16[128,8,512]{2,1,0:T(8,128)(2,1)S(1)}, u32[]{:S(2)}, u32[]{:S(2)}) async-start(bf16[128,8,512]{2,1,0:T(8,128)(2,1)} %bitcast.20), calls=%async_computation.1 | async-start | bytes 2097152 | tf_op jit(solution)/shard_map/all_to_all | solution.py:501
  56.3 1.0 fusion
  57.4 3.8 %collective-permute-start.3 = (bf16[34,256]{1,0:T(8,128)(2,1)S(1)}, bf16[34,256]{1,0:T(8,128)(2,1)S(1)}, u32[]{:S(2)}, u32[]{:S(2)}) collective-permute-start(bf16[34,256]{1,0:T(8,128)(2,1)S(1)} %pad_maximum_fusion.1), channel_id=1, source_target_pairs={{1,0},{2,1},{3,2},{4,3},{5,4},{6,5},{7,6},{8,7},{9,8},{10,9},{11,1... | collective-permute-start | bytes 52232 | tf_op jit(solution)/shard_map/ppermute | solution.py:493
  61.2 2.3 %collective-permute-start.2 = (bf16[34,256]{1,0:T(8,128)(2,1)S(1)}, bf16[34,256]{1,0:T(8,128)(2,1)S(1)}, u32[]{:S(2)}, u32[]{:S(2)}) collective-permute-start(bf16[34,256]{1,0:T(8,128)(2,1)S(1)} %pad_maximum_fusion), channel_id=1, source_target_pairs={{0,1},{1,2},{2,3},{3,4},{4,5},{5,6},{6,7},{7,8},{8,9},{9,10},{10,1... | collective-permute-start | bytes 52232 | tf_op jit(solution)/shard_map/ppermute | solution.py:492
  63.5 2.7 %backward_rows_phases.1.refs_1_.inv_any = bf16[1024,1024]{1,0:T(8,128)(2,1)} custom-call(), custom_call_target="tpu_custom_call" | custom-call | flops 8388608 | bytes 2097152 | tf_op jit(solution)/shard_map/backward_rows_phases/pallas_call | solution.py:108
  66.2 3.5 %block_tables.1 = (bf16[1024,1024]{1,0:T(8,128)(2,1)}, bf16[1024,1024]{1,0:T(8,128)(2,1)}, bf16[256,256]{1,0:T(8,128)(2,1)}) custom-call(bf16[2,4,64,64]{3,2,1,0:T(8,128)(2,1)S(1)} %copy-done.1, bf16[2,4,64,64]{3,2,1,0:T(8,128)(2,1)S(1)} %copy-done.2), custom_call_target="tpu_custom_call" | custom-call | flops 8388608 | bytes 4194304 | tf_op jit(solution)/shard_map/block_tables/pallas_call | solution.py:172
  69.6 2.3 %forward_rows_phases.1 = (bf16[1024,1024]{1,0:T(8,128)(2,1)S(1)}, f32[128,512]{1,0:T(8,128)}, f32[128,512]{1,0:T(8,128)}) custom-call(bf16[256,256]{1,0:T(8,128)(2,1)} %get-tuple-element.26.refs_0_.second_any, bf16[1024,1024]{1,0:T(8,128)(2,1)} %backward_rows_phases.1.refs_1_.inv_any), custom_call_target="tpu_custom_call" | custom-call | flops 8388608 | bytes 2097152 | tf_op jit(solution)/shard_map/forward_rows_phases/pallas_call | solution.py:108
  71.9 7.2 %collective-permute-done.3.right_ref = bf16[34,256]{1,0:T(8,128)(2,1)S(1)} collective-permute-done((bf16[34,256]{1,0:T(8,128)(2,1)S(1)}, bf16[34,256]{1,0:T(8,128)(2,1)S(1)}, u32[]{:S(2)}, u32[]{:S(2)}) %collective-permute-start.3) | collective-permute-done | bytes 17440 | tf_op jit(solution)/shard_map/ppermute | solution.py:493
  79.1 0.6 collective-permute-done.2.left_ref
  79.8 7.0 %all-to-all-done.1 = bf16[128,8,512]{2,1,0:T(8,128)(2,1)S(1)} async-done(((bf16[128,8,512]{2,1,0:T(8,128)(2,1)}), bf16[128,8,512]{2,1,0:T(8,128)(2,1)S(1)}, u32[]{:S(2)}, u32[]{:S(2)}) %all-to-all-start.1) | async-done | bytes 1048608 | tf_op jit(solution)/shard_map/all_to_all | solution.py:501
  86.7 7.7 %filter_rows.1 = bf16[1024,512]{1,0:T(8,128)(2,1)} custom-call(bf16[1024,512]{1,0:T(8,128)(2,1)S(1)} %bitcast.19, bf16[1024,1024]{1,0:T(8,128)(2,1)S(1)} %get-tuple-element.27.fwd, f32[128,512]{1,0:T(8,128)} %get-tuple-element.28.cos_any, f32[128,512]{1,0:T(8,128)} %get-tuple-element.29.sin_any, bf16[1024,1024]{1,0:T(8,128)(2,1)} %get-tuple-element.30.first_any, ...), custom_call_target="tpu_custom_call" | custom-call | flops 5368709120 | bytes 2097152 | tf_op jit(solution)/shard_map/filter_rows/pallas_call | solution.py:454
  94.5 0.0 copy-start.7
  94.5 8.1 %all-to-all-start.2 = ((bf16[128,8,512]{2,1,0:T(8,128)(2,1)}), bf16[128,8,512]{2,1,0:T(8,128)(2,1)S(1)}, u32[]{:S(2)}, u32[]{:S(2)}) async-start(bf16[128,8,512]{2,1,0:T(8,128)(2,1)} %bitcast.22), calls=%async_computation.2 | async-start | bytes 2097152 | tf_op jit(solution)/shard_map/all_to_all | solution.py:510
  102.6 0.6 reshape.31.taps_ref
  103.2 1.1 backward_columns_phases.1.table_ref
  104.3 5.1 %stencil.1.base_ref = f32[32,64,256]{2,1,0:T(8,128)} custom-call(bf16[32,64,256]{2,1,0:T(8,128)(2,1)} %x_ref.3, bf16[32,64,256]{2,1,0:T(8,128)(2,1)} %home_norm.1.normed_ref, bf16[64,256]{1,0:T(8,128)(2,1)} %copy-done.3, bf16[64,256]{1,0:T(8,128)(2,1)} %copy-done.4, bf16[34,256]{1,0:T(8,128)(2,1)} %copy-done.6, bf16[34,256]{1,0:T(8,128)(2,1)} %copy-done.5, ...), custom_call_target="tpu_custom_call" | custom-call | flops 16777216 | bytes 4194304 | tf_op jit(solution)/shard_map/stencil/pallas_call | solution.py:375
  109.4 23.5 %all-to-all-done.2 = bf16[128,8,512]{2,1,0:T(8,128)(2,1)S(1)} async-done(((bf16[128,8,512]{2,1,0:T(8,128)(2,1)}), bf16[128,8,512]{2,1,0:T(8,128)(2,1)S(1)}, u32[]{:S(2)}, u32[]{:S(2)}) %all-to-all-start.2) | async-done | bytes 1048608 | tf_op jit(solution)/shard_map/all_to_all | solution.py:510
  133.0 2.0 %along_columns.3 = bf16[1024,512]{1,0:T(8,128)(2,1)} custom-call(bf16[1024,1024]{1,0:T(8,128)(2,1)S(1)} %backward_columns_phases.1.table_ref, bf16[1024,512]{1,0:T(8,128)(2,1)S(1)} %bitcast.18), custom_call_target="tpu_custom_call" | custom-call | flops 1073741824 | bytes 2097152 | tf_op jit(solution)/shard_map/along_columns/pallas_call | solution.py:327
  135.0 31.3 %all_to_all.20.home_ref = bf16[16,64,512]{2,1,0:T(8,128)(2,1)S(1)} all-to-all(bf16[16,64,512]{2,1,0:T(8,128)(2,1)} %bitcast.21), channel_id=1, replica_groups=mesh['row'=32,'yl'=4,'x'=4] {'yl','x'}, dimensions={0} | all-to-all | bytes 2097152 | tf_op jit(solution)/shard_map/all_to_all | solution.py:514
  166.2 1.9 %unpack_add.1 = bf16[32,64,256]{2,1,0:T(8,128)(2,1)} custom-call(f32[32,64,256]{2,1,0:T(8,128)S(1)} %copy-done, bf16[16,64,512]{2,1,0:T(8,128)(2,1)S(1)} %all_to_all.20.home_ref), custom_call_target="tpu_custom_call" | custom-call | tf_op jit(solution)/shard_map/unpack_add/pallas_call | solution.py:285
  (19 shorter events, 0.1 us)
Async XLA Ops:
  4.4 34.9 %all-to-all-start = ((bf16[16,64,512]{2,1,0:T(8,128)(2,1)}), bf16[16,64,512]{2,1,0:T(8,128)(2,1)S(1)}, u32[]{:S(2)}, u32[]{:S(2)}) async-start(bf16[16,64,512]{2,1,0:T(8,128)(2,1)} %norm_pack.1), calls=%async_computation | async-start | bytes 2097152 | tf_op jit(solution)/shard_map/all_to_all | solution.py:482
  18.6 18.3 %collective-permute-start = (bf16[64,256]{1,0:T(8,128)(2,1)S(1)}, bf16[64,256]{1,0:T(8,128)(2,1)S(1)}, u32[]{:S(2)}, u32[]{:S(2)}) collective-permute-start(bf16[64,256]{1,0:T(8,128)(2,1)S(1)} %get-tuple-element.42), channel_id=1, source_target_pairs={{0,16},{16,32},{32,48},{48,64},{64,80},{80,96},{96,112},{112,128},... | collective-permute-start | bytes 98312 | tf_op jit(solution)/shard_map/ppermute | solution.py:492
  20.6 16.3 %collective-permute-start.1 = (bf16[64,256]{1,0:T(8,128)(2,1)S(1)}, bf16[64,256]{1,0:T(8,128)(2,1)S(1)}, u32[]{:S(2)}, u32[]{:S(2)}) collective-permute-start(bf16[64,256]{1,0:T(8,128)(2,1)S(1)} %get-tuple-element.41), channel_id=1, source_target_pairs={{16,0},{32,16},{48,32},{64,48},{80,64},{96,80},{112,96},{128,112},... | collective-permute-start | bytes 98312 | tf_op jit(solution)/shard_map/ppermute | solution.py:493
  36.9 20.5 %copy-start.3 = (bf16[64,256]{1,0:T(8,128)(2,1)}, bf16[64,256]{1,0:T(8,128)(2,1)S(1)}, u32[]{:S(2)}) copy-start(bf16[64,256]{1,0:T(8,128)(2,1)S(1)} %collective-permute-done.top_ref) | copy-start | bytes 98308
  36.9 20.5 %copy-start.4 = (bf16[64,256]{1,0:T(8,128)(2,1)}, bf16[64,256]{1,0:T(8,128)(2,1)S(1)}, u32[]{:S(2)}) copy-start(bf16[64,256]{1,0:T(8,128)(2,1)S(1)} %collective-permute-done.1.bottom_ref) | copy-start | bytes 98308
  41.3 24.8 %copy-start.1 = (bf16[2,4,64,64]{3,2,1,0:T(8,128)(2,1)S(1)}, bf16[2,4,64,64]{3,2,1,0:T(8,128)(2,1)}, u32[]{:S(2)}) copy-start(bf16[2,4,64,64]{3,2,1,0:T(8,128)(2,1)} %first_w.1) | copy-start | bytes 196612
  41.3 24.8 %copy-start.2 = (bf16[2,4,64,64]{3,2,1,0:T(8,128)(2,1)S(1)}, bf16[2,4,64,64]{3,2,1,0:T(8,128)(2,1)}, u32[]{:S(2)}) copy-start(bf16[2,4,64,64]{3,2,1,0:T(8,128)(2,1)} %second_w.1) | copy-start | bytes 196612
  41.3 45.4 %all-to-all-start.1 = ((bf16[128,8,512]{2,1,0:T(8,128)(2,1)}), bf16[128,8,512]{2,1,0:T(8,128)(2,1)S(1)}, u32[]{:S(2)}, u32[]{:S(2)}) async-start(bf16[128,8,512]{2,1,0:T(8,128)(2,1)} %bitcast.20), calls=%async_computation.1 | async-start | bytes 2097152 | tf_op jit(solution)/shard_map/all_to_all | solution.py:501
  57.4 21.7 %collective-permute-start.3 = (bf16[34,256]{1,0:T(8,128)(2,1)S(1)}, bf16[34,256]{1,0:T(8,128)(2,1)S(1)}, u32[]{:S(2)}, u32[]{:S(2)}) collective-permute-start(bf16[34,256]{1,0:T(8,128)(2,1)S(1)} %pad_maximum_fusion.1), channel_id=1, source_target_pairs={{1,0},{2,1},{3,2},{4,3},{5,4},{6,5},{7,6},{8,7},{9,8},{10,9},{11,1... | collective-permute-start | bytes 52232 | tf_op jit(solution)/shard_map/ppermute | solution.py:493
  61.2 18.5 %collective-permute-start.2 = (bf16[34,256]{1,0:T(8,128)(2,1)S(1)}, bf16[34,256]{1,0:T(8,128)(2,1)S(1)}, u32[]{:S(2)}, u32[]{:S(2)}) collective-permute-start(bf16[34,256]{1,0:T(8,128)(2,1)S(1)} %pad_maximum_fusion), channel_id=1, source_target_pairs={{0,1},{1,2},{2,3},{3,4},{4,5},{5,6},{6,7},{7,8},{8,9},{9,10},{10,1... | collective-permute-start | bytes 52232 | tf_op jit(solution)/shard_map/ppermute | solution.py:492
  79.1 15.3 %copy-start.5 = (bf16[34,256]{1,0:T(8,128)(2,1)}, bf16[34,256]{1,0:T(8,128)(2,1)S(1)}, u32[]{:S(2)}) copy-start(bf16[34,256]{1,0:T(8,128)(2,1)S(1)} %collective-permute-done.3.right_ref) | copy-start | bytes 52228
  79.8 14.7 %copy-start.6 = (bf16[34,256]{1,0:T(8,128)(2,1)}, bf16[34,256]{1,0:T(8,128)(2,1)S(1)}, u32[]{:S(2)}) copy-start(bf16[34,256]{1,0:T(8,128)(2,1)S(1)} %collective-permute-done.2.left_ref) | copy-start | bytes 52228
  94.5 8.1 %copy-start.7 = (f32[3,3,256]{2,1,0:T(4,128)S(1)}, f32[3,3,256]{2,1,0:T(4,128)}, u32[]{:S(2)}) copy-start(f32[3,3,256]{2,1,0:T(4,128)} %param.9) | copy-start | bytes 27652
  94.5 38.5 %all-to-all-start.2 = ((bf16[128,8,512]{2,1,0:T(8,128)(2,1)}), bf16[128,8,512]{2,1,0:T(8,128)(2,1)S(1)}, u32[]{:S(2)}, u32[]{:S(2)}) async-start(bf16[128,8,512]{2,1,0:T(8,128)(2,1)} %bitcast.22), calls=%async_computation.2 | async-start | bytes 2097152 | tf_op jit(solution)/shard_map/all_to_all | solution.py:510
  135.0 31.3 %copy-start = (f32[32,64,256]{2,1,0:T(8,128)S(1)}, f32[32,64,256]{2,1,0:T(8,128)}, u32[]{:S(2)}) copy-start(f32[32,64,256]{2,1,0:T(8,128)} %stencil.1.base_ref) | copy-start | bytes 6291460

commit v6 on v5

--- a/solution.py
+++ b/solution.py
@@ -86,7 +86,8 @@
         c, s = cos_sin(ib)
         fc[...], fs[...] = c * weight, s * weight
         if with_twiddles:
-            angle = iota((128, 512), 0) * (iota((128, 512), 1) >> 6)
+            lane = iota((128, 512), 1)
+            angle = iota((128, 512), 0) * ((lane >> 7) + 4 * digit(lane, 6, 1))
             refs[1][...], refs[2][...] = cos_sin(angle)
 
     first = 0 if stay else steps * pl.program_id(0)
@@ -120,68 +121,55 @@
     return out if with_twiddles else out[0]
 
 
-def blocks_kernel(first_w, second_w, first_ref, eight_ref, second_ref, acc, ass, bcc):
+def blocks_kernel(first_w, second_w, first_ref, last_ref, second_ref, fc, fs, bc):
     block = lax.axis_index("x")
     low = low_half(64)
+    a, lane = iota((16, 256), 0), iota((16, 256), 1)
+    t, ri, row_e = a >> 2, digit(a, 1, 1), a & 1
+    ro, lane_e = lane >> 7, digit(lane, 6, 1)
+    fc[...], fs[...] = cos_sin(128 * lane_e * (t + 4 * row_e) + 256 * (ro - ri))
+    bc[...], _unused = cos_sin(128 * row_e * (t + 4 * lane_e) - 256 * (ro - ri))
 
     def twice(ref, n):
         w = ref[n, block].astype(F32)
         return jnp.concatenate([w, w], axis=1)
 
-    @pl.when(pl.program_id(0) == 0)
-    def _():
-        a, lane = iota((16, 1024), 0), iota((16, 1024), 1)
-        q1 = 2 * digit(lane, 8, 2) + digit(lane, 6, 1)
-        acc[...], ass[...] = cos_sin(
-            128 * q1 * digit(a, 0, 3) + 256 * (digit(lane, 7, 1) - digit(a, 3, 1))
-        )
-        q1 = 2 * digit(a, 2, 2) + digit(a, 0, 1)
-        bcc[...], _unused = cos_sin(
-            128 * q1 * digit(lane, 6, 3) - 256 * (digit(lane, 9, 1) - digit(a, 1, 1))
-        )
-        w0, w1 = twice(second_w, 0), twice(second_w, 1)
-        zero = jnp.zeros_like(w0)
-        for half in range(2):
-            def own(v):
-                return (jnp.where(low, v, zero) if half == 0 else jnp.where(low, zero, v)).astype(BF16)
-
-            re, im = slice(64 * half, 64 * half + 64), slice(128 + 64 * half, 192 + 64 * half)
-            second_ref[re, :128], second_ref[re, 128:] = own(w0), own(w1)
-            second_ref[im, :128], second_ref[im, 128:] = own(-w1), own(w0)
+    w0, w1 = twice(second_w, 0), twice(second_w, 1)
+    zero = jnp.zeros_like(w0)
+    for half in range(2):
+        def own(v):
+            return (jnp.where(low, v, zero) if half == 0 else jnp.where(low, zero, v)).astype(BF16)
+
+        re, im = slice(64 * half, 64 * half + 64), slice(128 + 64 * half, 192 + 64 * half)
+        second_ref[re, :128], second_ref[re, 128:] = own(w0), own(w1)
+        second_ref[im, :128], second_ref[im, 128:] = own(-w1), own(w0)
 
     w0, w1 = twice(first_w, 0), twice(first_w, 1)
     eye = jnp.where(iota((64, 128), 0) == (iota((64, 128), 1) & 63), 1.0, 0.0)
-    first = 4 * pl.program_id(0)
-
-    def step(a, carry):
-        rows = pl.ds(pl.multiple_of(64 * a, 64), 64)
-        row = pl.ds(first + a, 1)
-        c, s, back = acc[row, :], ass[row, :], bcc[row, :]
-        for t in range(8):
-            lanes = slice(128 * t, 128 * t + 128)
-            first_ref[rows, lanes] = (c[:, lanes] * w0 + s[:, lanes] * w1).astype(BF16)
-            eight_ref[rows, lanes] = (back[:, lanes] * eye).astype(BF16)
-        return carry
-
-    lax.fori_loop(0, 4, step, 0)
+    for n in range(16):
+        rows = slice(64 * n, 64 * n + 64)
+        for lanes in (slice(0, 128), slice(128, 256)):
+            first_ref[rows, lanes] = (
+                fc[n : n + 1, lanes] * w0 + fs[n : n + 1, lanes] * w1
+            ).astype(BF16)
+            last_ref[rows, lanes] = (bc[n : n + 1, lanes] * eye).astype(BF16)
 
 
 def block_tables(w_first, w_second):
     vmem = pl.BlockSpec(memory_space=pltpu.VMEM)
-    quarter = pl.BlockSpec((256, 1024), lambda g: (g, 0))
     return pl.pallas_call(
         blocks_kernel,
-        grid=(4,),
+        grid=(1,),
         in_specs=[vmem, vmem],
-        out_specs=[quarter, quarter, pl.BlockSpec((256, 256), lambda g: (0, 0))],
-        out_shape=[
-            pltpu.HBM((1024, 1024), BF16),
-            pltpu.HBM((1024, 1024), BF16),
-            pltpu.HBM((256, 256), BF16),
+        out_specs=[
+            pl.BlockSpec((1024, 256), lambda g: (0, 0)),
+            pl.BlockSpec((1024, 256), lambda g: (0, 0)),
+            pl.BlockSpec((256, 256), lambda g: (0, 0)),
         ],
-        scratch_shapes=[pltpu.VMEM((16, 1024), F32)] * 3,
-        cost_estimate=pl.CostEstimate(flops=2**23, bytes_accessed=2**22, transcendentals=0),
-        compiler_params=pltpu.CompilerParams(vmem_limit_bytes=8 * MIB),
+        out_shape=[pltpu.HBM((n, 256), BF16) for n in (1024, 1024, 256)],
+        scratch_shapes=[pltpu.VMEM((16, 256), F32)] * 3,
+        cost_estimate=pl.CostEstimate(flops=2**21, bytes_accessed=2**20, transcendentals=0),
+        compiler_params=pltpu.CompilerParams(vmem_limit_bytes=6 * MIB),
         name="block_tables",
     )(w_first, w_second)
 
@@ -194,9 +182,8 @@
     return pltpu.roll(v, 64, 1)
 
 
-def normed_halves(x_ref, gain_ref):
+def normed_halves(x, gain_ref):
     ones = jnp.ones((256, 128), BF16)
-    x = x_ref[...].reshape(512, 256)
     mean = dot(x, ones) * (1.0 / 256.0)
     d0, d1 = x[:, :128].astype(F32) - mean, x[:, 128:].astype(F32) - mean
     square = d0 * d0 + d1 * d1
@@ -210,29 +197,31 @@
 def norm_kernel(x_any, gain_ref, out_any, x_all, packed, in_sems, out_sems):
     low = low_half(64)
     fetches, sends = [], []
-    for g in range(4):
-        rows = slice(8 * g, 8 * g + 8)
-        fetches.append(pltpu.make_async_copy(x_any.at[rows], x_all.at[rows], in_sems.at[g]))
+    for n in range(2):
+        rows = slice(16 * n, 16 * n + 16)
+        fetches.append(pltpu.make_async_copy(x_any.at[rows], x_all.at[rows], in_sems.at[n]))
         fetches[-1].start()
-    for g in range(4):
-        fetches[g].wait()
-        halves = normed_halves(x_all.at[8 * g : 8 * g + 8], gain_ref)
-        for t in range(4):
-            lanes = slice(128 * t, 128 * t + 128)
-            for m in range(2):
-                a = halves[m][128 * t : 128 * t + 64]
-                b = halves[m][128 * t + 64 : 128 * t + 128]
-                packed[4 * g + 2 * m, :, lanes] = jnp.where(low, a, swap(b)).astype(BF16)
-                packed[4 * g + 2 * m + 1, :, lanes] = jnp.where(low, swap(a), b).astype(BF16)
-        parts = slice(4 * g, 4 * g + 4)
-        sends.append(pltpu.make_async_copy(packed.at[parts], out_any.at[parts], out_sems.at[g]))
+    for n in range(2):
+        fetches[n].wait()
+        halves = normed_halves(x_all[16 * n : 16 * n + 16].reshape(1024, 256), gain_ref)
+        for g in range(2):
+            first = 4 * (2 * n + g)
+            for t in range(4):
+                lanes = slice(128 * t, 128 * t + 128)
+                for m in range(2):
+                    a = halves[m][512 * g + 64 * t : 512 * g + 64 * t + 64]
+                    b = halves[m][512 * g + 64 * t + 256 : 512 * g + 64 * t + 320]
+                    packed[first + 2 * m, :, lanes] = jnp.where(low, a, swap(b)).astype(BF16)
+                    packed[first + 2 * m + 1, :, lanes] = jnp.where(low, swap(a), b).astype(BF16)
+        parts = slice(8 * n, 8 * n + 8)
+        sends.append(pltpu.make_async_copy(packed.at[parts], out_any.at[parts], out_sems.at[n]))
         sends[-1].start()
     for send in sends:
         send.wait()
 
 
 def home_norm_kernel(x_ref, gain_ref, out_ref):
-    for m, half in enumerate(normed_halves(x_ref, gain_ref)):
+    for m, half in enumerate(normed_halves(x_ref[...].reshape(512, 256), gain_ref)):
         out_ref[:, :, 128 * m : 128 * m + 128] = half.astype(BF16).reshape(8, 64, 128)
 
 
@@ -259,8 +248,8 @@
         scratch_shapes=[
             pltpu.VMEM((32, 64, 256), BF16),
             pltpu.VMEM((16, 64, 512), BF16),
-            pltpu.SemaphoreType.DMA((4,)),
-            pltpu.SemaphoreType.DMA((4,)),
+            pltpu.SemaphoreType.DMA((2,)),
+            pltpu.SemaphoreType.DMA((2,)),
         ],
         compiler_params=pltpu.CompilerParams(vmem_limit_bytes=16 * MIB),
         name="norm_pack",
@@ -269,7 +258,7 @@
 
 def final_kernel(base_ref, home_ref, out_ref):
     low = low_half(64)
-    first = 4 * pl.program_id(0)
+    first, row = 4 * pl.program_id(0), 8 * pl.program_id(0)
     for t in range(4):
         lanes = slice(128 * t, 128 * t + 128)
         for m in range(2):
@@ -277,23 +266,20 @@
             v = home_ref[first + 2 * m + 1, :, lanes].astype(F32)
             chans = slice(128 * m, 128 * m + 128)
             even, odd = jnp.where(low, u, swap(v)), jnp.where(low, swap(u), v)
-            out_ref[2 * t, :, chans] = (base_ref[2 * t, :, chans] + even).astype(BF16)
-            out_ref[2 * t + 1, :, chans] = (base_ref[2 * t + 1, :, chans] + odd).astype(BF16)
+            out_ref[t, :, chans] = (base_ref[row + t, :, chans] + even).astype(BF16)
+            out_ref[t + 4, :, chans] = (base_ref[row + t + 4, :, chans] + odd).astype(BF16)
 
 
 def unpack_and_add(base, home):
     return pl.pallas_call(
         final_kernel,
         grid=(4,),
-        in_specs=[
-            pl.BlockSpec((8, 64, 256), lambda g: (g, 0, 0)),
-            pl.BlockSpec(memory_space=pltpu.VMEM),
-        ],
+        in_specs=[pl.BlockSpec(memory_space=pltpu.VMEM)] * 2,
         out_specs=pl.BlockSpec((8, 64, 256), lambda g: (g, 0, 0)),
         out_shape=jax.ShapeDtypeStruct((32, 64, 256), BF16),
         compiler_params=pltpu.CompilerParams(vmem_limit_bytes=8 * MIB),
         name="unpack_add",
-    )(base, resident(home))
+    )(resident(base), resident(home))
 
 
 def dot(a, b):
@@ -362,7 +348,7 @@
 
         left = jnp.where(column == 0, left_sum[pl.ds(h, 1), :], pltpu.roll(part(0), 1, 0))
         right = jnp.where(column == 63, right_sum[pl.ds(h, 1), :], pltpu.roll(part(2), 63, 0))
-        out_ref[r] = x_ref[r].astype(F32) + (left + part(1) + right)
+        out_ref[h] = x_ref[r].astype(F32) + (left + part(1) + right)
         return carry
 
     lax.fori_loop(0, 8, step, 0)
@@ -381,8 +367,8 @@
             row, row, side, side,
             pl.BlockSpec((9, 256), lambda g: (0, 0)),
         ],
-        out_specs=block,
-        out_shape=pltpu.HBM((32, 64, 256), F32),
+        out_specs=pl.BlockSpec(memory_space=pltpu.VMEM),
+        out_shape=pltpu.VMEM((32, 64, 256), F32),
         scratch_shapes=[
             pltpu.VMEM((34, 64, 256), BF16),
             pltpu.VMEM((34, 256), F32),
@@ -395,9 +381,26 @@
     )(*[remaining(v) for v in (x, normed, top, bottom, left, right, taps)])
 
 
+def butterfly(x, sign):
+    re, im = [v[:, :128] for v in x], [v[:, 128:] for v in x]
+
+    def pair(v):
+        return v[0] + v[2], v[0] - v[2], v[1] + v[3], v[1] - v[3]
+
+    (er, dr, fr, gr), (ei, di, fi, gi) = pair(re), pair(im)
+    plus, minus = (dr - gi, di + gr), (dr + gi, di - gr)
+    if sign < 0:
+        plus, minus = minus, plus
+    return (er + fr, ei + fi), plus, (er - fr, ei - fi), minus
+
+
+def beside(pair):
+    return jnp.concatenate(pair, axis=1)
+
+
 def middle_kernel(
-    z, fwd, cos_any, sin_any, first_any, eight_any, inv_any, second_any, out_any,
-    cos_ref, sin_ref, first, eight, inv, second_ref, held, done, sems, fetch_sems,
+    z, fwd, cos_any, sin_any, first_any, second_any, last_any, inv_any, out_any,
+    cos_ref, sin_ref, first, second, last, inv, held, done, sems, fetch_sems,
 ):
     fetches = []
     for n, (src, dst) in enumerate(
@@ -405,51 +408,55 @@
             (cos_any, cos_ref),
             (sin_any, sin_ref),
             (first_any, first),
-            (eight_any, eight),
+            (second_any, second),
+            (last_any, last),
             (inv_any, inv),
-            (second_any, second_ref),
         )
     ):
         fetches.append(pltpu.make_async_copy(src, dst, fetch_sems.at[n]))
-    for n in (0, 1, 2, 5):
-        fetches[n].start()
+        fetches[-1].start()
     rows = 512 // CHUNKS
     groups = 8 // CHUNKS
+    shape = (groups, 4, 16, 128)
     for m in range(CHUNKS):
         u = dot(fwd[2 * rows * m : 2 * rows * (m + 1), :], z[...])
-        shape = (groups, 4, 16, 512)
-        ur, ui = u[:rows].reshape(shape), u[rows:].reshape(shape)
         if m == 0:
-            fetches[0].wait()
-            fetches[1].wait()
-            fetches[3].start()
-        c = cos_ref[16 * groups * m : 16 * groups * (m + 1), :].reshape(groups, 1, 16, 512)
-        s = sin_ref[16 * groups * m : 16 * groups * (m + 1), :].reshape(groups, 1, 16, 512)
-        vr = (ur * c + ui * s).astype(BF16).reshape(rows, 512)
-        vi = (ui * c - ur * s).astype(BF16).reshape(rows, 512)
-        if m == 0:
-            fetches[2].wait()
-            fetches[5].wait()
-            fetches[4].start()
-        hidden = jnp.tanh(dot(vr, first[:512, :]) + dot(vi, first[512:, :])).astype(BF16)
+            for fetch in fetches[:4]:
+                fetch.wait()
+
+        def twiddles(t):
+            part = (slice(16 * groups * m, 16 * groups * (m + 1)), slice(128 * t, 128 * t + 128))
+            return [ref[part].reshape(groups, 1, 16, 128) for ref in (cos_ref, sin_ref)]
+
         parts = []
         for t in range(4):
-            v = dot(hidden[:, 256 * t : 256 * t + 256], second_ref[...])
-            v = jnp.where(v > 0.25, v - 0.25, jnp.where(v < -0.25, v + 0.25, 0.0 * v))
-            parts.append(v.astype(BF16))
+            ur = u[:rows, 128 * t : 128 * t + 128].reshape(shape)
+            ui = u[rows:, 128 * t : 128 * t + 128].reshape(shape)
+            c, s = twiddles(t)
+            vr, vi = (ur * c + ui * s).reshape(rows, 128), (ui * c - ur * s).reshape(rows, 128)
+            parts.append(dot(beside((vr.astype(BF16), vi.astype(BF16))), first[256 * t : 256 * t + 256, :]))
+        kept = []
+        for part in butterfly(parts, -1):
+            v = dot(jnp.tanh(beside(part)).astype(BF16), second[...])
+            kept.append(jnp.where(v > 0.25, v - 0.25, jnp.where(v < -0.25, v + 0.25, 0.0 * v)))
         if m == 0:
-            fetches[3].wait()
-        y = dot(jnp.concatenate(parts, axis=1), eight[...])
-        yr, yi = y[:, :512].reshape(shape), y[:, 512:].reshape(shape)
-        held[2 * rows * m : 2 * rows * m + rows, :] = (yr * c - yi * s).astype(BF16).reshape(rows, 512)
-        held[2 * rows * m + rows : 2 * rows * (m + 1), :] = (
-            (yi * c + yr * s).astype(BF16).reshape(rows, 512)
-        )
-    fetches[4].wait()
+            fetches[4].wait()
+        for t, part in enumerate(butterfly(kept, 1)):
+            y = dot(beside(part).astype(BF16), last[256 * t : 256 * t + 256, :])
+            yr, yi = y[:, :128].reshape(shape), y[:, 128:].reshape(shape)
+            c, s = twiddles(t)
+            lanes = slice(128 * t, 128 * t + 128)
+            held[2 * rows * m : 2 * rows * m + rows, lanes] = (
+                (yr * c - yi * s).astype(BF16).reshape(rows, 128)
+            )
+            held[2 * rows * m + rows : 2 * rows * (m + 1), lanes] = (
+                (yi * c + yr * s).astype(BF16).reshape(rows, 128)
+            )
+    fetches[5].wait()
     stream_dot(inv, held, done, out_any, sems)
 
 
-def middle(z, fwd, first, eight, inv, second, cos, sin):
+def middle(z, fwd, cos, sin, first, second, last, inv):
     vmem, hbm = pl.BlockSpec(memory_space=pltpu.VMEM), pl.BlockSpec(memory_space=pltpu.HBM)
     return pl.pallas_call(
         middle_kernel,
@@ -459,21 +466,20 @@
         scratch_shapes=[
             pltpu.VMEM((128, 512), F32),
             pltpu.VMEM((128, 512), F32),
+            pltpu.VMEM((1024, 256), BF16),
+            pltpu.VMEM((256, 256), BF16),
+            pltpu.VMEM((1024, 256), BF16),
             pltpu.VMEM((1024, 1024), BF16),
-            pltpu.VMEM((1024, 1024), BF16),
-            pltpu.VMEM((1024, 1024), BF16),
-            pltpu.VMEM((256, 256), BF16),
             pltpu.VMEM((1024, 512), BF16),
             pltpu.VMEM((1024, 512), BF16),
             pltpu.SemaphoreType.DMA((4,)),
             pltpu.SemaphoreType.DMA((6,)),
         ],
-        cost_estimate=pl.CostEstimate(flops=5 * 2**30, bytes_accessed=2**21, transcendentals=2**19),
-        compiler_params=pltpu.CompilerParams(vmem_limit_bytes=28 * MIB),
+        cost_estimate=pl.CostEstimate(flops=3 * 2**30, bytes_accessed=2**21, transcendentals=2**19),
+        compiler_params=pltpu.CompilerParams(vmem_limit_bytes=24 * MIB),
         name="filter_rows",
     )(
-        resident(z), resident(fwd), remaining(cos), remaining(sin), remaining(first),
-        remaining(eight), remaining(inv), remaining(second),
+        resident(z), resident(fwd), *[remaining(v) for v in (cos, sin, first, second, last, inv)]
     )
 
 
@@ -484,7 +490,7 @@
     fwd_w = table(pltpu.VMEM, forward_columns_phases)
     inv_w = table(pltpu.VMEM, backward_columns_phases)
     inv_h = table(pltpu.HBM, backward_rows_phases)
-    first, eight, second = block_tables(w_first, w_second)
+    first, last, second = block_tables(w_first, w_second)
     fwd_h, cos, sin = table(pltpu.VMEM, forward_rows_phases, True, (second, inv_h))
 
     def neighbours(first, last, axis):
@@ -494,24 +500,26 @@
         return before, after
 
     normed = home_norm(patches, norm_gain)
-    top, bottom = neighbours(normed[0], normed[31], "row")
-    lines, top, bottom = lax.optimization_barrier((lines, top, bottom))
+    lines, normed = lax.optimization_barrier((lines, normed))
 
     freqs = columns(fwd_w, lines)
     whole = lax.all_to_all(freqs.reshape(128, 8, 512), ("row", "yl"), 0, 0, tiled=True)
+    top, bottom = neighbours(normed[0], normed[31], "row")
+    whole, top, bottom = lax.optimization_barrier((whole, top, bottom))
+
+    filtered = middle(whole.reshape(1024, 512), fwd_h, cos, sin, first, second, last, inv_h)
+    filtered, top, bottom, normed = lax.optimization_barrier((filtered, top, bottom, normed))
+    back = lax.all_to_all(filtered.reshape(128, 8, 512), ("row", "yl"), 0, 0, tiled=True)
     sides = [
         jnp.concatenate([top[w : w + 1], normed[:, w], bottom[w : w + 1]], axis=0) for w in (0, 63)
     ]
     left, right = neighbours(sides[0], sides[1], ("yl", "x"))
-    whole, left, right = lax.optimization_barrier((whole, left, right))
-
-    filtered = middle(whole.reshape(1024, 512), fwd_h, first, eight, inv_h, second, cos, sin)
-    filtered, left, right = lax.optimization_barrier((filtered, left, right))
-    back = lax.all_to_all(filtered.reshape(128, 8, 512), ("row", "yl"), 0, 0, tiled=True)
+    back, left, right = lax.optimization_barrier((back, left, right))
+
+    spectral = columns(inv_w, back.reshape(1024, 512))
+    spectral, left, right = lax.optimization_barrier((spectral, left, right))
+    home = lax.all_to_all(spectral.reshape(16, 64, 512), ("yl", "x"), 0, 0, tiled=True)
     base = stencil(patches, normed, top, bottom, left, right, depth_kernel.reshape(9, 256))
-    spectral = columns(inv_w, back.reshape(1024, 512))
-    spectral, base = lax.optimization_barrier((spectral, base))
-    home = lax.all_to_all(spectral.reshape(16, 64, 512), ("yl", "x"), 0, 0, tiled=True)
     return unpack_and_add(base, home)
 
 

time: 169 us -> 165 us (0.976)
  blocking collectives: 31.3 us -> 0 us
  waiting for transfers between devices: 45 us -> 74.7 us
  Pallas kernels: 37.9 us -> 32.2 us
  starting transfers between devices: 51.2 us -> 55.1 us
    all_to_all x1 -> x0, blocking collectives: 31.3 us -> none  [local(): lax.all_to_all(spectral.reshape(16, 64, 512), ('yl', 'x'), 0, 0, tiled=True)]
    all_to_all x0 -> x1, waiting for transfers between devices: none -> 20.3 us  [local(): lax.all_to_all(spectral.reshape(16, 64, 512), ('yl', 'x'), 0, 0, tiled=True)]
    all_to_all x1, waiting for transfers between devices: 23.5 us -> 6.96 us  [local(): lax.all_to_all(filtered.reshape(128, 8, 512), ('row', 'yl'), 0, 0, tiled=...]
    all_to_all x1, waiting for transfers between devices: 2.43 us -> 18.9 us  [local(): lax.all_to_all(packed, ('yl', 'x'), 0, 0, tiled=True).reshape(1024, 512)]
    ppermute x2, waiting for transfers between devices: 4.9 us -> 13.4 us  [neighbours(): before = lax.ppermute(last, axis, [(i, (i + 1) % n) for i in range(n)])]
    ppermute x2, waiting for transfers between devices: 7.23 us -> 15.2 us  [neighbours(): after = lax.ppermute(first, axis, [((i + 1) % n, i) for i in range(n)])]
    all_to_all x1, waiting for transfers between devices: 6.96 us -> 0.01 us  [local(): lax.all_to_all(freqs.reshape(128, 8, 512), ('row', 'yl'), 0, 0, tiled=True)]
    all_to_all x0 -> x1, starting transfers between devices: none -> 6.29 us  [local(): lax.all_to_all(spectral.reshape(16, 64, 512), ('yl', 'x'), 0, 0, tiled=True)]
  transfers between devices with their start and end apart: 7 -> 8, of which waited for: 6 -> 6; matrix products, arithmetic and copies ran while one was open for 1% -> 1% of each run, Pallas kernels for 12% -> 10%
where the time goes in v6:
time: 165 us; the launch traced here: 164 us
  waiting for transfers between devices  74.7 us (45%)
  starting transfers between devices  55.1 us (33%)
  Pallas kernels  32.2 us (20%)
  local copies, waits for them, and re-layouts  2.03 us (1%)
    all_to_all x1, waiting for transfers between devices, local(): lax.all_to_all(spectral.reshape(16, 64, 512), ('yl', 'x'), 0, 0, tiled=True)  20.3 us
    all_to_all x1, waiting for transfers between devices, local(): lax.all_to_all(packed, ('yl', 'x'), 0, 0, tiled=True).reshape(1024, 512)  18.9 us
    ppermute x2, waiting for transfers between devices, neighbours(): after = lax.ppermute(first, axis, [((i + 1) % n, i) for i in range(n)])  15.2 us
    all_to_all x1, starting transfers between devices, local(): lax.all_to_all(freqs.reshape(128, 8, 512), ('row', 'yl'), 0, 0, tiled=True)  15 us
    ppermute x2, waiting for transfers between devices, neighbours(): before = lax.ppermute(last, axis, [(i, (i + 1) % n) for i in range(n)])  13.4 us
    ppermute x2, starting transfers between devices, neighbours(): after = lax.ppermute(first, axis, [((i + 1) % n, i) for i in range(n)])  13.3 us
    all_to_all x1, starting transfers between devices, local(): lax.all_to_all(packed, ('yl', 'x'), 0, 0, tiled=True).reshape(1024, 512)  9.3 us
    pallas_call x4, Pallas kernels, table(): pl.pallas_call(functools.partial(table_kernel, phases, with_twiddles, sta...  7.15 us
  transfers between devices with their start and end apart: 8, of which 6 were waited for; matrix products, arithmetic and copies ran while one was open for 1% of the time, Pallas kernels for 10%

profile of v6, /device:TPU:8, one launch (start us, length us, event | category | flops | bytes accessed | tf_op | source)
XLA Modules:
  0.0 164.2 jit_solution(9566130606332054455)
XLA Ops:
  0.0 3.9 %norm_pack.1 = bf16[16,64,512]{2,1,0:T(8,128)(2,1)} custom-call(bf16[32,64,256]{2,1,0:T(8,128)(2,1)} %x_ref.3, f32[1,256]{1,0:T(1,128)} %bitcast.21), custom_call_target="tpu_custom_call" | custom-call | tf_op jit(solution)/shard_map/norm_pack/pallas_call | solution.py:243
  3.9 9.3 %all-to-all-start = ((bf16[16,64,512]{2,1,0:T(8,128)(2,1)}), bf16[16,64,512]{2,1,0:T(8,128)(2,1)S(1)}, u32[]{:S(2)}, u32[]{:S(2)}) async-start(bf16[16,64,512]{2,1,0:T(8,128)(2,1)} %norm_pack.1), calls=%async_computation | async-start | bytes 2097152 | tf_op jit(solution)/shard_map/all_to_all | solution.py:488
  13.2 1.1 forward_columns_phases.1.table_ref
  14.4 4.2 %home_norm.1.normed_ref = bf16[32,64,256]{2,1,0:T(8,128)(2,1)} custom-call(bf16[32,64,256]{2,1,0:T(8,128)(2,1)} %x_ref.3, f32[1,256]{1,0:T(1,128)} %bitcast.22), custom_call_target="tpu_custom_call" | custom-call | flops 16777216 | bytes 2097152 | tf_op jit(solution)/shard_map/home_norm/pallas_call | solution.py:230
  18.5 18.9 %all-to-all-done = bf16[16,64,512]{2,1,0:T(8,128)(2,1)S(1)} async-done(((bf16[16,64,512]{2,1,0:T(8,128)(2,1)}), bf16[16,64,512]{2,1,0:T(8,128)(2,1)S(1)}, u32[]{:S(2)}, u32[]{:S(2)}) %all-to-all-start) | async-done | bytes 1048608 | tf_op jit(solution)/shard_map/all_to_all | solution.py:488
  37.5 2.0 %along_columns.2 = bf16[1024,512]{1,0:T(8,128)(2,1)} custom-call(bf16[1024,1024]{1,0:T(8,128)(2,1)S(1)} %forward_columns_phases.1.table_ref, bf16[1024,512]{1,0:T(8,128)(2,1)S(1)} %bitcast.16), custom_call_target="tpu_custom_call" | custom-call | flops 1073741824 | bytes 2097152 | tf_op jit(solution)/shard_map/along_columns/pallas_call | solution.py:313
  39.5 0.0 copy-start
  39.5 15.0 %all-to-all-start.1 = ((bf16[128,8,512]{2,1,0:T(8,128)(2,1)}), bf16[128,8,512]{2,1,0:T(8,128)(2,1)S(1)}, u32[]{:S(2)}, u32[]{:S(2)}) async-start(bf16[128,8,512]{2,1,0:T(8,128)(2,1)} %bitcast.18), calls=%async_computation.1 | async-start | bytes 2097152 | tf_op jit(solution)/shard_map/all_to_all | solution.py:506
  54.5 0.8 slice_bitcast_fusion
  55.2 2.0 %collective-permute-start = (bf16[64,256]{1,0:T(8,128)(2,1)S(1)}, bf16[64,256]{1,0:T(8,128)(2,1)S(1)}, u32[]{:S(2)}, u32[]{:S(2)}) collective-permute-start(bf16[64,256]{1,0:T(8,128)(2,1)S(1)} %get-tuple-element.50), channel_id=1, source_target_pairs={{0,16},{16,32},{32,48},{48,64},{64,80},{80,96},{96,112},{112,128},... | collective-permute-start | bytes 98312 | tf_op jit(solution)/shard_map/ppermute | solution.py:498
  57.3 9.5 %collective-permute-start.1 = (bf16[64,256]{1,0:T(8,128)(2,1)S(1)}, bf16[64,256]{1,0:T(8,128)(2,1)S(1)}, u32[]{:S(2)}, u32[]{:S(2)}) collective-permute-start(bf16[64,256]{1,0:T(8,128)(2,1)S(1)} %get-tuple-element.49), channel_id=1, source_target_pairs={{16,0},{32,16},{48,32},{64,48},{80,64},{96,80},{112,96},{128,112},... | collective-permute-start | bytes 98312 | tf_op jit(solution)/shard_map/ppermute | solution.py:499
  66.9 1.2 block_tables.1
  68.0 2.6 %backward_rows_phases.1.refs_1_.inv_any = bf16[1024,1024]{1,0:T(8,128)(2,1)} custom-call(), custom_call_target="tpu_custom_call" | custom-call | flops 8388608 | bytes 2097152 | tf_op jit(solution)/shard_map/backward_rows_phases/pallas_call | solution.py:109
  70.7 2.3 %forward_rows_phases.1 = (bf16[1024,1024]{1,0:T(8,128)(2,1)S(1)}, f32[128,512]{1,0:T(8,128)}, f32[128,512]{1,0:T(8,128)}) custom-call(bf16[256,256]{1,0:T(8,128)(2,1)} %get-tuple-element.29.refs_0_.second_any, bf16[1024,1024]{1,0:T(8,128)(2,1)} %backward_rows_phases.1.refs_1_.inv_any), custom_call_target="tpu_custom_call" | custom-call | flops 8388608 | bytes 2097152 | tf_op jit(solution)/shard_map/forward_rows_phases/pallas_call | solution.py:109
  73.0 12.8 %collective-permute-done.top_ref = bf16[64,256]{1,0:T(8,128)(2,1)S(1)} collective-permute-done((bf16[64,256]{1,0:T(8,128)(2,1)S(1)}, bf16[64,256]{1,0:T(8,128)(2,1)S(1)}, u32[]{:S(2)}, u32[]{:S(2)}) %collective-permute-start) | collective-permute-done | bytes 32800 | tf_op jit(solution)/shard_map/ppermute | solution.py:498
  85.7 5.8 %filter_rows.1 = bf16[1024,512]{1,0:T(8,128)(2,1)} custom-call(bf16[1024,512]{1,0:T(8,128)(2,1)S(1)} %bitcast.17, bf16[1024,1024]{1,0:T(8,128)(2,1)S(1)} %get-tuple-element.30.fwd, f32[128,512]{1,0:T(8,128)} %get-tuple-element.31.cos_any, f32[128,512]{1,0:T(8,128)} %get-tuple-element.32.sin_any, bf16[1024,256]{1,0:T(8,128)(2,1)} %get-tuple-element.33.first_any, ...), custom_call_target="tpu_custom_call" | custom-call | flops 3221225472 | bytes 2097152 | tf_op jit(solution)/shard_map/filter_rows/pallas_call | solution.py:461
  91.5 0.0 copy-start.2
  91.5 7.1 %all-to-all-start.2 = ((bf16[128,8,512]{2,1,0:T(8,128)(2,1)}), bf16[128,8,512]{2,1,0:T(8,128)(2,1)S(1)}, u32[]{:S(2)}, u32[]{:S(2)}) async-start(bf16[128,8,512]{2,1,0:T(8,128)(2,1)} %bitcast.20), calls=%async_computation.2 | async-start | bytes 2097152 | tf_op jit(solution)/shard_map/all_to_all | solution.py:512
  98.7 0.6 copy.6
  99.4 3.8 %collective-permute-start.3 = (bf16[34,256]{1,0:T(8,128)(2,1)S(1)}, bf16[34,256]{1,0:T(8,128)(2,1)S(1)}, u32[]{:S(2)}, u32[]{:S(2)}) collective-permute-start(bf16[34,256]{1,0:T(8,128)(2,1)S(1)} %pad_maximum_fusion.1), channel_id=1, source_target_pairs={{1,0},{2,1},{3,2},{4,3},{5,4},{6,5},{7,6},{8,7},{9,8},{10,9},{11,1... | collective-permute-start | bytes 52232 | tf_op jit(solution)/shard_map/ppermute | solution.py:499
  103.1 2.1 %collective-permute-start.2 = (bf16[34,256]{1,0:T(8,128)(2,1)S(1)}, bf16[34,256]{1,0:T(8,128)(2,1)S(1)}, u32[]{:S(2)}, u32[]{:S(2)}) collective-permute-start(bf16[34,256]{1,0:T(8,128)(2,1)S(1)} %pad_maximum_fusion), channel_id=1, source_target_pairs={{0,1},{1,2},{2,3},{3,4},{4,5},{5,6},{6,7},{7,8},{8,9},{9,10},{10,1... | collective-permute-start | bytes 52232 | tf_op jit(solution)/shard_map/ppermute | solution.py:498
  105.2 1.1 backward_columns_phases.1.table_ref
  106.4 15.1 %collective-permute-done.3.right_ref = bf16[34,256]{1,0:T(8,128)(2,1)S(1)} collective-permute-done((bf16[34,256]{1,0:T(8,128)(2,1)S(1)}, bf16[34,256]{1,0:T(8,128)(2,1)S(1)}, u32[]{:S(2)}, u32[]{:S(2)}) %collective-permute-start.3) | collective-permute-done | bytes 17440 | tf_op jit(solution)/shard_map/ppermute | solution.py:499
  121.5 0.6 collective-permute-done.2.left_ref
  122.1 7.0 %all-to-all-done.2 = bf16[128,8,512]{2,1,0:T(8,128)(2,1)S(1)} async-done(((bf16[128,8,512]{2,1,0:T(8,128)(2,1)}), bf16[128,8,512]{2,1,0:T(8,128)(2,1)S(1)}, u32[]{:S(2)}, u32[]{:S(2)}) %all-to-all-start.2) | async-done | bytes 1048608 | tf_op jit(solution)/shard_map/all_to_all | solution.py:512
  129.1 2.0 %along_columns.3 = bf16[1024,512]{1,0:T(8,128)(2,1)} custom-call(bf16[1024,1024]{1,0:T(8,128)(2,1)S(1)} %backward_columns_phases.1.table_ref, bf16[1024,512]{1,0:T(8,128)(2,1)S(1)} %bitcast.15), custom_call_target="tpu_custom_call" | custom-call | flops 1073741824 | bytes 2097152 | tf_op jit(solution)/shard_map/along_columns/pallas_call | solution.py:313
  131.1 0.0 copy-start.7
  131.1 6.3 %all-to-all-start.3 = ((bf16[16,64,512]{2,1,0:T(8,128)(2,1)}), bf16[16,64,512]{2,1,0:T(8,128)(2,1)S(1)}, u32[]{:S(2)}, u32[]{:S(2)}) async-start(bf16[16,64,512]{2,1,0:T(8,128)(2,1)} %bitcast.19), calls=%async_computation.3 | async-start | bytes 2097152 | tf_op jit(solution)/shard_map/all_to_all | solution.py:521
  137.4 0.6 reshape.31.taps_ref
  138.0 4.1 %stencil.1.base_ref = f32[32,64,256]{2,1,0:T(8,128)S(1)} custom-call(bf16[32,64,256]{2,1,0:T(8,128)(2,1)} %x_ref.3, bf16[32,64,256]{2,1,0:T(8,128)(2,1)} %home_norm.1.normed_ref, bf16[64,256]{1,0:T(8,128)(2,1)} %copy-done.3, bf16[64,256]{1,0:T(8,128)(2,1)} %copy-done.4, bf16[34,256]{1,0:T(8,128)(2,1)} %copy-done.6, bf16[34,256]{1,0:T(8,128)(2,1)} %copy-done.5, ...), custom_call_target="tpu_custom_call" | custom-call | flops 16777216 | bytes 4194304 | tf_op jit(solution)/shard_map/stencil/pallas_call | solution.py:361
  142.1 20.3 %all-to-all-done.3.home_ref = bf16[16,64,512]{2,1,0:T(8,128)(2,1)S(1)} async-done(((bf16[16,64,512]{2,1,0:T(8,128)(2,1)}), bf16[16,64,512]{2,1,0:T(8,128)(2,1)S(1)}, u32[]{:S(2)}, u32[]{:S(2)}) %all-to-all-start.3) | async-done | bytes 1048608 | tf_op jit(solution)/shard_map/all_to_all | solution.py:521
  162.3 1.9 %unpack_add.1 = bf16[32,64,256]{2,1,0:T(8,128)(2,1)} custom-call(f32[32,64,256]{2,1,0:T(8,128)S(1)} %stencil.1.base_ref, bf16[16,64,512]{2,1,0:T(8,128)(2,1)S(1)} %all-to-all-done.3.home_ref), custom_call_target="tpu_custom_call" | custom-call | tf_op jit(solution)/shard_map/unpack_add/pallas_call | solution.py:274
  (19 shorter events, 0.1 us)
Async XLA Ops:
  3.9 33.5 %all-to-all-start = ((bf16[16,64,512]{2,1,0:T(8,128)(2,1)}), bf16[16,64,512]{2,1,0:T(8,128)(2,1)S(1)}, u32[]{:S(2)}, u32[]{:S(2)}) async-start(bf16[16,64,512]{2,1,0:T(8,128)(2,1)} %norm_pack.1), calls=%async_computation | async-start | bytes 2097152 | tf_op jit(solution)/shard_map/all_to_all | solution.py:488
  39.5 27.4 %copy-start = (bf16[2,4,64,64]{3,2,1,0:T(8,128)(2,1)S(1)}, bf16[2,4,64,64]{3,2,1,0:T(8,128)(2,1)}, u32[]{:S(2)}) copy-start(bf16[2,4,64,64]{3,2,1,0:T(8,128)(2,1)} %first_w.1) | copy-start | bytes 196612
  39.5 27.4 %copy-start.1 = (bf16[2,4,64,64]{3,2,1,0:T(8,128)(2,1)S(1)}, bf16[2,4,64,64]{3,2,1,0:T(8,128)(2,1)}, u32[]{:S(2)}) copy-start(bf16[2,4,64,64]{3,2,1,0:T(8,128)(2,1)} %second_w.1) | copy-start | bytes 196612
  39.5 46.2 %all-to-all-start.1 = ((bf16[128,8,512]{2,1,0:T(8,128)(2,1)}), bf16[128,8,512]{2,1,0:T(8,128)(2,1)S(1)}, u32[]{:S(2)}, u32[]{:S(2)}) async-start(bf16[128,8,512]{2,1,0:T(8,128)(2,1)} %bitcast.18), calls=%async_computation.1 | async-start | bytes 2097152 | tf_op jit(solution)/shard_map/all_to_all | solution.py:506
  55.2 30.5 %collective-permute-start = (bf16[64,256]{1,0:T(8,128)(2,1)S(1)}, bf16[64,256]{1,0:T(8,128)(2,1)S(1)}, u32[]{:S(2)}, u32[]{:S(2)}) collective-permute-start(bf16[64,256]{1,0:T(8,128)(2,1)S(1)} %get-tuple-element.50), channel_id=1, source_target_pairs={{0,16},{16,32},{32,48},{48,64},{64,80},{80,96},{96,112},{112,128},... | collective-permute-start | bytes 98312 | tf_op jit(solution)/shard_map/ppermute | solution.py:498
  57.3 28.4 %collective-permute-start.1 = (bf16[64,256]{1,0:T(8,128)(2,1)S(1)}, bf16[64,256]{1,0:T(8,128)(2,1)S(1)}, u32[]{:S(2)}, u32[]{:S(2)}) collective-permute-start(bf16[64,256]{1,0:T(8,128)(2,1)S(1)} %get-tuple-element.49), channel_id=1, source_target_pairs={{16,0},{32,16},{48,32},{64,48},{80,64},{96,80},{112,96},{128,112},... | collective-permute-start | bytes 98312 | tf_op jit(solution)/shard_map/ppermute | solution.py:499
  85.7 13.6 %copy-start.3 = (bf16[64,256]{1,0:T(8,128)(2,1)}, bf16[64,256]{1,0:T(8,128)(2,1)S(1)}, u32[]{:S(2)}) copy-start(bf16[64,256]{1,0:T(8,128)(2,1)S(1)} %collective-permute-done.top_ref) | copy-start | bytes 98308
  85.7 13.6 %copy-start.4 = (bf16[64,256]{1,0:T(8,128)(2,1)}, bf16[64,256]{1,0:T(8,128)(2,1)S(1)}, u32[]{:S(2)}) copy-start(bf16[64,256]{1,0:T(8,128)(2,1)S(1)} %collective-permute-done.1.bottom_ref) | copy-start | bytes 98308
  91.5 7.2 %copy-start.2 = (bf16[32,64,256]{2,1,0:T(8,128)(2,1)S(1)}, bf16[32,64,256]{2,1,0:T(8,128)(2,1)}, u32[]{:S(2)}) copy-start(bf16[32,64,256]{2,1,0:T(8,128)(2,1)} %home_norm.1.normed_ref) | copy-start | bytes 3145732
  91.5 37.5 %all-to-all-start.2 = ((bf16[128,8,512]{2,1,0:T(8,128)(2,1)}), bf16[128,8,512]{2,1,0:T(8,128)(2,1)S(1)}, u32[]{:S(2)}, u32[]{:S(2)}) async-start(bf16[128,8,512]{2,1,0:T(8,128)(2,1)} %bitcast.20), calls=%async_computation.2 | async-start | bytes 2097152 | tf_op jit(solution)/shard_map/all_to_all | solution.py:512
  99.4 22.2 %collective-permute-start.3 = (bf16[34,256]{1,0:T(8,128)(2,1)S(1)}, bf16[34,256]{1,0:T(8,128)(2,1)S(1)}, u32[]{:S(2)}, u32[]{:S(2)}) collective-permute-start(bf16[34,256]{1,0:T(8,128)(2,1)S(1)} %pad_maximum_fusion.1), channel_id=1, source_target_pairs={{1,0},{2,1},{3,2},{4,3},{5,4},{6,5},{7,6},{8,7},{9,8},{10,9},{11,1... | collective-permute-start | bytes 52232 | tf_op jit(solution)/shard_map/ppermute | solution.py:499
  103.1 19.0 %collective-permute-start.2 = (bf16[34,256]{1,0:T(8,128)(2,1)S(1)}, bf16[34,256]{1,0:T(8,128)(2,1)S(1)}, u32[]{:S(2)}, u32[]{:S(2)}) collective-permute-start(bf16[34,256]{1,0:T(8,128)(2,1)S(1)} %pad_maximum_fusion), channel_id=1, source_target_pairs={{0,1},{1,2},{2,3},{3,4},{4,5},{5,6},{6,7},{7,8},{8,9},{9,10},{10,1... | collective-permute-start | bytes 52232 | tf_op jit(solution)/shard_map/ppermute | solution.py:498
  121.5 9.6 %copy-start.5 = (bf16[34,256]{1,0:T(8,128)(2,1)}, bf16[34,256]{1,0:T(8,128)(2,1)S(1)}, u32[]{:S(2)}) copy-start(bf16[34,256]{1,0:T(8,128)(2,1)S(1)} %collective-permute-done.3.right_ref) | copy-start | bytes 52228
  122.1 9.0 %copy-start.6 = (bf16[34,256]{1,0:T(8,128)(2,1)}, bf16[34,256]{1,0:T(8,128)(2,1)S(1)}, u32[]{:S(2)}) copy-start(bf16[34,256]{1,0:T(8,128)(2,1)S(1)} %collective-permute-done.2.left_ref) | copy-start | bytes 52228
  131.1 6.3 %copy-start.7 = (f32[3,3,256]{2,1,0:T(4,128)S(1)}, f32[3,3,256]{2,1,0:T(4,128)}, u32[]{:S(2)}) copy-start(f32[3,3,256]{2,1,0:T(4,128)} %param.9) | copy-start | bytes 27652
  131.1 31.2 %all-to-all-start.3 = ((bf16[16,64,512]{2,1,0:T(8,128)(2,1)}), bf16[16,64,512]{2,1,0:T(8,128)(2,1)S(1)}, u32[]{:S(2)}, u32[]{:S(2)}) async-start(bf16[16,64,512]{2,1,0:T(8,128)(2,1)} %bitcast.19), calls=%async_computation.3 | async-start | bytes 2097152 | tf_op jit(solution)/shard_map/all_to_all | solution.py:521

commit v7 on v6

--- a/solution.py
+++ b/solution.py
@@ -331,10 +331,13 @@
 
     @pl.when(pl.program_id(0) == 0)
     def _():
-        rows[0], rows[33] = top_ref[...], bottom_ref[...]
+        rows[0], rows[33] = top_ref[:64, :], bottom_ref[:64, :]
         rows[1:33] = normed_ref[...]
+        above, below = top_ref[64:66, :].astype(F32), bottom_ref[64:66, :].astype(F32)
         for rim_ref, sum_ref, j in ((left_ref, left_sum, 0), (right_ref, right_sum, 2)):
-            side[...] = rim_ref[...].astype(F32)
+            corner = slice(j // 2, j // 2 + 1)
+            side[0:1, :], side[33:34, :] = above[corner], below[corner]
+            side[1:33, :] = rim_ref[...].astype(F32)
             sum_ref[...] = side[0:32] * tap(0, j) + side[1:33] * tap(1, j) + side[2:34] * tap(2, j)
 
     column = iota((64, 256), 0)
@@ -356,8 +359,8 @@
 
 def stencil(x, normed, top, bottom, left, right, taps):
     block = pl.BlockSpec((8, 64, 256), lambda g: (g, 0, 0))
-    row = pl.BlockSpec((64, 256), lambda g: (0, 0))
-    side = pl.BlockSpec((34, 256), lambda g: (0, 0))
+    row = pl.BlockSpec((66, 256), lambda g: (0, 0))
+    side = pl.BlockSpec((32, 256), lambda g: (0, 0))
     return pl.pallas_call(
         stencil_kernel,
         grid=(4,),
@@ -504,20 +507,17 @@
 
     freqs = columns(fwd_w, lines)
     whole = lax.all_to_all(freqs.reshape(128, 8, 512), ("row", "yl"), 0, 0, tiled=True)
-    top, bottom = neighbours(normed[0], normed[31], "row")
-    whole, top, bottom = lax.optimization_barrier((whole, top, bottom))
+    left, right = neighbours(normed[:, 0], normed[:, 63], ("yl", "x"))
+    whole, left, right = lax.optimization_barrier((whole, left, right))
 
     filtered = middle(whole.reshape(1024, 512), fwd_h, cos, sin, first, second, last, inv_h)
-    filtered, top, bottom, normed = lax.optimization_barrier((filtered, top, bottom, normed))
+    filtered, left, right, normed = lax.optimization_barrier((filtered, left, right, normed))
     back = lax.all_to_all(filtered.reshape(128, 8, 512), ("row", "yl"), 0, 0, tiled=True)
-    sides = [
-        jnp.concatenate([top[w : w + 1], normed[:, w], bottom[w : w + 1]], axis=0) for w in (0, 63)
-    ]
-    left, right = neighbours(sides[0], sides[1], ("yl", "x"))
-    back, left, right = lax.optimization_barrier((back, left, right))
+    wide = [jnp.concatenate([normed[h], left[h : h + 1], right[h : h + 1]], axis=0) for h in (0, 31)]
+    top, bottom = neighbours(wide[0], wide[1], "row")
 
     spectral = columns(inv_w, back.reshape(1024, 512))
-    spectral, left, right = lax.optimization_barrier((spectral, left, right))
+    spectral, top, bottom = lax.optimization_barrier((spectral, top, bottom))
     home = lax.all_to_all(spectral.reshape(16, 64, 512), ("yl", "x"), 0, 0, tiled=True)
     base = stencil(patches, normed, top, bottom, left, right, depth_kernel.reshape(9, 256))
     return unpack_and_add(base, home)

time: 165 us -> 166 us (level)
  starting transfers between devices: 55.1 us -> 58.1 us
  waiting for transfers between devices: 74.7 us -> 72.4 us
    ppermute x2, waiting for transfers between devices: 15.2 us -> 0.01 us  [neighbours(): after = lax.ppermute(first, axis, [((i + 1) % n, i) for i in range(n)])]
    all_to_all x1, waiting for transfers between devices: 6.96 us -> 17.5 us  [local(): lax.all_to_all(filtered.reshape(128, 8, 512), ('row', 'yl'), 0, 0, tiled=...]
    all_to_all x1, waiting for transfers between devices: 0.01 us -> 7.08 us  [local(): lax.all_to_all(freqs.reshape(128, 8, 512), ('row', 'yl'), 0, 0, tiled=True)]
    ppermute x2, waiting for transfers between devices: 13.4 us -> 8.59 us  [neighbours(): before = lax.ppermute(last, axis, [(i, (i + 1) % n) for i in range(n)])]
  transfers between devices with their start and end apart: 8 -> 8, of which waited for: 6 -> 5; matrix products, arithmetic and copies ran while one was open for 1% -> 1% of each run, Pallas kernels for 10% -> 11%
where the time goes in v7:
time: 166 us; the launch traced here: 165 us
  waiting for transfers between devices  72.4 us (44%)
  starting transfers between devices  58.1 us (35%)
  Pallas kernels  32.2 us (19%)
  local copies, waits for them, and re-layouts  2.03 us (1%)
    all_to_all x1, waiting for transfers between devices, local(): lax.all_to_all(spectral.reshape(16, 64, 512), ('yl', 'x'), 0, 0, tiled=True)  20.2 us
    all_to_all x1, waiting for transfers between devices, local(): lax.all_to_all(packed, ('yl', 'x'), 0, 0, tiled=True).reshape(1024, 512)  18.9 us
    all_to_all x1, waiting for transfers between devices, local(): lax.all_to_all(filtered.reshape(128, 8, 512), ('row', 'yl'), 0, 0, tiled=...  17.5 us
    all_to_all x1, starting transfers between devices, local(): lax.all_to_all(freqs.reshape(128, 8, 512), ('row', 'yl'), 0, 0, tiled=True)  15 us
    ppermute x2, starting transfers between devices, neighbours(): after = lax.ppermute(first, axis, [((i + 1) % n, i) for i in range(n)])  14.4 us
    all_to_all x1, starting transfers between devices, local(): lax.all_to_all(packed, ('yl', 'x'), 0, 0, tiled=True).reshape(1024, 512)  9.3 us
    ppermute x2, waiting for transfers between devices, neighbours(): before = lax.ppermute(last, axis, [(i, (i + 1) % n) for i in range(n)])  8.59 us
    all_to_all x1, starting transfers between devices, local(): lax.all_to_all(filtered.reshape(128, 8, 512), ('row', 'yl'), 0, 0, tiled=...  8.19 us
  transfers between devices with their start and end apart: 8, of which 5 were waited for; matrix products, arithmetic and copies ran while one was open for 1% of the time, Pallas kernels for 11%

profile of v7, /device:TPU:8, one launch (start us, length us, event | category | flops | bytes accessed | tf_op | source)
XLA Modules:
  0.0 165.0 jit_solution(13147981757153892871)
XLA Ops:
  0.0 3.9 %norm_pack.1 = bf16[16,64,512]{2,1,0:T(8,128)(2,1)} custom-call(bf16[32,64,256]{2,1,0:T(8,128)(2,1)} %x_ref.3, f32[1,256]{1,0:T(1,128)} %bitcast.21), custom_call_target="tpu_custom_call" | custom-call | tf_op jit(solution)/shard_map/norm_pack/pallas_call | solution.py:243
  3.9 9.3 %all-to-all-start = ((bf16[16,64,512]{2,1,0:T(8,128)(2,1)}), bf16[16,64,512]{2,1,0:T(8,128)(2,1)S(1)}, u32[]{:S(2)}, u32[]{:S(2)}) async-start(bf16[16,64,512]{2,1,0:T(8,128)(2,1)} %norm_pack.1), calls=%async_computation | async-start | bytes 2097152 | tf_op jit(solution)/shard_map/all_to_all | solution.py:491
  13.2 1.1 forward_columns_phases.1.table_ref
  14.4 4.2 %home_norm.1.normed_ref = bf16[32,64,256]{2,1,0:T(8,128)(2,1)} custom-call(bf16[32,64,256]{2,1,0:T(8,128)(2,1)} %x_ref.3, f32[1,256]{1,0:T(1,128)} %bitcast.22), custom_call_target="tpu_custom_call" | custom-call | flops 16777216 | bytes 2097152 | tf_op jit(solution)/shard_map/home_norm/pallas_call | solution.py:230
  18.5 18.9 %all-to-all-done = bf16[16,64,512]{2,1,0:T(8,128)(2,1)S(1)} async-done(((bf16[16,64,512]{2,1,0:T(8,128)(2,1)}), bf16[16,64,512]{2,1,0:T(8,128)(2,1)S(1)}, u32[]{:S(2)}, u32[]{:S(2)}) %all-to-all-start) | async-done | bytes 1048608 | tf_op jit(solution)/shard_map/all_to_all | solution.py:491
  37.5 2.0 %along_columns.2 = bf16[1024,512]{1,0:T(8,128)(2,1)} custom-call(bf16[1024,1024]{1,0:T(8,128)(2,1)S(1)} %forward_columns_phases.1.table_ref, bf16[1024,512]{1,0:T(8,128)(2,1)S(1)} %bitcast.16), custom_call_target="tpu_custom_call" | custom-call | flops 1073741824 | bytes 2097152 | tf_op jit(solution)/shard_map/along_columns/pallas_call | solution.py:313
  39.5 0.0 copy-start.2
  39.5 0.0 copy-start
  39.5 0.0 copy-start.1
  39.5 15.0 %all-to-all-start.1 = ((bf16[128,8,512]{2,1,0:T(8,128)(2,1)}), bf16[128,8,512]{2,1,0:T(8,128)(2,1)S(1)}, u32[]{:S(2)}, u32[]{:S(2)}) async-start(bf16[128,8,512]{2,1,0:T(8,128)(2,1)} %bitcast.18), calls=%async_computation.1 | async-start | bytes 2097152 | tf_op jit(solution)/shard_map/all_to_all | solution.py:509
  54.5 0.6 copy.6
  55.1 2.5 %collective-permute-start = (bf16[32,256]{1,0:T(8,128)(2,1)S(1)}, bf16[32,256]{1,0:T(8,128)(2,1)S(1)}, u32[]{:S(2)}, u32[]{:S(2)}) collective-permute-start(bf16[32,256]{1,0:T(8,128)(2,1)S(1)} %get-tuple-element.44), channel_id=1, source_target_pairs={{0,1},{1,2},{2,3},{3,4},{4,5},{5,6},{6,7},{7,8},{8,9},{9,10},{10,1... | collective-permute-start | bytes 49160 | tf_op jit(solution)/shard_map/ppermute | solution.py:501
  57.6 5.5 %collective-permute-start.1 = (bf16[32,256]{1,0:T(8,128)(2,1)S(1)}, bf16[32,256]{1,0:T(8,128)(2,1)S(1)}, u32[]{:S(2)}, u32[]{:S(2)}) collective-permute-start(bf16[32,256]{1,0:T(8,128)(2,1)S(1)} %get-tuple-element.43), channel_id=1, source_target_pairs={{1,0},{2,1},{3,2},{4,3},{5,4},{6,5},{7,6},{8,7},{9,8},{10,9},{11,1... | collective-permute-start | bytes 49160 | tf_op jit(solution)/shard_map/ppermute | solution.py:502
  63.1 1.2 block_tables.1
  64.3 2.6 %backward_rows_phases.1.refs_1_.inv_any = bf16[1024,1024]{1,0:T(8,128)(2,1)} custom-call(), custom_call_target="tpu_custom_call" | custom-call | flops 8388608 | bytes 2097152 | tf_op jit(solution)/shard_map/backward_rows_phases/pallas_call | solution.py:109
  66.9 2.3 %forward_rows_phases.1 = (bf16[1024,1024]{1,0:T(8,128)(2,1)S(1)}, f32[128,512]{1,0:T(8,128)}, f32[128,512]{1,0:T(8,128)}) custom-call(bf16[256,256]{1,0:T(8,128)(2,1)} %get-tuple-element.26.refs_0_.second_any, bf16[1024,1024]{1,0:T(8,128)(2,1)} %backward_rows_phases.1.refs_1_.inv_any), custom_call_target="tpu_custom_call" | custom-call | flops 8388608 | bytes 2097152 | tf_op jit(solution)/shard_map/forward_rows_phases/pallas_call | solution.py:109
  69.2 8.6 %collective-permute-done.left_ref = bf16[32,256]{1,0:T(8,128)(2,1)S(1)} collective-permute-done((bf16[32,256]{1,0:T(8,128)(2,1)S(1)}, bf16[32,256]{1,0:T(8,128)(2,1)S(1)}, u32[]{:S(2)}, u32[]{:S(2)}) %collective-permute-start) | collective-permute-done | bytes 16416 | tf_op jit(solution)/shard_map/ppermute | solution.py:501
  77.8 7.1 %all-to-all-done.1 = bf16[128,8,512]{2,1,0:T(8,128)(2,1)S(1)} async-done(((bf16[128,8,512]{2,1,0:T(8,128)(2,1)}), bf16[128,8,512]{2,1,0:T(8,128)(2,1)S(1)}, u32[]{:S(2)}, u32[]{:S(2)}) %all-to-all-start.1) | async-done | bytes 1048608 | tf_op jit(solution)/shard_map/all_to_all | solution.py:509
  84.9 5.8 %filter_rows.1 = bf16[1024,512]{1,0:T(8,128)(2,1)} custom-call(bf16[1024,512]{1,0:T(8,128)(2,1)S(1)} %bitcast.17, bf16[1024,1024]{1,0:T(8,128)(2,1)S(1)} %get-tuple-element.27.fwd, f32[128,512]{1,0:T(8,128)} %get-tuple-element.28.cos_any, f32[128,512]{1,0:T(8,128)} %get-tuple-element.29.sin_any, bf16[1024,256]{1,0:T(8,128)(2,1)} %get-tuple-element.30.first_any, ...), custom_call_target="tpu_custom_call" | custom-call | flops 3221225472 | bytes 2097152 | tf_op jit(solution)/shard_map/filter_rows/pallas_call | solution.py:464
  90.6 8.2 %all-to-all-start.2 = ((bf16[128,8,512]{2,1,0:T(8,128)(2,1)}), bf16[128,8,512]{2,1,0:T(8,128)(2,1)S(1)}, u32[]{:S(2)}, u32[]{:S(2)}) async-start(bf16[128,8,512]{2,1,0:T(8,128)(2,1)} %bitcast.20), calls=%async_computation.2 | async-start | bytes 2097152 | tf_op jit(solution)/shard_map/all_to_all | solution.py:515
  98.8 1.1 backward_columns_phases.1.table_ref
  100.0 0.8 slice_bitcast_fusion
  100.8 9.0 %collective-permute-start.3 = (bf16[66,256]{1,0:T(8,128)(2,1)S(1)}, bf16[66,256]{1,0:T(8,128)(2,1)S(1)}, u32[]{:S(2)}, u32[]{:S(2)}) collective-permute-start(bf16[66,256]{1,0:T(8,128)(2,1)S(1)} %pad_maximum_fusion.1), channel_id=1, source_target_pairs={{16,0},{32,16},{48,32},{64,48},{80,64},{96,80},{112,96},{128,112},... | collective-permute-start | bytes 101384 | tf_op jit(solution)/shard_map/ppermute | solution.py:502
  109.8 1.9 %collective-permute-start.2 = (bf16[66,256]{1,0:T(8,128)(2,1)S(1)}, bf16[66,256]{1,0:T(8,128)(2,1)S(1)}, u32[]{:S(2)}, u32[]{:S(2)}) collective-permute-start(bf16[66,256]{1,0:T(8,128)(2,1)S(1)} %pad_maximum_fusion), channel_id=1, source_target_pairs={{0,16},{16,32},{32,48},{48,64},{64,80},{80,96},{96,112},{112,128},... | collective-permute-start | bytes 101384 | tf_op jit(solution)/shard_map/ppermute | solution.py:501
  111.7 17.5 %all-to-all-done.2 = bf16[128,8,512]{2,1,0:T(8,128)(2,1)S(1)} async-done(((bf16[128,8,512]{2,1,0:T(8,128)(2,1)}), bf16[128,8,512]{2,1,0:T(8,128)(2,1)S(1)}, u32[]{:S(2)}, u32[]{:S(2)}) %all-to-all-start.2) | async-done | bytes 1048608 | tf_op jit(solution)/shard_map/all_to_all | solution.py:515
  129.2 2.0 %along_columns.3 = bf16[1024,512]{1,0:T(8,128)(2,1)} custom-call(bf16[1024,1024]{1,0:T(8,128)(2,1)S(1)} %backward_columns_phases.1.table_ref, bf16[1024,512]{1,0:T(8,128)(2,1)S(1)} %bitcast.15), custom_call_target="tpu_custom_call" | custom-call | flops 1073741824 | bytes 2097152 | tf_op jit(solution)/shard_map/along_columns/pallas_call | solution.py:313
  131.2 0.0 copy-start.7
  131.3 6.8 %all-to-all-start.3 = ((bf16[16,64,512]{2,1,0:T(8,128)(2,1)}), bf16[16,64,512]{2,1,0:T(8,128)(2,1)S(1)}, u32[]{:S(2)}, u32[]{:S(2)}) async-start(bf16[16,64,512]{2,1,0:T(8,128)(2,1)} %bitcast.19), calls=%async_computation.3 | async-start | bytes 2097152 | tf_op jit(solution)/shard_map/all_to_all | solution.py:521
  138.1 0.6 reshape.31.taps_ref
  138.8 4.1 %stencil.1.base_ref = f32[32,64,256]{2,1,0:T(8,128)S(1)} custom-call(bf16[32,64,256]{2,1,0:T(8,128)(2,1)} %x_ref.3, bf16[32,64,256]{2,1,0:T(8,128)(2,1)} %home_norm.1.normed_ref, bf16[66,256]{1,0:T(8,128)(2,1)} %copy-done.4, bf16[66,256]{1,0:T(8,128)(2,1)} %copy-done.3, bf16[32,256]{1,0:T(8,128)(2,1)} %copy-done.5, bf16[32,256]{1,0:T(8,128)(2,1)} %copy-done.6, ...), custom_call_target="tpu_custom_call" | custom-call | flops 16777216 | bytes 4194304 | tf_op jit(solution)/shard_map/stencil/pallas_call | solution.py:364
  142.8 20.2 %all-to-all-done.3.home_ref = bf16[16,64,512]{2,1,0:T(8,128)(2,1)S(1)} async-done(((bf16[16,64,512]{2,1,0:T(8,128)(2,1)}), bf16[16,64,512]{2,1,0:T(8,128)(2,1)S(1)}, u32[]{:S(2)}, u32[]{:S(2)}) %all-to-all-start.3) | async-done | bytes 1048608 | tf_op jit(solution)/shard_map/all_to_all | solution.py:521
  163.1 1.9 %unpack_add.1 = bf16[32,64,256]{2,1,0:T(8,128)(2,1)} custom-call(f32[32,64,256]{2,1,0:T(8,128)S(1)} %stencil.1.base_ref, bf16[16,64,512]{2,1,0:T(8,128)(2,1)S(1)} %all-to-all-done.3.home_ref), custom_call_target="tpu_custom_call" | custom-call | tf_op jit(solution)/shard_map/unpack_add/pallas_call | solution.py:274
  (19 shorter events, 0.1 us)
Async XLA Ops:
  3.9 33.5 %all-to-all-start = ((bf16[16,64,512]{2,1,0:T(8,128)(2,1)}), bf16[16,64,512]{2,1,0:T(8,128)(2,1)S(1)}, u32[]{:S(2)}, u32[]{:S(2)}) async-start(bf16[16,64,512]{2,1,0:T(8,128)(2,1)} %norm_pack.1), calls=%async_computation | async-start | bytes 2097152 | tf_op jit(solution)/shard_map/all_to_all | solution.py:491
  39.5 15.0 %copy-start.2 = (bf16[32,64,256]{2,1,0:T(8,128)(2,1)S(1)}, bf16[32,64,256]{2,1,0:T(8,128)(2,1)}, u32[]{:S(2)}) copy-start(bf16[32,64,256]{2,1,0:T(8,128)(2,1)} %home_norm.1.normed_ref) | copy-start | bytes 3145732
  39.5 23.6 %copy-start = (bf16[2,4,64,64]{3,2,1,0:T(8,128)(2,1)S(1)}, bf16[2,4,64,64]{3,2,1,0:T(8,128)(2,1)}, u32[]{:S(2)}) copy-start(bf16[2,4,64,64]{3,2,1,0:T(8,128)(2,1)} %first_w.1) | copy-start | bytes 196612
  39.5 23.6 %copy-start.1 = (bf16[2,4,64,64]{3,2,1,0:T(8,128)(2,1)S(1)}, bf16[2,4,64,64]{3,2,1,0:T(8,128)(2,1)}, u32[]{:S(2)}) copy-start(bf16[2,4,64,64]{3,2,1,0:T(8,128)(2,1)} %second_w.1) | copy-start | bytes 196612
  39.5 45.4 %all-to-all-start.1 = ((bf16[128,8,512]{2,1,0:T(8,128)(2,1)}), bf16[128,8,512]{2,1,0:T(8,128)(2,1)S(1)}, u32[]{:S(2)}, u32[]{:S(2)}) async-start(bf16[128,8,512]{2,1,0:T(8,128)(2,1)} %bitcast.18), calls=%async_computation.1 | async-start | bytes 2097152 | tf_op jit(solution)/shard_map/all_to_all | solution.py:509
  55.1 22.7 %collective-permute-start = (bf16[32,256]{1,0:T(8,128)(2,1)S(1)}, bf16[32,256]{1,0:T(8,128)(2,1)S(1)}, u32[]{:S(2)}, u32[]{:S(2)}) collective-permute-start(bf16[32,256]{1,0:T(8,128)(2,1)S(1)} %get-tuple-element.44), channel_id=1, source_target_pairs={{0,1},{1,2},{2,3},{3,4},{4,5},{5,6},{6,7},{7,8},{8,9},{9,10},{10,1... | collective-permute-start | bytes 49160 | tf_op jit(solution)/shard_map/ppermute | solution.py:501
  57.6 20.2 %collective-permute-start.1 = (bf16[32,256]{1,0:T(8,128)(2,1)S(1)}, bf16[32,256]{1,0:T(8,128)(2,1)S(1)}, u32[]{:S(2)}, u32[]{:S(2)}) collective-permute-start(bf16[32,256]{1,0:T(8,128)(2,1)S(1)} %get-tuple-element.43), channel_id=1, source_target_pairs={{1,0},{2,1},{3,2},{4,3},{5,4},{6,5},{7,6},{8,7},{9,8},{10,9},{11,1... | collective-permute-start | bytes 49160 | tf_op jit(solution)/shard_map/ppermute | solution.py:502
  77.8 22.2 %copy-start.5 = (bf16[32,256]{1,0:T(8,128)(2,1)}, bf16[32,256]{1,0:T(8,128)(2,1)S(1)}, u32[]{:S(2)}) copy-start(bf16[32,256]{1,0:T(8,128)(2,1)S(1)} %collective-permute-done.left_ref) | copy-start | bytes 49156
  77.8 22.2 %copy-start.6 = (bf16[32,256]{1,0:T(8,128)(2,1)}, bf16[32,256]{1,0:T(8,128)(2,1)S(1)}, u32[]{:S(2)}) copy-start(bf16[32,256]{1,0:T(8,128)(2,1)S(1)} %collective-permute-done.1.right_ref) | copy-start | bytes 49156
  90.6 38.6 %all-to-all-start.2 = ((bf16[128,8,512]{2,1,0:T(8,128)(2,1)}), bf16[128,8,512]{2,1,0:T(8,128)(2,1)S(1)}, u32[]{:S(2)}, u32[]{:S(2)}) async-start(bf16[128,8,512]{2,1,0:T(8,128)(2,1)} %bitcast.20), calls=%async_computation.2 | async-start | bytes 2097152 | tf_op jit(solution)/shard_map/all_to_all | solution.py:515
  100.8 30.5 %collective-permute-start.3 = (bf16[66,256]{1,0:T(8,128)(2,1)S(1)}, bf16[66,256]{1,0:T(8,128)(2,1)S(1)}, u32[]{:S(2)}, u32[]{:S(2)}) collective-permute-start(bf16[66,256]{1,0:T(8,128)(2,1)S(1)} %pad_maximum_fusion.1), channel_id=1, source_target_pairs={{16,0},{32,16},{48,32},{64,48},{80,64},{96,80},{112,96},{128,112},... | collective-permute-start | bytes 101384 | tf_op jit(solution)/shard_map/ppermute | solution.py:502
  109.8 21.5 %collective-permute-start.2 = (bf16[66,256]{1,0:T(8,128)(2,1)S(1)}, bf16[66,256]{1,0:T(8,128)(2,1)S(1)}, u32[]{:S(2)}, u32[]{:S(2)}) collective-permute-start(bf16[66,256]{1,0:T(8,128)(2,1)S(1)} %pad_maximum_fusion), channel_id=1, source_target_pairs={{0,16},{16,32},{32,48},{48,64},{64,80},{80,96},{96,112},{112,128},... | collective-permute-start | bytes 101384 | tf_op jit(solution)/shard_map/ppermute | solution.py:501
  131.2 6.9 %copy-start.7 = (f32[3,3,256]{2,1,0:T(4,128)S(1)}, f32[3,3,256]{2,1,0:T(4,128)}, u32[]{:S(2)}) copy-start(f32[3,3,256]{2,1,0:T(4,128)} %param.9) | copy-start | bytes 27652
  131.3 7.5 %copy-start.3 = (bf16[66,256]{1,0:T(8,128)(2,1)}, bf16[66,256]{1,0:T(8,128)(2,1)S(1)}, u32[]{:S(2)}) copy-start(bf16[66,256]{1,0:T(8,128)(2,1)S(1)} %collective-permute-done.3.bottom_ref) | copy-start | bytes 101380
  131.3 7.5 %copy-start.4 = (bf16[66,256]{1,0:T(8,128)(2,1)}, bf16[66,256]{1,0:T(8,128)(2,1)S(1)}, u32[]{:S(2)}) copy-start(bf16[66,256]{1,0:T(8,128)(2,1)S(1)} %collective-permute-done.2.top_ref) | copy-start | bytes 101380
  131.3 31.8 %all-to-all-start.3 = ((bf16[16,64,512]{2,1,0:T(8,128)(2,1)}), bf16[16,64,512]{2,1,0:T(8,128)(2,1)S(1)}, u32[]{:S(2)}, u32[]{:S(2)}) async-start(bf16[16,64,512]{2,1,0:T(8,128)(2,1)} %bitcast.19), calls=%async_computation.3 | async-start | bytes 2097152 | tf_op jit(solution)/shard_map/all_to_all | solution.py:521

commit v8 on v6

--- a/solution.py
+++ b/solution.py
@@ -256,27 +256,33 @@
     )(remaining(patches), remaining(gain.reshape(1, 256)))
 
 
-def final_kernel(base_ref, home_ref, out_ref):
+def final_kernel(base_ref, home_ref, out_any, held, sems):
     low = low_half(64)
-    first, row = 4 * pl.program_id(0), 8 * pl.program_id(0)
-    for t in range(4):
-        lanes = slice(128 * t, 128 * t + 128)
-        for m in range(2):
-            u = home_ref[first + 2 * m, :, lanes].astype(F32)
-            v = home_ref[first + 2 * m + 1, :, lanes].astype(F32)
-            chans = slice(128 * m, 128 * m + 128)
-            even, odd = jnp.where(low, u, swap(v)), jnp.where(low, swap(u), v)
-            out_ref[t, :, chans] = (base_ref[row + t, :, chans] + even).astype(BF16)
-            out_ref[t + 4, :, chans] = (base_ref[row + t + 4, :, chans] + odd).astype(BF16)
+    sends = []
+    for g in range(4):
+        for t in range(4):
+            lanes = slice(128 * t, 128 * t + 128)
+            for m in range(2):
+                u = home_ref[4 * g + 2 * m, :, lanes].astype(F32)
+                v = home_ref[4 * g + 2 * m + 1, :, lanes].astype(F32)
+                chans, row = slice(128 * m, 128 * m + 128), 8 * g + t
+                even, odd = jnp.where(low, u, swap(v)), jnp.where(low, swap(u), v)
+                held[row, :, chans] = (base_ref[row, :, chans] + even).astype(BF16)
+                held[row + 4, :, chans] = (base_ref[row + 4, :, chans] + odd).astype(BF16)
+        rows = slice(8 * g, 8 * g + 8)
+        sends.append(pltpu.make_async_copy(held.at[rows], out_any.at[rows], sems.at[g]))
+        sends[-1].start()
+    for send in sends:
+        send.wait()
 
 
 def unpack_and_add(base, home):
     return pl.pallas_call(
         final_kernel,
-        grid=(4,),
         in_specs=[pl.BlockSpec(memory_space=pltpu.VMEM)] * 2,
-        out_specs=pl.BlockSpec((8, 64, 256), lambda g: (g, 0, 0)),
-        out_shape=jax.ShapeDtypeStruct((32, 64, 256), BF16),
+        out_specs=pl.BlockSpec(memory_space=pltpu.HBM),
+        out_shape=pltpu.HBM((32, 64, 256), BF16),
+        scratch_shapes=[pltpu.VMEM((32, 64, 256), BF16), pltpu.SemaphoreType.DMA((4,))],
         compiler_params=pltpu.CompilerParams(vmem_limit_bytes=8 * MIB),
         name="unpack_add",
     )(resident(base), resident(home))
@@ -500,22 +506,19 @@
         return before, after
 
     normed = home_norm(patches, norm_gain)
-    lines, normed = lax.optimization_barrier((lines, normed))
+    top, bottom = neighbours(normed[0], normed[31], "row")
 
     freqs = columns(fwd_w, lines)
+    freqs, top, bottom, normed = lax.optimization_barrier((freqs, top, bottom, normed))
     whole = lax.all_to_all(freqs.reshape(128, 8, 512), ("row", "yl"), 0, 0, tiled=True)
-    top, bottom = neighbours(normed[0], normed[31], "row")
-    whole, top, bottom = lax.optimization_barrier((whole, top, bottom))
-
-    filtered = middle(whole.reshape(1024, 512), fwd_h, cos, sin, first, second, last, inv_h)
-    filtered, top, bottom, normed = lax.optimization_barrier((filtered, top, bottom, normed))
-    back = lax.all_to_all(filtered.reshape(128, 8, 512), ("row", "yl"), 0, 0, tiled=True)
     sides = [
         jnp.concatenate([top[w : w + 1], normed[:, w], bottom[w : w + 1]], axis=0) for w in (0, 63)
     ]
     left, right = neighbours(sides[0], sides[1], ("yl", "x"))
-    back, left, right = lax.optimization_barrier((back, left, right))
-
+    whole, left, right = lax.optimization_barrier((whole, left, right))
+
+    filtered = middle(whole.reshape(1024, 512), fwd_h, cos, sin, first, second, last, inv_h)
+    back = lax.all_to_all(filtered.reshape(128, 8, 512), ("row", "yl"), 0, 0, tiled=True)
     spectral = columns(inv_w, back.reshape(1024, 512))
     spectral, left, right = lax.optimization_barrier((spectral, left, right))
     home = lax.all_to_all(spectral.reshape(16, 64, 512), ("yl", "x"), 0, 0, tiled=True)

time: 165 us -> 166 us (level)
  starting transfers between devices: 55.1 us -> 57.1 us
    all_to_all x1, waiting for transfers between devices: 6.96 us -> 29.3 us  [local(): lax.all_to_all(filtered.reshape(128, 8, 512), ('row', 'yl'), 0, 0, tiled=...]
    ppermute x2, waiting for transfers between devices: 13.4 us -> 0.61 us  [neighbours(): before = lax.ppermute(last, axis, [(i, (i + 1) % n) for i in range(n)])]
    all_to_all x1, waiting for transfers between devices: 18.9 us -> 6.73 us  [local(): lax.all_to_all(packed, ('yl', 'x'), 0, 0, tiled=True).reshape(1024, 512)]
    all_to_all x1, waiting for transfers between devices: 0.01 us -> 6.96 us  [local(): lax.all_to_all(freqs.reshape(128, 8, 512), ('row', 'yl'), 0, 0, tiled=True)]
    ppermute x2, waiting for transfers between devices: 15.2 us -> 10.1 us  [neighbours(): after = lax.ppermute(first, axis, [((i + 1) % n, i) for i in range(n)])]
  transfers between devices with their start and end apart: 8 -> 8, of which waited for: 6 -> 6; matrix products, arithmetic and copies ran while one was open for 1% -> 1% of each run, Pallas kernels for 10% -> 11%
where the time goes in v8:
time: 166 us; the launch traced here: 165 us
  waiting for transfers between devices  74 us (45%)
  starting transfers between devices  57.1 us (34%)
  Pallas kernels  31.5 us (19%)
  local copies, waits for them, and re-layouts  2.02 us (1%)
    all_to_all x1, waiting for transfers between devices, local(): lax.all_to_all(filtered.reshape(128, 8, 512), ('row', 'yl'), 0, 0, tiled=...  29.3 us
    all_to_all x1, waiting for transfers between devices, local(): lax.all_to_all(spectral.reshape(16, 64, 512), ('yl', 'x'), 0, 0, tiled=True)  20.3 us
    all_to_all x1, starting transfers between devices, local(): lax.all_to_all(freqs.reshape(128, 8, 512), ('row', 'yl'), 0, 0, tiled=True)  15 us
    ppermute x2, starting transfers between devices, neighbours(): after = lax.ppermute(first, axis, [((i + 1) % n, i) for i in range(n)])  14.7 us
    ppermute x2, waiting for transfers between devices, neighbours(): after = lax.ppermute(first, axis, [((i + 1) % n, i) for i in range(n)])  10.1 us
    all_to_all x1, starting transfers between devices, local(): lax.all_to_all(packed, ('yl', 'x'), 0, 0, tiled=True).reshape(1024, 512)  9.3 us
    all_to_all x1, starting transfers between devices, local(): lax.all_to_all(filtered.reshape(128, 8, 512), ('row', 'yl'), 0, 0, tiled=...  8.27 us
    pallas_call x4, Pallas kernels, table(): pl.pallas_call(functools.partial(table_kernel, phases, with_twiddles, sta...  7.16 us
  transfers between devices with their start and end apart: 8, of which 6 were waited for; matrix products, arithmetic and copies ran while one was open for 1% of the time, Pallas kernels for 11%

profile of v8, /device:TPU:8, one launch (start us, length us, event | category | flops | bytes accessed | tf_op | source)
XLA Modules:
  0.0 165.0 jit_solution(14365692217076443712)
XLA Ops:
  0.0 3.9 %norm_pack.1 = bf16[16,64,512]{2,1,0:T(8,128)(2,1)} custom-call(bf16[32,64,256]{2,1,0:T(8,128)(2,1)} %x_ref.3, f32[1,256]{1,0:T(1,128)} %bitcast.21), custom_call_target="tpu_custom_call" | custom-call | tf_op jit(solution)/shard_map/norm_pack/pallas_call | solution.py:243
  3.9 9.3 %all-to-all-start = ((bf16[16,64,512]{2,1,0:T(8,128)(2,1)}), bf16[16,64,512]{2,1,0:T(8,128)(2,1)S(1)}, u32[]{:S(2)}, u32[]{:S(2)}) async-start(bf16[16,64,512]{2,1,0:T(8,128)(2,1)} %norm_pack.1), calls=%async_computation | async-start | bytes 2097152 | tf_op jit(solution)/shard_map/all_to_all | solution.py:494
  13.2 4.2 %home_norm.1.normed_ref = bf16[32,64,256]{2,1,0:T(8,128)(2,1)} custom-call(bf16[32,64,256]{2,1,0:T(8,128)(2,1)} %x_ref.3, f32[1,256]{1,0:T(1,128)} %bitcast.22), custom_call_target="tpu_custom_call" | custom-call | flops 16777216 | bytes 2097152 | tf_op jit(solution)/shard_map/home_norm/pallas_call | solution.py:230
  17.4 0.8 slice_bitcast_fusion
  18.2 1.9 %collective-permute-start = (bf16[64,256]{1,0:T(8,128)(2,1)S(1)}, bf16[64,256]{1,0:T(8,128)(2,1)S(1)}, u32[]{:S(2)}, u32[]{:S(2)}) collective-permute-start(bf16[64,256]{1,0:T(8,128)(2,1)S(1)} %get-tuple-element.40), channel_id=1, source_target_pairs={{0,16},{16,32},{32,48},{48,64},{64,80},{80,96},{96,112},{112,128},... | collective-permute-start | bytes 98312 | tf_op jit(solution)/shard_map/ppermute | solution.py:504
  20.1 10.9 %collective-permute-start.1 = (bf16[64,256]{1,0:T(8,128)(2,1)S(1)}, bf16[64,256]{1,0:T(8,128)(2,1)S(1)}, u32[]{:S(2)}, u32[]{:S(2)}) collective-permute-start(bf16[64,256]{1,0:T(8,128)(2,1)S(1)} %get-tuple-element.39), channel_id=1, source_target_pairs={{16,0},{32,16},{48,32},{64,48},{80,64},{96,80},{112,96},{128,112},... | collective-permute-start | bytes 98312 | tf_op jit(solution)/shard_map/ppermute | solution.py:505
  31.0 1.1 forward_columns_phases.1.table_ref
  32.1 6.7 %all-to-all-done = bf16[16,64,512]{2,1,0:T(8,128)(2,1)S(1)} async-done(((bf16[16,64,512]{2,1,0:T(8,128)(2,1)}), bf16[16,64,512]{2,1,0:T(8,128)(2,1)S(1)}, u32[]{:S(2)}, u32[]{:S(2)}) %all-to-all-start) | async-done | bytes 1048608 | tf_op jit(solution)/shard_map/all_to_all | solution.py:494
  38.9 2.0 %along_columns.2 = bf16[1024,512]{1,0:T(8,128)(2,1)} custom-call(bf16[1024,1024]{1,0:T(8,128)(2,1)S(1)} %forward_columns_phases.1.table_ref, bf16[1024,512]{1,0:T(8,128)(2,1)S(1)} %bitcast.15), custom_call_target="tpu_custom_call" | custom-call | flops 1073741824 | bytes 2097152 | tf_op jit(solution)/shard_map/along_columns/pallas_call | solution.py:319
  40.9 0.0 copy-start.2
  40.9 0.0 copy-start
  40.9 0.0 copy-start.1
  40.9 15.0 %all-to-all-start.1 = ((bf16[128,8,512]{2,1,0:T(8,128)(2,1)}), bf16[128,8,512]{2,1,0:T(8,128)(2,1)S(1)}, u32[]{:S(2)}, u32[]{:S(2)}) async-start(bf16[128,8,512]{2,1,0:T(8,128)(2,1)} %bitcast.18), calls=%async_computation.1 | async-start | bytes 2097152 | tf_op jit(solution)/shard_map/all_to_all | solution.py:513
  55.9 0.6 copy.6
  56.6 3.8 %collective-permute-start.3 = (bf16[34,256]{1,0:T(8,128)(2,1)S(1)}, bf16[34,256]{1,0:T(8,128)(2,1)S(1)}, u32[]{:S(2)}, u32[]{:S(2)}) collective-permute-start(bf16[34,256]{1,0:T(8,128)(2,1)S(1)} %pad_maximum_fusion.1), channel_id=1, source_target_pairs={{1,0},{2,1},{3,2},{4,3},{5,4},{6,5},{7,6},{8,7},{9,8},{10,9},{11,1... | collective-permute-start | bytes 52232 | tf_op jit(solution)/shard_map/ppermute | solution.py:505
  60.4 2.1 %collective-permute-start.2 = (bf16[34,256]{1,0:T(8,128)(2,1)S(1)}, bf16[34,256]{1,0:T(8,128)(2,1)S(1)}, u32[]{:S(2)}, u32[]{:S(2)}) collective-permute-start(bf16[34,256]{1,0:T(8,128)(2,1)S(1)} %pad_maximum_fusion), channel_id=1, source_target_pairs={{0,1},{1,2},{2,3},{3,4},{4,5},{5,6},{6,7},{7,8},{8,9},{9,10},{10,1... | collective-permute-start | bytes 52232 | tf_op jit(solution)/shard_map/ppermute | solution.py:504
  62.5 1.2 block_tables.1
  63.7 2.6 %backward_rows_phases.1.refs_1_.inv_any = bf16[1024,1024]{1,0:T(8,128)(2,1)} custom-call(), custom_call_target="tpu_custom_call" | custom-call | flops 8388608 | bytes 2097152 | tf_op jit(solution)/shard_map/backward_rows_phases/pallas_call | solution.py:109
  66.3 2.3 %forward_rows_phases.1 = (bf16[1024,1024]{1,0:T(8,128)(2,1)S(1)}, f32[128,512]{1,0:T(8,128)}, f32[128,512]{1,0:T(8,128)}) custom-call(bf16[256,256]{1,0:T(8,128)(2,1)} %get-tuple-element.26.refs_0_.second_any, bf16[1024,1024]{1,0:T(8,128)(2,1)} %backward_rows_phases.1.refs_1_.inv_any), custom_call_target="tpu_custom_call" | custom-call | flops 8388608 | bytes 2097152 | tf_op jit(solution)/shard_map/forward_rows_phases/pallas_call | solution.py:109
  68.6 10.1 %collective-permute-done.3.right_ref = bf16[34,256]{1,0:T(8,128)(2,1)S(1)} collective-permute-done((bf16[34,256]{1,0:T(8,128)(2,1)S(1)}, bf16[34,256]{1,0:T(8,128)(2,1)S(1)}, u32[]{:S(2)}, u32[]{:S(2)}) %collective-permute-start.3) | collective-permute-done | bytes 17440 | tf_op jit(solution)/shard_map/ppermute | solution.py:505
  78.8 0.6 collective-permute-done.2.left_ref
  79.4 7.0 %all-to-all-done.1 = bf16[128,8,512]{2,1,0:T(8,128)(2,1)S(1)} async-done(((bf16[128,8,512]{2,1,0:T(8,128)(2,1)}), bf16[128,8,512]{2,1,0:T(8,128)(2,1)S(1)}, u32[]{:S(2)}, u32[]{:S(2)}) %all-to-all-start.1) | async-done | bytes 1048608 | tf_op jit(solution)/shard_map/all_to_all | solution.py:513
  86.3 5.8 %filter_rows.1 = bf16[1024,512]{1,0:T(8,128)(2,1)} custom-call(bf16[1024,512]{1,0:T(8,128)(2,1)S(1)} %bitcast.17, bf16[1024,1024]{1,0:T(8,128)(2,1)S(1)} %get-tuple-element.27.fwd, f32[128,512]{1,0:T(8,128)} %get-tuple-element.28.cos_any, f32[128,512]{1,0:T(8,128)} %get-tuple-element.29.sin_any, bf16[1024,256]{1,0:T(8,128)(2,1)} %get-tuple-element.30.first_any, ...), custom_call_target="tpu_custom_call" | custom-call | flops 3221225472 | bytes 2097152 | tf_op jit(solution)/shard_map/filter_rows/pallas_call | solution.py:467
  92.1 8.3 %all-to-all-start.2 = ((bf16[128,8,512]{2,1,0:T(8,128)(2,1)}), bf16[128,8,512]{2,1,0:T(8,128)(2,1)S(1)}, u32[]{:S(2)}, u32[]{:S(2)}) async-start(bf16[128,8,512]{2,1,0:T(8,128)(2,1)} %bitcast.20), calls=%async_computation.2 | async-start | bytes 2097152 | tf_op jit(solution)/shard_map/all_to_all | solution.py:521
  100.4 1.1 backward_columns_phases.1.table_ref
  101.5 29.3 %all-to-all-done.2 = bf16[128,8,512]{2,1,0:T(8,128)(2,1)S(1)} async-done(((bf16[128,8,512]{2,1,0:T(8,128)(2,1)}), bf16[128,8,512]{2,1,0:T(8,128)(2,1)S(1)}, u32[]{:S(2)}, u32[]{:S(2)}) %all-to-all-start.2) | async-done | bytes 1048608 | tf_op jit(solution)/shard_map/all_to_all | solution.py:521
  130.8 2.0 %along_columns.3 = bf16[1024,512]{1,0:T(8,128)(2,1)} custom-call(bf16[1024,1024]{1,0:T(8,128)(2,1)S(1)} %backward_columns_phases.1.table_ref, bf16[1024,512]{1,0:T(8,128)(2,1)S(1)} %bitcast.16), custom_call_target="tpu_custom_call" | custom-call | flops 1073741824 | bytes 2097152 | tf_op jit(solution)/shard_map/along_columns/pallas_call | solution.py:319
  132.8 5.9 %all-to-all-start.3 = ((bf16[16,64,512]{2,1,0:T(8,128)(2,1)}), bf16[16,64,512]{2,1,0:T(8,128)(2,1)S(1)}, u32[]{:S(2)}, u32[]{:S(2)}) async-start(bf16[16,64,512]{2,1,0:T(8,128)(2,1)} %bitcast.19), calls=%async_computation.3 | async-start | bytes 2097152 | tf_op jit(solution)/shard_map/all_to_all | solution.py:524
  138.7 0.6 reshape.31.taps_ref
  139.3 4.1 %stencil.1.base_ref = f32[32,64,256]{2,1,0:T(8,128)S(1)} custom-call(bf16[32,64,256]{2,1,0:T(8,128)(2,1)} %x_ref.3, bf16[32,64,256]{2,1,0:T(8,128)(2,1)} %home_norm.1.normed_ref, bf16[64,256]{1,0:T(8,128)(2,1)} %copy-done.3, bf16[64,256]{1,0:T(8,128)(2,1)} %copy-done.4, bf16[34,256]{1,0:T(8,128)(2,1)} %copy-done.6, bf16[34,256]{1,0:T(8,128)(2,1)} %copy-done.5, ...), custom_call_target="tpu_custom_call" | custom-call | flops 16777216 | bytes 4194304 | tf_op jit(solution)/shard_map/stencil/pallas_call | solution.py:367
  143.4 20.3 %all-to-all-done.3.home_ref = bf16[16,64,512]{2,1,0:T(8,128)(2,1)S(1)} async-done(((bf16[16,64,512]{2,1,0:T(8,128)(2,1)}), bf16[16,64,512]{2,1,0:T(8,128)(2,1)S(1)}, u32[]{:S(2)}, u32[]{:S(2)}) %all-to-all-start.3) | async-done | bytes 1048608 | tf_op jit(solution)/shard_map/all_to_all | solution.py:524
  163.7 1.2 unpack_add.1
  (19 shorter events, 0.1 us)
Async XLA Ops:
  3.9 34.9 %all-to-all-start = ((bf16[16,64,512]{2,1,0:T(8,128)(2,1)}), bf16[16,64,512]{2,1,0:T(8,128)(2,1)S(1)}, u32[]{:S(2)}, u32[]{:S(2)}) async-start(bf16[16,64,512]{2,1,0:T(8,128)(2,1)} %norm_pack.1), calls=%async_computation | async-start | bytes 2097152 | tf_op jit(solution)/shard_map/all_to_all | solution.py:494
  18.2 22.7 %collective-permute-start = (bf16[64,256]{1,0:T(8,128)(2,1)S(1)}, bf16[64,256]{1,0:T(8,128)(2,1)S(1)}, u32[]{:S(2)}, u32[]{:S(2)}) collective-permute-start(bf16[64,256]{1,0:T(8,128)(2,1)S(1)} %get-tuple-element.40), channel_id=1, source_target_pairs={{0,16},{16,32},{32,48},{48,64},{64,80},{80,96},{96,112},{112,128},... | collective-permute-start | bytes 98312 | tf_op jit(solution)/shard_map/ppermute | solution.py:504
  20.1 20.8 %collective-permute-start.1 = (bf16[64,256]{1,0:T(8,128)(2,1)S(1)}, bf16[64,256]{1,0:T(8,128)(2,1)S(1)}, u32[]{:S(2)}, u32[]{:S(2)}) collective-permute-start(bf16[64,256]{1,0:T(8,128)(2,1)S(1)} %get-tuple-element.39), channel_id=1, source_target_pairs={{16,0},{32,16},{48,32},{64,48},{80,64},{96,80},{112,96},{128,112},... | collective-permute-start | bytes 98312 | tf_op jit(solution)/shard_map/ppermute | solution.py:505
  40.9 15.1 %copy-start.2 = (bf16[32,64,256]{2,1,0:T(8,128)(2,1)S(1)}, bf16[32,64,256]{2,1,0:T(8,128)(2,1)}, u32[]{:S(2)}) copy-start(bf16[32,64,256]{2,1,0:T(8,128)(2,1)} %home_norm.1.normed_ref) | copy-start | bytes 3145732
  40.9 15.6 %copy-start.3 = (bf16[64,256]{1,0:T(8,128)(2,1)}, bf16[64,256]{1,0:T(8,128)(2,1)S(1)}, u32[]{:S(2)}) copy-start(bf16[64,256]{1,0:T(8,128)(2,1)S(1)} %collective-permute-done.top_ref) | copy-start | bytes 98308
  40.9 15.6 %copy-start.4 = (bf16[64,256]{1,0:T(8,128)(2,1)}, bf16[64,256]{1,0:T(8,128)(2,1)S(1)}, u32[]{:S(2)}) copy-start(bf16[64,256]{1,0:T(8,128)(2,1)S(1)} %collective-permute-done.1.bottom_ref) | copy-start | bytes 98308
  40.9 21.6 %copy-start = (bf16[2,4,64,64]{3,2,1,0:T(8,128)(2,1)S(1)}, bf16[2,4,64,64]{3,2,1,0:T(8,128)(2,1)}, u32[]{:S(2)}) copy-start(bf16[2,4,64,64]{3,2,1,0:T(8,128)(2,1)} %first_w.1) | copy-start | bytes 196612
  40.9 21.5 %copy-start.1 = (bf16[2,4,64,64]{3,2,1,0:T(8,128)(2,1)S(1)}, bf16[2,4,64,64]{3,2,1,0:T(8,128)(2,1)}, u32[]{:S(2)}) copy-start(bf16[2,4,64,64]{3,2,1,0:T(8,128)(2,1)} %second_w.1) | copy-start | bytes 196612
  40.9 45.4 %all-to-all-start.1 = ((bf16[128,8,512]{2,1,0:T(8,128)(2,1)}), bf16[128,8,512]{2,1,0:T(8,128)(2,1)S(1)}, u32[]{:S(2)}, u32[]{:S(2)}) async-start(bf16[128,8,512]{2,1,0:T(8,128)(2,1)} %bitcast.18), calls=%async_computation.1 | async-start | bytes 2097152 | tf_op jit(solution)/shard_map/all_to_all | solution.py:513
  56.6 22.2 %collective-permute-start.3 = (bf16[34,256]{1,0:T(8,128)(2,1)S(1)}, bf16[34,256]{1,0:T(8,128)(2,1)S(1)}, u32[]{:S(2)}, u32[]{:S(2)}) collective-permute-start(bf16[34,256]{1,0:T(8,128)(2,1)S(1)} %pad_maximum_fusion.1), channel_id=1, source_target_pairs={{1,0},{2,1},{3,2},{4,3},{5,4},{6,5},{7,6},{8,7},{9,8},{10,9},{11,1... | collective-permute-start | bytes 52232 | tf_op jit(solution)/shard_map/ppermute | solution.py:505
  60.4 19.0 %collective-permute-start.2 = (bf16[34,256]{1,0:T(8,128)(2,1)S(1)}, bf16[34,256]{1,0:T(8,128)(2,1)S(1)}, u32[]{:S(2)}, u32[]{:S(2)}) collective-permute-start(bf16[34,256]{1,0:T(8,128)(2,1)S(1)} %pad_maximum_fusion), channel_id=1, source_target_pairs={{0,1},{1,2},{2,3},{3,4},{4,5},{5,6},{6,7},{7,8},{8,9},{9,10},{10,1... | collective-permute-start | bytes 52232 | tf_op jit(solution)/shard_map/ppermute | solution.py:504
  78.7 13.3 %copy-start.5 = (bf16[34,256]{1,0:T(8,128)(2,1)}, bf16[34,256]{1,0:T(8,128)(2,1)S(1)}, u32[]{:S(2)}) copy-start(bf16[34,256]{1,0:T(8,128)(2,1)S(1)} %collective-permute-done.3.right_ref) | copy-start | bytes 52228
  79.4 12.7 %copy-start.6 = (bf16[34,256]{1,0:T(8,128)(2,1)}, bf16[34,256]{1,0:T(8,128)(2,1)S(1)}, u32[]{:S(2)}) copy-start(bf16[34,256]{1,0:T(8,128)(2,1)S(1)} %collective-permute-done.2.left_ref) | copy-start | bytes 52228
  92.1 38.7 %all-to-all-start.2 = ((bf16[128,8,512]{2,1,0:T(8,128)(2,1)}), bf16[128,8,512]{2,1,0:T(8,128)(2,1)S(1)}, u32[]{:S(2)}, u32[]{:S(2)}) async-start(bf16[128,8,512]{2,1,0:T(8,128)(2,1)} %bitcast.20), calls=%async_computation.2 | async-start | bytes 2097152 | tf_op jit(solution)/shard_map/all_to_all | solution.py:521
  132.8 6.0 %copy-start.7 = (f32[3,3,256]{2,1,0:T(4,128)S(1)}, f32[3,3,256]{2,1,0:T(4,128)}, u32[]{:S(2)}) copy-start(f32[3,3,256]{2,1,0:T(4,128)} %param.9) | copy-start | bytes 27652
  132.8 30.9 %all-to-all-start.3 = ((bf16[16,64,512]{2,1,0:T(8,128)(2,1)}), bf16[16,64,512]{2,1,0:T(8,128)(2,1)S(1)}, u32[]{:S(2)}, u32[]{:S(2)}) async-start(bf16[16,64,512]{2,1,0:T(8,128)(2,1)} %bitcast.19), calls=%async_computation.3 | async-start | bytes 2097152 | tf_op jit(solution)/shard_map/all_to_all | solution.py:524

commit v9 on v8

--- a/solution.py
+++ b/solution.py
@@ -506,19 +506,21 @@
         return before, after
 
     normed = home_norm(patches, norm_gain)
+    lines, normed = lax.optimization_barrier((lines, normed))
+
+    freqs = columns(fwd_w, lines)
+    whole = lax.all_to_all(freqs.reshape(128, 8, 512), ("row", "yl"), 0, 0, tiled=True)
     top, bottom = neighbours(normed[0], normed[31], "row")
 
-    freqs = columns(fwd_w, lines)
-    freqs, top, bottom, normed = lax.optimization_barrier((freqs, top, bottom, normed))
-    whole = lax.all_to_all(freqs.reshape(128, 8, 512), ("row", "yl"), 0, 0, tiled=True)
+    filtered = middle(whole.reshape(1024, 512), fwd_h, cos, sin, first, second, last, inv_h)
+    filtered, top, bottom, normed = lax.optimization_barrier((filtered, top, bottom, normed))
+    back = lax.all_to_all(filtered.reshape(128, 8, 512), ("row", "yl"), 0, 0, tiled=True)
     sides = [
         jnp.concatenate([top[w : w + 1], normed[:, w], bottom[w : w + 1]], axis=0) for w in (0, 63)
     ]
     left, right = neighbours(sides[0], sides[1], ("yl", "x"))
-    whole, left, right = lax.optimization_barrier((whole, left, right))
-
-    filtered = middle(whole.reshape(1024, 512), fwd_h, cos, sin, first, second, last, inv_h)
-    back = lax.all_to_all(filtered.reshape(128, 8, 512), ("row", "yl"), 0, 0, tiled=True)
+    back, left, right = lax.optimization_barrier((back, left, right))
+
     spectral = columns(inv_w, back.reshape(1024, 512))
     spectral, left, right = lax.optimization_barrier((spectral, left, right))
     home = lax.all_to_all(spectral.reshape(16, 64, 512), ("yl", "x"), 0, 0, tiled=True)

time: 166 us -> 164 us (0.988)
  waiting for transfers between devices: 74 us -> 71.7 us
    all_to_all x1, waiting for transfers between devices: 29.3 us -> 6.95 us  [local(): lax.all_to_all(filtered.reshape(128, 8, 512), ('row', 'yl'), 0, 0, tiled=...]
    ppermute x2, waiting for transfers between devices: 0.61 us -> 13.7 us  [neighbours(): before = lax.ppermute(last, axis, [(i, (i + 1) % n) for i in range(n)])]
    all_to_all x1, waiting for transfers between devices: 6.73 us -> 18.9 us  [local(): lax.all_to_all(packed, ('yl', 'x'), 0, 0, tiled=True).reshape(1024, 512)]
    ppermute x2, waiting for transfers between devices: 10.1 us -> 0.01 us  [neighbours(): after = lax.ppermute(first, axis, [((i + 1) % n, i) for i in range(n)])]
    all_to_all x1, waiting for transfers between devices: 6.96 us -> 11.9 us  [local(): lax.all_to_all(freqs.reshape(128, 8, 512), ('row', 'yl'), 0, 0, tiled=True)]
  transfers between devices with their start and end apart: 8 -> 8, of which waited for: 6 -> 5; matrix products, arithmetic and copies ran while one was open for 1% -> 1% of each run, Pallas kernels for 11% -> 14%
where the time goes in v9:
time: 164 us
  waiting for transfers between devices  71.7 us (44%)
  starting transfers between devices  58 us (35%)
  Pallas kernels  31.5 us (19%)
  local copies, waits for them, and re-layouts  2.02 us (1%)
    all_to_all x1, waiting for transfers between devices, local(): lax.all_to_all(spectral.reshape(16, 64, 512), ('yl', 'x'), 0, 0, tiled=True)  20.3 us
    all_to_all x1, waiting for transfers between devices, local(): lax.all_to_all(packed, ('yl', 'x'), 0, 0, tiled=True).reshape(1024, 512)  18.9 us
    ppermute x2, starting transfers between devices, neighbours(): after = lax.ppermute(first, axis, [((i + 1) % n, i) for i in range(n)])  15 us
    all_to_all x1, starting transfers between devices, local(): lax.all_to_all(freqs.reshape(128, 8, 512), ('row', 'yl'), 0, 0, tiled=True)  15 us
    ppermute x2, waiting for transfers between devices, neighbours(): before = lax.ppermute(last, axis, [(i, (i + 1) % n) for i in range(n)])  13.7 us
    all_to_all x1, waiting for transfers between devices, local(): lax.all_to_all(freqs.reshape(128, 8, 512), ('row', 'yl'), 0, 0, tiled=True)  11.9 us
    all_to_all x1, starting transfers between devices, local(): lax.all_to_all(packed, ('yl', 'x'), 0, 0, tiled=True).reshape(1024, 512)  9.3 us
    all_to_all x1, starting transfers between devices, local(): lax.all_to_all(filtered.reshape(128, 8, 512), ('row', 'yl'), 0, 0, tiled=...  7.9 us
  transfers between devices with their start and end apart: 8, of which 5 were waited for; matrix products, arithmetic and copies ran while one was open for 1% of the time, Pallas kernels for 14%

profile of v9, /device:TPU:8, one launch (start us, length us, event | category | flops | bytes accessed | tf_op | source)
XLA Modules:
  0.0 163.6 jit_solution(6190108776737415345)
XLA Ops:
  0.0 3.9 %norm_pack.1 = bf16[16,64,512]{2,1,0:T(8,128)(2,1)} custom-call(bf16[32,64,256]{2,1,0:T(8,128)(2,1)} %x_ref.3, f32[1,256]{1,0:T(1,128)} %bitcast.21), custom_call_target="tpu_custom_call" | custom-call | tf_op jit(solution)/shard_map/norm_pack/pallas_call | solution.py:243
  3.9 9.3 %all-to-all-start = ((bf16[16,64,512]{2,1,0:T(8,128)(2,1)}), bf16[16,64,512]{2,1,0:T(8,128)(2,1)S(1)}, u32[]{:S(2)}, u32[]{:S(2)}) async-start(bf16[16,64,512]{2,1,0:T(8,128)(2,1)} %norm_pack.1), calls=%async_computation | async-start | bytes 2097152 | tf_op jit(solution)/shard_map/all_to_all | solution.py:494
  13.2 1.1 forward_columns_phases.1.table_ref
  14.4 4.2 %home_norm.1.normed_ref = bf16[32,64,256]{2,1,0:T(8,128)(2,1)} custom-call(bf16[32,64,256]{2,1,0:T(8,128)(2,1)} %x_ref.3, f32[1,256]{1,0:T(1,128)} %bitcast.22), custom_call_target="tpu_custom_call" | custom-call | flops 16777216 | bytes 2097152 | tf_op jit(solution)/shard_map/home_norm/pallas_call | solution.py:230
  18.5 18.9 %all-to-all-done = bf16[16,64,512]{2,1,0:T(8,128)(2,1)S(1)} async-done(((bf16[16,64,512]{2,1,0:T(8,128)(2,1)}), bf16[16,64,512]{2,1,0:T(8,128)(2,1)S(1)}, u32[]{:S(2)}, u32[]{:S(2)}) %all-to-all-start) | async-done | bytes 1048608 | tf_op jit(solution)/shard_map/all_to_all | solution.py:494
  37.5 2.0 %along_columns.2 = bf16[1024,512]{1,0:T(8,128)(2,1)} custom-call(bf16[1024,1024]{1,0:T(8,128)(2,1)S(1)} %forward_columns_phases.1.table_ref, bf16[1024,512]{1,0:T(8,128)(2,1)S(1)} %bitcast.16), custom_call_target="tpu_custom_call" | custom-call | flops 1073741824 | bytes 2097152 | tf_op jit(solution)/shard_map/along_columns/pallas_call | solution.py:319
  39.5 0.0 copy-start
  39.5 0.0 copy-start.1
  39.5 15.0 %all-to-all-start.1 = ((bf16[128,8,512]{2,1,0:T(8,128)(2,1)}), bf16[128,8,512]{2,1,0:T(8,128)(2,1)S(1)}, u32[]{:S(2)}, u32[]{:S(2)}) async-start(bf16[128,8,512]{2,1,0:T(8,128)(2,1)} %bitcast.18), calls=%async_computation.1 | async-start | bytes 2097152 | tf_op jit(solution)/shard_map/all_to_all | solution.py:512
  54.5 1.2 block_tables.1
  55.7 2.6 %backward_rows_phases.1.refs_1_.inv_any = bf16[1024,1024]{1,0:T(8,128)(2,1)} custom-call(), custom_call_target="tpu_custom_call" | custom-call | flops 8388608 | bytes 2097152 | tf_op jit(solution)/shard_map/backward_rows_phases/pallas_call | solution.py:109
  58.3 2.3 %forward_rows_phases.1 = (bf16[1024,1024]{1,0:T(8,128)(2,1)S(1)}, f32[128,512]{1,0:T(8,128)}, f32[128,512]{1,0:T(8,128)}) custom-call(bf16[256,256]{1,0:T(8,128)(2,1)} %get-tuple-element.24.refs_0_.second_any, bf16[1024,1024]{1,0:T(8,128)(2,1)} %backward_rows_phases.1.refs_1_.inv_any), custom_call_target="tpu_custom_call" | custom-call | flops 8388608 | bytes 2097152 | tf_op jit(solution)/shard_map/forward_rows_phases/pallas_call | solution.py:109
  60.6 0.8 slice_bitcast_fusion
  61.4 2.0 %collective-permute-start = (bf16[64,256]{1,0:T(8,128)(2,1)S(1)}, bf16[64,256]{1,0:T(8,128)(2,1)S(1)}, u32[]{:S(2)}, u32[]{:S(2)}) collective-permute-start(bf16[64,256]{1,0:T(8,128)(2,1)S(1)} %get-tuple-element.44), channel_id=1, source_target_pairs={{0,16},{16,32},{32,48},{48,64},{64,80},{80,96},{96,112},{112,128},... | collective-permute-start | bytes 98312 | tf_op jit(solution)/shard_map/ppermute | solution.py:504
  63.4 9.5 %collective-permute-start.1 = (bf16[64,256]{1,0:T(8,128)(2,1)S(1)}, bf16[64,256]{1,0:T(8,128)(2,1)S(1)}, u32[]{:S(2)}, u32[]{:S(2)}) collective-permute-start(bf16[64,256]{1,0:T(8,128)(2,1)S(1)} %get-tuple-element.43), channel_id=1, source_target_pairs={{16,0},{32,16},{48,32},{64,48},{80,64},{96,80},{112,96},{128,112},... | collective-permute-start | bytes 98312 | tf_op jit(solution)/shard_map/ppermute | solution.py:505
  73.0 11.9 %all-to-all-done.1 = bf16[128,8,512]{2,1,0:T(8,128)(2,1)S(1)} async-done(((bf16[128,8,512]{2,1,0:T(8,128)(2,1)}), bf16[128,8,512]{2,1,0:T(8,128)(2,1)S(1)}, u32[]{:S(2)}, u32[]{:S(2)}) %all-to-all-start.1) | async-done | bytes 1048608 | tf_op jit(solution)/shard_map/all_to_all | solution.py:512
  84.9 5.8 %filter_rows.1 = bf16[1024,512]{1,0:T(8,128)(2,1)} custom-call(bf16[1024,512]{1,0:T(8,128)(2,1)S(1)} %bitcast.17, bf16[1024,1024]{1,0:T(8,128)(2,1)S(1)} %get-tuple-element.25.fwd, f32[128,512]{1,0:T(8,128)} %get-tuple-element.26.cos_any, f32[128,512]{1,0:T(8,128)} %get-tuple-element.27.sin_any, bf16[1024,256]{1,0:T(8,128)(2,1)} %get-tuple-element.28.first_any, ...), custom_call_target="tpu_custom_call" | custom-call | flops 3221225472 | bytes 2097152 | tf_op jit(solution)/shard_map/filter_rows/pallas_call | solution.py:467
  90.6 0.0 copy-start.2
  90.7 7.9 %all-to-all-start.2 = ((bf16[128,8,512]{2,1,0:T(8,128)(2,1)}), bf16[128,8,512]{2,1,0:T(8,128)(2,1)S(1)}, u32[]{:S(2)}, u32[]{:S(2)}) async-start(bf16[128,8,512]{2,1,0:T(8,128)(2,1)} %bitcast.20), calls=%async_computation.2 | async-start | bytes 2097152 | tf_op jit(solution)/shard_map/all_to_all | solution.py:517
  98.6 0.6 copy.6
  99.3 2.5 %collective-permute-start.2 = (bf16[34,256]{1,0:T(8,128)(2,1)S(1)}, bf16[34,256]{1,0:T(8,128)(2,1)S(1)}, u32[]{:S(2)}, u32[]{:S(2)}) collective-permute-start(bf16[34,256]{1,0:T(8,128)(2,1)S(1)} %pad_maximum_fusion), channel_id=1, source_target_pairs={{0,1},{1,2},{2,3},{3,4},{4,5},{5,6},{6,7},{7,8},{8,9},{9,10},{10,1... | collective-permute-start | bytes 52232 | tf_op jit(solution)/shard_map/ppermute | solution.py:504
  101.8 5.5 %collective-permute-start.3 = (bf16[34,256]{1,0:T(8,128)(2,1)S(1)}, bf16[34,256]{1,0:T(8,128)(2,1)S(1)}, u32[]{:S(2)}, u32[]{:S(2)}) collective-permute-start(bf16[34,256]{1,0:T(8,128)(2,1)S(1)} %pad_maximum_fusion.1), channel_id=1, source_target_pairs={{1,0},{2,1},{3,2},{4,3},{5,4},{6,5},{7,6},{8,7},{9,8},{10,9},{11,1... | collective-permute-start | bytes 52232 | tf_op jit(solution)/shard_map/ppermute | solution.py:505
  107.2 1.1 backward_columns_phases.1.table_ref
  108.4 13.6 %collective-permute-done.2.left_ref = bf16[34,256]{1,0:T(8,128)(2,1)S(1)} collective-permute-done((bf16[34,256]{1,0:T(8,128)(2,1)S(1)}, bf16[34,256]{1,0:T(8,128)(2,1)S(1)}, u32[]{:S(2)}, u32[]{:S(2)}) %collective-permute-start.2) | collective-permute-done | bytes 17440 | tf_op jit(solution)/shard_map/ppermute | solution.py:504
  122.0 7.0 %all-to-all-done.2 = bf16[128,8,512]{2,1,0:T(8,128)(2,1)S(1)} async-done(((bf16[128,8,512]{2,1,0:T(8,128)(2,1)}), bf16[128,8,512]{2,1,0:T(8,128)(2,1)S(1)}, u32[]{:S(2)}, u32[]{:S(2)}) %all-to-all-start.2) | async-done | bytes 1048608 | tf_op jit(solution)/shard_map/all_to_all | solution.py:517
  129.0 2.0 %along_columns.3 = bf16[1024,512]{1,0:T(8,128)(2,1)} custom-call(bf16[1024,1024]{1,0:T(8,128)(2,1)S(1)} %backward_columns_phases.1.table_ref, bf16[1024,512]{1,0:T(8,128)(2,1)S(1)} %bitcast.15), custom_call_target="tpu_custom_call" | custom-call | flops 1073741824 | bytes 2097152 | tf_op jit(solution)/shard_map/along_columns/pallas_call | solution.py:319
  131.0 0.0 copy-start.7
  131.0 6.3 %all-to-all-start.3 = ((bf16[16,64,512]{2,1,0:T(8,128)(2,1)}), bf16[16,64,512]{2,1,0:T(8,128)(2,1)S(1)}, u32[]{:S(2)}, u32[]{:S(2)}) async-start(bf16[16,64,512]{2,1,0:T(8,128)(2,1)} %bitcast.19), calls=%async_computation.3 | async-start | bytes 2097152 | tf_op jit(solution)/shard_map/all_to_all | solution.py:526
  137.3 0.6 reshape.31.taps_ref
  137.9 4.1 %stencil.1.base_ref = f32[32,64,256]{2,1,0:T(8,128)S(1)} custom-call(bf16[32,64,256]{2,1,0:T(8,128)(2,1)} %x_ref.3, bf16[32,64,256]{2,1,0:T(8,128)(2,1)} %home_norm.1.normed_ref, bf16[64,256]{1,0:T(8,128)(2,1)} %copy-done.3, bf16[64,256]{1,0:T(8,128)(2,1)} %copy-done.4, bf16[34,256]{1,0:T(8,128)(2,1)} %copy-done.5, bf16[34,256]{1,0:T(8,128)(2,1)} %copy-done.6, ...), custom_call_target="tpu_custom_call" | custom-call | flops 16777216 | bytes 4194304 | tf_op jit(solution)/shard_map/stencil/pallas_call | solution.py:367
  142.0 20.3 %all-to-all-done.3.home_ref = bf16[16,64,512]{2,1,0:T(8,128)(2,1)S(1)} async-done(((bf16[16,64,512]{2,1,0:T(8,128)(2,1)}), bf16[16,64,512]{2,1,0:T(8,128)(2,1)S(1)}, u32[]{:S(2)}, u32[]{:S(2)}) %all-to-all-start.3) | async-done | bytes 1048608 | tf_op jit(solution)/shard_map/all_to_all | solution.py:526
  162.2 1.2 unpack_add.1
  (19 shorter events, 0.1 us)
Async XLA Ops:
  3.9 33.5 %all-to-all-start = ((bf16[16,64,512]{2,1,0:T(8,128)(2,1)}), bf16[16,64,512]{2,1,0:T(8,128)(2,1)S(1)}, u32[]{:S(2)}, u32[]{:S(2)}) async-start(bf16[16,64,512]{2,1,0:T(8,128)(2,1)} %norm_pack.1), calls=%async_computation | async-start | bytes 2097152 | tf_op jit(solution)/shard_map/all_to_all | solution.py:494
  39.5 15.0 %copy-start = (bf16[2,4,64,64]{3,2,1,0:T(8,128)(2,1)S(1)}, bf16[2,4,64,64]{3,2,1,0:T(8,128)(2,1)}, u32[]{:S(2)}) copy-start(bf16[2,4,64,64]{3,2,1,0:T(8,128)(2,1)} %first_w.1) | copy-start | bytes 196612
  39.5 15.0 %copy-start.1 = (bf16[2,4,64,64]{3,2,1,0:T(8,128)(2,1)S(1)}, bf16[2,4,64,64]{3,2,1,0:T(8,128)(2,1)}, u32[]{:S(2)}) copy-start(bf16[2,4,64,64]{3,2,1,0:T(8,128)(2,1)} %second_w.1) | copy-start | bytes 196612
  39.5 45.4 %all-to-all-start.1 = ((bf16[128,8,512]{2,1,0:T(8,128)(2,1)}), bf16[128,8,512]{2,1,0:T(8,128)(2,1)S(1)}, u32[]{:S(2)}, u32[]{:S(2)}) async-start(bf16[128,8,512]{2,1,0:T(8,128)(2,1)} %bitcast.18), calls=%async_computation.1 | async-start | bytes 2097152 | tf_op jit(solution)/shard_map/all_to_all | solution.py:512
  61.4 29.3 %collective-permute-start = (bf16[64,256]{1,0:T(8,128)(2,1)S(1)}, bf16[64,256]{1,0:T(8,128)(2,1)S(1)}, u32[]{:S(2)}, u32[]{:S(2)}) collective-permute-start(bf16[64,256]{1,0:T(8,128)(2,1)S(1)} %get-tuple-element.44), channel_id=1, source_target_pairs={{0,16},{16,32},{32,48},{48,64},{64,80},{80,96},{96,112},{112,128},... | collective-permute-start | bytes 98312 | tf_op jit(solution)/shard_map/ppermute | solution.py:504
  63.4 27.2 %collective-permute-start.1 = (bf16[64,256]{1,0:T(8,128)(2,1)S(1)}, bf16[64,256]{1,0:T(8,128)(2,1)S(1)}, u32[]{:S(2)}, u32[]{:S(2)}) collective-permute-start(bf16[64,256]{1,0:T(8,128)(2,1)S(1)} %get-tuple-element.43), channel_id=1, source_target_pairs={{16,0},{32,16},{48,32},{64,48},{80,64},{96,80},{112,96},{128,112},... | collective-permute-start | bytes 98312 | tf_op jit(solution)/shard_map/ppermute | solution.py:505
  90.6 8.0 %copy-start.2 = (bf16[32,64,256]{2,1,0:T(8,128)(2,1)S(1)}, bf16[32,64,256]{2,1,0:T(8,128)(2,1)}, u32[]{:S(2)}) copy-start(bf16[32,64,256]{2,1,0:T(8,128)(2,1)} %home_norm.1.normed_ref) | copy-start | bytes 3145732
  90.7 8.5 %copy-start.3 = (bf16[64,256]{1,0:T(8,128)(2,1)}, bf16[64,256]{1,0:T(8,128)(2,1)S(1)}, u32[]{:S(2)}) copy-start(bf16[64,256]{1,0:T(8,128)(2,1)S(1)} %collective-permute-done.top_ref) | copy-start | bytes 98308
  90.7 8.5 %copy-start.4 = (bf16[64,256]{1,0:T(8,128)(2,1)}, bf16[64,256]{1,0:T(8,128)(2,1)S(1)}, u32[]{:S(2)}) copy-start(bf16[64,256]{1,0:T(8,128)(2,1)S(1)} %collective-permute-done.1.bottom_ref) | copy-start | bytes 98308
  90.7 38.3 %all-to-all-start.2 = ((bf16[128,8,512]{2,1,0:T(8,128)(2,1)}), bf16[128,8,512]{2,1,0:T(8,128)(2,1)S(1)}, u32[]{:S(2)}, u32[]{:S(2)}) async-start(bf16[128,8,512]{2,1,0:T(8,128)(2,1)} %bitcast.20), calls=%async_computation.2 | async-start | bytes 2097152 | tf_op jit(solution)/shard_map/all_to_all | solution.py:517
  99.3 22.8 %collective-permute-start.2 = (bf16[34,256]{1,0:T(8,128)(2,1)S(1)}, bf16[34,256]{1,0:T(8,128)(2,1)S(1)}, u32[]{:S(2)}, u32[]{:S(2)}) collective-permute-start(bf16[34,256]{1,0:T(8,128)(2,1)S(1)} %pad_maximum_fusion), channel_id=1, source_target_pairs={{0,1},{1,2},{2,3},{3,4},{4,5},{5,6},{6,7},{7,8},{8,9},{9,10},{10,1... | collective-permute-start | bytes 52232 | tf_op jit(solution)/shard_map/ppermute | solution.py:504
  101.8 20.3 %collective-permute-start.3 = (bf16[34,256]{1,0:T(8,128)(2,1)S(1)}, bf16[34,256]{1,0:T(8,128)(2,1)S(1)}, u32[]{:S(2)}, u32[]{:S(2)}) collective-permute-start(bf16[34,256]{1,0:T(8,128)(2,1)S(1)} %pad_maximum_fusion.1), channel_id=1, source_target_pairs={{1,0},{2,1},{3,2},{4,3},{5,4},{6,5},{7,6},{8,7},{9,8},{10,9},{11,1... | collective-permute-start | bytes 52232 | tf_op jit(solution)/shard_map/ppermute | solution.py:505
  122.0 9.0 %copy-start.5 = (bf16[34,256]{1,0:T(8,128)(2,1)}, bf16[34,256]{1,0:T(8,128)(2,1)S(1)}, u32[]{:S(2)}) copy-start(bf16[34,256]{1,0:T(8,128)(2,1)S(1)} %collective-permute-done.2.left_ref) | copy-start | bytes 52228
  122.0 9.0 %copy-start.6 = (bf16[34,256]{1,0:T(8,128)(2,1)}, bf16[34,256]{1,0:T(8,128)(2,1)S(1)}, u32[]{:S(2)}) copy-start(bf16[34,256]{1,0:T(8,128)(2,1)S(1)} %collective-permute-done.3.right_ref) | copy-start | bytes 52228
  131.0 6.3 %copy-start.7 = (f32[3,3,256]{2,1,0:T(4,128)S(1)}, f32[3,3,256]{2,1,0:T(4,128)}, u32[]{:S(2)}) copy-start(f32[3,3,256]{2,1,0:T(4,128)} %param.9) | copy-start | bytes 27652
  131.0 31.2 %all-to-all-start.3 = ((bf16[16,64,512]{2,1,0:T(8,128)(2,1)}), bf16[16,64,512]{2,1,0:T(8,128)(2,1)S(1)}, u32[]{:S(2)}, u32[]{:S(2)}) async-start(bf16[16,64,512]{2,1,0:T(8,128)(2,1)} %bitcast.19), calls=%async_computation.3 | async-start | bytes 2097152 | tf_op jit(solution)/shard_map/all_to_all | solution.py:526

commit v10 on v9

--- a/solution.py
+++ b/solution.py
@@ -194,16 +194,19 @@
     return d0 * scale * gain_ref[:, :128], d1 * scale * gain_ref[:, 128:]
 
 
-def norm_kernel(x_any, gain_ref, out_any, x_all, packed, in_sems, out_sems):
-    low = low_half(64)
+def norm_kernel(x_any, gain_any, out_any, x_all, packed, gain, in_sems, out_sems, gain_sem):
     fetches, sends = [], []
     for n in range(2):
         rows = slice(16 * n, 16 * n + 16)
         fetches.append(pltpu.make_async_copy(x_any.at[rows], x_all.at[rows], in_sems.at[n]))
         fetches[-1].start()
+    gain_fetch = pltpu.make_async_copy(gain_any, gain, gain_sem)
+    gain_fetch.start()
+    gain_fetch.wait()
     for n in range(2):
         fetches[n].wait()
-        halves = normed_halves(x_all[16 * n : 16 * n + 16].reshape(1024, 256), gain_ref)
+        x = x_all[16 * n : 16 * n + 16].reshape(1024, 256)
+        halves = [half.astype(BF16) for half in normed_halves(x, gain)]
         for g in range(2):
             first = 4 * (2 * n + g)
             for t in range(4):
@@ -211,8 +214,8 @@
                 for m in range(2):
                     a = halves[m][512 * g + 64 * t : 512 * g + 64 * t + 64]
                     b = halves[m][512 * g + 64 * t + 256 : 512 * g + 64 * t + 320]
-                    packed[first + 2 * m, :, lanes] = jnp.where(low, a, swap(b)).astype(BF16)
-                    packed[first + 2 * m + 1, :, lanes] = jnp.where(low, swap(a), b).astype(BF16)
+                    packed[first + 2 * m, :, lanes] = beside((a[:, :64], b[:, :64]))
+                    packed[first + 2 * m + 1, :, lanes] = beside((a[:, 64:], b[:, 64:]))
         parts = slice(8 * n, 8 * n + 8)
         sends.append(pltpu.make_async_copy(packed.at[parts], out_any.at[parts], out_sems.at[n]))
         sends[-1].start()
@@ -242,14 +245,16 @@
 def norm_and_pack(patches, gain):
     return pl.pallas_call(
         norm_kernel,
-        in_specs=[pl.BlockSpec(memory_space=pltpu.HBM), pl.BlockSpec(memory_space=pltpu.VMEM)],
+        in_specs=[pl.BlockSpec(memory_space=pltpu.HBM)] * 2,
         out_specs=pl.BlockSpec(memory_space=pltpu.HBM),
         out_shape=pltpu.HBM((16, 64, 512), BF16),
         scratch_shapes=[
             pltpu.VMEM((32, 64, 256), BF16),
             pltpu.VMEM((16, 64, 512), BF16),
+            pltpu.VMEM((1, 256), F32),
             pltpu.SemaphoreType.DMA((2,)),
             pltpu.SemaphoreType.DMA((2,)),
+            pltpu.SemaphoreType.DMA,
         ],
         compiler_params=pltpu.CompilerParams(vmem_limit_bytes=16 * MIB),
         name="norm_pack",
@@ -302,8 +307,7 @@
 
 def stream_dot(table, operand, held, out, sems):
     copies = []
-    for m in range(4):
-        rows = slice(256 * m, 256 * m + 256)
+    for m, rows in enumerate((slice(0, 512), slice(512, 896), slice(896, 1024))):
         held[rows, :] = dot(table[rows, :], operand[...]).astype(BF16)
         copies.append(pltpu.make_async_copy(held.at[rows, :], out.at[rows, :], sems.at[m]))
         copies[-1].start()
@@ -321,7 +325,7 @@
         in_specs=[pl.BlockSpec(memory_space=pltpu.VMEM)] * 2,
         out_specs=pl.BlockSpec(memory_space=pltpu.HBM),
         out_shape=pltpu.HBM((1024, 512), BF16),
-        scratch_shapes=[pltpu.VMEM((1024, 512), BF16), pltpu.SemaphoreType.DMA((4,))],
+        scratch_shapes=[pltpu.VMEM((1024, 512), BF16), pltpu.SemaphoreType.DMA((3,))],
         cost_estimate=pl.CostEstimate(flops=2**30, bytes_accessed=2**21, transcendentals=0),
         compiler_params=pltpu.CompilerParams(vmem_limit_bytes=12 * MIB),
         name="along_columns",
@@ -478,7 +482,7 @@
             pltpu.VMEM((1024, 1024), BF16),
             pltpu.VMEM((1024, 512), BF16),
             pltpu.VMEM((1024, 512), BF16),
-            pltpu.SemaphoreType.DMA((4,)),
+            pltpu.SemaphoreType.DMA((3,)),
             pltpu.SemaphoreType.DMA((6,)),
         ],
         cost_estimate=pl.CostEstimate(flops=3 * 2**30, bytes_accessed=2**21, transcendentals=2**19),

time: 164 us -> 164 us (level)
  no operation moved by 1% of the time
where the time goes in v10:
time: 164 us; the launch traced here: 163 us
  waiting for transfers between devices  71.7 us (44%)
  starting transfers between devices  58 us (35%)
  Pallas kernels  30.6 us (19%)
  local copies, waits for them, and re-layouts  2.02 us (1%)
    all_to_all x1, waiting for transfers between devices, local(): lax.all_to_all(spectral.reshape(16, 64, 512), ('yl', 'x'), 0, 0, tiled=True)  20.3 us
    all_to_all x1, waiting for transfers between devices, local(): lax.all_to_all(packed, ('yl', 'x'), 0, 0, tiled=True).reshape(1024, 512)  18.9 us
    ppermute x2, starting transfers between devices, neighbours(): after = lax.ppermute(first, axis, [((i + 1) % n, i) for i in range(n)])  15 us
    all_to_all x1, starting transfers between devices, local(): lax.all_to_all(freqs.reshape(128, 8, 512), ('row', 'yl'), 0, 0, tiled=True)  15 us
    ppermute x2, waiting for transfers between devices, neighbours(): before = lax.ppermute(last, axis, [(i, (i + 1) % n) for i in range(n)])  13.7 us
    all_to_all x1, waiting for transfers between devices, local(): lax.all_to_all(freqs.reshape(128, 8, 512), ('row', 'yl'), 0, 0, tiled=True)  11.9 us
    all_to_all x1, starting transfers between devices, local(): lax.all_to_all(packed, ('yl', 'x'), 0, 0, tiled=True).reshape(1024, 512)  9.3 us
    all_to_all x1, starting transfers between devices, local(): lax.all_to_all(filtered.reshape(128, 8, 512), ('row', 'yl'), 0, 0, tiled=...  7.9 us
  transfers between devices with their start and end apart: 8, of which 5 were waited for; matrix products, arithmetic and copies ran while one was open for 1% of the time, Pallas kernels for 14%

profile of v10, /device:TPU:8, one launch (start us, length us, event | category | flops | bytes accessed | tf_op | source)
XLA Modules:
  0.0 162.8 jit_solution(165791235942094189)
XLA Ops:
  0.0 3.2 %norm_pack.1 = bf16[16,64,512]{2,1,0:T(8,128)(2,1)} custom-call(bf16[32,64,256]{2,1,0:T(8,128)(2,1)} %x_ref.3, f32[1,256]{1,0:T(1,128)} %bitcast.21), custom_call_target="tpu_custom_call" | custom-call | tf_op jit(solution)/shard_map/norm_pack/pallas_call | solution.py:246
  3.2 9.3 %all-to-all-start = ((bf16[16,64,512]{2,1,0:T(8,128)(2,1)}), bf16[16,64,512]{2,1,0:T(8,128)(2,1)S(1)}, u32[]{:S(2)}, u32[]{:S(2)}) async-start(bf16[16,64,512]{2,1,0:T(8,128)(2,1)} %norm_pack.1), calls=%async_computation | async-start | bytes 2097152 | tf_op jit(solution)/shard_map/all_to_all | solution.py:498
  12.5 1.1 forward_columns_phases.1.table_ref
  13.7 4.2 %home_norm.1.normed_ref = bf16[32,64,256]{2,1,0:T(8,128)(2,1)} custom-call(bf16[32,64,256]{2,1,0:T(8,128)(2,1)} %x_ref.3, f32[1,256]{1,0:T(1,128)} %bitcast.22), custom_call_target="tpu_custom_call" | custom-call | flops 16777216 | bytes 2097152 | tf_op jit(solution)/shard_map/home_norm/pallas_call | solution.py:233
  17.8 18.9 %all-to-all-done = bf16[16,64,512]{2,1,0:T(8,128)(2,1)S(1)} async-done(((bf16[16,64,512]{2,1,0:T(8,128)(2,1)}), bf16[16,64,512]{2,1,0:T(8,128)(2,1)S(1)}, u32[]{:S(2)}, u32[]{:S(2)}) %all-to-all-start) | async-done | bytes 1048608 | tf_op jit(solution)/shard_map/all_to_all | solution.py:498
  36.8 1.9 %along_columns.2 = bf16[1024,512]{1,0:T(8,128)(2,1)} custom-call(bf16[1024,1024]{1,0:T(8,128)(2,1)S(1)} %forward_columns_phases.1.table_ref, bf16[1024,512]{1,0:T(8,128)(2,1)S(1)} %bitcast.16), custom_call_target="tpu_custom_call" | custom-call | flops 1073741824 | bytes 2097152 | tf_op jit(solution)/shard_map/along_columns/pallas_call | solution.py:323
  38.7 0.0 copy-start
  38.7 0.0 copy-start.1
  38.8 15.0 %all-to-all-start.1 = ((bf16[128,8,512]{2,1,0:T(8,128)(2,1)}), bf16[128,8,512]{2,1,0:T(8,128)(2,1)S(1)}, u32[]{:S(2)}, u32[]{:S(2)}) async-start(bf16[128,8,512]{2,1,0:T(8,128)(2,1)} %bitcast.18), calls=%async_computation.1 | async-start | bytes 2097152 | tf_op jit(solution)/shard_map/all_to_all | solution.py:516
  53.8 1.2 block_tables.1
  54.9 2.6 %backward_rows_phases.1.refs_1_.inv_any = bf16[1024,1024]{1,0:T(8,128)(2,1)} custom-call(), custom_call_target="tpu_custom_call" | custom-call | flops 8388608 | bytes 2097152 | tf_op jit(solution)/shard_map/backward_rows_phases/pallas_call | solution.py:109
  57.6 2.3 %forward_rows_phases.1 = (bf16[1024,1024]{1,0:T(8,128)(2,1)S(1)}, f32[128,512]{1,0:T(8,128)}, f32[128,512]{1,0:T(8,128)}) custom-call(bf16[256,256]{1,0:T(8,128)(2,1)} %get-tuple-element.24.refs_0_.second_any, bf16[1024,1024]{1,0:T(8,128)(2,1)} %backward_rows_phases.1.refs_1_.inv_any), custom_call_target="tpu_custom_call" | custom-call | flops 8388608 | bytes 2097152 | tf_op jit(solution)/shard_map/forward_rows_phases/pallas_call | solution.py:109
  59.9 0.8 slice_bitcast_fusion
  60.6 2.0 %collective-permute-start = (bf16[64,256]{1,0:T(8,128)(2,1)S(1)}, bf16[64,256]{1,0:T(8,128)(2,1)S(1)}, u32[]{:S(2)}, u32[]{:S(2)}) collective-permute-start(bf16[64,256]{1,0:T(8,128)(2,1)S(1)} %get-tuple-element.44), channel_id=1, source_target_pairs={{0,16},{16,32},{32,48},{48,64},{64,80},{80,96},{96,112},{112,128},... | collective-permute-start | bytes 98312 | tf_op jit(solution)/shard_map/ppermute | solution.py:508
  62.7 9.5 %collective-permute-start.1 = (bf16[64,256]{1,0:T(8,128)(2,1)S(1)}, bf16[64,256]{1,0:T(8,128)(2,1)S(1)}, u32[]{:S(2)}, u32[]{:S(2)}) collective-permute-start(bf16[64,256]{1,0:T(8,128)(2,1)S(1)} %get-tuple-element.43), channel_id=1, source_target_pairs={{16,0},{32,16},{48,32},{64,48},{80,64},{96,80},{112,96},{128,112},... | collective-permute-start | bytes 98312 | tf_op jit(solution)/shard_map/ppermute | solution.py:509
  72.2 11.9 %all-to-all-done.1 = bf16[128,8,512]{2,1,0:T(8,128)(2,1)S(1)} async-done(((bf16[128,8,512]{2,1,0:T(8,128)(2,1)}), bf16[128,8,512]{2,1,0:T(8,128)(2,1)S(1)}, u32[]{:S(2)}, u32[]{:S(2)}) %all-to-all-start.1) | async-done | bytes 1048608 | tf_op jit(solution)/shard_map/all_to_all | solution.py:516
  84.1 5.7 %filter_rows.1 = bf16[1024,512]{1,0:T(8,128)(2,1)} custom-call(bf16[1024,512]{1,0:T(8,128)(2,1)S(1)} %bitcast.17, bf16[1024,1024]{1,0:T(8,128)(2,1)S(1)} %get-tuple-element.25.fwd, f32[128,512]{1,0:T(8,128)} %get-tuple-element.26.cos_any, f32[128,512]{1,0:T(8,128)} %get-tuple-element.27.sin_any, bf16[1024,256]{1,0:T(8,128)(2,1)} %get-tuple-element.28.first_any, ...), custom_call_target="tpu_custom_call" | custom-call | flops 3221225472 | bytes 2097152 | tf_op jit(solution)/shard_map/filter_rows/pallas_call | solution.py:471
  89.8 0.0 copy-start.2
  89.9 7.9 %all-to-all-start.2 = ((bf16[128,8,512]{2,1,0:T(8,128)(2,1)}), bf16[128,8,512]{2,1,0:T(8,128)(2,1)S(1)}, u32[]{:S(2)}, u32[]{:S(2)}) async-start(bf16[128,8,512]{2,1,0:T(8,128)(2,1)} %bitcast.20), calls=%async_computation.2 | async-start | bytes 2097152 | tf_op jit(solution)/shard_map/all_to_all | solution.py:521
  97.8 0.6 copy.6
  98.5 2.5 %collective-permute-start.2 = (bf16[34,256]{1,0:T(8,128)(2,1)S(1)}, bf16[34,256]{1,0:T(8,128)(2,1)S(1)}, u32[]{:S(2)}, u32[]{:S(2)}) collective-permute-start(bf16[34,256]{1,0:T(8,128)(2,1)S(1)} %pad_maximum_fusion), channel_id=1, source_target_pairs={{0,1},{1,2},{2,3},{3,4},{4,5},{5,6},{6,7},{7,8},{8,9},{9,10},{10,1... | collective-permute-start | bytes 52232 | tf_op jit(solution)/shard_map/ppermute | solution.py:508
  101.0 5.5 %collective-permute-start.3 = (bf16[34,256]{1,0:T(8,128)(2,1)S(1)}, bf16[34,256]{1,0:T(8,128)(2,1)S(1)}, u32[]{:S(2)}, u32[]{:S(2)}) collective-permute-start(bf16[34,256]{1,0:T(8,128)(2,1)S(1)} %pad_maximum_fusion.1), channel_id=1, source_target_pairs={{1,0},{2,1},{3,2},{4,3},{5,4},{6,5},{7,6},{8,7},{9,8},{10,9},{11,1... | collective-permute-start | bytes 52232 | tf_op jit(solution)/shard_map/ppermute | solution.py:509
  106.5 1.1 backward_columns_phases.1.table_ref
  107.6 13.6 %collective-permute-done.2.left_ref = bf16[34,256]{1,0:T(8,128)(2,1)S(1)} collective-permute-done((bf16[34,256]{1,0:T(8,128)(2,1)S(1)}, bf16[34,256]{1,0:T(8,128)(2,1)S(1)}, u32[]{:S(2)}, u32[]{:S(2)}) %collective-permute-start.2) | collective-permute-done | bytes 17440 | tf_op jit(solution)/shard_map/ppermute | solution.py:508
  121.2 7.0 %all-to-all-done.2 = bf16[128,8,512]{2,1,0:T(8,128)(2,1)S(1)} async-done(((bf16[128,8,512]{2,1,0:T(8,128)(2,1)}), bf16[128,8,512]{2,1,0:T(8,128)(2,1)S(1)}, u32[]{:S(2)}, u32[]{:S(2)}) %all-to-all-start.2) | async-done | bytes 1048608 | tf_op jit(solution)/shard_map/all_to_all | solution.py:521
  128.2 1.9 %along_columns.3 = bf16[1024,512]{1,0:T(8,128)(2,1)} custom-call(bf16[1024,1024]{1,0:T(8,128)(2,1)S(1)} %backward_columns_phases.1.table_ref, bf16[1024,512]{1,0:T(8,128)(2,1)S(1)} %bitcast.15), custom_call_target="tpu_custom_call" | custom-call | flops 1073741824 | bytes 2097152 | tf_op jit(solution)/shard_map/along_columns/pallas_call | solution.py:323
  130.2 0.0 copy-start.7
  130.2 6.3 %all-to-all-start.3 = ((bf16[16,64,512]{2,1,0:T(8,128)(2,1)}), bf16[16,64,512]{2,1,0:T(8,128)(2,1)S(1)}, u32[]{:S(2)}, u32[]{:S(2)}) async-start(bf16[16,64,512]{2,1,0:T(8,128)(2,1)} %bitcast.19), calls=%async_computation.3 | async-start | bytes 2097152 | tf_op jit(solution)/shard_map/all_to_all | solution.py:530
  136.5 0.6 reshape.31.taps_ref
  137.1 4.1 %stencil.1.base_ref = f32[32,64,256]{2,1,0:T(8,128)S(1)} custom-call(bf16[32,64,256]{2,1,0:T(8,128)(2,1)} %x_ref.3, bf16[32,64,256]{2,1,0:T(8,128)(2,1)} %home_norm.1.normed_ref, bf16[64,256]{1,0:T(8,128)(2,1)} %copy-done.3, bf16[64,256]{1,0:T(8,128)(2,1)} %copy-done.4, bf16[34,256]{1,0:T(8,128)(2,1)} %copy-done.5, bf16[34,256]{1,0:T(8,128)(2,1)} %copy-done.6, ...), custom_call_target="tpu_custom_call" | custom-call | flops 16777216 | bytes 4194304 | tf_op jit(solution)/shard_map/stencil/pallas_call | solution.py:371
  141.1 20.3 %all-to-all-done.3.home_ref = bf16[16,64,512]{2,1,0:T(8,128)(2,1)S(1)} async-done(((bf16[16,64,512]{2,1,0:T(8,128)(2,1)}), bf16[16,64,512]{2,1,0:T(8,128)(2,1)S(1)}, u32[]{:S(2)}, u32[]{:S(2)}) %all-to-all-start.3) | async-done | bytes 1048608 | tf_op jit(solution)/shard_map/all_to_all | solution.py:530
  161.4 1.2 unpack_add.1
  (19 shorter events, 0.1 us)
Async XLA Ops:
  3.2 33.5 %all-to-all-start = ((bf16[16,64,512]{2,1,0:T(8,128)(2,1)}), bf16[16,64,512]{2,1,0:T(8,128)(2,1)S(1)}, u32[]{:S(2)}, u32[]{:S(2)}) async-start(bf16[16,64,512]{2,1,0:T(8,128)(2,1)} %norm_pack.1), calls=%async_computation | async-start | bytes 2097152 | tf_op jit(solution)/shard_map/all_to_all | solution.py:498
  38.7 15.0 %copy-start = (bf16[2,4,64,64]{3,2,1,0:T(8,128)(2,1)S(1)}, bf16[2,4,64,64]{3,2,1,0:T(8,128)(2,1)}, u32[]{:S(2)}) copy-start(bf16[2,4,64,64]{3,2,1,0:T(8,128)(2,1)} %first_w.1) | copy-start | bytes 196612
  38.7 15.0 %copy-start.1 = (bf16[2,4,64,64]{3,2,1,0:T(8,128)(2,1)S(1)}, bf16[2,4,64,64]{3,2,1,0:T(8,128)(2,1)}, u32[]{:S(2)}) copy-start(bf16[2,4,64,64]{3,2,1,0:T(8,128)(2,1)} %second_w.1) | copy-start | bytes 196612
  38.8 45.4 %all-to-all-start.1 = ((bf16[128,8,512]{2,1,0:T(8,128)(2,1)}), bf16[128,8,512]{2,1,0:T(8,128)(2,1)S(1)}, u32[]{:S(2)}, u32[]{:S(2)}) async-start(bf16[128,8,512]{2,1,0:T(8,128)(2,1)} %bitcast.18), calls=%async_computation.1 | async-start | bytes 2097152 | tf_op jit(solution)/shard_map/all_to_all | solution.py:516
  60.6 29.2 %collective-permute-start = (bf16[64,256]{1,0:T(8,128)(2,1)S(1)}, bf16[64,256]{1,0:T(8,128)(2,1)S(1)}, u32[]{:S(2)}, u32[]{:S(2)}) collective-permute-start(bf16[64,256]{1,0:T(8,128)(2,1)S(1)} %get-tuple-element.44), channel_id=1, source_target_pairs={{0,16},{16,32},{32,48},{48,64},{64,80},{80,96},{96,112},{112,128},... | collective-permute-start | bytes 98312 | tf_op jit(solution)/shard_map/ppermute | solution.py:508
  62.7 27.2 %collective-permute-start.1 = (bf16[64,256]{1,0:T(8,128)(2,1)S(1)}, bf16[64,256]{1,0:T(8,128)(2,1)S(1)}, u32[]{:S(2)}, u32[]{:S(2)}) collective-permute-start(bf16[64,256]{1,0:T(8,128)(2,1)S(1)} %get-tuple-element.43), channel_id=1, source_target_pairs={{16,0},{32,16},{48,32},{64,48},{80,64},{96,80},{112,96},{128,112},... | collective-permute-start | bytes 98312 | tf_op jit(solution)/shard_map/ppermute | solution.py:509
  89.8 8.0 %copy-start.2 = (bf16[32,64,256]{2,1,0:T(8,128)(2,1)S(1)}, bf16[32,64,256]{2,1,0:T(8,128)(2,1)}, u32[]{:S(2)}) copy-start(bf16[32,64,256]{2,1,0:T(8,128)(2,1)} %home_norm.1.normed_ref) | copy-start | bytes 3145732
  89.9 8.5 %copy-start.3 = (bf16[64,256]{1,0:T(8,128)(2,1)}, bf16[64,256]{1,0:T(8,128)(2,1)S(1)}, u32[]{:S(2)}) copy-start(bf16[64,256]{1,0:T(8,128)(2,1)S(1)} %collective-permute-done.top_ref) | copy-start | bytes 98308
  89.9 8.5 %copy-start.4 = (bf16[64,256]{1,0:T(8,128)(2,1)}, bf16[64,256]{1,0:T(8,128)(2,1)S(1)}, u32[]{:S(2)}) copy-start(bf16[64,256]{1,0:T(8,128)(2,1)S(1)} %collective-permute-done.1.bottom_ref) | copy-start | bytes 98308
  89.9 38.3 %all-to-all-start.2 = ((bf16[128,8,512]{2,1,0:T(8,128)(2,1)}), bf16[128,8,512]{2,1,0:T(8,128)(2,1)S(1)}, u32[]{:S(2)}, u32[]{:S(2)}) async-start(bf16[128,8,512]{2,1,0:T(8,128)(2,1)} %bitcast.20), calls=%async_computation.2 | async-start | bytes 2097152 | tf_op jit(solution)/shard_map/all_to_all | solution.py:521
  98.5 22.8 %collective-permute-start.2 = (bf16[34,256]{1,0:T(8,128)(2,1)S(1)}, bf16[34,256]{1,0:T(8,128)(2,1)S(1)}, u32[]{:S(2)}, u32[]{:S(2)}) collective-permute-start(bf16[34,256]{1,0:T(8,128)(2,1)S(1)} %pad_maximum_fusion), channel_id=1, source_target_pairs={{0,1},{1,2},{2,3},{3,4},{4,5},{5,6},{6,7},{7,8},{8,9},{9,10},{10,1... | collective-permute-start | bytes 52232 | tf_op jit(solution)/shard_map/ppermute | solution.py:508
  101.0 20.3 %collective-permute-start.3 = (bf16[34,256]{1,0:T(8,128)(2,1)S(1)}, bf16[34,256]{1,0:T(8,128)(2,1)S(1)}, u32[]{:S(2)}, u32[]{:S(2)}) collective-permute-start(bf16[34,256]{1,0:T(8,128)(2,1)S(1)} %pad_maximum_fusion.1), channel_id=1, source_target_pairs={{1,0},{2,1},{3,2},{4,3},{5,4},{6,5},{7,6},{8,7},{9,8},{10,9},{11,1... | collective-permute-start | bytes 52232 | tf_op jit(solution)/shard_map/ppermute | solution.py:509
  121.2 8.9 %copy-start.5 = (bf16[34,256]{1,0:T(8,128)(2,1)}, bf16[34,256]{1,0:T(8,128)(2,1)S(1)}, u32[]{:S(2)}) copy-start(bf16[34,256]{1,0:T(8,128)(2,1)S(1)} %collective-permute-done.2.left_ref) | copy-start | bytes 52228
  121.2 8.9 %copy-start.6 = (bf16[34,256]{1,0:T(8,128)(2,1)}, bf16[34,256]{1,0:T(8,128)(2,1)S(1)}, u32[]{:S(2)}) copy-start(bf16[34,256]{1,0:T(8,128)(2,1)S(1)} %collective-permute-done.3.right_ref) | copy-start | bytes 52228
  130.2 6.3 %copy-start.7 = (f32[3,3,256]{2,1,0:T(4,128)S(1)}, f32[3,3,256]{2,1,0:T(4,128)}, u32[]{:S(2)}) copy-start(f32[3,3,256]{2,1,0:T(4,128)} %param.9) | copy-start | bytes 27652
  130.2 31.2 %all-to-all-start.3 = ((bf16[16,64,512]{2,1,0:T(8,128)(2,1)}), bf16[16,64,512]{2,1,0:T(8,128)(2,1)S(1)}, u32[]{:S(2)}, u32[]{:S(2)}) async-start(bf16[16,64,512]{2,1,0:T(8,128)(2,1)} %bitcast.19), calls=%async_computation.3 | async-start | bytes 2097152 | tf_op jit(solution)/shard_map/all_to_all | solution.py:530

commit v11 on v10

--- a/solution.py
+++ b/solution.py
@@ -509,8 +509,8 @@
         after = lax.ppermute(first, axis, [((i + 1) % n, i) for i in range(n)])
         return before, after
 
-    normed = home_norm(patches, norm_gain)
-    lines, normed = lax.optimization_barrier((lines, normed))
+    lines, here = lax.optimization_barrier((lines, patches))
+    normed = home_norm(here, norm_gain)
 
     freqs = columns(fwd_w, lines)
     whole = lax.all_to_all(freqs.reshape(128, 8, 512), ("row", "yl"), 0, 0, tiled=True)

time: 164 us -> 164 us (level)
    all_to_all x1, waiting for transfers between devices: 18.9 us -> 23.1 us  [local(): lax.all_to_all(packed, ('yl', 'x'), 0, 0, tiled=True).reshape(1024, 512)]
    all_to_all x1, waiting for transfers between devices: 11.9 us -> 7.73 us  [local(): lax.all_to_all(freqs.reshape(128, 8, 512), ('row', 'yl'), 0, 0, tiled=True)]
where the time goes in v11:
time: 164 us; the launch traced here: 163 us
  waiting for transfers between devices  71.7 us (44%)
  starting transfers between devices  58 us (35%)
  Pallas kernels  30.6 us (19%)
  local copies, waits for them, and re-layouts  2.02 us (1%)
    all_to_all x1, waiting for transfers between devices, local(): lax.all_to_all(packed, ('yl', 'x'), 0, 0, tiled=True).reshape(1024, 512)  23.1 us
    all_to_all x1, waiting for transfers between devices, local(): lax.all_to_all(spectral.reshape(16, 64, 512), ('yl', 'x'), 0, 0, tiled=True)  20.3 us
    ppermute x2, starting transfers between devices, neighbours(): after = lax.ppermute(first, axis, [((i + 1) % n, i) for i in range(n)])  15 us
    all_to_all x1, starting transfers between devices, local(): lax.all_to_all(freqs.reshape(128, 8, 512), ('row', 'yl'), 0, 0, tiled=True)  15 us
    ppermute x2, waiting for transfers between devices, neighbours(): before = lax.ppermute(last, axis, [(i, (i + 1) % n) for i in range(n)])  13.7 us
    all_to_all x1, starting transfers between devices, local(): lax.all_to_all(packed, ('yl', 'x'), 0, 0, tiled=True).reshape(1024, 512)  9.3 us
    all_to_all x1, starting transfers between devices, local(): lax.all_to_all(filtered.reshape(128, 8, 512), ('row', 'yl'), 0, 0, tiled=...  7.9 us
    all_to_all x1, waiting for transfers between devices, local(): lax.all_to_all(freqs.reshape(128, 8, 512), ('row', 'yl'), 0, 0, tiled=True)  7.73 us
  transfers between devices with their start and end apart: 8, of which 5 were waited for; matrix products, arithmetic and copies ran while one was open for 1% of the time, Pallas kernels for 14%

profile of v11, /device:TPU:8, one launch (start us, length us, event | category | flops | bytes accessed | tf_op | source)
XLA Modules:
  0.0 162.8 jit_solution(10563670397370673918)
XLA Ops:
  0.0 3.2 %norm_pack.1 = bf16[16,64,512]{2,1,0:T(8,128)(2,1)} custom-call(bf16[32,64,256]{2,1,0:T(8,128)(2,1)} %x_ref.2, f32[1,256]{1,0:T(1,128)} %bitcast.21), custom_call_target="tpu_custom_call" | custom-call | tf_op jit(solution)/shard_map/norm_pack/pallas_call | solution.py:246
  3.2 9.3 %all-to-all-start = ((bf16[16,64,512]{2,1,0:T(8,128)(2,1)}), bf16[16,64,512]{2,1,0:T(8,128)(2,1)S(1)}, u32[]{:S(2)}, u32[]{:S(2)}) async-start(bf16[16,64,512]{2,1,0:T(8,128)(2,1)} %norm_pack.1), calls=%async_computation | async-start | bytes 2097152 | tf_op jit(solution)/shard_map/all_to_all | solution.py:498
  12.5 1.1 forward_columns_phases.1.table_ref
  13.7 23.1 %all-to-all-done = bf16[16,64,512]{2,1,0:T(8,128)(2,1)S(1)} async-done(((bf16[16,64,512]{2,1,0:T(8,128)(2,1)}), bf16[16,64,512]{2,1,0:T(8,128)(2,1)S(1)}, u32[]{:S(2)}, u32[]{:S(2)}) %all-to-all-start) | async-done | bytes 1048608 | tf_op jit(solution)/shard_map/all_to_all | solution.py:498
  36.8 1.9 %along_columns.2 = bf16[1024,512]{1,0:T(8,128)(2,1)} custom-call(bf16[1024,1024]{1,0:T(8,128)(2,1)S(1)} %forward_columns_phases.1.table_ref, bf16[1024,512]{1,0:T(8,128)(2,1)S(1)} %bitcast.16), custom_call_target="tpu_custom_call" | custom-call | flops 1073741824 | bytes 2097152 | tf_op jit(solution)/shard_map/along_columns/pallas_call | solution.py:323
  38.7 0.0 copy-start
  38.7 0.0 copy-start.1
  38.7 15.0 %all-to-all-start.1 = ((bf16[128,8,512]{2,1,0:T(8,128)(2,1)}), bf16[128,8,512]{2,1,0:T(8,128)(2,1)S(1)}, u32[]{:S(2)}, u32[]{:S(2)}) async-start(bf16[128,8,512]{2,1,0:T(8,128)(2,1)} %bitcast.18), calls=%async_computation.1 | async-start | bytes 2097152 | tf_op jit(solution)/shard_map/all_to_all | solution.py:516
  53.7 1.2 block_tables.1
  54.9 2.6 %backward_rows_phases.1.refs_1_.inv_any = bf16[1024,1024]{1,0:T(8,128)(2,1)} custom-call(), custom_call_target="tpu_custom_call" | custom-call | flops 8388608 | bytes 2097152 | tf_op jit(solution)/shard_map/backward_rows_phases/pallas_call | solution.py:109
  57.6 2.3 %forward_rows_phases.1 = (bf16[1024,1024]{1,0:T(8,128)(2,1)S(1)}, f32[128,512]{1,0:T(8,128)}, f32[128,512]{1,0:T(8,128)}) custom-call(bf16[256,256]{1,0:T(8,128)(2,1)} %get-tuple-element.24.refs_0_.second_any, bf16[1024,1024]{1,0:T(8,128)(2,1)} %backward_rows_phases.1.refs_1_.inv_any), custom_call_target="tpu_custom_call" | custom-call | flops 8388608 | bytes 2097152 | tf_op jit(solution)/shard_map/forward_rows_phases/pallas_call | solution.py:109
  59.8 4.2 %home_norm.1.normed_ref = bf16[32,64,256]{2,1,0:T(8,128)(2,1)} custom-call(bf16[32,64,256]{2,1,0:T(8,128)(2,1)} %x_ref.2, f32[1,256]{1,0:T(1,128)} %bitcast.22), custom_call_target="tpu_custom_call" | custom-call | flops 16777216 | bytes 2097152 | tf_op jit(solution)/shard_map/home_norm/pallas_call | solution.py:233
  64.0 0.8 slice_bitcast_fusion
  64.8 2.0 %collective-permute-start = (bf16[64,256]{1,0:T(8,128)(2,1)S(1)}, bf16[64,256]{1,0:T(8,128)(2,1)S(1)}, u32[]{:S(2)}, u32[]{:S(2)}) collective-permute-start(bf16[64,256]{1,0:T(8,128)(2,1)S(1)} %get-tuple-element.44), channel_id=1, source_target_pairs={{0,16},{16,32},{32,48},{48,64},{64,80},{80,96},{96,112},{112,128},... | collective-permute-start | bytes 98312 | tf_op jit(solution)/shard_map/ppermute | solution.py:508
  66.8 9.5 %collective-permute-start.1 = (bf16[64,256]{1,0:T(8,128)(2,1)S(1)}, bf16[64,256]{1,0:T(8,128)(2,1)S(1)}, u32[]{:S(2)}, u32[]{:S(2)}) collective-permute-start(bf16[64,256]{1,0:T(8,128)(2,1)S(1)} %get-tuple-element.43), channel_id=1, source_target_pairs={{16,0},{32,16},{48,32},{64,48},{80,64},{96,80},{112,96},{128,112},... | collective-permute-start | bytes 98312 | tf_op jit(solution)/shard_map/ppermute | solution.py:509
  76.4 7.7 %all-to-all-done.1 = bf16[128,8,512]{2,1,0:T(8,128)(2,1)S(1)} async-done(((bf16[128,8,512]{2,1,0:T(8,128)(2,1)}), bf16[128,8,512]{2,1,0:T(8,128)(2,1)S(1)}, u32[]{:S(2)}, u32[]{:S(2)}) %all-to-all-start.1) | async-done | bytes 1048608 | tf_op jit(solution)/shard_map/all_to_all | solution.py:516
  84.1 5.7 %filter_rows.1 = bf16[1024,512]{1,0:T(8,128)(2,1)} custom-call(bf16[1024,512]{1,0:T(8,128)(2,1)S(1)} %bitcast.17, bf16[1024,1024]{1,0:T(8,128)(2,1)S(1)} %get-tuple-element.25.fwd, f32[128,512]{1,0:T(8,128)} %get-tuple-element.26.cos_any, f32[128,512]{1,0:T(8,128)} %get-tuple-element.27.sin_any, bf16[1024,256]{1,0:T(8,128)(2,1)} %get-tuple-element.28.first_any, ...), custom_call_target="tpu_custom_call" | custom-call | flops 3221225472 | bytes 2097152 | tf_op jit(solution)/shard_map/filter_rows/pallas_call | solution.py:471
  89.8 0.0 copy-start.2
  89.9 7.9 %all-to-all-start.2 = ((bf16[128,8,512]{2,1,0:T(8,128)(2,1)}), bf16[128,8,512]{2,1,0:T(8,128)(2,1)S(1)}, u32[]{:S(2)}, u32[]{:S(2)}) async-start(bf16[128,8,512]{2,1,0:T(8,128)(2,1)} %bitcast.20), calls=%async_computation.2 | async-start | bytes 2097152 | tf_op jit(solution)/shard_map/all_to_all | solution.py:521
  97.8 0.6 copy.6
  98.5 2.5 %collective-permute-start.2 = (bf16[34,256]{1,0:T(8,128)(2,1)S(1)}, bf16[34,256]{1,0:T(8,128)(2,1)S(1)}, u32[]{:S(2)}, u32[]{:S(2)}) collective-permute-start(bf16[34,256]{1,0:T(8,128)(2,1)S(1)} %pad_maximum_fusion), channel_id=1, source_target_pairs={{0,1},{1,2},{2,3},{3,4},{4,5},{5,6},{6,7},{7,8},{8,9},{9,10},{10,1... | collective-permute-start | bytes 52232 | tf_op jit(solution)/shard_map/ppermute | solution.py:508
  101.0 5.5 %collective-permute-start.3 = (bf16[34,256]{1,0:T(8,128)(2,1)S(1)}, bf16[34,256]{1,0:T(8,128)(2,1)S(1)}, u32[]{:S(2)}, u32[]{:S(2)}) collective-permute-start(bf16[34,256]{1,0:T(8,128)(2,1)S(1)} %pad_maximum_fusion.1), channel_id=1, source_target_pairs={{1,0},{2,1},{3,2},{4,3},{5,4},{6,5},{7,6},{8,7},{9,8},{10,9},{11,1... | collective-permute-start | bytes 52232 | tf_op jit(solution)/shard_map/ppermute | solution.py:509
  106.5 1.1 backward_columns_phases.1.table_ref
  107.6 13.6 %collective-permute-done.2.left_ref = bf16[34,256]{1,0:T(8,128)(2,1)S(1)} collective-permute-done((bf16[34,256]{1,0:T(8,128)(2,1)S(1)}, bf16[34,256]{1,0:T(8,128)(2,1)S(1)}, u32[]{:S(2)}, u32[]{:S(2)}) %collective-permute-start.2) | collective-permute-done | bytes 17440 | tf_op jit(solution)/shard_map/ppermute | solution.py:508
  121.2 7.0 %all-to-all-done.2 = bf16[128,8,512]{2,1,0:T(8,128)(2,1)S(1)} async-done(((bf16[128,8,512]{2,1,0:T(8,128)(2,1)}), bf16[128,8,512]{2,1,0:T(8,128)(2,1)S(1)}, u32[]{:S(2)}, u32[]{:S(2)}) %all-to-all-start.2) | async-done | bytes 1048608 | tf_op jit(solution)/shard_map/all_to_all | solution.py:521
  128.2 1.9 %along_columns.3 = bf16[1024,512]{1,0:T(8,128)(2,1)} custom-call(bf16[1024,1024]{1,0:T(8,128)(2,1)S(1)} %backward_columns_phases.1.table_ref, bf16[1024,512]{1,0:T(8,128)(2,1)S(1)} %bitcast.15), custom_call_target="tpu_custom_call" | custom-call | flops 1073741824 | bytes 2097152 | tf_op jit(solution)/shard_map/along_columns/pallas_call | solution.py:323
  130.2 0.0 copy-start.7
  130.2 6.3 %all-to-all-start.3 = ((bf16[16,64,512]{2,1,0:T(8,128)(2,1)}), bf16[16,64,512]{2,1,0:T(8,128)(2,1)S(1)}, u32[]{:S(2)}, u32[]{:S(2)}) async-start(bf16[16,64,512]{2,1,0:T(8,128)(2,1)} %bitcast.19), calls=%async_computation.3 | async-start | bytes 2097152 | tf_op jit(solution)/shard_map/all_to_all | solution.py:530
  136.5 0.6 reshape.31.taps_ref
  137.1 4.1 %stencil.1.base_ref = f32[32,64,256]{2,1,0:T(8,128)S(1)} custom-call(bf16[32,64,256]{2,1,0:T(8,128)(2,1)} %x_ref.2, bf16[32,64,256]{2,1,0:T(8,128)(2,1)} %home_norm.1.normed_ref, bf16[64,256]{1,0:T(8,128)(2,1)} %copy-done.3, bf16[64,256]{1,0:T(8,128)(2,1)} %copy-done.4, bf16[34,256]{1,0:T(8,128)(2,1)} %copy-done.5, bf16[34,256]{1,0:T(8,128)(2,1)} %copy-done.6, ...), custom_call_target="tpu_custom_call" | custom-call | flops 16777216 | bytes 4194304 | tf_op jit(solution)/shard_map/stencil/pallas_call | solution.py:371
  141.1 20.3 %all-to-all-done.3.home_ref = bf16[16,64,512]{2,1,0:T(8,128)(2,1)S(1)} async-done(((bf16[16,64,512]{2,1,0:T(8,128)(2,1)}), bf16[16,64,512]{2,1,0:T(8,128)(2,1)S(1)}, u32[]{:S(2)}, u32[]{:S(2)}) %all-to-all-start.3) | async-done | bytes 1048608 | tf_op jit(solution)/shard_map/all_to_all | solution.py:530
  161.4 1.2 unpack_add.1
  (19 shorter events, 0.1 us)
Async XLA Ops:
  3.2 33.5 %all-to-all-start = ((bf16[16,64,512]{2,1,0:T(8,128)(2,1)}), bf16[16,64,512]{2,1,0:T(8,128)(2,1)S(1)}, u32[]{:S(2)}, u32[]{:S(2)}) async-start(bf16[16,64,512]{2,1,0:T(8,128)(2,1)} %norm_pack.1), calls=%async_computation | async-start | bytes 2097152 | tf_op jit(solution)/shard_map/all_to_all | solution.py:498
  38.7 15.0 %copy-start = (bf16[2,4,64,64]{3,2,1,0:T(8,128)(2,1)S(1)}, bf16[2,4,64,64]{3,2,1,0:T(8,128)(2,1)}, u32[]{:S(2)}) copy-start(bf16[2,4,64,64]{3,2,1,0:T(8,128)(2,1)} %first_w.1) | copy-start | bytes 196612
  38.7 15.0 %copy-start.1 = (bf16[2,4,64,64]{3,2,1,0:T(8,128)(2,1)S(1)}, bf16[2,4,64,64]{3,2,1,0:T(8,128)(2,1)}, u32[]{:S(2)}) copy-start(bf16[2,4,64,64]{3,2,1,0:T(8,128)(2,1)} %second_w.1) | copy-start | bytes 196612
  38.7 45.4 %all-to-all-start.1 = ((bf16[128,8,512]{2,1,0:T(8,128)(2,1)}), bf16[128,8,512]{2,1,0:T(8,128)(2,1)S(1)}, u32[]{:S(2)}, u32[]{:S(2)}) async-start(bf16[128,8,512]{2,1,0:T(8,128)(2,1)} %bitcast.18), calls=%async_computation.1 | async-start | bytes 2097152 | tf_op jit(solution)/shard_map/all_to_all | solution.py:516
  64.8 25.1 %collective-permute-start = (bf16[64,256]{1,0:T(8,128)(2,1)S(1)}, bf16[64,256]{1,0:T(8,128)(2,1)S(1)}, u32[]{:S(2)}, u32[]{:S(2)}) collective-permute-start(bf16[64,256]{1,0:T(8,128)(2,1)S(1)} %get-tuple-element.44), channel_id=1, source_target_pairs={{0,16},{16,32},{32,48},{48,64},{64,80},{80,96},{96,112},{112,128},... | collective-permute-start | bytes 98312 | tf_op jit(solution)/shard_map/ppermute | solution.py:508
  66.8 23.0 %collective-permute-start.1 = (bf16[64,256]{1,0:T(8,128)(2,1)S(1)}, bf16[64,256]{1,0:T(8,128)(2,1)S(1)}, u32[]{:S(2)}, u32[]{:S(2)}) collective-permute-start(bf16[64,256]{1,0:T(8,128)(2,1)S(1)} %get-tuple-element.43), channel_id=1, source_target_pairs={{16,0},{32,16},{48,32},{64,48},{80,64},{96,80},{112,96},{128,112},... | collective-permute-start | bytes 98312 | tf_op jit(solution)/shard_map/ppermute | solution.py:509
  89.8 8.0 %copy-start.2 = (bf16[32,64,256]{2,1,0:T(8,128)(2,1)S(1)}, bf16[32,64,256]{2,1,0:T(8,128)(2,1)}, u32[]{:S(2)}) copy-start(bf16[32,64,256]{2,1,0:T(8,128)(2,1)} %home_norm.1.normed_ref) | copy-start | bytes 3145732
  89.9 8.5 %copy-start.3 = (bf16[64,256]{1,0:T(8,128)(2,1)}, bf16[64,256]{1,0:T(8,128)(2,1)S(1)}, u32[]{:S(2)}) copy-start(bf16[64,256]{1,0:T(8,128)(2,1)S(1)} %collective-permute-done.top_ref) | copy-start | bytes 98308
  89.9 8.5 %copy-start.4 = (bf16[64,256]{1,0:T(8,128)(2,1)}, bf16[64,256]{1,0:T(8,128)(2,1)S(1)}, u32[]{:S(2)}) copy-start(bf16[64,256]{1,0:T(8,128)(2,1)S(1)} %collective-permute-done.1.bottom_ref) | copy-start | bytes 98308
  89.9 38.3 %all-to-all-start.2 = ((bf16[128,8,512]{2,1,0:T(8,128)(2,1)}), bf16[128,8,512]{2,1,0:T(8,128)(2,1)S(1)}, u32[]{:S(2)}, u32[]{:S(2)}) async-start(bf16[128,8,512]{2,1,0:T(8,128)(2,1)} %bitcast.20), calls=%async_computation.2 | async-start | bytes 2097152 | tf_op jit(solution)/shard_map/all_to_all | solution.py:521
  98.5 22.8 %collective-permute-start.2 = (bf16[34,256]{1,0:T(8,128)(2,1)S(1)}, bf16[34,256]{1,0:T(8,128)(2,1)S(1)}, u32[]{:S(2)}, u32[]{:S(2)}) collective-permute-start(bf16[34,256]{1,0:T(8,128)(2,1)S(1)} %pad_maximum_fusion), channel_id=1, source_target_pairs={{0,1},{1,2},{2,3},{3,4},{4,5},{5,6},{6,7},{7,8},{8,9},{9,10},{10,1... | collective-permute-start | bytes 52232 | tf_op jit(solution)/shard_map/ppermute | solution.py:508
  101.0 20.3 %collective-permute-start.3 = (bf16[34,256]{1,0:T(8,128)(2,1)S(1)}, bf16[34,256]{1,0:T(8,128)(2,1)S(1)}, u32[]{:S(2)}, u32[]{:S(2)}) collective-permute-start(bf16[34,256]{1,0:T(8,128)(2,1)S(1)} %pad_maximum_fusion.1), channel_id=1, source_target_pairs={{1,0},{2,1},{3,2},{4,3},{5,4},{6,5},{7,6},{8,7},{9,8},{10,9},{11,1... | collective-permute-start | bytes 52232 | tf_op jit(solution)/shard_map/ppermute | solution.py:509
  121.2 8.9 %copy-start.5 = (bf16[34,256]{1,0:T(8,128)(2,1)}, bf16[34,256]{1,0:T(8,128)(2,1)S(1)}, u32[]{:S(2)}) copy-start(bf16[34,256]{1,0:T(8,128)(2,1)S(1)} %collective-permute-done.2.left_ref) | copy-start | bytes 52228
  121.2 8.9 %copy-start.6 = (bf16[34,256]{1,0:T(8,128)(2,1)}, bf16[34,256]{1,0:T(8,128)(2,1)S(1)}, u32[]{:S(2)}) copy-start(bf16[34,256]{1,0:T(8,128)(2,1)S(1)} %collective-permute-done.3.right_ref) | copy-start | bytes 52228
  130.2 6.3 %copy-start.7 = (f32[3,3,256]{2,1,0:T(4,128)S(1)}, f32[3,3,256]{2,1,0:T(4,128)}, u32[]{:S(2)}) copy-start(f32[3,3,256]{2,1,0:T(4,128)} %param.9) | copy-start | bytes 27652
  130.2 31.2 %all-to-all-start.3 = ((bf16[16,64,512]{2,1,0:T(8,128)(2,1)}), bf16[16,64,512]{2,1,0:T(8,128)(2,1)S(1)}, u32[]{:S(2)}, u32[]{:S(2)}) async-start(bf16[16,64,512]{2,1,0:T(8,128)(2,1)} %bitcast.19), calls=%async_computation.3 | async-start | bytes 2097152 | tf_op jit(solution)/shard_map/all_to_all | solution.py:530

commit v12 on v11

--- a/solution.py
+++ b/solution.py
@@ -74,7 +74,7 @@
     return 64 * a * q0[:16], 8 * digit(b, 3, 3) * q0 + 256 * (ro - digit(b, 2, 1)), weight
 
 
-def table_kernel(phases, with_twiddles, stay, waited, *refs):
+def table_kernel(phases, stay, waited, *refs):
     refs = refs[waited:]
     out_ref, (ec, es, fc, fs) = refs[0], refs[-4:]
     steps = 16 if stay else 4
@@ -85,10 +85,6 @@
         ec[...], es[...] = cos_sin(ia)
         c, s = cos_sin(ib)
         fc[...], fs[...] = c * weight, s * weight
-        if with_twiddles:
-            lane = iota((128, 512), 1)
-            angle = iota((128, 512), 0) * ((lane >> 7) + 4 * digit(lane, 6, 1))
-            refs[1][...], refs[2][...] = cos_sin(angle)
 
     first = 0 if stay else steps * pl.program_id(0)
 
@@ -102,23 +98,20 @@
     lax.fori_loop(0, steps, step, 0)
 
 
-def table(space, phases, with_twiddles=False, after=()):
+def table(space, phases, after=()):
     stay = space == pltpu.VMEM
     whole = pl.BlockSpec(memory_space=pltpu.VMEM)
-    twiddle_spec = pl.BlockSpec((128, 512), lambda g: (0, 0))
-    out = pl.pallas_call(
-        functools.partial(table_kernel, phases, with_twiddles, stay, len(after)),
+    return pl.pallas_call(
+        functools.partial(table_kernel, phases, stay, len(after)),
         grid=(1,) if stay else (4,),
         in_specs=[pl.BlockSpec(memory_space=pltpu.HBM)] * len(after),
-        out_specs=[whole if stay else pl.BlockSpec((256, 1024), lambda g: (g, 0))]
-        + [twiddle_spec] * (2 * with_twiddles),
-        out_shape=[space((1024, 1024), BF16)] + [pltpu.HBM((128, 512), F32)] * (2 * with_twiddles),
+        out_specs=whole if stay else pl.BlockSpec((256, 1024), lambda g: (g, 0)),
+        out_shape=space((1024, 1024), BF16),
         scratch_shapes=[pltpu.VMEM((n, 1024), F32) for n in (16, 16, 64, 64)],
         cost_estimate=pl.CostEstimate(flops=2**23, bytes_accessed=2**21, transcendentals=0),
         compiler_params=pltpu.CompilerParams(vmem_limit_bytes=6 * MIB),
         name=phases.__name__,
     )(*[remaining(v) for v in after])
-    return out if with_twiddles else out[0]
 
 
 def blocks_kernel(first_w, second_w, first_ref, last_ref, second_ref, fc, fs, bc):
@@ -409,14 +402,12 @@
 
 
 def middle_kernel(
-    z, fwd, cos_any, sin_any, first_any, second_any, last_any, inv_any, out_any,
+    z, fwd, first_any, second_any, last_any, inv_any, out_any,
     cos_ref, sin_ref, first, second, last, inv, held, done, sems, fetch_sems,
 ):
     fetches = []
     for n, (src, dst) in enumerate(
         (
-            (cos_any, cos_ref),
-            (sin_any, sin_ref),
             (first_any, first),
             (second_any, second),
             (last_any, last),
@@ -425,13 +416,17 @@
     ):
         fetches.append(pltpu.make_async_copy(src, dst, fetch_sems.at[n]))
         fetches[-1].start()
+    lane = iota((128, 512), 1)
+    cos_ref[...], sin_ref[...] = cos_sin(
+        iota((128, 512), 0) * ((lane >> 7) + 4 * digit(lane, 6, 1))
+    )
     rows = 512 // CHUNKS
     groups = 8 // CHUNKS
     shape = (groups, 4, 16, 128)
     for m in range(CHUNKS):
         u = dot(fwd[2 * rows * m : 2 * rows * (m + 1), :], z[...])
         if m == 0:
-            for fetch in fetches[:4]:
+            for fetch in fetches[:2]:
                 fetch.wait()
 
         def twiddles(t):
@@ -450,7 +445,7 @@
             v = dot(jnp.tanh(beside(part)).astype(BF16), second[...])
             kept.append(jnp.where(v > 0.25, v - 0.25, jnp.where(v < -0.25, v + 0.25, 0.0 * v)))
         if m == 0:
-            fetches[4].wait()
+            fetches[2].wait()
         for t, part in enumerate(butterfly(kept, 1)):
             y = dot(beside(part).astype(BF16), last[256 * t : 256 * t + 256, :])
             yr, yi = y[:, :128].reshape(shape), y[:, 128:].reshape(shape)
@@ -462,15 +457,15 @@
             held[2 * rows * m + rows : 2 * rows * (m + 1), lanes] = (
                 (yi * c + yr * s).astype(BF16).reshape(rows, 128)
             )
-    fetches[5].wait()
+    fetches[3].wait()
     stream_dot(inv, held, done, out_any, sems)
 
 
-def middle(z, fwd, cos, sin, first, second, last, inv):
+def middle(z, fwd, first, second, last, inv):
     vmem, hbm = pl.BlockSpec(memory_space=pltpu.VMEM), pl.BlockSpec(memory_space=pltpu.HBM)
     return pl.pallas_call(
         middle_kernel,
-        in_specs=[vmem] * 2 + [hbm] * 6,
+        in_specs=[vmem] * 2 + [hbm] * 4,
         out_specs=hbm,
         out_shape=pltpu.HBM((1024, 512), BF16),
         scratch_shapes=[
@@ -483,13 +478,13 @@
             pltpu.VMEM((1024, 512), BF16),
             pltpu.VMEM((1024, 512), BF16),
             pltpu.SemaphoreType.DMA((3,)),
-            pltpu.SemaphoreType.DMA((6,)),
+            pltpu.SemaphoreType.DMA((4,)),
         ],
         cost_estimate=pl.CostEstimate(flops=3 * 2**30, bytes_accessed=2**21, transcendentals=2**19),
         compiler_params=pltpu.CompilerParams(vmem_limit_bytes=24 * MIB),
         name="filter_rows",
     )(
-        resident(z), resident(fwd), *[remaining(v) for v in (cos, sin, first, second, last, inv)]
+        resident(z), resident(fwd), *[remaining(v) for v in (first, second, last, inv)]
     )
 
 
@@ -501,7 +496,7 @@
     inv_w = table(pltpu.VMEM, backward_columns_phases)
     inv_h = table(pltpu.HBM, backward_rows_phases)
     first, last, second = block_tables(w_first, w_second)
-    fwd_h, cos, sin = table(pltpu.VMEM, forward_rows_phases, True, (second, inv_h))
+    fwd_h = table(pltpu.VMEM, forward_rows_phases, (second, inv_h))
 
     def neighbours(first, last, axis):
         n = lax.axis_size(axis)
@@ -516,7 +511,7 @@
     whole = lax.all_to_all(freqs.reshape(128, 8, 512), ("row", "yl"), 0, 0, tiled=True)
     top, bottom = neighbours(normed[0], normed[31], "row")
 
-    filtered = middle(whole.reshape(1024, 512), fwd_h, cos, sin, first, second, last, inv_h)
+    filtered = middle(whole.reshape(1024, 512), fwd_h, first, second, last, inv_h)
     filtered, top, bottom, normed = lax.optimization_barrier((filtered, top, bottom, normed))
     back = lax.all_to_all(filtered.reshape(128, 8, 512), ("row", "yl"), 0, 0, tiled=True)
     sides = [

time: 164 us -> 163 us (level)
  transfers between devices with their start and end apart: 8 -> 8, of which waited for: 5 -> 5; matrix products, arithmetic and copies ran while one was open for 1% -> 1% of each run, Pallas kernels for 14% -> 13%
where the time goes in v12:
time: 163 us
  waiting for transfers between devices  72.9 us (45%)
  starting transfers between devices  58 us (36%)
  Pallas kernels  29.3 us (18%)
  local copies, waits for them, and re-layouts  2.03 us (1%)
    all_to_all x1, waiting for transfers between devices, local(): lax.all_to_all(packed, ('yl', 'x'), 0, 0, tiled=True).reshape(1024, 512)  23.1 us
    all_to_all x1, waiting for transfers between devices, local(): lax.all_to_all(spectral.reshape(16, 64, 512), ('yl', 'x'), 0, 0, tiled=True)  20.3 us
    ppermute x2, starting transfers between devices, neighbours(): after = lax.ppermute(first, axis, [((i + 1) % n, i) for i in range(n)])  15 us
    all_to_all x1, starting transfers between devices, local(): lax.all_to_all(freqs.reshape(128, 8, 512), ('row', 'yl'), 0, 0, tiled=True)  15 us
    ppermute x2, waiting for transfers between devices, neighbours(): before = lax.ppermute(last, axis, [(i, (i + 1) % n) for i in range(n)])  13.7 us
    all_to_all x1, starting transfers between devices, local(): lax.all_to_all(packed, ('yl', 'x'), 0, 0, tiled=True).reshape(1024, 512)  9.3 us
    all_to_all x1, waiting for transfers between devices, local(): lax.all_to_all(freqs.reshape(128, 8, 512), ('row', 'yl'), 0, 0, tiled=True)  8.88 us
    all_to_all x1, starting transfers between devices, local(): lax.all_to_all(filtered.reshape(128, 8, 512), ('row', 'yl'), 0, 0, tiled=...  7.89 us
  transfers between devices with their start and end apart: 8, of which 5 were waited for; matrix products, arithmetic and copies ran while one was open for 1% of the time, Pallas kernels for 13%

profile of v12, /device:TPU:8, one launch (start us, length us, event | category | flops | bytes accessed | tf_op | source)
XLA Modules:
  0.0 162.6 jit_solution(13753723984124642202)
XLA Ops:
  0.0 3.2 %norm_pack.1 = bf16[16,64,512]{2,1,0:T(8,128)(2,1)} custom-call(bf16[32,64,256]{2,1,0:T(8,128)(2,1)} %x_ref.2, f32[1,256]{1,0:T(1,128)} %bitcast.21), custom_call_target="tpu_custom_call" | custom-call | tf_op jit(solution)/shard_map/norm_pack/pallas_call | solution.py:239
  3.2 9.3 %all-to-all-start = ((bf16[16,64,512]{2,1,0:T(8,128)(2,1)}), bf16[16,64,512]{2,1,0:T(8,128)(2,1)S(1)}, u32[]{:S(2)}, u32[]{:S(2)}) async-start(bf16[16,64,512]{2,1,0:T(8,128)(2,1)} %norm_pack.1), calls=%async_computation | async-start | bytes 2097152 | tf_op jit(solution)/shard_map/all_to_all | solution.py:493
  12.5 1.1 forward_columns_phases.1.table_ref
  13.7 23.1 %all-to-all-done = bf16[16,64,512]{2,1,0:T(8,128)(2,1)S(1)} async-done(((bf16[16,64,512]{2,1,0:T(8,128)(2,1)}), bf16[16,64,512]{2,1,0:T(8,128)(2,1)S(1)}, u32[]{:S(2)}, u32[]{:S(2)}) %all-to-all-start) | async-done | bytes 1048608 | tf_op jit(solution)/shard_map/all_to_all | solution.py:493
  36.8 1.9 %along_columns.2 = bf16[1024,512]{1,0:T(8,128)(2,1)} custom-call(bf16[1024,1024]{1,0:T(8,128)(2,1)S(1)} %forward_columns_phases.1.table_ref, bf16[1024,512]{1,0:T(8,128)(2,1)S(1)} %bitcast.16), custom_call_target="tpu_custom_call" | custom-call | flops 1073741824 | bytes 2097152 | tf_op jit(solution)/shard_map/along_columns/pallas_call | solution.py:316
  38.7 0.0 copy-start
  38.7 0.0 copy-start.1
  38.7 15.0 %all-to-all-start.1 = ((bf16[128,8,512]{2,1,0:T(8,128)(2,1)}), bf16[128,8,512]{2,1,0:T(8,128)(2,1)S(1)}, u32[]{:S(2)}, u32[]{:S(2)}) async-start(bf16[128,8,512]{2,1,0:T(8,128)(2,1)} %bitcast.18), calls=%async_computation.1 | async-start | bytes 2097152 | tf_op jit(solution)/shard_map/all_to_all | solution.py:511
  53.7 1.2 block_tables.1
  54.9 2.6 %backward_rows_phases.1.refs_1_.inv_any = bf16[1024,1024]{1,0:T(8,128)(2,1)} custom-call(), custom_call_target="tpu_custom_call" | custom-call | flops 8388608 | bytes 2097152 | tf_op jit(solution)/shard_map/backward_rows_phases/pallas_call | solution.py:104
  57.5 1.1 forward_rows_phases.1.fwd
  58.7 4.2 %home_norm.1.normed_ref = bf16[32,64,256]{2,1,0:T(8,128)(2,1)} custom-call(bf16[32,64,256]{2,1,0:T(8,128)(2,1)} %x_ref.2, f32[1,256]{1,0:T(1,128)} %bitcast.22), custom_call_target="tpu_custom_call" | custom-call | flops 16777216 | bytes 2097152 | tf_op jit(solution)/shard_map/home_norm/pallas_call | solution.py:226
  62.9 0.8 slice_bitcast_fusion
  63.6 2.0 %collective-permute-start = (bf16[64,256]{1,0:T(8,128)(2,1)S(1)}, bf16[64,256]{1,0:T(8,128)(2,1)S(1)}, u32[]{:S(2)}, u32[]{:S(2)}) collective-permute-start(bf16[64,256]{1,0:T(8,128)(2,1)S(1)} %get-tuple-element.38), channel_id=1, source_target_pairs={{0,16},{16,32},{32,48},{48,64},{64,80},{80,96},{96,112},{112,128},... | collective-permute-start | bytes 98312 | tf_op jit(solution)/shard_map/ppermute | solution.py:503
  65.7 9.5 %collective-permute-start.1 = (bf16[64,256]{1,0:T(8,128)(2,1)S(1)}, bf16[64,256]{1,0:T(8,128)(2,1)S(1)}, u32[]{:S(2)}, u32[]{:S(2)}) collective-permute-start(bf16[64,256]{1,0:T(8,128)(2,1)S(1)} %get-tuple-element.37), channel_id=1, source_target_pairs={{16,0},{32,16},{48,32},{64,48},{80,64},{96,80},{112,96},{128,112},... | collective-permute-start | bytes 98312 | tf_op jit(solution)/shard_map/ppermute | solution.py:504
  75.2 8.9 %all-to-all-done.1 = bf16[128,8,512]{2,1,0:T(8,128)(2,1)S(1)} async-done(((bf16[128,8,512]{2,1,0:T(8,128)(2,1)}), bf16[128,8,512]{2,1,0:T(8,128)(2,1)S(1)}, u32[]{:S(2)}, u32[]{:S(2)}) %all-to-all-start.1) | async-done | bytes 1048608 | tf_op jit(solution)/shard_map/all_to_all | solution.py:511
  84.1 5.6 %filter_rows.1 = bf16[1024,512]{1,0:T(8,128)(2,1)} custom-call(bf16[1024,512]{1,0:T(8,128)(2,1)S(1)} %bitcast.17, bf16[1024,1024]{1,0:T(8,128)(2,1)S(1)} %forward_rows_phases.1.fwd, bf16[1024,256]{1,0:T(8,128)(2,1)} %get-tuple-element.22.first_any, bf16[256,256]{1,0:T(8,128)(2,1)} %get-tuple-element.21.refs_0_.second_any, ...), custom_call_target="tpu_custom_call" | custom-call | flops 3221225472 | bytes 2097152 | tf_op jit(solution)/shard_map/filter_rows/pallas_call | solution.py:466
  89.7 0.0 copy-start.2
  89.8 7.9 %all-to-all-start.2 = ((bf16[128,8,512]{2,1,0:T(8,128)(2,1)}), bf16[128,8,512]{2,1,0:T(8,128)(2,1)S(1)}, u32[]{:S(2)}, u32[]{:S(2)}) async-start(bf16[128,8,512]{2,1,0:T(8,128)(2,1)} %bitcast.20), calls=%async_computation.2 | async-start | bytes 2097152 | tf_op jit(solution)/shard_map/all_to_all | solution.py:516
  97.7 0.6 copy.6
  98.3 2.5 %collective-permute-start.2 = (bf16[34,256]{1,0:T(8,128)(2,1)S(1)}, bf16[34,256]{1,0:T(8,128)(2,1)S(1)}, u32[]{:S(2)}, u32[]{:S(2)}) collective-permute-start(bf16[34,256]{1,0:T(8,128)(2,1)S(1)} %pad_maximum_fusion), channel_id=1, source_target_pairs={{0,1},{1,2},{2,3},{3,4},{4,5},{5,6},{6,7},{7,8},{8,9},{9,10},{10,1... | collective-permute-start | bytes 52232 | tf_op jit(solution)/shard_map/ppermute | solution.py:503
  100.8 5.5 %collective-permute-start.3 = (bf16[34,256]{1,0:T(8,128)(2,1)S(1)}, bf16[34,256]{1,0:T(8,128)(2,1)S(1)}, u32[]{:S(2)}, u32[]{:S(2)}) collective-permute-start(bf16[34,256]{1,0:T(8,128)(2,1)S(1)} %pad_maximum_fusion.1), channel_id=1, source_target_pairs={{1,0},{2,1},{3,2},{4,3},{5,4},{6,5},{7,6},{8,7},{9,8},{10,9},{11,1... | collective-permute-start | bytes 52232 | tf_op jit(solution)/shard_map/ppermute | solution.py:504
  106.3 1.1 backward_columns_phases.1.table_ref
  107.4 13.6 %collective-permute-done.2.left_ref = bf16[34,256]{1,0:T(8,128)(2,1)S(1)} collective-permute-done((bf16[34,256]{1,0:T(8,128)(2,1)S(1)}, bf16[34,256]{1,0:T(8,128)(2,1)S(1)}, u32[]{:S(2)}, u32[]{:S(2)}) %collective-permute-start.2) | collective-permute-done | bytes 17440 | tf_op jit(solution)/shard_map/ppermute | solution.py:503
  121.1 7.0 %all-to-all-done.2 = bf16[128,8,512]{2,1,0:T(8,128)(2,1)S(1)} async-done(((bf16[128,8,512]{2,1,0:T(8,128)(2,1)}), bf16[128,8,512]{2,1,0:T(8,128)(2,1)S(1)}, u32[]{:S(2)}, u32[]{:S(2)}) %all-to-all-start.2) | async-done | bytes 1048608 | tf_op jit(solution)/shard_map/all_to_all | solution.py:516
  128.1 1.9 %along_columns.3 = bf16[1024,512]{1,0:T(8,128)(2,1)} custom-call(bf16[1024,1024]{1,0:T(8,128)(2,1)S(1)} %backward_columns_phases.1.table_ref, bf16[1024,512]{1,0:T(8,128)(2,1)S(1)} %bitcast.15), custom_call_target="tpu_custom_call" | custom-call | flops 1073741824 | bytes 2097152 | tf_op jit(solution)/shard_map/along_columns/pallas_call | solution.py:316
  130.0 0.0 copy-start.7
  130.0 6.3 %all-to-all-start.3 = ((bf16[16,64,512]{2,1,0:T(8,128)(2,1)}), bf16[16,64,512]{2,1,0:T(8,128)(2,1)S(1)}, u32[]{:S(2)}, u32[]{:S(2)}) async-start(bf16[16,64,512]{2,1,0:T(8,128)(2,1)} %bitcast.19), calls=%async_computation.3 | async-start | bytes 2097152 | tf_op jit(solution)/shard_map/all_to_all | solution.py:525
  136.3 0.6 reshape.31.taps_ref
  136.9 4.1 %stencil.1.base_ref = f32[32,64,256]{2,1,0:T(8,128)S(1)} custom-call(bf16[32,64,256]{2,1,0:T(8,128)(2,1)} %x_ref.2, bf16[32,64,256]{2,1,0:T(8,128)(2,1)} %home_norm.1.normed_ref, bf16[64,256]{1,0:T(8,128)(2,1)} %copy-done.3, bf16[64,256]{1,0:T(8,128)(2,1)} %copy-done.4, bf16[34,256]{1,0:T(8,128)(2,1)} %copy-done.5, bf16[34,256]{1,0:T(8,128)(2,1)} %copy-done.6, ...), custom_call_target="tpu_custom_call" | custom-call | flops 16777216 | bytes 4194304 | tf_op jit(solution)/shard_map/stencil/pallas_call | solution.py:364
  141.0 20.3 %all-to-all-done.3.home_ref = bf16[16,64,512]{2,1,0:T(8,128)(2,1)S(1)} async-done(((bf16[16,64,512]{2,1,0:T(8,128)(2,1)}), bf16[16,64,512]{2,1,0:T(8,128)(2,1)S(1)}, u32[]{:S(2)}, u32[]{:S(2)}) %all-to-all-start.3) | async-done | bytes 1048608 | tf_op jit(solution)/shard_map/all_to_all | solution.py:525
  161.2 1.2 unpack_add.1
  (19 shorter events, 0.1 us)
Async XLA Ops:
  3.2 33.5 %all-to-all-start = ((bf16[16,64,512]{2,1,0:T(8,128)(2,1)}), bf16[16,64,512]{2,1,0:T(8,128)(2,1)S(1)}, u32[]{:S(2)}, u32[]{:S(2)}) async-start(bf16[16,64,512]{2,1,0:T(8,128)(2,1)} %norm_pack.1), calls=%async_computation | async-start | bytes 2097152 | tf_op jit(solution)/shard_map/all_to_all | solution.py:493
  38.7 15.0 %copy-start = (bf16[2,4,64,64]{3,2,1,0:T(8,128)(2,1)S(1)}, bf16[2,4,64,64]{3,2,1,0:T(8,128)(2,1)}, u32[]{:S(2)}) copy-start(bf16[2,4,64,64]{3,2,1,0:T(8,128)(2,1)} %first_w.1) | copy-start | bytes 196612
  38.7 15.0 %copy-start.1 = (bf16[2,4,64,64]{3,2,1,0:T(8,128)(2,1)S(1)}, bf16[2,4,64,64]{3,2,1,0:T(8,128)(2,1)}, u32[]{:S(2)}) copy-start(bf16[2,4,64,64]{3,2,1,0:T(8,128)(2,1)} %second_w.1) | copy-start | bytes 196612
  38.7 45.4 %all-to-all-start.1 = ((bf16[128,8,512]{2,1,0:T(8,128)(2,1)}), bf16[128,8,512]{2,1,0:T(8,128)(2,1)S(1)}, u32[]{:S(2)}, u32[]{:S(2)}) async-start(bf16[128,8,512]{2,1,0:T(8,128)(2,1)} %bitcast.18), calls=%async_computation.1 | async-start | bytes 2097152 | tf_op jit(solution)/shard_map/all_to_all | solution.py:511
  63.6 26.1 %collective-permute-start = (bf16[64,256]{1,0:T(8,128)(2,1)S(1)}, bf16[64,256]{1,0:T(8,128)(2,1)S(1)}, u32[]{:S(2)}, u32[]{:S(2)}) collective-permute-start(bf16[64,256]{1,0:T(8,128)(2,1)S(1)} %get-tuple-element.38), channel_id=1, source_target_pairs={{0,16},{16,32},{32,48},{48,64},{64,80},{80,96},{96,112},{112,128},... | collective-permute-start | bytes 98312 | tf_op jit(solution)/shard_map/ppermute | solution.py:503
  65.7 24.1 %collective-permute-start.1 = (bf16[64,256]{1,0:T(8,128)(2,1)S(1)}, bf16[64,256]{1,0:T(8,128)(2,1)S(1)}, u32[]{:S(2)}, u32[]{:S(2)}) collective-permute-start(bf16[64,256]{1,0:T(8,128)(2,1)S(1)} %get-tuple-element.37), channel_id=1, source_target_pairs={{16,0},{32,16},{48,32},{64,48},{80,64},{96,80},{112,96},{128,112},... | collective-permute-start | bytes 98312 | tf_op jit(solution)/shard_map/ppermute | solution.py:504
  89.7 8.0 %copy-start.2 = (bf16[32,64,256]{2,1,0:T(8,128)(2,1)S(1)}, bf16[32,64,256]{2,1,0:T(8,128)(2,1)}, u32[]{:S(2)}) copy-start(bf16[32,64,256]{2,1,0:T(8,128)(2,1)} %home_norm.1.normed_ref) | copy-start | bytes 3145732
  89.7 8.5 %copy-start.3 = (bf16[64,256]{1,0:T(8,128)(2,1)}, bf16[64,256]{1,0:T(8,128)(2,1)S(1)}, u32[]{:S(2)}) copy-start(bf16[64,256]{1,0:T(8,128)(2,1)S(1)} %collective-permute-done.top_ref) | copy-start | bytes 98308
  89.8 8.5 %copy-start.4 = (bf16[64,256]{1,0:T(8,128)(2,1)}, bf16[64,256]{1,0:T(8,128)(2,1)S(1)}, u32[]{:S(2)}) copy-start(bf16[64,256]{1,0:T(8,128)(2,1)S(1)} %collective-permute-done.1.bottom_ref) | copy-start | bytes 98308
  89.8 38.3 %all-to-all-start.2 = ((bf16[128,8,512]{2,1,0:T(8,128)(2,1)}), bf16[128,8,512]{2,1,0:T(8,128)(2,1)S(1)}, u32[]{:S(2)}, u32[]{:S(2)}) async-start(bf16[128,8,512]{2,1,0:T(8,128)(2,1)} %bitcast.20), calls=%async_computation.2 | async-start | bytes 2097152 | tf_op jit(solution)/shard_map/all_to_all | solution.py:516
  98.3 22.8 %collective-permute-start.2 = (bf16[34,256]{1,0:T(8,128)(2,1)S(1)}, bf16[34,256]{1,0:T(8,128)(2,1)S(1)}, u32[]{:S(2)}, u32[]{:S(2)}) collective-permute-start(bf16[34,256]{1,0:T(8,128)(2,1)S(1)} %pad_maximum_fusion), channel_id=1, source_target_pairs={{0,1},{1,2},{2,3},{3,4},{4,5},{5,6},{6,7},{7,8},{8,9},{9,10},{10,1... | collective-permute-start | bytes 52232 | tf_op jit(solution)/shard_map/ppermute | solution.py:503
  100.8 20.3 %collective-permute-start.3 = (bf16[34,256]{1,0:T(8,128)(2,1)S(1)}, bf16[34,256]{1,0:T(8,128)(2,1)S(1)}, u32[]{:S(2)}, u32[]{:S(2)}) collective-permute-start(bf16[34,256]{1,0:T(8,128)(2,1)S(1)} %pad_maximum_fusion.1), channel_id=1, source_target_pairs={{1,0},{2,1},{3,2},{4,3},{5,4},{6,5},{7,6},{8,7},{9,8},{10,9},{11,1... | collective-permute-start | bytes 52232 | tf_op jit(solution)/shard_map/ppermute | solution.py:504
  121.1 8.9 %copy-start.5 = (bf16[34,256]{1,0:T(8,128)(2,1)}, bf16[34,256]{1,0:T(8,128)(2,1)S(1)}, u32[]{:S(2)}) copy-start(bf16[34,256]{1,0:T(8,128)(2,1)S(1)} %collective-permute-done.2.left_ref) | copy-start | bytes 52228
  121.1 8.9 %copy-start.6 = (bf16[34,256]{1,0:T(8,128)(2,1)}, bf16[34,256]{1,0:T(8,128)(2,1)S(1)}, u32[]{:S(2)}) copy-start(bf16[34,256]{1,0:T(8,128)(2,1)S(1)} %collective-permute-done.3.right_ref) | copy-start | bytes 52228
  130.0 6.3 %copy-start.7 = (f32[3,3,256]{2,1,0:T(4,128)S(1)}, f32[3,3,256]{2,1,0:T(4,128)}, u32[]{:S(2)}) copy-start(f32[3,3,256]{2,1,0:T(4,128)} %param.9) | copy-start | bytes 27652
  130.0 31.2 %all-to-all-start.3 = ((bf16[16,64,512]{2,1,0:T(8,128)(2,1)}), bf16[16,64,512]{2,1,0:T(8,128)(2,1)S(1)}, u32[]{:S(2)}, u32[]{:S(2)}) async-start(bf16[16,64,512]{2,1,0:T(8,128)(2,1)} %bitcast.19), calls=%async_computation.3 | async-start | bytes 2097152 | tf_op jit(solution)/shard_map/all_to_all | solution.py:525
